TPU v7x, 128 devices: a whole 4x4x4 slice. The times are simulated.
128 devices in a mesh: seq: 32 (over z, y_hi, x), head: 4 (over y_lo, core).
Axes of the slice: x: 4, y: 4 (y_hi: 2, y_lo: 2; y = y_hi * 2 + y_lo), z: 4, core: 2. Of those that a mesh axis runs over, the one named last changes fastest.
Arguments:
- tokens: bfloat16 [131072, 256], P('seq'), may hold values from -6 to 6
- fine_gain: float32 [256], replicated, may hold values from 0.1 to 1.9
- fine_gate: bfloat16 [256, 512], P(None, 'head'), may hold values from -0.375 to 0.375
- fine_value: bfloat16 [256, 512], P(None, 'head'), may hold values from -0.375 to 0.375
- fine_scans: bfloat16 [256, 512], replicated, may hold values from -0.375 to 0.375
- fine_steps: bfloat16 [256, 8], P(None, 'head'), may hold values from -0.375 to 0.375
- fine_kernel: float32 [4, 512], P(None, 'head'), may hold values from -3 to 3
- fine_taps: float32 [4, 512], replicated, may hold values from -3 to 3
- fine_bias: float32 [8], P('head'), may hold values from -3 to 1
- fine_decay: float32 [8], P('head'), may hold values from 7.6293945e-06 to 0.2
- fine_norm: float32 [512], P('head'), may hold values from 0.1 to 1.9
- fine_output: bfloat16 [512, 256], P('head'), may hold values from -0.25 to 0.25
- merge_weight: bfloat16 [1024, 1024], replicated, may hold values from -0.1875 to 0.1875
- coarse_gain: float32 [1024], replicated, may hold values from 0.1 to 1.9
- coarse_gate: bfloat16 [1024, 2048], P(None, 'head'), may hold values from -0.1875 to 0.1875
- coarse_value: bfloat16 [1024, 2048], P(None, 'head'), may hold values from -0.1875 to 0.1875
- coarse_scans: bfloat16 [1024, 512], replicated, may hold values from -0.1875 to 0.1875
- coarse_steps: bfloat16 [1024, 32], P(None, 'head'), may hold values from -0.1875 to 0.1875
- coarse_kernel: float32 [4, 2048], P(None, 'head'), may hold values from -3 to 3
- coarse_taps: float32 [4, 512], replicated, may hold values from -3 to 3
- coarse_bias: float32 [32], P('head'), may hold values from -3 to 1
- coarse_decay: float32 [32], P('head'), may hold values from 3.0517578e-05 to 0.2
- coarse_norm: float32 [2048], P('head'), may hold values from 0.1 to 1.9
- coarse_output: bfloat16 [2048, 1024], P('head'), may hold values from -0.125 to 0.125
Outputs:
- scene_tokens: bfloat16 [32768, 1024], P('seq', 'head')
All inputs are finite; a program needn't handle non-finite values.
Results may differ from a plain program's by a relative error of at most 0.02.
Values may be sent and summed in bfloat16 or wider, within the bound.
No kernel may reach another device: no remote copies, remote signals or barrier semaphores. Data moves between devices by JAX's collectives and lax.ppermute only.
A program may use at most 128 MiB of HBM per device.

v0:
```python
import jax
import jax.numpy as jnp
from jax import lax
from jax.experimental import pallas as pl
from jax.experimental.pallas import tpu as pltpu
from jax.sharding import Mesh
from jax.sharding import PartitionSpec as P

SEQ = ("z", "u", "x")
HEAD = ("y", "c")
ALL = ("z", "u", "x", "y", "c")
EPSILON = 1e-05
BLK = 256
BF = jnp.bfloat16
F32 = jnp.float32
NN = (((1,), (0,)), ((), ()))
NT = (((1,), (1,)), ((), ()))
TN = (((0,), (0,)), ((), ()))


def dot(a, b, dims=NN):
    return lax.dot_general(a, b, dims, preferred_element_type=F32)


def parts(x):
    hi = x.astype(BF).astype(F32)
    rest = x - hi
    mid = rest.astype(BF).astype(F32)
    low = rest - mid
    return jnp.concatenate([hi, mid, low, jnp.zeros_like(x)], 0).astype(BF)


def decay_rows(row):
    hi = row.astype(BF).astype(F32)
    rest = row - hi
    mid = rest.astype(BF).astype(F32)
    low = rest - mid
    return jnp.concatenate([hi, mid, low, jnp.zeros((13, row.shape[1]), F32)], 0).astype(BF)


def of_rows(rows):
    rows = rows.astype(F32)
    return rows[0:1] + rows[1:2] + rows[2:3]


def iota(shape, dim):
    return lax.broadcasted_iota(jnp.int32, shape, dim)


def head_sel(width):
    return iota((8, width), 0) == iota((8, width), 1) // 64


def expander(width):
    r, lane = iota((32, width), 0), iota((32, width), 1)
    return jnp.where((r < 24) & (r % 8 == lane // 64), 1.0, 0.0).astype(BF)


def upper():
    return jnp.where(iota((BLK, BLK), 0) <= iota((BLK, BLK), 1), 1.0, 0.0).astype(BF)


def silu(v):
    h = v * 0.5
    return h + h * jnp.tanh(h)


def softplus(v):
    return jnp.maximum(v, 0.0) + jnp.log1p(jnp.exp(-jnp.abs(v)))


def rms(x, gain):
    x = x.astype(F32)
    return (x * lax.rsqrt(jnp.mean(x * x, axis=-1, keepdims=True) + EPSILON) * gain).astype(BF)


def cumulate(logs, tri):
    s = dot(parts(logs), tri)
    return s[0:8] + s[8:16] + s[16:24]


def convolve(cv, act, taps, width, length, step=64):
    for c in range(width // 128):
        cols = slice(c * 128, (c + 1) * 128)
        for r in range(length // step):
            total = cv[pl.ds(13 + r * step, step), cols] * taps[0:1, cols]
            for k in range(1, 4):
                total = total + cv[pl.ds(13 + k + r * step, step), cols] * taps[k : k + 1, cols]
            act[pl.ds(r * step, step), cols] = silu(total).astype(BF)


def rounded(x):
    return x.astype(BF).astype(F32)


def state_chunk(x, rim, gain, wv, wb, wst, kv, ks, bias, decay, taps, cv, act):
    taps[:, 0:128] = kv[...]
    taps[:, 128:384] = ks[...]
    normed = rms(x, gain[...])
    before = rms(rim, gain[...])
    cv[0:16, 0:128] = rounded(dot(before, wv[...]))
    cv[0:16, 128:384] = rounded(dot(before, wb[...]))
    cv[16:1040, 0:128] = rounded(dot(normed, wv[...]))
    cv[16:1040, 128:384] = rounded(dot(normed, wb[...]))
    convolve(cv, act, taps, 384, 1024)
    raw = dot(wst[...], normed, NT)
    dt = softplus(raw + bias[:, 0:1])
    logs = -dt * decay[:, 0:1]
    tri = upper()
    carry = jnp.zeros((8, 1), F32)
    pieces = []
    for b in range(4):
        piece = cumulate(logs[:, b * BLK : (b + 1) * BLK], tri) + carry
        carry = piece[:, BLK - 1 : BLK]
        pieces.append(piece)
    cum = jnp.concatenate(pieces, 1)
    tail = jnp.exp(carry - cum) * dt
    spread = dot(parts(tail), expander(128), TN)
    scaled = (act[:, 0:128].astype(F32) * spread).astype(BF)
    local = dot(act[:, 128:384], scaled, TN)
    total = jnp.sum(
        jnp.where(head_sel(128), jnp.broadcast_to(carry, (8, 128)), 0.0), axis=0, keepdims=True
    )
    return local, total


def later_chunks_kernel(x, rim, gain, wv, wb, wst, kv, ks, bias, decay, local, total, taps, cv, act):
    state, logs = state_chunk(
        x[...], rim[...], gain, wv, wb, wst, kv, ks, bias, decay, taps, cv, act
    )
    local[0] = state
    total[0] = jnp.broadcast_to(logs, (8, 128))


def first_chunk_kernel(
    x, rim, gain, wv, wb, wst, kv, ks, bias, decay, later, later_total,
    local, total, whole, whole_total, message, taps, cv, act,
):
    state, logs = state_chunk(
        x[...], rim[...], gain, wv, wb, wst, kv, ks, bias, decay, taps, cv, act
    )
    local[...] = state
    total[...] = jnp.broadcast_to(logs, (8, 128))
    for j in range(3):
        piece = later_total[j, 0:1, :]
        state = state * jnp.exp(piece) + later[j]
        logs = logs + piece
    whole[...] = state
    whole_total[...] = jnp.broadcast_to(logs, (8, 128))
    message[0:256, :] = state.astype(BF)
    message[256:272, :] = decay_rows(logs)


def sds(shape, dtype=F32):
    return jax.ShapeDtypeStruct(shape, dtype)


def whole_spec(shape):
    return pl.BlockSpec(shape, lambda *_: (0,) * len(shape))


PARAMS = pltpu.CompilerParams(dimension_semantics=("arbitrary",), vmem_limit_bytes=48 << 20)


def fine_states(tokens, rim, gain, wv, scans, wst, kv, ks, bias, decay):
    common = [
        whole_spec((1, 256)),
        whole_spec((256, 128)),
        whole_spec((256, 256)),
        whole_spec((8, 256)),
        whole_spec((4, 128)),
        whole_spec((4, 256)),
        whole_spec((8, 128)),
        whole_spec((8, 128)),
    ]
    scratch = [
        pltpu.VMEM((4, 384), F32),
        pltpu.VMEM((1040, 384), F32),
        pltpu.VMEM((1024, 384), BF),
    ]
    later, later_total = pl.pallas_call(
        later_chunks_kernel,
        grid=(3,),
        in_specs=[
            pl.BlockSpec((1024, 256), lambda i: (i + 1, 0)),
            pl.BlockSpec((16, 256), lambda i: ((i + 1) * 64 - 1, 0)),
        ]
        + common,
        out_specs=[
            pl.BlockSpec((1, 256, 128), lambda i: (i, 0, 0)),
            pl.BlockSpec((1, 8, 128), lambda i: (i, 0, 0)),
        ],
        out_shape=[sds((3, 256, 128)), sds((3, 8, 128))],
        scratch_shapes=scratch,
        compiler_params=PARAMS,
        name="later_chunks",
    )(tokens, tokens, gain, wv, scans, wst, kv, ks, bias, decay)
    first = pl.pallas_call(
        first_chunk_kernel,
        grid=(1,),
        in_specs=[pl.BlockSpec((1024, 256), lambda i: (0, 0)), whole_spec((16, 256))]
        + common
        + [whole_spec((3, 256, 128)), whole_spec((3, 8, 128))],
        out_specs=[
            whole_spec((256, 128)),
            whole_spec((8, 128)),
            whole_spec((256, 128)),
            whole_spec((8, 128)),
            whole_spec((272, 128)),
        ],
        out_shape=[
            sds((256, 128)),
            sds((8, 128)),
            sds((256, 128)),
            sds((8, 128)),
            sds((272, 128), BF),
        ],
        scratch_shapes=scratch,
        compiler_params=PARAMS,
        name="first_chunk",
    )(tokens, rim, gain, wv, scans, wst, kv, ks, bias, decay, later, later_total)
    return later, later_total, first


def combine(i, count, own, own_total, prior, prior_total, received):
    state = jnp.zeros_like(own)
    logs = jnp.zeros_like(own_total)
    zero = jnp.zeros((), F32)
    got = [(r[0:256, :].astype(F32), of_rows(r[256:272, :])) for r in received]
    for k in range(count - 1, 0, -1):
        s, l = got[k - 1]
        valid = i >= k
        state = jnp.where(valid, state * jnp.exp(l) + s, state)
        logs = jnp.where(valid, logs + l, logs)
    new_prior = state * jnp.exp(prior_total) + prior
    new_prior_total = logs + prior_total
    state = state * jnp.exp(own_total) + own
    logs = logs + own_total
    for m in range(1, count):
        s, l = got[count - m - 1]
        valid = i + m < count
        state = jnp.where(valid, state * jnp.exp(l) + s, state)
        logs = jnp.where(valid, logs + l, logs)
    return new_prior, new_prior_total, state, logs


def middle_kernel(count, pos, own, own_total, prior, prior_total, *refs):
    received, (np_ref, npt_ref, ns_ref, nst_ref, message) = refs[: count - 1], refs[count - 1 :]
    p, pt, s, st = combine(
        pos[0], count, own[...], own_total[0:1, :], prior[...], prior_total[0:1, :], received
    )
    np_ref[...] = p
    npt_ref[...] = jnp.broadcast_to(pt, (8, 128))
    ns_ref[...] = s
    nst_ref[...] = jnp.broadcast_to(st, (8, 128))
    message[0:256, :] = s.astype(BF)
    message[256:272, :] = decay_rows(st)


SMEM = pl.BlockSpec(memory_space=pltpu.SMEM)
VM = pl.BlockSpec(memory_space=pltpu.VMEM)


def middle_stage(count, pos, own, own_total, prior, prior_total, received, name):
    return pl.pallas_call(
        lambda *refs: middle_kernel(count, *refs),
        in_specs=[SMEM] + [VM] * (4 + len(received)),
        out_specs=[VM] * 5,
        out_shape=[
            sds((256, 128)),
            sds((8, 128)),
            sds((256, 128)),
            sds((8, 128)),
            sds((272, 128), BF),
        ],
        name=name,
    )(pos, own, own_total, prior, prior_total, *received)


def last_kernel(pos, own, own_total, prior, prior_total, r1, r2, r3, l0, t0, later, later_total,
                o0, o1, o2, o3, sub):
    p, _, _, _ = combine(
        pos[0], 4, own[...], own_total[0:1, :], prior[...], prior_total[0:1, :], (r1, r2, r3)
    )
    sub[0] = p
    p = p * jnp.exp(t0[0:1, :]) + l0[...]
    sub[1] = p
    for j in range(2):
        p = p * jnp.exp(later_total[j, 0:1, :]) + later[j]
        sub[j + 2] = p
    h = pos[1]
    for k, out in enumerate((o0, o1, o2, o3)):
        out[...] = sub[h ^ k].astype(BF)


def last_stage(pos, own, own_total, prior, prior_total, received, l0, t0, later, later_total):
    return pl.pallas_call(
        last_kernel,
        in_specs=[SMEM] + [VM] * 11,
        out_specs=[VM] * 4,
        out_shape=[sds((256, 128), BF)] * 4,
        scratch_shapes=[pltpu.VMEM((4, 256, 128), F32)],
        name="chain_last",
    )(pos, own, own_total, prior, prior_total, *received, l0, t0, later, later_total)


def scan_block(
    normed, wg, wv, ws, wst, taps, bias, decay, first, rim_normed,
    lead, tail_out, maps_out, cv, act, sc, run, run_log,
):
    @pl.when(first)
    def _():
        before = rim_normed()
        cv[0:16, 0:512] = rounded(dot(before, wv[...]))
        cv[0:16, 512:1024] = rounded(dot(before, ws[...]))
        run[...] = jnp.zeros_like(run)
        run_log[...] = jnp.zeros_like(run_log)

    cv[16:272, 0:512] = rounded(dot(normed, wv[...]))
    cv[16:272, 512:1024] = rounded(dot(normed, ws[...]))
    convolve(cv, act, taps, 1024, BLK)
    cv[0:16, :] = cv[256:272, :]
    raw = dot(wst[...], normed, NT)
    dt = softplus(raw + bias[...])
    logs = -dt * decay[...]
    cum = cumulate(logs, upper())
    last = cum[:, BLK - 1 : BLK]
    before_log = run_log[:, 0:1]
    stacked = jnp.concatenate(
        [jnp.exp(cum), jnp.exp(cum + before_log), jnp.exp(last - cum) * dt], 1
    )
    spread = dot(parts(stacked), expander(512), TN)
    run_log[...] = run_log[...] + last
    columns = dot(parts(cum), jnp.where(
        (iota((32, 128), 0) < 24) & (iota((32, 128), 0) % 8 == iota((32, 128), 1)), 1.0, 0.0
    ).astype(BF), TN)
    rows = cum - jnp.log(dt)
    in_map = act[:, 512:768]
    out_map = act[:, 768:1024]
    maps_out[...] = out_map
    sc[...] = dot(out_map, in_map, NT)
    carried = dot(out_map, run[...].astype(BF))
    low_tri = iota((128, 128), 0) >= iota((128, 128), 1)
    lane_low = iota((BLK, 128), 1) < 64
    for p in range(4):
        cols = slice(p * 128, (p + 1) * 128)
        vals = act[:, cols].astype(F32)
        v0 = jnp.where(lane_low, vals, 0.0).astype(BF)
        v1 = jnp.where(lane_low, 0.0, vals).astype(BF)
        upper_w, lower_w = [], []
        for h in (2 * p, 2 * p + 1):
            c0, c1 = columns[0:128, h : h + 1], columns[128:256, h : h + 1]
            r0, r1 = rows[h : h + 1, 0:128], rows[h : h + 1, 128:256]
            upper_w.append(
                (sc[0:128, 0:128] * jnp.exp(jnp.where(low_tri, c0 - r0, -jnp.inf))).astype(BF)
            )
            lower_w.append((sc[128:256, 0:128] * jnp.exp(c1 - r0)).astype(BF))
            lower_w.append(
                (sc[128:256, 128:256] * jnp.exp(jnp.where(low_tri, c1 - r1, -jnp.inf))).astype(BF)
            )
        top = dot(
            jnp.concatenate(upper_w, 1), jnp.concatenate([v0[0:128], v1[0:128]], 0)
        )
        bottom = dot(jnp.concatenate(lower_w, 1), jnp.concatenate([v0, v1], 0))
        gate = silu(rounded(dot(normed, wg[:, cols])))
        lead[0:128, cols] = (top + spread[0:128, cols] * carried[0:128, cols]) * gate[0:128]
        lead[128:256, cols] = (
            bottom + spread[128:256, cols] * carried[128:256, cols]
        ) * gate[128:256]
        tail_out[:, cols] = spread[256:512, cols] * gate
        scaled = (vals * spread[512:768, cols]).astype(BF)
        run[:, cols] = run[:, cols] * spread[255:256, cols] + dot(in_map, scaled, TN)


SCAN_SCRATCH = [
    pltpu.VMEM((272, 1024), F32),
    pltpu.VMEM((BLK, 1024), BF),
    pltpu.VMEM((BLK, BLK), F32),
    pltpu.VMEM((256, 512), F32),
    pltpu.VMEM((8, 128), F32),
]


def fine_main_kernel(
    h, x, rim_here, rim_there, gain, ws, ks, p0, p1, p2, p3, f0, f1, f2, f3,
    lead, tail_out, maps_out,
    wg, wv, wst, taps, bias, decay, cv, act, sc, run, run_log,
):
    first = pl.program_id(0) == 0

    @pl.when(first)
    def _():
        taps[:, 512:1024] = ks[...]
        for j, (p, f) in enumerate(((p0, f0), (p1, f1), (p2, f2), (p3, f3))):
            cols = slice(j * 128, (j + 1) * 128)
            wg[:, cols] = p[0:256, 0:128]
            wv[:, cols] = p[0:256, 128:256]
            taps[:, cols] = f[0:4, 0:128]
            wst[2 * j : 2 * j + 2, :] = f[8:10, :]
            bias[2 * j : 2 * j + 2, :] = f[10:12, 0:128]
            decay[2 * j : 2 * j + 2, :] = f[12:14, 0:128]

    def rim_normed():
        rim = jnp.where(h[0] == 0, rim_there[...].astype(F32), rim_here[...].astype(F32))
        return rms(rim, gain[...])

    scan_block(
        rms(x[...], gain[...]), wg, wv, ws, wst[...].astype(BF), taps, bias[:, 0:1], decay[:, 0:1],
        first, rim_normed, lead, tail_out, maps_out, cv, act, sc, run, run_log,
    )


def fine_main(h, tokens, rim, gain, scans, ks, packs, smalls):
    return pl.pallas_call(
        fine_main_kernel,
        grid_spec=pltpu.PrefetchScalarGridSpec(
            num_scalar_prefetch=1,
            grid=(4,),
            in_specs=[
                pl.BlockSpec((BLK, 256), lambda i, h: (h[0] * 4 + i, 0)),
                pl.BlockSpec((16, 256), lambda i, h: (jnp.maximum(h[0] * 64 - 1, 0), 0)),
                whole_spec((16, 256)),
                whole_spec((1, 256)),
                whole_spec((256, 512)),
                whole_spec((4, 512)),
            ]
            + [whole_spec((384, 256))] * 4
            + [whole_spec((16, 256))] * 4,
            out_specs=[
                pl.BlockSpec((BLK, 512), lambda i, h: (i, 0)),
                pl.BlockSpec((BLK, 512), lambda i, h: (i, 0)),
                pl.BlockSpec((BLK, 256), lambda i, h: (i, 0)),
            ],
            scratch_shapes=[
                pltpu.VMEM((256, 512), BF),
                pltpu.VMEM((256, 512), BF),
                pltpu.VMEM((8, 256), F32),
                pltpu.VMEM((4, 1024), F32),
                pltpu.VMEM((8, 128), F32),
                pltpu.VMEM((8, 128), F32),
            ]
            + SCAN_SCRATCH,
        ),
        out_shape=[sds((1024, 512)), sds((1024, 512)), sds((1024, 256), BF)],
        compiler_params=PARAMS,
        name="fine_main",
    )(h, tokens, tokens, rim, gain, scans, ks, *packs, *smalls)


def fine_close_kernel(
    h, lead, tail, maps, x, s0, s1, s2, s3, w0, w1, w2, w3, f0, f1, f2, f3, merge,
    merged, end_rows, hidden,
):
    i = pl.program_id(0)
    gated = []
    for j, s in enumerate((s0, s1, s2, s3)):
        cols = slice(j * 128, (j + 1) * 128)
        gated.append(lead[:, cols] + tail[:, cols] * dot(maps[...], s[...]))
    squares = sum(jnp.sum(g * g, axis=1, keepdims=True) for g in gated)
    factor = lax.rsqrt(squares / 512.0 + EPSILON)
    out = x[...].astype(F32)
    total = None
    for g, w, f in zip(gated, (w0, w1, w2, w3), (f0, f1, f2, f3)):
        piece = dot((g * factor * f[4:5, 0:128]).astype(BF), w[...])
        total = piece if total is None else total + piece
    start = pl.multiple_of(i * BLK, BLK)
    hidden[0, pl.ds(start, BLK), :] = rounded(out[:, 0:128] + total[:, 0:128])
    hidden[1, pl.ds(start, BLK), :] = rounded(out[:, 128:256] + total[:, 128:256])

    @pl.when(i == pl.num_programs(0) - 1)
    def _():
        total = None
        for odd in range(2):
            for half in range(2):
                rows = hidden[half, pl.ds(odd, 512, stride=2), :].reshape(8, 2, 32, 128)
                for line in range(2):
                    tile = rows[:, line].reshape(256, 128).astype(BF)
                    at = (2 * line + odd) * 256 + half * 128
                    piece = dot(tile, merge[at : at + 128, :])
                    total = piece if total is None else total + piece
        result = total.astype(BF)
        merged[...] = result
        end_rows[...] = result[240:256]


def fine_close(h, lead, tail, maps, tokens, states, packs, smalls, merge):
    return pl.pallas_call(
        fine_close_kernel,
        grid_spec=pltpu.PrefetchScalarGridSpec(
            num_scalar_prefetch=1,
            grid=(4,),
            in_specs=[
                pl.BlockSpec((BLK, 512), lambda i, h: (i, 0)),
                pl.BlockSpec((BLK, 512), lambda i, h: (i, 0)),
                pl.BlockSpec((BLK, 256), lambda i, h: (i, 0)),
                pl.BlockSpec((BLK, 256), lambda i, h: (h[0] * 4 + i, 0)),
            ]
            + [whole_spec((256, 128))] * 4
            + [pl.BlockSpec((128, 256), lambda i, h: (2, 0))] * 4
            + [whole_spec((16, 256))] * 4
            + [whole_spec((1024, 1024))],
            out_specs=[whole_spec((256, 1024)), whole_spec((16, 1024))],
            scratch_shapes=[pltpu.VMEM((2, 1024, 128), F32)],
        ),
        out_shape=[sds((256, 1024), BF), sds((16, 1024), BF)],
        compiler_params=PARAMS,
        name="fine_close",
    )(h, lead, tail, maps, tokens, *states, *packs, *smalls, merge)


def coarse_main_kernel(
    pos, q0, q1, q2, q3, ra, rb, rc, gain, wg, wv, ws, wst, kv, ks, bias, decay,
    lead, tail_out, maps_out, share, message,
    xs, sems, taps, cv, act, sc, run, run_log,
):
    i = pl.program_id(0)
    first = i == 0
    h = pos[0]

    @pl.when(first)
    def _():
        copies = [
            pltpu.make_async_copy(q, xs.at[h ^ k], sems.at[k])
            for k, q in enumerate((q0, q1, q2, q3))
        ]
        for copy in copies:
            copy.start()
        taps[:, 0:512] = kv[...]
        taps[:, 512:1024] = ks[...]
        for copy in copies:
            copy.wait()

    def rim_normed():
        rim = ra[...].astype(F32) + rb[...].astype(F32) + rc[...].astype(F32)
        return rms(rim, gain[...])

    share[...] = xs[i, :, pl.ds(pl.multiple_of(h * 256, 256), 256)]
    scan_block(
        rms(xs[i], gain[...]), wg, wv, ws, wst[...], taps, bias[:, 0:1], decay[:, 0:1],
        first, rim_normed, lead, tail_out, maps_out, cv, act, sc, run, run_log,
    )

    @pl.when(i == pl.num_programs(0) - 1)
    def _():
        total = jnp.broadcast_to(run_log[:, 0:1], (8, 512))
        row = jnp.sum(jnp.where(head_sel(512), total, 0.0), axis=0, keepdims=True)
        extra = decay_rows(row)
        for n in range(16):
            for half in range(2):
                cols = slice(half * 256, (half + 1) * 256)
                message[2 * n + half, 0:16, :] = run[n * 16 : (n + 1) * 16, cols].astype(BF)
                message[2 * n + half, 16:32, :] = extra[:, cols]


def single(shape):
    return pl.BlockSpec(shape, lambda *_: (0,) * len(shape), pipeline_mode=pl.Buffered(1))


ANY = pl.BlockSpec(memory_space=pl.ANY)


def coarse_main(pos, pieces, rims, gain, wg, wv, ws, wst, kv, ks, bias, decay):
    return pl.pallas_call(
        coarse_main_kernel,
        grid=(4,),
        in_specs=[SMEM]
        + [ANY] * 4
        + [whole_spec((16, 1024))] * 3
        + [
            whole_spec((1, 1024)),
            single((1024, 512)),
            single((1024, 512)),
            single((1024, 512)),
            whole_spec((8, 1024)),
            whole_spec((4, 512)),
            whole_spec((4, 512)),
            whole_spec((8, 128)),
            whole_spec((8, 128)),
        ],
        out_specs=[
            pl.BlockSpec((BLK, 512), lambda i: (i, 0)),
            pl.BlockSpec((BLK, 512), lambda i: (i, 0)),
            pl.BlockSpec((BLK, 256), lambda i: (i, 0)),
            pl.BlockSpec((BLK, 256), lambda i: (i, 0)),
            whole_spec((32, 32, 256)),
        ],
        out_shape=[
            sds((1024, 512)),
            sds((1024, 512)),
            sds((1024, 256), BF),
            sds((1024, 256), BF),
            sds((32, 32, 256), BF),
        ],
        scratch_shapes=[
            pltpu.VMEM((4, 256, 1024), BF),
            pltpu.SemaphoreType.DMA((4,)),
            pltpu.VMEM((4, 1024), F32),
        ]
        + SCAN_SCRATCH,
        compiler_params=PARAMS,
        name="coarse_main",
    )(pos, *pieces, *rims, gain, wg, wv, ws, wst, kv, ks, bias, decay)


def prefix_kernel(got, out):
    state = jnp.zeros((16, 256), F32)
    for d in range(32):
        out[d] = state.astype(BF)
        state = state * jnp.exp(of_rows(got[d, 16:32, :])) + got[d, 0:16, :].astype(F32)


def prefix(got):
    return pl.pallas_call(
        prefix_kernel,
        in_specs=[VM],
        out_specs=VM,
        out_shape=sds((32, 16, 256), BF),
        name="prefix",
    )(got)


def coarse_close_kernel(pos, lead, tail, maps, got, norm, wo, kk, ks, sk, ss, squares, state):
    @pl.when(pl.program_id(0) == 0)
    def _():
        for n in range(16):
            for half in range(2):
                cols = slice(half * 256, (half + 1) * 256)
                state[n * 16 : (n + 1) * 16, cols] = got[2 * n + half]

    gated = lead[...] + tail[...] * dot(maps[...], state[...])
    sq = gated * gated
    hi = sq.astype(BF)
    low = (sq - hi.astype(F32)).astype(BF)
    ones = jnp.ones((8, 512), BF)
    squares[...] = dot(ones, hi, NT) + dot(ones, low, NT)
    scaled = (gated * norm[...]).astype(BF)
    h = pos[0]
    for k, out in enumerate((kk, sk, ks, ss)):
        at = pl.multiple_of((h ^ k) * 256, 256)
        out[...] = dot(scaled, wo[:, pl.ds(at, 256)]).astype(BF)


def coarse_close(pos, lead, tail, maps, got, norm, wo):
    rows = pl.BlockSpec((BLK, 256), lambda i: (i, 0))
    return pl.pallas_call(
        coarse_close_kernel,
        grid=(4,),
        in_specs=[
            SMEM,
            pl.BlockSpec((BLK, 512), lambda i: (i, 0)),
            pl.BlockSpec((BLK, 512), lambda i: (i, 0)),
            rows,
            whole_spec((32, 16, 256)),
            whole_spec((1, 512)),
            single((512, 1024)),
        ],
        out_specs=[rows] * 4 + [pl.BlockSpec((8, BLK), lambda i: (0, i))],
        out_shape=[sds((1024, 256), BF)] * 4 + [sds((8, 1024))],
        scratch_shapes=[pltpu.VMEM((256, 512), BF)],
        compiler_params=PARAMS,
        name="coarse_close",
    )(pos, lead, tail, maps, got, norm, wo)


def final_kernel(share, kk, sk, far, sq, sq_far, out):
    factor = lax.rsqrt((sq[...] + sq_far[...]) / 2048.0 + EPSILON)
    pick = jnp.where(iota((32, 256), 0) % 8 == 0, 1.0, 0.0).astype(BF)
    spread = dot(parts(factor), pick, TN)
    total = kk[...].astype(F32) + sk[...].astype(F32) + far[...].astype(F32)
    out[...] = (share[...].astype(F32) + total * spread).astype(BF)


def final(share, kk, sk, far, sq, sq_far):
    return pl.pallas_call(
        final_kernel,
        in_specs=[VM] * 6,
        out_specs=VM,
        out_shape=sds((1024, 256), BF),
        name="final",
    )(share, kk, sk, far, sq, sq_far)


def passed(x, axes, pairs):
    return lax.ppermute(x, axes, pairs)


def swapped(x, mask):
    return passed(x, HEAD, [(j, j ^ mask) for j in range(4)])


def round_of(x, axis):
    return [passed(x, axis, [(j, (j + k) % 4) for j in range(4)]) for k in (1, 2, 3)]


def lanes(v):
    return jnp.broadcast_to(v[:, None], (v.shape[0], 128))


def shards(
    tokens, fine_gain, fine_gate, fine_value, fine_scans, fine_steps, fine_kernel, fine_taps,
    fine_bias, fine_decay, fine_norm, fine_output, merge_weight, coarse_gain, coarse_gate,
    coarse_value, coarse_scans, coarse_steps, coarse_kernel, coarse_taps, coarse_bias,
    coarse_decay, coarse_norm, coarse_output,
):
    head = lax.axis_index(HEAD).astype(jnp.int32)

    def position(axis):
        return jnp.stack([lax.axis_index(axis).astype(jnp.int32), head])

    here = head[None]
    rim = passed(tokens[4080:], SEQ, [(i, i + 1) for i in range(31)])

    pack = jnp.concatenate([jnp.concatenate([fine_gate, fine_value], 1), fine_output], 0)
    zeros = jnp.zeros((4, 128), F32)
    small = jnp.concatenate(
        [
            jnp.concatenate([fine_kernel, zeros], 1),
            jnp.concatenate([fine_norm[None], jnp.zeros((1, 128), F32)], 1),
            jnp.zeros((3, 256), F32),
            fine_steps.T.astype(F32),
            jnp.broadcast_to(fine_bias[:, None], (2, 256)),
            jnp.broadcast_to(fine_decay[:, None], (2, 256)),
            jnp.zeros((2, 256), F32),
        ],
        0,
    )
    packs = [pack] + [swapped(pack, m) for m in (1, 2, 3)]
    smalls = [small] + [swapped(small, m) for m in (1, 2, 3)]

    gain = fine_gain[None]
    wst = jnp.concatenate([fine_steps.T, jnp.zeros((6, 256), BF)], 0)
    bias = jnp.concatenate([lanes(fine_bias), jnp.zeros((6, 128), F32)], 0)
    decay = jnp.concatenate([lanes(fine_decay), jnp.zeros((6, 128), F32)], 0)
    later, later_total, (l0, t0, own, own_total, message) = fine_states(
        tokens, rim, gain, fine_value, fine_scans, wst, fine_kernel, fine_taps, bias, decay
    )
    got = round_of(message, "x")
    lead, tail, maps = fine_main(here, tokens, rim, gain, fine_scans, fine_taps, packs, smalls)
    prior, prior_total = jnp.zeros((256, 128), F32), jnp.zeros((8, 128), F32)
    prior, prior_total, own, own_total, message = middle_stage(
        4, position("x"), own, own_total, prior, prior_total, got, "chain_x"
    )
    got = [passed(message, "u", [(0, 1), (1, 0)])]
    prior, prior_total, own, own_total, message = middle_stage(
        2, position("u"), own, own_total, prior, prior_total, got, "chain_u"
    )
    got = round_of(message, "z")
    subs = last_stage(
        position("z"), own, own_total, prior, prior_total, got, l0, t0, later, later_total
    )
    states = [subs[0]] + [swapped(subs[m], m) for m in (1, 2, 3)]
    merged, end_rows = fine_close(
        here, lead, tail, maps, tokens, states, packs, smalls, merge_weight
    )

    across = swapped(merged, 2)
    beside = swapped(merged, 1)
    rim_a = passed(end_rows, ALL, [(4 * s + 3, 4 * s + 4) for s in range(31)])
    rim_b = passed(end_rows, ALL, [(4 * s + 3, 4 * s + 7) for s in range(31)])
    rim_c = swapped(rim_a + rim_b, 1)
    both = swapped(across, 1)
    lead, tail, maps, share, message = coarse_main(
        here,
        (merged, beside, across, both),
        (rim_a, rim_b, rim_c),
        coarse_gain[None],
        coarse_gate,
        coarse_value,
        coarse_scans,
        coarse_steps.T,
        coarse_kernel,
        coarse_taps,
        lanes(coarse_bias),
        lanes(coarse_decay),
    )
    got = lax.all_to_all(message, SEQ, split_axis=0, concat_axis=0, tiled=True)
    got = lax.all_to_all(prefix(got), SEQ, split_axis=0, concat_axis=0, tiled=True)
    kk, ks, sk, ss, squares = coarse_close(
        here, lead, tail, maps, got, coarse_norm[None], coarse_output
    )
    from_ss = swapped(ss, 1)
    from_sk = swapped(sk, 1)
    squares = squares + swapped(squares, 1)
    far = (ks.astype(F32) + from_ss.astype(F32)).astype(BF)
    return final(share, kk, from_sk, swapped(far, 2), squares, swapped(squares, 2))


def solution(mesh):
    finer = Mesh(mesh.devices.reshape(4, 2, 4, 2, 2), ALL)
    cols = P(None, HEAD)
    return jax.shard_map(
        shards,
        mesh=finer,
        in_specs=(
            P(SEQ, None), P(), cols, cols, P(), cols, cols, P(), P(HEAD), P(HEAD), P(HEAD),
            P(HEAD, None), P(), P(), cols, cols, P(), cols, cols, P(), P(HEAD), P(HEAD), P(HEAD),
            P(HEAD, None),
        ),
        out_specs=P(SEQ, HEAD),
        check_vma=False,
    )
```

profile of v0, /device:TPU:1, one launch (start us, length us, event | category | flops | bytes accessed | tf_op | source)
XLA Modules:
  0.0 191.9 jit_solution(13164658372225810802)
XLA Ops:
  0.0 0.7 slice.3
  0.7 3.9 %collective-permute-start = (bf16[16,256]{1,0:T(8,128)(2,1)S(1)}, bf16[16,256]{1,0:T(8,128)(2,1)S(1)}, u32[]{:S(2)}, u32[]{:S(2)}) collective-permute-start(bf16[16,256]{1,0:T(8,128)(2,1)S(1)} %slice.3), channel_id=1, source_target_pairs={{0,4},{4,8},{8,12},{12,16},{16,20},{20,24},{24,28},{28,32},{32,36}... | collective-permute-start | bytes 24584 | tf_op jit(solution)/shard_map/ppermute | solution.py:684
  4.6 0.9 pad_maximum_fusion.p0.w0
  5.6 2.2 %collective-permute-start.3 = (bf16[384,256]{1,0:T(8,128)(2,1)S(1)}, bf16[384,256]{1,0:T(8,128)(2,1)S(1)}, u32[]{:S(2)}, u32[]{:S(2)}) collective-permute-start(bf16[384,256]{1,0:T(8,128)(2,1)S(1)} %pad_maximum_fusion.p0.w0), channel_id=1, source_target_pairs={{0,3},{1,2},{2,1},{3,0},{4,7},{5,6},{6,5},{7,4},{8,11},{9,10},{10,... | collective-permute-start | bytes 589832 | tf_op jit(solution)/shard_map/ppermute | solution.py:684
  7.8 0.7 concatenate.34
  8.4 0.7 concatenate.36
  9.1 0.7 concatenate.33.wst
  9.9 1.6 copy-done
  11.5 0.9 copy-done.1
  12.5 0.8 copy-done.9
  13.3 0.7 copy-done.17
  14.0 0.7 copy-done.21
  14.7 0.7 copy-done.24
  15.4 8.1 %later_chunks.1 = (f32[3,256,128]{2,1,0:T(8,128)S(1)}, f32[3,8,128]{2,1,0:T(8,128)S(1)}) custom-call(bf16[4096,256]{1,0:T(8,128)(2,1)S(1)} %copy-done, bf16[4096,256]{1,0:T(8,128)(2,1)S(1)} %copy-done, f32[1,256]{1,0:T(1,128)S(1)} %bitcast.12, bf16[256,128]{1,0:T(8,128)(2,1)S(1)} %copy-done.9, bf16[256,512]{1,0:T(8,128)(2,1)S(1)} %copy-done.1, ...), custom_call_target="tpu_custom_call" | custom-call | tf_op jit(solution)/shard_map/later_chunks/pallas_call | solution.py:181
  23.6 2.7 %first_chunk.1 = (f32[256,128]{1,0:T(8,128)S(1)}, f32[8,128]{1,0:T(8,128)S(1)}, f32[256,128]{1,0:T(8,128)S(1)}, f32[8,128]{1,0:T(8,128)S(1)}, bf16[272,128]{1,0:T(8,128)(2,1)S(1)}) custom-call(bf16[4096,256]{1,0:T(8,128)(2,1)S(1)} %copy-done, bf16[16,256]{1,0:T(8,128)(2,1)S(1)} %collective-permute-done.rim_there.rim, f32[1,256]{1,0:T(1,128)S(1)} %bitcast.13, ...), custom_call_target="tpu_custom_call" | custom-call | tf_op jit(solution)/shard_map/first_chunk/pallas_call | solution.py:198
  26.3 0.6 copy-done.15
  27.0 0.6 copy-done.16
  28.2 0.6 copy-done.30
  28.8 3.2 %collective-permute-start.9 = (bf16[272,128]{1,0:T(8,128)(2,1)S(1)}, bf16[272,128]{1,0:T(8,128)(2,1)S(1)}, u32[]{:S(2)}, u32[]{:S(2)}) collective-permute-start(bf16[272,128]{1,0:T(8,128)(2,1)S(1)} %get-tuple-element.48), channel_id=1, source_target_pairs={{0,12},{4,0},{8,4},{12,8},{1,13},{5,1},{9,5},{13,9},{2,14},{6,2},{... | collective-permute-start | bytes 208904 | tf_op jit(solution)/shard_map/ppermute | solution.py:684
  32.6 0.7 pad_add_fusion.2.refs_0_
  33.2 1.9 collective-permute-done.9.refs_7_
  35.1 2.1 %collective-permute-done.8.refs_6_ = bf16[272,128]{1,0:T(8,128)(2,1)S(1)} collective-permute-done((bf16[272,128]{1,0:T(8,128)(2,1)S(1)}, bf16[272,128]{1,0:T(8,128)(2,1)S(1)}, u32[]{:S(2)}, u32[]{:S(2)}) %collective-permute-start.8) | collective-permute-done | bytes 69664 | tf_op jit(solution)/shard_map/ppermute | solution.py:684
  37.2 1.2 collective-permute-done.7.refs_5_
  38.5 0.6 broadcast_in_dim.34.refs_4_
  39.1 0.7 broadcast_in_dim.33.refs_3_
  39.8 1.9 chain_x.1
  41.7 3.0 %collective-permute-start.10 = (bf16[272,128]{1,0:T(8,128)(2,1)}, bf16[272,128]{1,0:T(8,128)(2,1)S(1)}, u32[]{:S(2)}, u32[]{:S(2)}) collective-permute-start(bf16[272,128]{1,0:T(8,128)(2,1)} %get-tuple-element.53), channel_id=1, source_target_pairs={{0,16},{16,0},{1,17},{17,1},{2,18},{18,2},{3,19},{19,3},{4,20},{20... | collective-permute-start | bytes 208904 | tf_op jit(solution)/shard_map/ppermute | solution.py:684
  44.7 0.6 pad_add_fusion.1.refs_0_
  45.4 1.3 collective-permute-done.10.refs_5_
  46.6 0.6 copy-done.41
  47.2 1.8 chain_u.1
  49.0 3.7 %collective-permute-start.13 = (bf16[272,128]{1,0:T(8,128)(2,1)}, bf16[272,128]{1,0:T(8,128)(2,1)S(1)}, u32[]{:S(2)}, u32[]{:S(2)}) collective-permute-start(bf16[272,128]{1,0:T(8,128)(2,1)} %get-tuple-element.58), channel_id=1, source_target_pairs={{0,96},{32,0},{64,32},{96,64},{1,97},{33,1},{65,33},{97,65},{2,98}... | collective-permute-start | bytes 208904 | tf_op jit(solution)/shard_map/ppermute | solution.py:684
  52.7 0.7 collective-permute-start.11
  53.7 3.8 %collective-permute-start.6 = (f32[16,256]{1,0:T(8,128)S(1)}, f32[16,256]{1,0:T(8,128)S(1)}, u32[]{:S(2)}, u32[]{:S(2)}) collective-permute-start(f32[16,256]{1,0:T(8,128)S(1)} %concatenate.32.f0), channel_id=1, source_target_pairs={{0,3},{1,2},{2,1},{3,0},{4,7},{5,6},{6,5},{7,4},{8,11},{9,10},{10,... | collective-permute-start | bytes 49160 | tf_op jit(solution)/shard_map/ppermute | solution.py:684
  57.5 1.8 collective-permute-done.6.f3
  59.3 1.7 collective-permute-start.1
  61.5 0.9 collective-permute-start.4
  62.4 0.6 pad_add_fusion.pos
  63.1 2.0 %chain_last.1 = (bf16[256,128]{1,0:T(8,128)(2,1)}, bf16[256,128]{1,0:T(8,128)(2,1)}, bf16[256,128]{1,0:T(8,128)(2,1)}, bf16[256,128]{1,0:T(8,128)(2,1)}) custom-call(s32[2]{0:T(128)} %pad_add_fusion.pos, f32[256,128]{1,0:T(8,128)} %get-tuple-element.54.own, f32[8,128]{1,0:T(8,128)} %get-tuple-element.55.own_total, f32[256,128]{1,0:T(8,128)} %get-tuple-element.56.prior, ...), custom_call_target="tpu_custom_call" | custom-call | tf_op jit(solution)/shard_map/chain_last/pallas_call | solution.py:297
  65.6 1.4 collective-permute-start.14
  67.0 1.6 collective-permute-start.16
  68.6 11.6 %fine_main.1 = (f32[1024,512]{1,0:T(8,128)S(1)}, f32[1024,512]{1,0:T(8,128)S(1)}, bf16[1024,256]{1,0:T(8,128)(2,1)S(1)}) custom-call(s32[1]{0:T(128)} %bitcast.h.pos, bf16[4096,256]{1,0:T(8,128)(2,1)} %x.17, bf16[4096,256]{1,0:T(8,128)(2,1)} %x.17, bf16[16,256]{1,0:T(8,128)(2,1)S(1)} %collective-permute-done.rim_there.rim, f32[1,256]{1,0:T(1,128)S(1)} %bitcast.14, ...), custom_call_target="tpu_custom_call" | custom-call | tf_op jit(solution)/shard_map/fine_main/pallas_call | solution.py:414
  80.2 1.3 copy-done.3
  81.6 6.8 %fine_close.1 = (bf16[256,1024]{1,0:T(8,128)(2,1)S(1)}, bf16[16,1024]{1,0:T(8,128)(2,1)S(1)}) custom-call(s32[1]{0:T(128)} %bitcast.h.pos, f32[1024,512]{1,0:T(8,128)S(1)} %get-tuple-element.41.lead, f32[1024,512]{1,0:T(8,128)} %copy-done.3, bf16[1024,256]{1,0:T(8,128)(2,1)S(1)} %get-tuple-element.43.maps, bf16[4096,256]{1,0:T(8,128)(2,1)} %x.17, ...), custom_call_target="tpu_custom_call" | custom-call | tf_op jit(solution)/shard_map/fine_close/pallas_call | solution.py:487
  88.5 0.7 collective-permute-start.17
  89.3 12.5 %collective-permute-done.18.q2 = bf16[256,1024]{1,0:T(8,128)(2,1)S(1)} collective-permute-done((bf16[256,1024]{1,0:T(8,128)(2,1)S(1)}, bf16[256,1024]{1,0:T(8,128)(2,1)S(1)}, u32[]{:S(2)}, u32[]{:S(2)}) %collective-permute-start.18) | collective-permute-done | bytes 524320 | tf_op jit(solution)/shard_map/ppermute | solution.py:684
  101.7 1.1 collective-permute-start.19
  102.8 0.7 collective-permute-start.21
  103.5 0.7 collective-permute-start.20
  104.3 1.2 collective-permute-done.22.rc
  105.7 16.1 %coarse_main.1 = (f32[1024,512]{1,0:T(8,128)}, f32[1024,512]{1,0:T(8,128)}, bf16[1024,256]{1,0:T(8,128)(2,1)S(1)}, bf16[1024,256]{1,0:T(8,128)(2,1)S(1)}, bf16[32,32,256]{2,1,0:T(8,128)(2,1)S(1)}) custom-call(s32[1]{0:T(128)} %bitcast.h.pos, bf16[256,1024]{1,0:T(8,128)(2,1)S(1)} %get-tuple-element.65.q0, bf16[256,1024]{1,0:T(8,128)(2,1)S(1)} %collective-permute-done.17.q1, ...), custom_call_target="tpu_custom_call" | custom-call | tf_op jit(solution)/shard_map/coarse_main/pallas_call | solution.py:563
  121.8 0.8 copy-done.11
  122.5 0.8 copy-done.13
  123.4 24.4 %all_to_all.10.got = bf16[32,32,256]{2,1,0:T(8,128)(2,1)} all-to-all(bf16[32,32,256]{2,1,0:T(8,128)(2,1)S(1)} %get-tuple-element.71), channel_id=1, replica_groups=mesh['z'=4,'u'=2,'x'=4,'y'=2,'c'=2] {'z','u','x'}, dimensions={0} | all-to-all | bytes 1048576 | tf_op jit(solution)/shard_map/all_to_all | solution.py:776
  147.8 1.9 prefix.1
  149.7 14.3 %all_to_all.11.got = bf16[32,16,256]{2,1,0:T(8,128)(2,1)S(1)} all-to-all(bf16[32,16,256]{2,1,0:T(8,128)(2,1)} %prefix.1), channel_id=1, replica_groups=mesh['z'=4,'u'=2,'x'=4,'y'=2,'c'=2] {'z','u','x'}, dimensions={0} | all-to-all | bytes 524288 | tf_op jit(solution)/shard_map/all_to_all | solution.py:777
  164.1 1.0 copy-done.12
  165.1 4.5 %coarse_close.1 = (bf16[1024,256]{1,0:T(8,128)(2,1)S(1)}, bf16[1024,256]{1,0:T(8,128)(2,1)S(1)}, bf16[1024,256]{1,0:T(8,128)(2,1)S(1)}, bf16[1024,256]{1,0:T(8,128)(2,1)S(1)}, f32[8,1024]{1,0:T(8,128)S(1)}) custom-call(s32[1]{0:T(128)} %bitcast.h.pos, f32[1024,512]{1,0:T(8,128)S(1)} %copy-done.4, f32[1024,512]{1,0:T(8,128)} %get-tuple-element.69.tail, ...), custom_call_target="tpu_custom_call" | custom-call | tf_op jit(solution)/shard_map/coarse_close/pallas_call | solution.py:645
  169.6 3.0 %collective-permute-start.24 = (bf16[1024,256]{1,0:T(8,128)(2,1)S(1)}, bf16[1024,256]{1,0:T(8,128)(2,1)S(1)}, u32[]{:S(2)}, u32[]{:S(2)}) collective-permute-start(bf16[1024,256]{1,0:T(8,128)(2,1)S(1)} %get-tuple-element.75), channel_id=1, source_target_pairs={{0,1},{1,0},{2,3},{3,2},{4,5},{5,4},{6,7},{7,6},{8,9},{9,8},{10,11... | collective-permute-start | bytes 1572872 | tf_op jit(solution)/shard_map/ppermute | solution.py:684
  172.7 1.4 collective-permute-done.24
  174.9 0.9 collective-permute-done.26
  175.7 1.7 collective-permute-start.27
  177.4 10.8 %collective-permute-done.27.sq_far = f32[8,1024]{1,0:T(8,128)S(1)} collective-permute-done((f32[8,1024]{1,0:T(8,128)S(1)}, f32[8,1024]{1,0:T(8,128)S(1)}, u32[]{:S(2)}, u32[]{:S(2)}) %collective-permute-start.27) | collective-permute-done | bytes 32800 | tf_op jit(solution)/shard_map/ppermute | solution.py:684
  189.2 2.7 %final.1 = bf16[1024,256]{1,0:T(8,128)(2,1)} custom-call(bf16[1024,256]{1,0:T(8,128)(2,1)} %copy-done.13, bf16[1024,256]{1,0:T(8,128)(2,1)} %copy-done.14, bf16[1024,256]{1,0:T(8,128)(2,1)} %copy-done.32, bf16[1024,256]{1,0:T(8,128)(2,1)} %copy-done.33, f32[8,1024]{1,0:T(8,128)} %copy-done.34, f32[8,1024]{1,0:T(8,128)} %copy-done.42), custom_call_target="tpu_custom_call" | custom-call | tf_op jit(solution)/shard_map/final/pallas_call | solution.py:674
  (128 shorter events, 4.8 us)
Async XLA Ops:
  0.7 22.9 %collective-permute-start = (bf16[16,256]{1,0:T(8,128)(2,1)S(1)}, bf16[16,256]{1,0:T(8,128)(2,1)S(1)}, u32[]{:S(2)}, u32[]{:S(2)}) collective-permute-start(bf16[16,256]{1,0:T(8,128)(2,1)S(1)} %slice.3), channel_id=1, source_target_pairs={{0,4},{4,8},{8,12},{12,16},{16,20},{20,24},{24,28},{28,32},{32,36}... | collective-permute-start | bytes 24584 | tf_op jit(solution)/shard_map/ppermute | solution.py:684
  5.6 61.4 %collective-permute-start.3 = (bf16[384,256]{1,0:T(8,128)(2,1)S(1)}, bf16[384,256]{1,0:T(8,128)(2,1)S(1)}, u32[]{:S(2)}, u32[]{:S(2)}) collective-permute-start(bf16[384,256]{1,0:T(8,128)(2,1)S(1)} %pad_maximum_fusion.p0.w0), channel_id=1, source_target_pairs={{0,3},{1,2},{2,1},{3,0},{4,7},{5,6},{6,5},{7,4},{8,11},{9,10},{10,... | collective-permute-start | bytes 589832 | tf_op jit(solution)/shard_map/ppermute | solution.py:684
  9.9 1.6 copy-start
  11.5 0.9 copy-start.1
  15.4 8.2 %copy-start.2 = (bf16[256,512]{1,0:T(8,128)(2,1)S(1)}, bf16[256,512]{1,0:T(8,128)(2,1)}, u32[]{:S(2)}) copy-start(bf16[256,512]{1,0:T(8,128)(2,1)} %wb.3) | copy-start | bytes 786436
  15.4 8.2 %copy-start.10 = (bf16[256,128]{1,0:T(8,128)(2,1)S(1)}, bf16[256,128]{1,0:T(8,128)(2,1)}, u32[]{:S(2)}) copy-start(bf16[256,128]{1,0:T(8,128)(2,1)} %wv.4) | copy-start | bytes 196612
  23.5 39.6 %copy-start.5 = (f32[3,256,128]{2,1,0:T(8,128)}, f32[3,256,128]{2,1,0:T(8,128)S(1)}, u32[]{:S(2)}) copy-start(f32[3,256,128]{2,1,0:T(8,128)S(1)} %get-tuple-element.44.later) | copy-start | bytes 1179652
  23.5 39.6 %copy-start.20 = (f32[3,8,128]{2,1,0:T(8,128)}, f32[3,8,128]{2,1,0:T(8,128)S(1)}, u32[]{:S(2)}) copy-start(f32[3,8,128]{2,1,0:T(8,128)S(1)} %get-tuple-element.45.later_total) | copy-start | bytes 36868
  23.5 29.9 %copy-start.43 = (bf16[256,2]{0,1:T(2,128)(2,1)S(1)}, bf16[256,2]{0,1:T(2,128)(2,1)}, u32[]{:S(2)}) copy-start(bf16[256,2]{0,1:T(2,128)(2,1)} %param.29) | copy-start | bytes 3076
  23.5 29.9 %copy-start.22 = (f32[4,128]{1,0:T(4,128)S(1)}, f32[4,128]{1,0:T(4,128)}, u32[]{:S(2)}) copy-start(f32[4,128]{1,0:T(4,128)} %kv.4) | copy-start | bytes 6148
  23.5 29.9 %copy-start.48 = (f32[128]{0:T(128)S(1)}, f32[128]{0:T(128)}, u32[]{:S(2)}) copy-start(f32[128]{0:T(128)} %param.34) | copy-start | bytes 1540
  23.5 29.9 %copy-start.44 = (f32[2]{0:T(128)S(1)}, f32[2]{0:T(128)}, u32[]{:S(2)}) copy-start(f32[2]{0:T(128)} %param.32) | copy-start | bytes 28
  23.6 30.0 %copy-start.45 = (f32[2]{0:T(128)S(1)}, f32[2]{0:T(128)}, u32[]{:S(2)}) copy-start(f32[2]{0:T(128)} %param.33) | copy-start | bytes 28
  23.6 45.0 %copy-start.18 = (f32[4,512]{1,0:T(4,128)S(1)}, f32[4,512]{1,0:T(4,128)}, u32[]{:S(2)}) copy-start(f32[4,512]{1,0:T(4,128)} %ks.6) | copy-start | bytes 24580
  23.6 45.0 %copy-start.25 = (f32[256]{0:T(256)S(1)}, f32[256]{0:T(256)}, u32[]{:S(2)}) copy-start(f32[256]{0:T(256)} %param.25) | copy-start | bytes 3076
  28.8 6.4 %collective-permute-start.9 = (bf16[272,128]{1,0:T(8,128)(2,1)S(1)}, bf16[272,128]{1,0:T(8,128)(2,1)S(1)}, u32[]{:S(2)}, u32[]{:S(2)}) collective-permute-start(bf16[272,128]{1,0:T(8,128)(2,1)S(1)} %get-tuple-element.48), channel_id=1, source_target_pairs={{0,12},{4,0},{8,4},{12,8},{1,13},{5,1},{9,5},{13,9},{2,14},{6,2},{... | collective-permute-start | bytes 208904 | tf_op jit(solution)/shard_map/ppermute | solution.py:684
  32.0 5.3 %collective-permute-start.8 = (bf16[272,128]{1,0:T(8,128)(2,1)S(1)}, bf16[272,128]{1,0:T(8,128)(2,1)S(1)}, u32[]{:S(2)}, u32[]{:S(2)}) collective-permute-start(bf16[272,128]{1,0:T(8,128)(2,1)S(1)} %get-tuple-element.48), channel_id=1, source_target_pairs={{0,8},{4,12},{8,0},{12,4},{1,9},{5,13},{9,1},{13,5},{2,10},{6,14},... | collective-permute-start | bytes 208904 | tf_op jit(solution)/shard_map/ppermute | solution.py:684
  32.0 6.5 %collective-permute-start.7 = (bf16[272,128]{1,0:T(8,128)(2,1)S(1)}, bf16[272,128]{1,0:T(8,128)(2,1)S(1)}, u32[]{:S(2)}, u32[]{:S(2)}) collective-permute-start(bf16[272,128]{1,0:T(8,128)(2,1)S(1)} %get-tuple-element.48), channel_id=1, source_target_pairs={{0,4},{4,8},{8,12},{12,0},{1,5},{5,9},{9,13},{13,1},{2,6},{6,10},{... | collective-permute-start | bytes 208904 | tf_op jit(solution)/shard_map/ppermute | solution.py:684
  35.1 4.6 %copy-start.38 = (bf16[272,128]{1,0:T(8,128)(2,1)}, bf16[272,128]{1,0:T(8,128)(2,1)S(1)}, u32[]{:S(2)}) copy-start(bf16[272,128]{1,0:T(8,128)(2,1)S(1)} %collective-permute-done.9.refs_7_) | copy-start | bytes 208900
  37.2 2.5 %copy-start.39 = (bf16[272,128]{1,0:T(8,128)(2,1)}, bf16[272,128]{1,0:T(8,128)(2,1)S(1)}, u32[]{:S(2)}) copy-start(bf16[272,128]{1,0:T(8,128)(2,1)S(1)} %collective-permute-done.8.refs_6_) | copy-start | bytes 208900
  38.5 1.3 copy-start.40
  41.7 4.9 %collective-permute-start.10 = (bf16[272,128]{1,0:T(8,128)(2,1)}, bf16[272,128]{1,0:T(8,128)(2,1)S(1)}, u32[]{:S(2)}, u32[]{:S(2)}) collective-permute-start(bf16[272,128]{1,0:T(8,128)(2,1)} %get-tuple-element.53), channel_id=1, source_target_pairs={{0,16},{16,0},{1,17},{17,1},{2,18},{18,2},{3,19},{19,3},{4,20},{20... | collective-permute-start | bytes 208904 | tf_op jit(solution)/shard_map/ppermute | solution.py:684
  49.0 10.3 %collective-permute-start.13 = (bf16[272,128]{1,0:T(8,128)(2,1)}, bf16[272,128]{1,0:T(8,128)(2,1)S(1)}, u32[]{:S(2)}, u32[]{:S(2)}) collective-permute-start(bf16[272,128]{1,0:T(8,128)(2,1)} %get-tuple-element.58), channel_id=1, source_target_pairs={{0,96},{32,0},{64,32},{96,64},{1,97},{33,1},{65,33},{97,65},{2,98}... | collective-permute-start | bytes 208904 | tf_op jit(solution)/shard_map/ppermute | solution.py:684
  52.7 8.3 %collective-permute-start.12 = (bf16[272,128]{1,0:T(8,128)(2,1)}, bf16[272,128]{1,0:T(8,128)(2,1)S(1)}, u32[]{:S(2)}, u32[]{:S(2)}) collective-permute-start(bf16[272,128]{1,0:T(8,128)(2,1)} %get-tuple-element.58), channel_id=1, source_target_pairs={{0,64},{32,96},{64,0},{96,32},{1,65},{33,97},{65,1},{97,33},{2,66}... | collective-permute-start | bytes 208904 | tf_op jit(solution)/shard_map/ppermute | solution.py:684
  52.7 8.8 %collective-permute-start.11 = (bf16[272,128]{1,0:T(8,128)(2,1)}, bf16[272,128]{1,0:T(8,128)(2,1)S(1)}, u32[]{:S(2)}, u32[]{:S(2)}) collective-permute-start(bf16[272,128]{1,0:T(8,128)(2,1)} %get-tuple-element.58), channel_id=1, source_target_pairs={{0,32},{32,64},{64,96},{96,0},{1,33},{33,65},{65,97},{97,1},{2,34}... | collective-permute-start | bytes 208904 | tf_op jit(solution)/shard_map/ppermute | solution.py:684
  53.7 5.6 %collective-permute-start.6 = (f32[16,256]{1,0:T(8,128)S(1)}, f32[16,256]{1,0:T(8,128)S(1)}, u32[]{:S(2)}, u32[]{:S(2)}) collective-permute-start(f32[16,256]{1,0:T(8,128)S(1)} %concatenate.32.f0), channel_id=1, source_target_pairs={{0,3},{1,2},{2,1},{3,0},{4,7},{5,6},{6,5},{7,4},{8,11},{9,10},{10,... | collective-permute-start | bytes 49160 | tf_op jit(solution)/shard_map/ppermute | solution.py:684
  59.3 9.3 %collective-permute-start.2 = (bf16[384,256]{1,0:T(8,128)(2,1)S(1)}, bf16[384,256]{1,0:T(8,128)(2,1)S(1)}, u32[]{:S(2)}, u32[]{:S(2)}) collective-permute-start(bf16[384,256]{1,0:T(8,128)(2,1)S(1)} %pad_maximum_fusion.p0.w0), channel_id=1, source_target_pairs={{0,2},{1,3},{2,0},{3,1},{4,6},{5,7},{6,4},{7,5},{8,10},{9,11},{10,... | collective-permute-start | bytes 589832 | tf_op jit(solution)/shard_map/ppermute | solution.py:684
  59.3 3.8 %copy-start.35 = (bf16[272,128]{1,0:T(8,128)(2,1)}, bf16[272,128]{1,0:T(8,128)(2,1)S(1)}, u32[]{:S(2)}) copy-start(bf16[272,128]{1,0:T(8,128)(2,1)S(1)} %collective-permute-done.13.r3) | copy-start | bytes 208900
  59.3 9.3 %collective-permute-start.1 = (bf16[384,256]{1,0:T(8,128)(2,1)S(1)}, bf16[384,256]{1,0:T(8,128)(2,1)S(1)}, u32[]{:S(2)}, u32[]{:S(2)}) collective-permute-start(bf16[384,256]{1,0:T(8,128)(2,1)S(1)} %pad_maximum_fusion.p0.w0), channel_id=1, source_target_pairs={{0,1},{1,0},{2,3},{3,2},{4,5},{5,4},{6,7},{7,6},{8,9},{9,8},{10,11... | collective-permute-start | bytes 589832 | tf_op jit(solution)/shard_map/ppermute | solution.py:684
  61.0 2.0 %copy-start.36 = (bf16[272,128]{1,0:T(8,128)(2,1)}, bf16[272,128]{1,0:T(8,128)(2,1)S(1)}, u32[]{:S(2)}) copy-start(bf16[272,128]{1,0:T(8,128)(2,1)S(1)} %collective-permute-done.12.r2) | copy-start | bytes 208900
  61.0 4.5 %collective-permute-start.5 = (f32[16,256]{1,0:T(8,128)S(1)}, f32[16,256]{1,0:T(8,128)S(1)}, u32[]{:S(2)}, u32[]{:S(2)}) collective-permute-start(f32[16,256]{1,0:T(8,128)S(1)} %concatenate.32.f0), channel_id=1, source_target_pairs={{0,2},{1,3},{2,0},{3,1},{4,6},{5,7},{6,4},{7,5},{8,10},{9,11},{10,... | collective-permute-start | bytes 49160 | tf_op jit(solution)/shard_map/ppermute | solution.py:684
  61.5 1.6 copy-start.37
  61.5 5.4 %collective-permute-start.4 = (f32[16,256]{1,0:T(8,128)S(1)}, f32[16,256]{1,0:T(8,128)S(1)}, u32[]{:S(2)}, u32[]{:S(2)}) collective-permute-start(f32[16,256]{1,0:T(8,128)S(1)} %concatenate.32.f0), channel_id=1, source_target_pairs={{0,1},{1,0},{2,3},{3,2},{4,5},{5,4},{6,7},{7,6},{8,9},{9,8},{10,11... | collective-permute-start | bytes 49160 | tf_op jit(solution)/shard_map/ppermute | solution.py:684
  65.6 15.9 %collective-permute-start.14 = (bf16[256,128]{1,0:T(8,128)(2,1)}, bf16[256,128]{1,0:T(8,128)(2,1)S(1)}, u32[]{:S(2)}, u32[]{:S(2)}) collective-permute-start(bf16[256,128]{1,0:T(8,128)(2,1)} %get-tuple-element.62), channel_id=1, source_target_pairs={{0,1},{1,0},{2,3},{3,2},{4,5},{5,4},{6,7},{7,6},{8,9},{9,8},{10,11... | collective-permute-start | bytes 196616 | tf_op jit(solution)/shard_map/ppermute | solution.py:684
  66.9 14.5 %collective-permute-start.15 = (bf16[256,128]{1,0:T(8,128)(2,1)}, bf16[256,128]{1,0:T(8,128)(2,1)S(1)}, u32[]{:S(2)}, u32[]{:S(2)}) collective-permute-start(bf16[256,128]{1,0:T(8,128)(2,1)} %get-tuple-element.63), channel_id=1, source_target_pairs={{0,2},{1,3},{2,0},{3,1},{4,6},{5,7},{6,4},{7,5},{8,10},{9,11},{10,... | collective-permute-start | bytes 196616 | tf_op jit(solution)/shard_map/ppermute | solution.py:684
  67.0 14.5 %copy-start.19 = (bf16[256,128]{1,0:T(8,128)(2,1)S(1)}, bf16[256,128]{1,0:T(8,128)(2,1)}, u32[]{:S(2)}) copy-start(bf16[256,128]{1,0:T(8,128)(2,1)} %get-tuple-element.61.s0) | copy-start | bytes 196612
  67.0 14.5 %collective-permute-start.16 = (bf16[256,128]{1,0:T(8,128)(2,1)}, bf16[256,128]{1,0:T(8,128)(2,1)S(1)}, u32[]{:S(2)}, u32[]{:S(2)}) collective-permute-start(bf16[256,128]{1,0:T(8,128)(2,1)} %get-tuple-element.64), channel_id=1, source_target_pairs={{0,3},{1,2},{2,1},{3,0},{4,7},{5,6},{6,5},{7,4},{8,11},{9,10},{10,... | collective-permute-start | bytes 196616 | tf_op jit(solution)/shard_map/ppermute | solution.py:684
  80.2 1.3 copy-start.3
  81.5 24.0 %copy-start.46 = (f32[8]{0:T(128)S(1)}, f32[8]{0:T(128)}, u32[]{:S(2)}) copy-start(f32[8]{0:T(128)} %param.44) | copy-start | bytes 100
  81.5 24.1 %copy-start.47 = (f32[8]{0:T(128)S(1)}, f32[8]{0:T(128)}, u32[]{:S(2)}) copy-start(f32[8]{0:T(128)} %param.45) | copy-start | bytes 100
  81.5 24.1 %copy-start.6 = (bf16[1024,512]{1,0:T(8,128)(2,1)S(1)}, bf16[1024,512]{1,0:T(8,128)(2,1)}, u32[]{:S(2)}) copy-start(bf16[1024,512]{1,0:T(8,128)(2,1)} %wg.1) | copy-start | bytes 3145732
  81.5 24.1 %copy-start.7 = (bf16[1024,512]{1,0:T(8,128)(2,1)S(1)}, bf16[1024,512]{1,0:T(8,128)(2,1)}, u32[]{:S(2)}) copy-start(bf16[1024,512]{1,0:T(8,128)(2,1)} %wv.5) | copy-start | bytes 3145732
  81.5 24.1 %copy-start.23 = (bf16[1024,8]{0,1:T(8,128)(2,1)S(1)}, bf16[1024,8]{0,1:T(8,128)(2,1)}, u32[]{:S(2)}) copy-start(bf16[1024,8]{0,1:T(8,128)(2,1)} %param.41) | copy-start | bytes 49156
  81.6 24.1 %copy-start.26 = (f32[4,512]{1,0:T(4,128)S(1)}, f32[4,512]{1,0:T(4,128)}, u32[]{:S(2)}) copy-start(f32[4,512]{1,0:T(4,128)} %kv.5) | copy-start | bytes 24580
  81.6 24.1 %copy-start.27 = (f32[4,512]{1,0:T(4,128)S(1)}, f32[4,512]{1,0:T(4,128)}, u32[]{:S(2)}) copy-start(f32[4,512]{1,0:T(4,128)} %ks.7) | copy-start | bytes 24580
  81.6 24.1 %copy-start.28 = (f32[1024]{0:T(1024)S(1)}, f32[1024]{0:T(1024)}, u32[]{:S(2)}) copy-start(f32[1024]{0:T(1024)} %param.37) | copy-start | bytes 12292
  88.4 13.3 %collective-permute-start.18 = (bf16[256,1024]{1,0:T(8,128)(2,1)S(1)}, bf16[256,1024]{1,0:T(8,128)(2,1)S(1)}, u32[]{:S(2)}, u32[]{:S(2)}) collective-permute-start(bf16[256,1024]{1,0:T(8,128)(2,1)S(1)} %get-tuple-element.65.q0), channel_id=1, source_target_pairs={{0,2},{1,3},{2,0},{3,1},{4,6},{5,7},{6,4},{7,5},{8,10},{9,11},{10,... | collective-permute-start | bytes 1572872 | tf_op jit(solution)/shard_map/ppermute | solution.py:684
  88.5 17.0 %collective-permute-start.17 = (bf16[256,1024]{1,0:T(8,128)(2,1)S(1)}, bf16[256,1024]{1,0:T(8,128)(2,1)S(1)}, u32[]{:S(2)}, u32[]{:S(2)}) collective-permute-start(bf16[256,1024]{1,0:T(8,128)(2,1)S(1)} %get-tuple-element.65.q0), channel_id=1, source_target_pairs={{0,1},{1,0},{2,3},{3,2},{4,5},{5,4},{6,7},{7,6},{8,9},{9,8},{10,11... | collective-permute-start | bytes 1572872 | tf_op jit(solution)/shard_map/ppermute | solution.py:684
  101.7 3.8 %collective-permute-start.19 = (bf16[256,1024]{1,0:T(8,128)(2,1)S(1)}, bf16[256,1024]{1,0:T(8,128)(2,1)S(1)}, u32[]{:S(2)}, u32[]{:S(2)}) collective-permute-start(bf16[256,1024]{1,0:T(8,128)(2,1)S(1)} %collective-permute-done.18.q2), channel_id=1, source_target_pairs={{0,1},{1,0},{2,3},{3,2},{4,5},{5,4},{6,7},{7,6},{8,9},{9,8},{10,11... | collective-permute-start | bytes 1572872 | tf_op jit(solution)/shard_map/ppermute | solution.py:684
  102.8 1.3 collective-permute-start.21
  103.5 0.7 collective-permute-start.20
  104.2 1.3 collective-permute-start.22
  105.7 58.4 %copy-start.8 = (bf16[512,1024]{1,0:T(8,128)(2,1)S(1)}, bf16[512,1024]{1,0:T(8,128)(2,1)}, u32[]{:S(2)}) copy-start(bf16[512,1024]{1,0:T(8,128)(2,1)} %wo.1) | copy-start | bytes 3145732
  123.3 40.7 %copy-start.4 = (f32[1024,512]{1,0:T(8,128)S(1)}, f32[1024,512]{1,0:T(8,128)}, u32[]{:S(2)}) copy-start(f32[1024,512]{1,0:T(8,128)} %get-tuple-element.68.lead) | copy-start | bytes 6291460
  123.4 40.7 %copy-start.31 = (f32[512]{0:T(512)S(1)}, f32[512]{0:T(512)}, u32[]{:S(2)}) copy-start(f32[512]{0:T(512)} %param.46) | copy-start | bytes 6148
  164.0 1.0 copy-start.12
  169.6 4.7 %copy-start.14 = (bf16[1024,256]{1,0:T(8,128)(2,1)}, bf16[1024,256]{1,0:T(8,128)(2,1)S(1)}, u32[]{:S(2)}) copy-start(bf16[1024,256]{1,0:T(8,128)(2,1)S(1)} %get-tuple-element.72.kk) | copy-start | bytes 1572868
  169.6 4.6 %collective-permute-start.24 = (bf16[1024,256]{1,0:T(8,128)(2,1)S(1)}, bf16[1024,256]{1,0:T(8,128)(2,1)S(1)}, u32[]{:S(2)}, u32[]{:S(2)}) collective-permute-start(bf16[1024,256]{1,0:T(8,128)(2,1)S(1)} %get-tuple-element.75), channel_id=1, source_target_pairs={{0,1},{1,0},{2,3},{3,2},{4,5},{5,4},{6,7},{7,6},{8,9},{9,8},{10,11... | collective-permute-start | bytes 1572872 | tf_op jit(solution)/shard_map/ppermute | solution.py:684
  172.6 15.6 %collective-permute-start.23 = (bf16[1024,256]{1,0:T(8,128)(2,1)S(1)}, bf16[1024,256]{1,0:T(8,128)(2,1)S(1)}, u32[]{:S(2)}, u32[]{:S(2)}) collective-permute-start(bf16[1024,256]{1,0:T(8,128)(2,1)S(1)} %get-tuple-element.73), channel_id=1, source_target_pairs={{0,1},{1,0},{2,3},{3,2},{4,5},{5,4},{6,7},{7,6},{8,9},{9,8},{10,11... | collective-permute-start | bytes 1572872 | tf_op jit(solution)/shard_map/ppermute | solution.py:684
  174.3 13.9 %collective-permute-start.25 = (bf16[1024,256]{1,0:T(8,128)(2,1)S(1)}, bf16[1024,256]{1,0:T(8,128)(2,1)S(1)}, u32[]{:S(2)}, u32[]{:S(2)}) collective-permute-start(bf16[1024,256]{1,0:T(8,128)(2,1)S(1)} %add_convert_fusion), channel_id=1, source_target_pairs={{0,2},{1,3},{2,0},{3,1},{4,6},{5,7},{6,4},{7,5},{8,10},{9,11},{10,... | collective-permute-start | bytes 1572872 | tf_op jit(solution)/shard_map/ppermute | solution.py:684
  174.4 1.3 collective-permute-start.26
  175.7 12.5 %copy-start.34 = (f32[8,1024]{1,0:T(8,128)}, f32[8,1024]{1,0:T(8,128)S(1)}, u32[]{:S(2)}) copy-start(f32[8,1024]{1,0:T(8,128)S(1)} %add.25.sq) | copy-start | bytes 98308
  175.7 12.5 %collective-permute-start.27 = (f32[8,1024]{1,0:T(8,128)S(1)}, f32[8,1024]{1,0:T(8,128)S(1)}, u32[]{:S(2)}, u32[]{:S(2)}) collective-permute-start(f32[8,1024]{1,0:T(8,128)S(1)} %add.25.sq), channel_id=1, source_target_pairs={{0,2},{1,3},{2,0},{3,1},{4,6},{5,7},{6,4},{7,5},{8,10},{9,11},{10,... | collective-permute-start | bytes 98312 | tf_op jit(solution)/shard_map/ppermute | solution.py:684
  188.2 1.0 copy-start.33
  (13 other events, 9.0 us)
where the time goes:
time: 193 us; the launch traced here: 192 us
  Pallas kernels  60.1 us (31%)
  blocking collectives  38.8 us (20%)
  starting transfers between devices  36 us (19%)
  waiting for transfers between devices  35.6 us (18%)
  local copies, waits for them, and re-layouts  18 us (9%)
  other arithmetic  3.04 us (2%)
    ppermute x28, starting transfers between devices, passed(): return lax.ppermute(x, axes, pairs)  36 us
    ppermute x28, waiting for transfers between devices, passed(): return lax.ppermute(x, axes, pairs)  35.6 us
    all_to_all x1, blocking collectives, shards(): got = lax.all_to_all(message, SEQ, split_axis=0, concat_axis=0, tiled=True)  24.4 us
    pallas_call x1, Pallas kernels, coarse_main(): pl.pallas_call(coarse_main_kernel, grid=(4,), in_specs=[SMEM] + [ANY] * 4...  16.1 us
    all_to_all x1, blocking collectives, shards(): lax.all_to_all(prefix(got), SEQ, split_axis=0, concat_axis=0, tiled=True)  14.3 us
    unnamed x98, local copies, waits for them, and re-layouts  13.6 us
    pallas_call x1, Pallas kernels, fine_main(): pl.pallas_call(fine_main_kernel, grid_spec=pltpu.PrefetchScalarGridSpec(n...  11.6 us
    pallas_call x1, Pallas kernels, fine_states(): pl.pallas_call(later_chunks_kernel, grid=(3,), in_specs=[pl.BlockSpec((10...  8.12 us
  transfers between devices with their start and end apart: 28, of which 11 were waited for; matrix products, arithmetic and copies ran while one was open for 3% of the time, Pallas kernels for 15%

commit v1 on v0

--- a/solution.py
+++ b/solution.py
@@ -5,6 +5,7 @@
 from jax.experimental.pallas import tpu as pltpu
 from jax.sharding import Mesh
 from jax.sharding import PartitionSpec as P
+
 
 SEQ = ("z", "u", "x")
 HEAD = ("y", "c")
@@ -79,33 +80,94 @@
     return s[0:8] + s[8:16] + s[16:24]
 
 
-def convolve(cv, act, taps, width, length, step=64):
-    for c in range(width // 128):
-        cols = slice(c * 128, (c + 1) * 128)
-        for r in range(length // step):
-            total = cv[pl.ds(13 + r * step, step), cols] * taps[0:1, cols]
-            for k in range(1, 4):
-                total = total + cv[pl.ds(13 + k + r * step, step), cols] * taps[k : k + 1, cols]
-            act[pl.ds(r * step, step), cols] = silu(total).astype(BF)
+def convolve(cv, act, half_taps, length):
+    apart = 32
+
+    def slab(c, carry):
+        taps = half_taps[c]
+        for base in range(0, length, 8 * apart):
+            rows = [cv[c, pl.ds(base + 13 + i, 8, stride=apart), :] for i in range(3)]
+            for i in range(apart):
+                rows.append(cv[c, pl.ds(base + 16 + i, 8, stride=apart), :])
+                h = rows[i] * taps[0:1]
+                for k in range(1, 4):
+                    h = h + rows[i + k] * taps[k : k + 1]
+                act[c, pl.ds(base + i, 8, stride=apart), :] = h + h * jnp.tanh(h)
+        return carry
+
+    lax.fori_loop(0, cv.shape[0], slab, 0)
+
+
+def project(rows, weights, cv, start, slab):
+    product = dot(rows, weights)
+    for j in range(product.shape[1] // 128):
+        cv[slab + j, start : start + rows.shape[0], :] = product[:, j * 128 : (j + 1) * 128]
 
 
 def rounded(x):
     return x.astype(BF).astype(F32)
 
 
-def state_chunk(x, rim, gain, wv, wb, wst, kv, ks, bias, decay, taps, cv, act):
-    taps[:, 0:128] = kv[...]
-    taps[:, 128:384] = ks[...]
+def small_rows(pack):
+    rows = pack[384:416, :].astype(F32)
+    kv = rows[0:4, 0:128] + rows[4:8, 0:128] + rows[8:12, 0:128]
+    right = rows[0:16, 128:256]
+    norm, b0, b1, d0, d1 = (of_rows(right[3 * j : 3 * j + 3]) for j in range(5))
+    return kv, norm, jnp.concatenate([b0, b1], 0), jnp.concatenate([d0, d1], 0), rows[16:18]
+
+
+def three(row):
+    hi = row.astype(BF).astype(F32)
+    rest = row - hi
+    mid = rest.astype(BF).astype(F32)
+    return [hi, mid, rest - mid]
+
+
+def pack_kernel(bias, decay, gate, value, output, steps, kv, norm, pack):
+    pack[0:256, 0:128] = gate[...]
+    pack[0:256, 128:256] = value[...]
+    pack[256:384, :] = output[...]
+    left = jnp.concatenate(three(kv[...]) + [jnp.zeros((4, 128), F32)], 0)
+    rows = three(norm[...])
+    for ref in (bias, decay):
+        for j in range(2):
+            rows = rows + three(jnp.full((1, 128), ref[j], F32))
+    right = jnp.concatenate(rows + [jnp.zeros((1, 128), F32)], 0)
+    below = jnp.concatenate([steps[...].astype(F32), jnp.zeros((14, 256), F32)], 0)
+    pack[384:416, :] = jnp.concatenate([jnp.concatenate([left, right], 1), below], 0).astype(BF)
+
+
+def packed(bias, decay, gate, value, output, steps, kv, norm):
+    return pl.pallas_call(
+        pack_kernel,
+        in_specs=[SMEM] * 2 + [VM] * 6,
+        out_specs=VM,
+        out_shape=sds((416, 256), BF),
+        compiler_params=few(8),
+        name="pack",
+    )(bias, decay, gate, value, output, steps, kv, norm)
+
+
+def state_chunk(x, rim, gain, pack, wb, ks, taps, cv, act):
+    kv, _, bias, decay, steps = small_rows(pack)
+    pad = jnp.zeros((6, 128), F32)
+    bias = jnp.concatenate([bias, pad], 0)[:, 0:1]
+    decay = jnp.concatenate([decay, pad], 0)[:, 0:1]
+    steps = jnp.concatenate([steps, jnp.zeros((6, 256), F32)], 0).astype(BF)
+    wv = pack[0:256, 128:256]
+    taps[0] = kv * 0.5
+    taps[1] = ks[:, 0:128] * 0.5
+    taps[2] = ks[:, 128:256] * 0.5
     normed = rms(x, gain[...])
     before = rms(rim, gain[...])
-    cv[0:16, 0:128] = rounded(dot(before, wv[...]))
-    cv[0:16, 128:384] = rounded(dot(before, wb[...]))
-    cv[16:1040, 0:128] = rounded(dot(normed, wv[...]))
-    cv[16:1040, 128:384] = rounded(dot(normed, wb[...]))
-    convolve(cv, act, taps, 384, 1024)
-    raw = dot(wst[...], normed, NT)
-    dt = softplus(raw + bias[:, 0:1])
-    logs = -dt * decay[:, 0:1]
+    project(before, wv, cv, 0, 0)
+    project(before, wb[...], cv, 0, 1)
+    project(normed, wv, cv, 16, 0)
+    project(normed, wb[...], cv, 16, 1)
+    convolve(cv, act, taps, 1024)
+    raw = dot(steps, normed, NT)
+    dt = softplus(raw + bias)
+    logs = -dt * decay
     tri = upper()
     carry = jnp.zeros((8, 1), F32)
     pieces = []
@@ -116,29 +178,25 @@
     cum = jnp.concatenate(pieces, 1)
     tail = jnp.exp(carry - cum) * dt
     spread = dot(parts(tail), expander(128), TN)
-    scaled = (act[:, 0:128].astype(F32) * spread).astype(BF)
-    local = dot(act[:, 128:384], scaled, TN)
+    scaled = (act[0] * spread).astype(BF)
+    local = dot(jnp.concatenate([act[1].astype(BF), act[2].astype(BF)], 1), scaled, TN)
     total = jnp.sum(
         jnp.where(head_sel(128), jnp.broadcast_to(carry, (8, 128)), 0.0), axis=0, keepdims=True
     )
     return local, total
 
 
-def later_chunks_kernel(x, rim, gain, wv, wb, wst, kv, ks, bias, decay, local, total, taps, cv, act):
-    state, logs = state_chunk(
-        x[...], rim[...], gain, wv, wb, wst, kv, ks, bias, decay, taps, cv, act
-    )
+def later_chunks_kernel(x, rim, gain, pack, wb, ks, local, total, taps, cv, act):
+    state, logs = state_chunk(x[...], rim[...], gain, pack, wb, ks, taps, cv, act)
     local[0] = state
     total[0] = jnp.broadcast_to(logs, (8, 128))
 
 
 def first_chunk_kernel(
-    x, rim, gain, wv, wb, wst, kv, ks, bias, decay, later, later_total,
+    x, rim, gain, pack, wb, ks, later, later_total,
     local, total, whole, whole_total, message, taps, cv, act,
 ):
-    state, logs = state_chunk(
-        x[...], rim[...], gain, wv, wb, wst, kv, ks, bias, decay, taps, cv, act
-    )
+    state, logs = state_chunk(x[...], rim[...], gain, pack, wb, ks, taps, cv, act)
     local[...] = state
     total[...] = jnp.broadcast_to(logs, (8, 128))
     for j in range(3):
@@ -159,24 +217,25 @@
     return pl.BlockSpec(shape, lambda *_: (0,) * len(shape))
 
 
-PARAMS = pltpu.CompilerParams(dimension_semantics=("arbitrary",), vmem_limit_bytes=48 << 20)
-
-
-def fine_states(tokens, rim, gain, wv, scans, wst, kv, ks, bias, decay):
+def few(mib):
+    return pltpu.CompilerParams(vmem_limit_bytes=mib << 20)
+
+
+SMEM = pl.BlockSpec(memory_space=pltpu.SMEM)
+VM = pl.BlockSpec(memory_space=pltpu.VMEM)
+
+
+def fine_states(tokens, rim, gain, pack, scans, ks):
     common = [
         whole_spec((1, 256)),
-        whole_spec((256, 128)),
+        whole_spec((416, 256)),
         whole_spec((256, 256)),
-        whole_spec((8, 256)),
-        whole_spec((4, 128)),
         whole_spec((4, 256)),
-        whole_spec((8, 128)),
-        whole_spec((8, 128)),
     ]
     scratch = [
-        pltpu.VMEM((4, 384), F32),
-        pltpu.VMEM((1040, 384), F32),
-        pltpu.VMEM((1024, 384), BF),
+        pltpu.VMEM((3, 4, 128), F32),
+        pltpu.VMEM((3, 1040, 128), F32),
+        pltpu.VMEM((3, 1024, 128), F32),
     ]
     later, later_total = pl.pallas_call(
         later_chunks_kernel,
@@ -192,9 +251,9 @@
         ],
         out_shape=[sds((3, 256, 128)), sds((3, 8, 128))],
         scratch_shapes=scratch,
-        compiler_params=PARAMS,
+        compiler_params=few(20),
         name="later_chunks",
-    )(tokens, tokens, gain, wv, scans, wst, kv, ks, bias, decay)
+    )(tokens, tokens, gain, pack, scans, ks)
     first = pl.pallas_call(
         first_chunk_kernel,
         grid=(1,),
@@ -216,9 +275,9 @@
             sds((272, 128), BF),
         ],
         scratch_shapes=scratch,
-        compiler_params=PARAMS,
+        compiler_params=few(20),
         name="first_chunk",
-    )(tokens, rim, gain, wv, scans, wst, kv, ks, bias, decay, later, later_total)
+    )(tokens, rim, gain, pack, scans, ks, later, later_total)
     return later, later_total, first
 
 
@@ -244,10 +303,14 @@
     return new_prior, new_prior_total, state, logs
 
 
-def middle_kernel(count, pos, own, own_total, prior, prior_total, *refs):
+def middle_kernel(axis, count, fresh, own, own_total, *refs):
+    if fresh:
+        prior, prior_total = jnp.zeros((256, 128), F32), jnp.zeros((1, 128), F32)
+    else:
+        prior, prior_total, refs = refs[0][...], refs[1][0:1, :], refs[2:]
     received, (np_ref, npt_ref, ns_ref, nst_ref, message) = refs[: count - 1], refs[count - 1 :]
     p, pt, s, st = combine(
-        pos[0], count, own[...], own_total[0:1, :], prior[...], prior_total[0:1, :], received
+        lax.axis_index(axis), count, own[...], own_total[0:1, :], prior, prior_total, received
     )
     np_ref[...] = p
     npt_ref[...] = jnp.broadcast_to(pt, (8, 128))
@@ -257,14 +320,10 @@
     message[256:272, :] = decay_rows(st)
 
 
-SMEM = pl.BlockSpec(memory_space=pltpu.SMEM)
-VM = pl.BlockSpec(memory_space=pltpu.VMEM)
-
-
-def middle_stage(count, pos, own, own_total, prior, prior_total, received, name):
+def middle_stage(axis, count, own, own_total, prior, received):
     return pl.pallas_call(
-        lambda *refs: middle_kernel(count, *refs),
-        in_specs=[SMEM] + [VM] * (4 + len(received)),
+        lambda *refs: middle_kernel(axis, count, not prior, *refs),
+        in_specs=[VM] * (2 + len(prior) + len(received)),
         out_specs=[VM] * 5,
         out_shape=[
             sds((256, 128)),
@@ -273,14 +332,15 @@
             sds((8, 128)),
             sds((272, 128), BF),
         ],
-        name=name,
-    )(pos, own, own_total, prior, prior_total, *received)
-
-
-def last_kernel(pos, own, own_total, prior, prior_total, r1, r2, r3, l0, t0, later, later_total,
+        compiler_params=few(4),
+    )(own, own_total, *prior, *received)
+
+
+def last_kernel(own, own_total, prior, prior_total, r1, r2, r3, l0, t0, later, later_total,
                 o0, o1, o2, o3, sub):
     p, _, _, _ = combine(
-        pos[0], 4, own[...], own_total[0:1, :], prior[...], prior_total[0:1, :], (r1, r2, r3)
+        lax.axis_index("z"), 4, own[...], own_total[0:1, :], prior[...], prior_total[0:1, :],
+        (r1, r2, r3),
     )
     sub[0] = p
     p = p * jnp.exp(t0[0:1, :]) + l0[...]
@@ -288,38 +348,38 @@
     for j in range(2):
         p = p * jnp.exp(later_total[j, 0:1, :]) + later[j]
         sub[j + 2] = p
-    h = pos[1]
+    h = lax.axis_index(HEAD)
     for k, out in enumerate((o0, o1, o2, o3)):
         out[...] = sub[h ^ k].astype(BF)
 
 
-def last_stage(pos, own, own_total, prior, prior_total, received, l0, t0, later, later_total):
+def last_stage(own, own_total, prior, received, l0, t0, later, later_total):
     return pl.pallas_call(
         last_kernel,
-        in_specs=[SMEM] + [VM] * 11,
+        in_specs=[VM] * 11,
         out_specs=[VM] * 4,
         out_shape=[sds((256, 128), BF)] * 4,
         scratch_shapes=[pltpu.VMEM((4, 256, 128), F32)],
+        compiler_params=few(6),
         name="chain_last",
-    )(pos, own, own_total, prior, prior_total, *received, l0, t0, later, later_total)
+    )(own, own_total, *prior, *received, l0, t0, later, later_total)
+
+
+def begin(before, wv, ws, cv, run, run_log):
+    project(before, wv[...], cv, 0, 0)
+    project(before, ws[...], cv, 0, 4)
+    run[...] = jnp.zeros_like(run)
+    run_log[...] = jnp.zeros_like(run_log)
 
 
 def scan_block(
-    normed, wg, wv, ws, wst, taps, bias, decay, first, rim_normed,
+    normed, wg, wv, ws, wst, taps, bias, decay,
     lead, tail_out, maps_out, cv, act, sc, run, run_log,
 ):
-    @pl.when(first)
-    def _():
-        before = rim_normed()
-        cv[0:16, 0:512] = rounded(dot(before, wv[...]))
-        cv[0:16, 512:1024] = rounded(dot(before, ws[...]))
-        run[...] = jnp.zeros_like(run)
-        run_log[...] = jnp.zeros_like(run_log)
-
-    cv[16:272, 0:512] = rounded(dot(normed, wv[...]))
-    cv[16:272, 512:1024] = rounded(dot(normed, ws[...]))
-    convolve(cv, act, taps, 1024, BLK)
-    cv[0:16, :] = cv[256:272, :]
+    project(normed, wv[...], cv, 16, 0)
+    project(normed, ws[...], cv, 16, 4)
+    convolve(cv, act, taps, BLK)
+    cv[:, 0:16, :] = cv[:, 256:272, :]
     raw = dot(wst[...], normed, NT)
     dt = softplus(raw + bias[...])
     logs = -dt * decay[...]
@@ -335,8 +395,8 @@
         (iota((32, 128), 0) < 24) & (iota((32, 128), 0) % 8 == iota((32, 128), 1)), 1.0, 0.0
     ).astype(BF), TN)
     rows = cum - jnp.log(dt)
-    in_map = act[:, 512:768]
-    out_map = act[:, 768:1024]
+    in_map = jnp.concatenate([act[4].astype(BF), act[5].astype(BF)], 1)
+    out_map = jnp.concatenate([act[6].astype(BF), act[7].astype(BF)], 1)
     maps_out[...] = out_map
     sc[...] = dot(out_map, in_map, NT)
     carried = dot(out_map, run[...].astype(BF))
@@ -344,7 +404,7 @@
     lane_low = iota((BLK, 128), 1) < 64
     for p in range(4):
         cols = slice(p * 128, (p + 1) * 128)
-        vals = act[:, cols].astype(F32)
+        vals = act[p]
         v0 = jnp.where(lane_low, vals, 0.0).astype(BF)
         v1 = jnp.where(lane_low, 0.0, vals).astype(BF)
         upper_w, lower_w = [], []
@@ -362,7 +422,7 @@
             jnp.concatenate(upper_w, 1), jnp.concatenate([v0[0:128], v1[0:128]], 0)
         )
         bottom = dot(jnp.concatenate(lower_w, 1), jnp.concatenate([v0, v1], 0))
-        gate = silu(rounded(dot(normed, wg[:, cols])))
+        gate = silu(dot(normed, wg[:, cols]))
         lead[0:128, cols] = (top + spread[0:128, cols] * carried[0:128, cols]) * gate[0:128]
         lead[128:256, cols] = (
             bottom + spread[128:256, cols] * carried[128:256, cols]
@@ -373,85 +433,110 @@
 
 
 SCAN_SCRATCH = [
-    pltpu.VMEM((272, 1024), F32),
-    pltpu.VMEM((BLK, 1024), BF),
+    pltpu.VMEM((8, 272, 128), F32),
+    pltpu.VMEM((8, BLK, 128), F32),
     pltpu.VMEM((BLK, BLK), F32),
     pltpu.VMEM((256, 512), F32),
     pltpu.VMEM((8, 128), F32),
 ]
 
 
-def fine_main_kernel(
-    h, x, rim_here, rim_there, gain, ws, ks, p0, p1, p2, p3, f0, f1, f2, f3,
-    lead, tail_out, maps_out,
-    wg, wv, wst, taps, bias, decay, cv, act, sc, run, run_log,
-):
-    first = pl.program_id(0) == 0
-
-    @pl.when(first)
+def fine_main_kernel(later, h, x, gain, ws, ks, p0, p1, p2, p3, *refs):
+    (
+        x0, x1, x2, lead, tail_out, maps_out, run, run_log, cv_end,
+        wg, wv, wst, taps, bias, decay, cv, act, sc,
+    ) = refs
+
+    @pl.when(pl.program_id(0) == 0)
     def _():
-        taps[:, 512:1024] = ks[...]
-        for j, (p, f) in enumerate(((p0, f0), (p1, f1), (p2, f2), (p3, f3))):
+        for j in range(4):
+            taps[4 + j] = ks[:, j * 128 : (j + 1) * 128] * 0.5
+        for j, p in enumerate((p0, p1, p2, p3)):
             cols = slice(j * 128, (j + 1) * 128)
+            two = slice(2 * j, 2 * j + 2)
             wg[:, cols] = p[0:256, 0:128]
             wv[:, cols] = p[0:256, 128:256]
-            taps[:, cols] = f[0:4, 0:128]
-            wst[2 * j : 2 * j + 2, :] = f[8:10, :]
-            bias[2 * j : 2 * j + 2, :] = f[10:12, 0:128]
-            decay[2 * j : 2 * j + 2, :] = f[12:14, 0:128]
-
-    def rim_normed():
-        rim = jnp.where(h[0] == 0, rim_there[...].astype(F32), rim_here[...].astype(F32))
-        return rms(rim, gain[...])
+            kv, _, bias[two, :], decay[two, :], wst[two, :] = small_rows(p)
+            taps[j] = kv * 0.5
+        if later:
+            run[...] = x0[...]
+            run_log[...] = x1[...]
+            cv[:, 0:16, :] = x2[...]
+        else:
+            rim = jnp.where(h[0] == 0, x0[...].astype(F32), x1[...].astype(F32))
+            begin(rms(rim, gain[...]), wv, ws, cv, run, run_log)
 
     scan_block(
         rms(x[...], gain[...]), wg, wv, ws, wst[...].astype(BF), taps, bias[:, 0:1], decay[:, 0:1],
-        first, rim_normed, lead, tail_out, maps_out, cv, act, sc, run, run_log,
-    )
-
-
-def fine_main(h, tokens, rim, gain, scans, ks, packs, smalls):
+        lead, tail_out, maps_out, cv, act, sc, run, run_log,
+    )
+    cv_end[...] = cv[:, 0:16, :]
+
+
+def fine_main(h, tokens, gain, scans, ks, packs, extra, later):
+    at = 2 if later else 0
+    if later:
+        specs = [whole_spec((256, 512)), whole_spec((8, 128)), whole_spec((8, 16, 128))]
+    else:
+        specs = [
+            whole_spec((16, 256)),
+            pl.BlockSpec((16, 256), lambda i, h: (jnp.maximum(h[0] * 64 - 1, 0), 0)),
+            whole_spec((8, 128)),
+        ]
     return pl.pallas_call(
-        fine_main_kernel,
+        lambda *refs: fine_main_kernel(later, *refs),
         grid_spec=pltpu.PrefetchScalarGridSpec(
             num_scalar_prefetch=1,
-            grid=(4,),
+            grid=(2,),
             in_specs=[
-                pl.BlockSpec((BLK, 256), lambda i, h: (h[0] * 4 + i, 0)),
-                pl.BlockSpec((16, 256), lambda i, h: (jnp.maximum(h[0] * 64 - 1, 0), 0)),
-                whole_spec((16, 256)),
+                pl.BlockSpec((BLK, 256), lambda i, h: (h[0] * 4 + at + i, 0)),
                 whole_spec((1, 256)),
                 whole_spec((256, 512)),
                 whole_spec((4, 512)),
             ]
-            + [whole_spec((384, 256))] * 4
-            + [whole_spec((16, 256))] * 4,
+            + [whole_spec((416, 256))] * 4
+            + specs,
             out_specs=[
                 pl.BlockSpec((BLK, 512), lambda i, h: (i, 0)),
                 pl.BlockSpec((BLK, 512), lambda i, h: (i, 0)),
                 pl.BlockSpec((BLK, 256), lambda i, h: (i, 0)),
+                whole_spec((256, 512)),
+                whole_spec((8, 128)),
+                whole_spec((8, 16, 128)),
             ],
             scratch_shapes=[
                 pltpu.VMEM((256, 512), BF),
                 pltpu.VMEM((256, 512), BF),
                 pltpu.VMEM((8, 256), F32),
-                pltpu.VMEM((4, 1024), F32),
+                pltpu.VMEM((8, 4, 128), F32),
                 pltpu.VMEM((8, 128), F32),
                 pltpu.VMEM((8, 128), F32),
             ]
-            + SCAN_SCRATCH,
+            + SCAN_SCRATCH[:3],
         ),
-        out_shape=[sds((1024, 512)), sds((1024, 512)), sds((1024, 256), BF)],
-        compiler_params=PARAMS,
-        name="fine_main",
-    )(h, tokens, tokens, rim, gain, scans, ks, *packs, *smalls)
+        out_shape=[
+            sds((512, 512)), sds((512, 512)), sds((512, 256), BF),
+            sds((256, 512)), sds((8, 128)), sds((8, 16, 128)),
+        ],
+        compiler_params=few(20),
+        name="fine_main_b" if later else "fine_main_a",
+    )(h, tokens, gain, scans, ks, *packs, *extra)
 
 
 def fine_close_kernel(
-    h, lead, tail, maps, x, s0, s1, s2, s3, w0, w1, w2, w3, f0, f1, f2, f3, merge,
-    merged, end_rows, hidden,
+    h, lead_a, lead_b, tail_a, tail_b, maps_a, maps_b, x, s0, s1, s2, s3, p0, p1, p2, p3, merge,
+    merged, end_rows, lead, tail, maps, hidden,
 ):
     i = pl.program_id(0)
+
+    @pl.when(i < 2)
+    def _():
+        lead[...], tail[...], maps[...] = lead_a[...], tail_a[...], maps_a[...]
+
+    @pl.when(i >= 2)
+    def _():
+        lead[...], tail[...], maps[...] = lead_b[...], tail_b[...], maps_b[...]
+
     gated = []
     for j, s in enumerate((s0, s1, s2, s3)):
         cols = slice(j * 128, (j + 1) * 128)
@@ -460,8 +545,9 @@
     factor = lax.rsqrt(squares / 512.0 + EPSILON)
     out = x[...].astype(F32)
     total = None
-    for g, w, f in zip(gated, (w0, w1, w2, w3), (f0, f1, f2, f3)):
-        piece = dot((g * factor * f[4:5, 0:128]).astype(BF), w[...])
+    for g, p in zip(gated, (p0, p1, p2, p3)):
+        norm = small_rows(p)[1]
+        piece = dot((g * factor * norm).astype(BF), p[256:384, :])
         total = piece if total is None else total + piece
     start = pl.multiple_of(i * BLK, BLK)
     hidden[0, pl.ds(start, BLK), :] = rounded(out[:, 0:128] + total[:, 0:128])
@@ -483,29 +569,37 @@
         end_rows[...] = result[240:256]
 
 
-def fine_close(h, lead, tail, maps, tokens, states, packs, smalls, merge):
+def fine_close(h, leads, tails, maps, tokens, states, packs, merge):
+    def halves(width):
+        return [
+            pl.BlockSpec((BLK, width), lambda i, h: (jnp.minimum(i, 1), 0)),
+            pl.BlockSpec((BLK, width), lambda i, h: (jnp.maximum(i - 2, 0), 0)),
+        ]
+
     return pl.pallas_call(
         fine_close_kernel,
         grid_spec=pltpu.PrefetchScalarGridSpec(
             num_scalar_prefetch=1,
             grid=(4,),
-            in_specs=[
-                pl.BlockSpec((BLK, 512), lambda i, h: (i, 0)),
-                pl.BlockSpec((BLK, 512), lambda i, h: (i, 0)),
-                pl.BlockSpec((BLK, 256), lambda i, h: (i, 0)),
-                pl.BlockSpec((BLK, 256), lambda i, h: (h[0] * 4 + i, 0)),
-            ]
+            in_specs=halves(512)
+            + halves(512)
+            + halves(256)
+            + [pl.BlockSpec((BLK, 256), lambda i, h: (h[0] * 4 + i, 0))]
             + [whole_spec((256, 128))] * 4
-            + [pl.BlockSpec((128, 256), lambda i, h: (2, 0))] * 4
-            + [whole_spec((16, 256))] * 4
+            + [whole_spec((416, 256))] * 4
             + [whole_spec((1024, 1024))],
             out_specs=[whole_spec((256, 1024)), whole_spec((16, 1024))],
-            scratch_shapes=[pltpu.VMEM((2, 1024, 128), F32)],
+            scratch_shapes=[
+                pltpu.VMEM((BLK, 512), F32),
+                pltpu.VMEM((BLK, 512), F32),
+                pltpu.VMEM((BLK, 256), BF),
+                pltpu.VMEM((2, 1024, 128), F32),
+            ],
         ),
         out_shape=[sds((256, 1024), BF), sds((16, 1024), BF)],
-        compiler_params=PARAMS,
+        compiler_params=few(20),
         name="fine_close",
-    )(h, lead, tail, maps, tokens, *states, *packs, *smalls, merge)
+    )(h, *leads, *tails, *maps, tokens, *states, *packs, merge)
 
 
 def coarse_main_kernel(
@@ -525,19 +619,19 @@
         ]
         for copy in copies:
             copy.start()
-        taps[:, 0:512] = kv[...]
-        taps[:, 512:1024] = ks[...]
+        for j in range(4):
+            cols = slice(j * 128, (j + 1) * 128)
+            taps[j] = kv[:, cols] * 0.5
+            taps[4 + j] = ks[:, cols] * 0.5
+        rim = ra[...].astype(F32) + rb[...].astype(F32) + rc[...].astype(F32)
+        begin(rms(rim, gain[...]), wv, ws, cv, run, run_log)
         for copy in copies:
             copy.wait()
-
-    def rim_normed():
-        rim = ra[...].astype(F32) + rb[...].astype(F32) + rc[...].astype(F32)
-        return rms(rim, gain[...])
 
     share[...] = xs[i, :, pl.ds(pl.multiple_of(h * 256, 256), 256)]
     scan_block(
         rms(xs[i], gain[...]), wg, wv, ws, wst[...], taps, bias[:, 0:1], decay[:, 0:1],
-        first, rim_normed, lead, tail_out, maps_out, cv, act, sc, run, run_log,
+        lead, tail_out, maps_out, cv, act, sc, run, run_log,
     )
 
     @pl.when(i == pl.num_programs(0) - 1)
@@ -594,10 +688,10 @@
         scratch_shapes=[
             pltpu.VMEM((4, 256, 1024), BF),
             pltpu.SemaphoreType.DMA((4,)),
-            pltpu.VMEM((4, 1024), F32),
+            pltpu.VMEM((8, 4, 128), F32),
         ]
         + SCAN_SCRATCH,
-        compiler_params=PARAMS,
+        compiler_params=few(20),
         name="coarse_main",
     )(pos, *pieces, *rims, gain, wg, wv, ws, wst, kv, ks, bias, decay)
 
@@ -615,6 +709,7 @@
         in_specs=[VM],
         out_specs=VM,
         out_shape=sds((32, 16, 256), BF),
+        compiler_params=few(4),
         name="prefix",
     )(got)
 
@@ -657,7 +752,7 @@
         out_specs=[rows] * 4 + [pl.BlockSpec((8, BLK), lambda i: (0, i))],
         out_shape=[sds((1024, 256), BF)] * 4 + [sds((8, 1024))],
         scratch_shapes=[pltpu.VMEM((256, 512), BF)],
-        compiler_params=PARAMS,
+        compiler_params=few(20),
         name="coarse_close",
     )(pos, lead, tail, maps, got, norm, wo)
 
@@ -671,11 +766,14 @@
 
 
 def final(share, kk, sk, far, sq, sq_far):
+    rows = pl.BlockSpec((BLK, 256), lambda i: (i, 0))
     return pl.pallas_call(
         final_kernel,
-        in_specs=[VM] * 6,
-        out_specs=VM,
+        grid=(4,),
+        in_specs=[rows] * 4 + [pl.BlockSpec((8, BLK), lambda i: (0, i))] * 2,
+        out_specs=rows,
         out_shape=sds((1024, 256), BF),
+        compiler_params=few(6),
         name="final",
     )(share, kk, sk, far, sq, sq_far)
 
@@ -689,7 +787,10 @@
 
 
 def round_of(x, axis):
-    return [passed(x, axis, [(j, (j + k) % 4) for j in range(4)]) for k in (1, 2, 3)]
+    got = []
+    for k in (1, 2, 3):
+        got.append(passed(x, axis, [(j, (j + k) % 4) for j in range(4)]))
+    return got
 
 
 def lanes(v):
@@ -702,61 +803,37 @@
     coarse_value, coarse_scans, coarse_steps, coarse_kernel, coarse_taps, coarse_bias,
     coarse_decay, coarse_norm, coarse_output,
 ):
-    head = lax.axis_index(HEAD).astype(jnp.int32)
-
-    def position(axis):
-        return jnp.stack([lax.axis_index(axis).astype(jnp.int32), head])
-
-    here = head[None]
+    here = lax.axis_index(HEAD).astype(jnp.int32)[None]
     rim = passed(tokens[4080:], SEQ, [(i, i + 1) for i in range(31)])
-
-    pack = jnp.concatenate([jnp.concatenate([fine_gate, fine_value], 1), fine_output], 0)
-    zeros = jnp.zeros((4, 128), F32)
-    small = jnp.concatenate(
-        [
-            jnp.concatenate([fine_kernel, zeros], 1),
-            jnp.concatenate([fine_norm[None], jnp.zeros((1, 128), F32)], 1),
-            jnp.zeros((3, 256), F32),
-            fine_steps.T.astype(F32),
-            jnp.broadcast_to(fine_bias[:, None], (2, 256)),
-            jnp.broadcast_to(fine_decay[:, None], (2, 256)),
-            jnp.zeros((2, 256), F32),
-        ],
-        0,
+    pack = packed(
+        fine_bias, fine_decay, fine_gate, fine_value, fine_output, fine_steps.T, fine_kernel,
+        fine_norm[None],
     )
     packs = [pack] + [swapped(pack, m) for m in (1, 2, 3)]
-    smalls = [small] + [swapped(small, m) for m in (1, 2, 3)]
-
     gain = fine_gain[None]
-    wst = jnp.concatenate([fine_steps.T, jnp.zeros((6, 256), BF)], 0)
-    bias = jnp.concatenate([lanes(fine_bias), jnp.zeros((6, 128), F32)], 0)
-    decay = jnp.concatenate([lanes(fine_decay), jnp.zeros((6, 128), F32)], 0)
     later, later_total, (l0, t0, own, own_total, message) = fine_states(
-        tokens, rim, gain, fine_value, fine_scans, wst, fine_kernel, fine_taps, bias, decay
+        tokens, rim, gain, pack, fine_scans, fine_taps
     )
     got = round_of(message, "x")
-    lead, tail, maps = fine_main(here, tokens, rim, gain, fine_scans, fine_taps, packs, smalls)
-    prior, prior_total = jnp.zeros((256, 128), F32), jnp.zeros((8, 128), F32)
-    prior, prior_total, own, own_total, message = middle_stage(
-        4, position("x"), own, own_total, prior, prior_total, got, "chain_x"
-    )
+    first = fine_main(here, tokens, gain, fine_scans, fine_taps, packs, (rim, tokens, t0), False)
+    *prior, own, own_total, message = middle_stage("x", 4, own, own_total, (), got)
     got = [passed(message, "u", [(0, 1), (1, 0)])]
-    prior, prior_total, own, own_total, message = middle_stage(
-        2, position("u"), own, own_total, prior, prior_total, got, "chain_u"
-    )
+    *prior, own, own_total, message = middle_stage("u", 2, own, own_total, prior, got)
     got = round_of(message, "z")
-    subs = last_stage(
-        position("z"), own, own_total, prior, prior_total, got, l0, t0, later, later_total
-    )
+    second = fine_main(
+        here, tokens, gain, fine_scans, fine_taps, packs, first[3:], True
+    )
+    subs = last_stage(own, own_total, prior, got, l0, t0, later, later_total)
     states = [subs[0]] + [swapped(subs[m], m) for m in (1, 2, 3)]
     merged, end_rows = fine_close(
-        here, lead, tail, maps, tokens, states, packs, smalls, merge_weight
-    )
-
+        here, (first[0], second[0]), (first[1], second[1]), (first[2], second[2]), tokens, states,
+        packs, merge_weight,
+    )
+
+    rim_a = passed(end_rows, ALL, [(4 * s + 3, 4 * s + 4) for s in range(31)])
+    rim_b = passed(end_rows, ALL, [(4 * s + 3, 4 * s + 7) for s in range(31)])
     across = swapped(merged, 2)
     beside = swapped(merged, 1)
-    rim_a = passed(end_rows, ALL, [(4 * s + 3, 4 * s + 4) for s in range(31)])
-    rim_b = passed(end_rows, ALL, [(4 * s + 3, 4 * s + 7) for s in range(31)])
     rim_c = swapped(rim_a + rim_b, 1)
     both = swapped(across, 1)
     lead, tail, maps, share, message = coarse_main(
@@ -782,7 +859,8 @@
     from_sk = swapped(sk, 1)
     squares = squares + swapped(squares, 1)
     far = (ks.astype(F32) + from_ss.astype(F32)).astype(BF)
-    return final(share, kk, from_sk, swapped(far, 2), squares, swapped(squares, 2))
+    far = swapped(far, 2)
+    return final(share, kk, from_sk, far, squares, swapped(squares, 2))
 
 
 def solution(mesh):

time: 193 us -> 179 us (0.927)
  local copies, waits for them, and re-layouts: 18 us -> 10.7 us
  other arithmetic: 3.04 us -> 0.16 us
  Pallas kernels: 60.1 us -> 57.4 us
    unnamed x98 -> x56, local copies, waits for them, and re-layouts: 13.6 us -> 9.85 us
    pallas_call x5 -> x7, Pallas kernels: 20 us -> 17.4 us  [the longest x2 13.8 us: fine_main(): pl.pallas_call(lambda *refs: fine_main_kernel(later, *refs), grid_spec=pl...]
    pallas_call x1, Pallas kernels: 8.12 us -> 10.6 us  [fine_states(): pl.pallas_call(later_chunks_kernel, grid=(3,), in_specs=[pl.BlockSpec((10...]
    concatenate x8 -> x0, local copies, waits for them, and re-layouts: 2.19 us -> none  [the longest x2 0.73 us: shards(): bias = jnp.concatenate([lanes(fine_bias), jnp.zeros((6, 128), F32)], 0)]
    another operation x3 -> x0, other arithmetic: 1.95 us -> none  [position(): return jnp.stack([lax.axis_index(axis).astype(jnp.int32), head])]
    ppermute x28 -> x25, waiting for transfers between devices: 35.6 us -> 34.5 us  [passed(): return lax.ppermute(x, axes, pairs)]
    ppermute x28 -> x25, starting transfers between devices: 36 us -> 36.5 us  [passed(): return lax.ppermute(x, axes, pairs)]
  transfers between devices with their start and end apart: 28 -> 25, of which waited for: 11 -> 10; matrix products, arithmetic and copies ran while one was open for 3% -> 0% of each run, Pallas kernels for 15% -> 15%
where the time goes in v1:
time: 179 us; the launch traced here: 178 us
  Pallas kernels  57.4 us (32%)
  blocking collectives  38.5 us (22%)
  starting transfers between devices  36.5 us (20%)
  waiting for transfers between devices  34.5 us (19%)
  local copies, waits for them, and re-layouts  10.7 us (6%)
    ppermute x25, starting transfers between devices, passed(): return lax.ppermute(x, axes, pairs)  36.5 us
    ppermute x25, waiting for transfers between devices, passed(): return lax.ppermute(x, axes, pairs)  34.5 us
    all_to_all x1, blocking collectives, shards(): got = lax.all_to_all(message, SEQ, split_axis=0, concat_axis=0, tiled=True)  24.3 us
    pallas_call x1, Pallas kernels, coarse_main(): pl.pallas_call(coarse_main_kernel, grid=(4,), in_specs=[SMEM] + [ANY] * 4...  17.7 us
    all_to_all x1, blocking collectives, shards(): lax.all_to_all(prefix(got), SEQ, split_axis=0, concat_axis=0, tiled=True)  14.2 us
    pallas_call x2, Pallas kernels, fine_main(): pl.pallas_call(lambda *refs: fine_main_kernel(later, *refs), grid_spec=pl...  13.8 us
    pallas_call x1, Pallas kernels, fine_states(): pl.pallas_call(later_chunks_kernel, grid=(3,), in_specs=[pl.BlockSpec((10...  10.6 us
    unnamed x56, local copies, waits for them, and re-layouts  9.85 us
  transfers between devices with their start and end apart: 25, of which 10 were waited for; matrix products, arithmetic and copies ran while one was open for 0% of the time, Pallas kernels for 15%

profile of v1, /device:TPU:1, one launch (start us, length us, event | category | flops | bytes accessed | tf_op | source)
XLA Modules:
  0.0 178.2 jit_solution(5440953024614549270)
XLA Ops:
  0.0 0.7 slice.3
  0.7 3.9 %collective-permute-start.3 = (bf16[16,256]{1,0:T(8,128)(2,1)S(1)}, bf16[16,256]{1,0:T(8,128)(2,1)S(1)}, u32[]{:S(2)}, u32[]{:S(2)}) collective-permute-start(bf16[16,256]{1,0:T(8,128)(2,1)S(1)} %slice.3), channel_id=1, source_target_pairs={{0,4},{4,8},{8,12},{12,16},{16,20},{20,24},{24,28},{28,32},{32,36}... | collective-permute-start | bytes 24584 | tf_op jit(solution)/shard_map/ppermute | solution.py:782
  4.6 0.8 copy-done.11
  5.5 0.8 copy-done.12
  6.3 0.8 copy-done.13
  7.2 0.7 copy-done.20
  7.8 0.7 copy-done.22
  8.5 0.7 copy-done.23
  9.2 0.7 copy-done.24
  9.8 0.7 copy-done.25
  10.5 0.6 pack.1.refs_5_.p0
  11.1 1.6 copy-done
  12.7 0.9 copy-done.2
  13.6 0.7 copy-done.9
  14.3 0.7 copy-done.15
  15.0 10.6 %later_chunks.1 = (f32[3,256,128]{2,1,0:T(8,128)S(1)}, f32[3,8,128]{2,1,0:T(8,128)S(1)}) custom-call(bf16[4096,256]{1,0:T(8,128)(2,1)S(1)} %copy-done, bf16[4096,256]{1,0:T(8,128)(2,1)S(1)} %copy-done, f32[1,256]{1,0:T(1,128)S(1)} %bitcast.8, bf16[416,256]{1,0:T(8,128)(2,1)S(1)} %pack.1.refs_5_.p0, bf16[256,512]{1,0:T(8,128)(2,1)S(1)} %copy-done.2, ...), custom_call_target="tpu_custom_call" | custom-call | tf_op jit(solution)/shard_map/later_chunks/pallas_call | solution.py:240
  25.7 3.5 %first_chunk.1 = (f32[256,128]{1,0:T(8,128)S(1)}, f32[8,128]{1,0:T(8,128)S(1)}, f32[256,128]{1,0:T(8,128)S(1)}, f32[8,128]{1,0:T(8,128)S(1)}, bf16[272,128]{1,0:T(8,128)(2,1)S(1)}) custom-call(bf16[4096,256]{1,0:T(8,128)(2,1)S(1)} %copy-done, bf16[16,256]{1,0:T(8,128)(2,1)S(1)} %collective-permute-done.3.rim.refs_9_, f32[1,256]{1,0:T(1,128)S(1)} %bitcast.9, ...), custom_call_target="tpu_custom_call" | custom-call | tf_op jit(solution)/shard_map/first_chunk/pallas_call | solution.py:257
  29.2 4.2 %collective-permute-start.6 = (bf16[272,128]{1,0:T(8,128)(2,1)S(1)}, bf16[272,128]{1,0:T(8,128)(2,1)S(1)}, u32[]{:S(2)}, u32[]{:S(2)}) collective-permute-start(bf16[272,128]{1,0:T(8,128)(2,1)S(1)} %get-tuple-element.61), channel_id=1, source_target_pairs={{0,12},{4,0},{8,4},{12,8},{1,13},{5,1},{9,5},{13,9},{2,14},{6,2},{... | collective-permute-start | bytes 208904 | tf_op jit(solution)/shard_map/ppermute | solution.py:782
  33.4 0.7 collective-permute-start.4
  34.0 1.8 %collective-permute-start.2 = (bf16[416,256]{1,0:T(8,128)(2,1)S(1)}, bf16[416,256]{1,0:T(8,128)(2,1)S(1)}, u32[]{:S(2)}, u32[]{:S(2)}) collective-permute-start(bf16[416,256]{1,0:T(8,128)(2,1)S(1)} %pack.1.refs_5_.p0), channel_id=1, source_target_pairs={{0,3},{1,2},{2,1},{3,0},{4,7},{5,6},{6,5},{7,4},{8,11},{9,10},{10,... | collective-permute-start | bytes 638984 | tf_op jit(solution)/shard_map/ppermute | solution.py:782
  35.8 2.3 %collective-permute-done.5.refs_3_ = bf16[272,128]{1,0:T(8,128)(2,1)S(1)} collective-permute-done((bf16[272,128]{1,0:T(8,128)(2,1)S(1)}, bf16[272,128]{1,0:T(8,128)(2,1)S(1)}, u32[]{:S(2)}, u32[]{:S(2)}) %collective-permute-start.5) | collective-permute-done | bytes 69664 | tf_op jit(solution)/shard_map/ppermute | solution.py:782
  38.1 0.4 collective-permute-done.4.refs_2_
  38.5 0.1 shard_map.226
  38.6 1.8 collective-permute-start.7
  40.4 1.0 collective-permute-start.1
  41.4 2.9 %collective-permute-start = (bf16[416,256]{1,0:T(8,128)(2,1)S(1)}, bf16[416,256]{1,0:T(8,128)(2,1)S(1)}, u32[]{:S(2)}, u32[]{:S(2)}) collective-permute-start(bf16[416,256]{1,0:T(8,128)(2,1)S(1)} %pack.1.refs_5_.p0), channel_id=1, source_target_pairs={{0,1},{1,0},{2,3},{3,2},{4,5},{5,4},{6,7},{7,6},{8,9},{9,8},{10,11... | collective-permute-start | bytes 638984 | tf_op jit(solution)/shard_map/ppermute | solution.py:782
  44.4 3.2 %collective-permute-start.10 = (bf16[272,128]{1,0:T(8,128)(2,1)S(1)}, bf16[272,128]{1,0:T(8,128)(2,1)S(1)}, u32[]{:S(2)}, u32[]{:S(2)}) collective-permute-start(bf16[272,128]{1,0:T(8,128)(2,1)S(1)} %get-tuple-element.71), channel_id=1, source_target_pairs={{0,96},{32,0},{64,32},{96,64},{1,97},{33,1},{65,33},{97,65},{2,98}... | collective-permute-start | bytes 208904 | tf_op jit(solution)/shard_map/ppermute | solution.py:782
  47.6 0.4 collective-permute-start.9
  48.0 1.0 collective-permute-done.10.r3
  49.0 0.6 collective-permute-start.8
  49.6 2.7 %collective-permute-done.9.r2 = bf16[272,128]{1,0:T(8,128)(2,1)S(1)} collective-permute-done((bf16[272,128]{1,0:T(8,128)(2,1)S(1)}, bf16[272,128]{1,0:T(8,128)(2,1)S(1)}, u32[]{:S(2)}, u32[]{:S(2)}) %collective-permute-start.9) | collective-permute-done | bytes 69664 | tf_op jit(solution)/shard_map/ppermute | solution.py:782
  52.3 1.4 collective-permute-done.8.r1
  53.7 0.8 chain_last.1
  54.5 5.7 %collective-permute-start.11 = (bf16[256,128]{1,0:T(8,128)(2,1)}, bf16[256,128]{1,0:T(8,128)(2,1)S(1)}, u32[]{:S(2)}, u32[]{:S(2)}) collective-permute-start(bf16[256,128]{1,0:T(8,128)(2,1)} %get-tuple-element.74), channel_id=1, source_target_pairs={{0,1},{1,0},{2,3},{3,2},{4,5},{5,4},{6,7},{7,6},{8,9},{9,8},{10,11... | collective-permute-start | bytes 196616 | tf_op jit(solution)/shard_map/ppermute | solution.py:782
  60.2 0.4 collective-permute-start.12
  60.6 1.2 collective-permute-start.13
  61.9 6.6 %fine_main_a.1 = (f32[512,512]{1,0:T(8,128)S(1)}, f32[512,512]{1,0:T(8,128)S(1)}, bf16[512,256]{1,0:T(8,128)(2,1)S(1)}, f32[256,512]{1,0:T(8,128)S(1)}, f32[8,128]{1,0:T(8,128)S(1)}, /*index=5*/f32[8,16,128]{2,1,0:T(8,128)S(1)}) custom-call(s32[1]{0:T(128)} %bitcast.refs_0_.h.pos, bf16[4096,256]{1,0:T(8,128)(2,1)S(1)} %copy-done.1, f32[1,256]{1,0:T(1,128)S(1)} %bitcast.10, ...), custom_call_target="tpu_custom_call" | custom-call | tf_op jit(solution)/shard_map/fine_main_a/pallas_call | solution.py:486
  68.5 7.2 %fine_main_b.1 = (f32[512,512]{1,0:T(8,128)S(1)}, f32[512,512]{1,0:T(8,128)S(1)}, bf16[512,256]{1,0:T(8,128)(2,1)S(1)}, f32[256,512]{1,0:T(8,128)}, f32[8,128]{1,0:T(8,128)}, /*index=5*/f32[8,16,128]{2,1,0:T(8,128)}) custom-call(s32[1]{0:T(128)} %bitcast.refs_0_.h.pos, bf16[4096,256]{1,0:T(8,128)(2,1)S(1)} %copy-done.1, f32[1,256]{1,0:T(1,128)S(1)} %bitcast.11, ...), custom_call_target="tpu_custom_call" | custom-call | tf_op jit(solution)/shard_map/fine_main_b/pallas_call | solution.py:486
  75.8 4.9 %fine_close.1 = (bf16[256,1024]{1,0:T(8,128)(2,1)S(1)}, bf16[16,1024]{1,0:T(8,128)(2,1)S(1)}) custom-call(s32[1]{0:T(128)} %bitcast.refs_0_.h.pos, f32[512,512]{1,0:T(8,128)S(1)} %get-tuple-element.50.lead_a, f32[512,512]{1,0:T(8,128)S(1)} %get-tuple-element.54.lead_b, f32[512,512]{1,0:T(8,128)S(1)} %get-tuple-element.55.tail_a, ...), custom_call_target="tpu_custom_call" | custom-call | tf_op jit(solution)/shard_map/fine_close/pallas_call | solution.py:579
  80.8 0.5 collective-permute-start.15
  81.3 0.5 collective-permute-start.14
  81.8 12.3 %collective-permute-done.15.q2 = bf16[256,1024]{1,0:T(8,128)(2,1)S(1)} collective-permute-done((bf16[256,1024]{1,0:T(8,128)(2,1)S(1)}, bf16[256,1024]{1,0:T(8,128)(2,1)S(1)}, u32[]{:S(2)}, u32[]{:S(2)}) %collective-permute-start.15) | collective-permute-done | bytes 524320 | tf_op jit(solution)/shard_map/ppermute | solution.py:782
  94.1 1.1 collective-permute-start.16
  95.2 0.7 collective-permute-start.18
  95.9 0.7 collective-permute-start.17
  96.6 0.1 collective-permute-start.19
  96.7 1.2 collective-permute-done.19.rc
  97.9 0.1 broadcast_in_dim.31.bias
  97.9 0.1 broadcast_in_dim.32.decay
  98.1 17.7 %coarse_main.1 = (f32[1024,512]{1,0:T(8,128)S(1)}, f32[1024,512]{1,0:T(8,128)S(1)}, bf16[1024,256]{1,0:T(8,128)(2,1)S(1)}, bf16[1024,256]{1,0:T(8,128)(2,1)S(1)}, bf16[32,32,256]{2,1,0:T(8,128)(2,1)S(1)}) custom-call(s32[1]{0:T(128)} %bitcast.refs_0_.h.pos, bf16[256,1024]{1,0:T(8,128)(2,1)S(1)} %get-tuple-element.77.q0, ...), custom_call_target="tpu_custom_call" | custom-call | tf_op jit(solution)/shard_map/coarse_main/pallas_call | solution.py:657
  115.8 24.3 %all_to_all.10.got = bf16[32,32,256]{2,1,0:T(8,128)(2,1)S(1)} all-to-all(bf16[32,32,256]{2,1,0:T(8,128)(2,1)S(1)} %get-tuple-element.83), channel_id=1, replica_groups=mesh['z'=4,'u'=2,'x'=4,'y'=2,'c'=2] {'z','u','x'}, dimensions={0} | all-to-all | bytes 1048576 | tf_op jit(solution)/shard_map/all_to_all | solution.py:853
  140.1 0.1 prefix.1
  140.2 14.2 %all_to_all.11.got = bf16[32,16,256]{2,1,0:T(8,128)(2,1)S(1)} all-to-all(bf16[32,16,256]{2,1,0:T(8,128)(2,1)S(1)} %prefix.1), channel_id=1, replica_groups=mesh['z'=4,'u'=2,'x'=4,'y'=2,'c'=2] {'z','u','x'}, dimensions={0} | all-to-all | bytes 524288 | tf_op jit(solution)/shard_map/all_to_all | solution.py:854
  154.4 3.1 %coarse_close.1 = (bf16[1024,256]{1,0:T(8,128)(2,1)S(1)}, bf16[1024,256]{1,0:T(8,128)(2,1)S(1)}, bf16[1024,256]{1,0:T(8,128)(2,1)S(1)}, bf16[1024,256]{1,0:T(8,128)(2,1)S(1)}, f32[8,1024]{1,0:T(8,128)S(1)}) custom-call(s32[1]{0:T(128)} %bitcast.refs_0_.h.pos, f32[1024,512]{1,0:T(8,128)S(1)} %get-tuple-element.80.lead, ...), custom_call_target="tpu_custom_call" | custom-call | tf_op jit(solution)/shard_map/coarse_close/pallas_call | solution.py:740
  157.6 2.9 %collective-permute-start.21 = (bf16[1024,256]{1,0:T(8,128)(2,1)S(1)}, bf16[1024,256]{1,0:T(8,128)(2,1)S(1)}, u32[]{:S(2)}, u32[]{:S(2)}) collective-permute-start(bf16[1024,256]{1,0:T(8,128)(2,1)S(1)} %get-tuple-element.87), channel_id=1, source_target_pairs={{0,1},{1,0},{2,3},{3,2},{4,5},{5,4},{6,7},{7,6},{8,9},{9,8},{10,11... | collective-permute-start | bytes 1572872 | tf_op jit(solution)/shard_map/ppermute | solution.py:782
  160.5 0.1 collective-permute-start.20
  160.6 1.4 collective-permute-done.21
  162.1 0.1 add_convert_fusion
  162.2 0.1 collective-permute-start.22
  162.3 0.5 collective-permute-start.23
  162.8 0.9 collective-permute-done.23
  163.6 1.7 collective-permute-start.24
  165.3 10.8 %collective-permute-done.24.sq_far = f32[8,1024]{1,0:T(8,128)S(1)} collective-permute-done((f32[8,1024]{1,0:T(8,128)S(1)}, f32[8,1024]{1,0:T(8,128)S(1)}, u32[]{:S(2)}, u32[]{:S(2)}) %collective-permute-start.24) | collective-permute-done | bytes 32800 | tf_op jit(solution)/shard_map/ppermute | solution.py:782
  176.1 2.1 %final.1 = bf16[1024,256]{1,0:T(8,128)(2,1)} custom-call(bf16[1024,256]{1,0:T(8,128)(2,1)S(1)} %get-tuple-element.79.share, bf16[1024,256]{1,0:T(8,128)(2,1)S(1)} %get-tuple-element.84.kk, bf16[1024,256]{1,0:T(8,128)(2,1)S(1)} %collective-permute-done.20.sk, bf16[1024,256]{1,0:T(8,128)(2,1)S(1)} %collective-permute-done.22.far, f32[8,1024]{1,0:T(8,128)S(1)} %add.15.sq, ...), custom_call_target="tpu_custom_call" | custom-call | tf_op jit(solution)/shard_map/final/pallas_call | solution.py:770
  (63 shorter events, 0.3 us)
Async XLA Ops:
  0.7 24.9 %collective-permute-start.3 = (bf16[16,256]{1,0:T(8,128)(2,1)S(1)}, bf16[16,256]{1,0:T(8,128)(2,1)S(1)}, u32[]{:S(2)}, u32[]{:S(2)}) collective-permute-start(bf16[16,256]{1,0:T(8,128)(2,1)S(1)} %slice.3), channel_id=1, source_target_pairs={{0,4},{4,8},{8,12},{12,16},{16,20},{20,24},{24,28},{28,32},{32,36}... | collective-permute-start | bytes 24584 | tf_op jit(solution)/shard_map/ppermute | solution.py:782
  4.6 0.8 copy-start.11
  5.5 0.8 copy-start.12
  6.3 0.8 copy-start.13
  7.2 0.7 copy-start.20
  7.8 0.7 copy-start.22
  8.5 0.7 copy-start.23
  9.2 0.7 copy-start.24
  9.8 0.7 copy-start.25
  11.1 1.6 copy-start
  12.7 0.9 copy-start.2
  13.6 0.7 copy-start.9
  14.3 0.7 copy-start.15
  25.6 36.3 %copy-start.1 = (bf16[4096,256]{1,0:T(8,128)(2,1)S(1)}, bf16[4096,256]{1,0:T(8,128)(2,1)}, u32[]{:S(2)}) copy-start(bf16[4096,256]{1,0:T(8,128)(2,1)} %x.5) | copy-start | bytes 6291460
  25.6 36.2 %copy-start.3 = (bf16[256,512]{1,0:T(8,128)(2,1)S(1)}, bf16[256,512]{1,0:T(8,128)(2,1)}, u32[]{:S(2)}) copy-start(bf16[256,512]{1,0:T(8,128)(2,1)} %refs_3_.3) | copy-start | bytes 786436
  25.6 36.2 %copy-start.10 = (f32[4,512]{1,0:T(4,128)S(1)}, f32[4,512]{1,0:T(4,128)}, u32[]{:S(2)}) copy-start(f32[4,512]{1,0:T(4,128)} %refs_4_.3) | copy-start | bytes 24580
  25.7 36.2 %copy-start.16 = (f32[256]{0:T(256)S(1)}, f32[256]{0:T(256)}, u32[]{:S(2)}) copy-start(f32[256]{0:T(256)} %param.25) | copy-start | bytes 3076
  29.2 6.6 %collective-permute-start.6 = (bf16[272,128]{1,0:T(8,128)(2,1)S(1)}, bf16[272,128]{1,0:T(8,128)(2,1)S(1)}, u32[]{:S(2)}, u32[]{:S(2)}) collective-permute-start(bf16[272,128]{1,0:T(8,128)(2,1)S(1)} %get-tuple-element.61), channel_id=1, source_target_pairs={{0,12},{4,0},{8,4},{12,8},{1,13},{5,1},{9,5},{13,9},{2,14},{6,2},{... | collective-permute-start | bytes 208904 | tf_op jit(solution)/shard_map/ppermute | solution.py:782
  33.4 4.8 %collective-permute-start.5 = (bf16[272,128]{1,0:T(8,128)(2,1)S(1)}, bf16[272,128]{1,0:T(8,128)(2,1)S(1)}, u32[]{:S(2)}, u32[]{:S(2)}) collective-permute-start(bf16[272,128]{1,0:T(8,128)(2,1)S(1)} %get-tuple-element.61), channel_id=1, source_target_pairs={{0,8},{4,12},{8,0},{12,4},{1,9},{5,13},{9,1},{13,5},{2,10},{6,14},... | collective-permute-start | bytes 208904 | tf_op jit(solution)/shard_map/ppermute | solution.py:782
  33.4 5.1 %collective-permute-start.4 = (bf16[272,128]{1,0:T(8,128)(2,1)S(1)}, bf16[272,128]{1,0:T(8,128)(2,1)S(1)}, u32[]{:S(2)}, u32[]{:S(2)}) collective-permute-start(bf16[272,128]{1,0:T(8,128)(2,1)S(1)} %get-tuple-element.61), channel_id=1, source_target_pairs={{0,4},{4,8},{8,12},{12,0},{1,5},{5,9},{9,13},{13,1},{2,6},{6,10},{... | collective-permute-start | bytes 208904 | tf_op jit(solution)/shard_map/ppermute | solution.py:782
  34.0 26.6 %collective-permute-start.2 = (bf16[416,256]{1,0:T(8,128)(2,1)S(1)}, bf16[416,256]{1,0:T(8,128)(2,1)S(1)}, u32[]{:S(2)}, u32[]{:S(2)}) collective-permute-start(bf16[416,256]{1,0:T(8,128)(2,1)S(1)} %pack.1.refs_5_.p0), channel_id=1, source_target_pairs={{0,3},{1,2},{2,1},{3,0},{4,7},{5,6},{6,5},{7,4},{8,11},{9,10},{10,... | collective-permute-start | bytes 638984 | tf_op jit(solution)/shard_map/ppermute | solution.py:782
  38.6 5.7 %collective-permute-start.7 = (bf16[272,128]{1,0:T(8,128)(2,1)S(1)}, bf16[272,128]{1,0:T(8,128)(2,1)S(1)}, u32[]{:S(2)}, u32[]{:S(2)}) collective-permute-start(bf16[272,128]{1,0:T(8,128)(2,1)S(1)} %get-tuple-element.66), channel_id=1, source_target_pairs={{0,16},{16,0},{1,17},{17,1},{2,18},{18,2},{3,19},{19,3},{4,20},{20... | collective-permute-start | bytes 208904 | tf_op jit(solution)/shard_map/ppermute | solution.py:782
  40.4 21.5 %collective-permute-start.1 = (bf16[416,256]{1,0:T(8,128)(2,1)S(1)}, bf16[416,256]{1,0:T(8,128)(2,1)S(1)}, u32[]{:S(2)}, u32[]{:S(2)}) collective-permute-start(bf16[416,256]{1,0:T(8,128)(2,1)S(1)} %pack.1.refs_5_.p0), channel_id=1, source_target_pairs={{0,2},{1,3},{2,0},{3,1},{4,6},{5,7},{6,4},{7,5},{8,10},{9,11},{10,... | collective-permute-start | bytes 638984 | tf_op jit(solution)/shard_map/ppermute | solution.py:782
  41.4 20.5 %collective-permute-start = (bf16[416,256]{1,0:T(8,128)(2,1)S(1)}, bf16[416,256]{1,0:T(8,128)(2,1)S(1)}, u32[]{:S(2)}, u32[]{:S(2)}) collective-permute-start(bf16[416,256]{1,0:T(8,128)(2,1)S(1)} %pack.1.refs_5_.p0), channel_id=1, source_target_pairs={{0,1},{1,0},{2,3},{3,2},{4,5},{5,4},{6,7},{7,6},{8,9},{9,8},{10,11... | collective-permute-start | bytes 638984 | tf_op jit(solution)/shard_map/ppermute | solution.py:782
  44.4 4.6 %collective-permute-start.10 = (bf16[272,128]{1,0:T(8,128)(2,1)S(1)}, bf16[272,128]{1,0:T(8,128)(2,1)S(1)}, u32[]{:S(2)}, u32[]{:S(2)}) collective-permute-start(bf16[272,128]{1,0:T(8,128)(2,1)S(1)} %get-tuple-element.71), channel_id=1, source_target_pairs={{0,96},{32,0},{64,32},{96,64},{1,97},{33,1},{65,33},{97,65},{2,98}... | collective-permute-start | bytes 208904 | tf_op jit(solution)/shard_map/ppermute | solution.py:782
  47.6 4.7 %collective-permute-start.9 = (bf16[272,128]{1,0:T(8,128)(2,1)S(1)}, bf16[272,128]{1,0:T(8,128)(2,1)S(1)}, u32[]{:S(2)}, u32[]{:S(2)}) collective-permute-start(bf16[272,128]{1,0:T(8,128)(2,1)S(1)} %get-tuple-element.71), channel_id=1, source_target_pairs={{0,64},{32,96},{64,0},{96,32},{1,65},{33,97},{65,1},{97,33},{2,66}... | collective-permute-start | bytes 208904 | tf_op jit(solution)/shard_map/ppermute | solution.py:782
  49.0 4.7 %collective-permute-start.8 = (bf16[272,128]{1,0:T(8,128)(2,1)S(1)}, bf16[272,128]{1,0:T(8,128)(2,1)S(1)}, u32[]{:S(2)}, u32[]{:S(2)}) collective-permute-start(bf16[272,128]{1,0:T(8,128)(2,1)S(1)} %get-tuple-element.71), channel_id=1, source_target_pairs={{0,32},{32,64},{64,96},{96,0},{1,33},{33,65},{65,97},{97,1},{2,34}... | collective-permute-start | bytes 208904 | tf_op jit(solution)/shard_map/ppermute | solution.py:782
  54.5 21.2 %collective-permute-start.11 = (bf16[256,128]{1,0:T(8,128)(2,1)}, bf16[256,128]{1,0:T(8,128)(2,1)S(1)}, u32[]{:S(2)}, u32[]{:S(2)}) collective-permute-start(bf16[256,128]{1,0:T(8,128)(2,1)} %get-tuple-element.74), channel_id=1, source_target_pairs={{0,1},{1,0},{2,3},{3,2},{4,5},{5,4},{6,7},{7,6},{8,9},{9,8},{10,11... | collective-permute-start | bytes 196616 | tf_op jit(solution)/shard_map/ppermute | solution.py:782
  60.2 15.5 %collective-permute-start.12 = (bf16[256,128]{1,0:T(8,128)(2,1)}, bf16[256,128]{1,0:T(8,128)(2,1)S(1)}, u32[]{:S(2)}, u32[]{:S(2)}) collective-permute-start(bf16[256,128]{1,0:T(8,128)(2,1)} %get-tuple-element.75), channel_id=1, source_target_pairs={{0,2},{1,3},{2,0},{3,1},{4,6},{5,7},{6,4},{7,5},{8,10},{9,11},{10,... | collective-permute-start | bytes 196616 | tf_op jit(solution)/shard_map/ppermute | solution.py:782
  60.6 15.1 %collective-permute-start.13 = (bf16[256,128]{1,0:T(8,128)(2,1)}, bf16[256,128]{1,0:T(8,128)(2,1)S(1)}, u32[]{:S(2)}, u32[]{:S(2)}) collective-permute-start(bf16[256,128]{1,0:T(8,128)(2,1)} %get-tuple-element.76), channel_id=1, source_target_pairs={{0,3},{1,2},{2,1},{3,0},{4,7},{5,6},{6,5},{7,4},{8,11},{9,10},{10,... | collective-permute-start | bytes 196616 | tf_op jit(solution)/shard_map/ppermute | solution.py:782
  68.5 7.2 %copy-start.4 = (bf16[1024,1024]{1,0:T(8,128)(2,1)S(1)}, bf16[1024,1024]{1,0:T(8,128)(2,1)}, u32[]{:S(2)}) copy-start(bf16[1024,1024]{1,0:T(8,128)(2,1)} %merge.1) | copy-start | bytes 6291460
  75.7 22.1 %copy-start.26 = (f32[8]{0:T(128)S(1)}, f32[8]{0:T(128)}, u32[]{:S(2)}) copy-start(f32[8]{0:T(128)} %param.44) | copy-start | bytes 100
  75.7 22.2 %copy-start.27 = (f32[8]{0:T(128)S(1)}, f32[8]{0:T(128)}, u32[]{:S(2)}) copy-start(f32[8]{0:T(128)} %param.45) | copy-start | bytes 100
  75.7 22.3 %copy-start.5 = (bf16[1024,512]{1,0:T(8,128)(2,1)S(1)}, bf16[1024,512]{1,0:T(8,128)(2,1)}, u32[]{:S(2)}) copy-start(bf16[1024,512]{1,0:T(8,128)(2,1)} %wg.1) | copy-start | bytes 3145732
  75.8 22.3 %copy-start.6 = (bf16[1024,512]{1,0:T(8,128)(2,1)S(1)}, bf16[1024,512]{1,0:T(8,128)(2,1)}, u32[]{:S(2)}) copy-start(bf16[1024,512]{1,0:T(8,128)(2,1)} %wv.1) | copy-start | bytes 3145732
  75.8 22.2 %copy-start.7 = (bf16[1024,512]{1,0:T(8,128)(2,1)S(1)}, bf16[1024,512]{1,0:T(8,128)(2,1)}, u32[]{:S(2)}) copy-start(bf16[1024,512]{1,0:T(8,128)(2,1)} %ws.1) | copy-start | bytes 3145732
  75.8 22.2 %copy-start.14 = (bf16[1024,8]{0,1:T(8,128)(2,1)S(1)}, bf16[1024,8]{0,1:T(8,128)(2,1)}, u32[]{:S(2)}) copy-start(bf16[1024,8]{0,1:T(8,128)(2,1)} %param.41) | copy-start | bytes 49156
  75.8 22.2 %copy-start.17 = (f32[4,512]{1,0:T(4,128)S(1)}, f32[4,512]{1,0:T(4,128)}, u32[]{:S(2)}) copy-start(f32[4,512]{1,0:T(4,128)} %kv.3) | copy-start | bytes 24580
  75.8 22.2 %copy-start.18 = (f32[4,512]{1,0:T(4,128)S(1)}, f32[4,512]{1,0:T(4,128)}, u32[]{:S(2)}) copy-start(f32[4,512]{1,0:T(4,128)} %ks.5) | copy-start | bytes 24580
  75.8 22.2 %copy-start.19 = (f32[1024]{0:T(1024)S(1)}, f32[1024]{0:T(1024)}, u32[]{:S(2)}) copy-start(f32[1024]{0:T(1024)} %param.37) | copy-start | bytes 12292
  80.8 13.3 %collective-permute-start.15 = (bf16[256,1024]{1,0:T(8,128)(2,1)S(1)}, bf16[256,1024]{1,0:T(8,128)(2,1)S(1)}, u32[]{:S(2)}, u32[]{:S(2)}) collective-permute-start(bf16[256,1024]{1,0:T(8,128)(2,1)S(1)} %get-tuple-element.77.q0), channel_id=1, source_target_pairs={{0,2},{1,3},{2,0},{3,1},{4,6},{5,7},{6,4},{7,5},{8,10},{9,11},{10,... | collective-permute-start | bytes 1572872 | tf_op jit(solution)/shard_map/ppermute | solution.py:782
  81.3 16.6 %collective-permute-start.14 = (bf16[256,1024]{1,0:T(8,128)(2,1)S(1)}, bf16[256,1024]{1,0:T(8,128)(2,1)S(1)}, u32[]{:S(2)}, u32[]{:S(2)}) collective-permute-start(bf16[256,1024]{1,0:T(8,128)(2,1)S(1)} %get-tuple-element.77.q0), channel_id=1, source_target_pairs={{0,1},{1,0},{2,3},{3,2},{4,5},{5,4},{6,7},{7,6},{8,9},{9,8},{10,11... | collective-permute-start | bytes 1572872 | tf_op jit(solution)/shard_map/ppermute | solution.py:782
  94.1 3.8 %collective-permute-start.16 = (bf16[256,1024]{1,0:T(8,128)(2,1)S(1)}, bf16[256,1024]{1,0:T(8,128)(2,1)S(1)}, u32[]{:S(2)}, u32[]{:S(2)}) collective-permute-start(bf16[256,1024]{1,0:T(8,128)(2,1)S(1)} %collective-permute-done.15.q2), channel_id=1, source_target_pairs={{0,1},{1,0},{2,3},{3,2},{4,5},{5,4},{6,7},{7,6},{8,9},{9,8},{10,11... | collective-permute-start | bytes 1572872 | tf_op jit(solution)/shard_map/ppermute | solution.py:782
  95.2 1.3 collective-permute-start.18
  95.9 0.7 collective-permute-start.17
  96.6 1.3 collective-permute-start.19
  115.8 38.7 %copy-start.8 = (bf16[512,1024]{1,0:T(8,128)(2,1)S(1)}, bf16[512,1024]{1,0:T(8,128)(2,1)}, u32[]{:S(2)}) copy-start(bf16[512,1024]{1,0:T(8,128)(2,1)} %wo.1) | copy-start | bytes 3145732
  115.8 38.7 %copy-start.21 = (f32[512]{0:T(512)S(1)}, f32[512]{0:T(512)}, u32[]{:S(2)}) copy-start(f32[512]{0:T(512)} %param.46) | copy-start | bytes 6148
  157.6 4.5 %collective-permute-start.21 = (bf16[1024,256]{1,0:T(8,128)(2,1)S(1)}, bf16[1024,256]{1,0:T(8,128)(2,1)S(1)}, u32[]{:S(2)}, u32[]{:S(2)}) collective-permute-start(bf16[1024,256]{1,0:T(8,128)(2,1)S(1)} %get-tuple-element.87), channel_id=1, source_target_pairs={{0,1},{1,0},{2,3},{3,2},{4,5},{5,4},{6,7},{7,6},{8,9},{9,8},{10,11... | collective-permute-start | bytes 1572872 | tf_op jit(solution)/shard_map/ppermute | solution.py:782
  160.5 15.6 %collective-permute-start.20 = (bf16[1024,256]{1,0:T(8,128)(2,1)S(1)}, bf16[1024,256]{1,0:T(8,128)(2,1)S(1)}, u32[]{:S(2)}, u32[]{:S(2)}) collective-permute-start(bf16[1024,256]{1,0:T(8,128)(2,1)S(1)} %get-tuple-element.85), channel_id=1, source_target_pairs={{0,1},{1,0},{2,3},{3,2},{4,5},{5,4},{6,7},{7,6},{8,9},{9,8},{10,11... | collective-permute-start | bytes 1572872 | tf_op jit(solution)/shard_map/ppermute | solution.py:782
  162.2 13.9 %collective-permute-start.22 = (bf16[1024,256]{1,0:T(8,128)(2,1)S(1)}, bf16[1024,256]{1,0:T(8,128)(2,1)S(1)}, u32[]{:S(2)}, u32[]{:S(2)}) collective-permute-start(bf16[1024,256]{1,0:T(8,128)(2,1)S(1)} %add_convert_fusion), channel_id=1, source_target_pairs={{0,2},{1,3},{2,0},{3,1},{4,6},{5,7},{6,4},{7,5},{8,10},{9,11},{10,... | collective-permute-start | bytes 1572872 | tf_op jit(solution)/shard_map/ppermute | solution.py:782
  162.3 1.3 collective-permute-start.23
  163.6 12.5 %collective-permute-start.24 = (f32[8,1024]{1,0:T(8,128)S(1)}, f32[8,1024]{1,0:T(8,128)S(1)}, u32[]{:S(2)}, u32[]{:S(2)}) collective-permute-start(f32[8,1024]{1,0:T(8,128)S(1)} %add.15.sq), channel_id=1, source_target_pairs={{0,2},{1,3},{2,0},{3,1},{4,6},{5,7},{6,4},{7,5},{8,10},{9,11},{10,... | collective-permute-start | bytes 98312 | tf_op jit(solution)/shard_map/ppermute | solution.py:782

commit v2 on v1

v2 whole, which is shorter than its diff:
```python
import jax
import jax.numpy as jnp
from jax import lax
from jax.experimental import pallas as pl
from jax.experimental.pallas import tpu as pltpu
from jax.sharding import Mesh
from jax.sharding import PartitionSpec as P


SEQ = ("z", "u", "x")
HEAD = ("y", "c")
ALL = ("z", "u", "x", "y", "c")
EPSILON = 1e-05
BLK = 256
BF = jnp.bfloat16
F32 = jnp.float32
NN = (((1,), (0,)), ((), ()))
NT = (((1,), (1,)), ((), ()))
TN = (((0,), (0,)), ((), ()))


def dot(a, b, dims=NN):
    return lax.dot_general(a, b, dims, preferred_element_type=F32)


def parts(x):
    hi = x.astype(BF).astype(F32)
    rest = x - hi
    mid = rest.astype(BF).astype(F32)
    low = rest - mid
    return jnp.concatenate([hi, mid, low, jnp.zeros_like(x)], 0).astype(BF)


def decay_rows(row):
    hi = row.astype(BF).astype(F32)
    rest = row - hi
    mid = rest.astype(BF).astype(F32)
    low = rest - mid
    return jnp.concatenate([hi, mid, low, jnp.zeros((13, row.shape[1]), F32)], 0).astype(BF)


def of_rows(rows):
    rows = rows.astype(F32)
    return rows[0:1] + rows[1:2] + rows[2:3]


def iota(shape, dim):
    return lax.broadcasted_iota(jnp.int32, shape, dim)


def head_sel(width):
    return iota((8, width), 0) == iota((8, width), 1) // 64


def expander(width):
    r, lane = iota((32, width), 0), iota((32, width), 1)
    return jnp.where((r < 24) & (r % 8 == lane // 64), 1.0, 0.0).astype(BF)


def upper():
    return jnp.where(iota((BLK, BLK), 0) <= iota((BLK, BLK), 1), 1.0, 0.0).astype(BF)


def silu(v):
    h = v * 0.5
    return h + h * jnp.tanh(h)


def softplus(v):
    return jnp.maximum(v, 0.0) + jnp.log1p(jnp.exp(-jnp.abs(v)))


def rms(x, gain):
    x = x.astype(F32)
    return (x * lax.rsqrt(jnp.mean(x * x, axis=-1, keepdims=True) + EPSILON) * gain).astype(BF)


def cumulate(logs, tri):
    s = dot(parts(logs), tri)
    return s[0:8] + s[8:16] + s[16:24]


def spaced(length):
    return length // 8 + 1


def convolve(cv, act, half_taps, length):
    apart = spaced(length)

    def slab(c, carry):
        taps = half_taps[c]
        rows = [cv[c, pl.ds(13 + i, 8, stride=apart), :] for i in range(3)]
        for i in range(apart):
            rows.append(cv[c, pl.ds(16 + i, 8, stride=apart), :])
            h = rows[i] * taps[0:1]
            for k in range(1, 4):
                h = h + rows[i + k] * taps[k : k + 1]
            act[c, pl.ds(i, 8, stride=apart), :] = h + h * jnp.tanh(h)
        return carry

    lax.fori_loop(0, cv.shape[0], slab, 0)


def project(rows, weights, cv, start, slab):
    product = dot(rows, weights)
    for j in range(product.shape[1] // 128):
        cv[slab + j, start : start + rows.shape[0], :] = product[:, j * 128 : (j + 1) * 128]


def rounded(x):
    return x.astype(BF).astype(F32)


def small_rows(pack):
    rows = pack[384:416, :].astype(F32)
    kv = rows[0:4, 0:128] + rows[4:8, 0:128] + rows[8:12, 0:128]
    right = rows[0:16, 128:256]
    norm, b0, b1, d0, d1 = (of_rows(right[3 * j : 3 * j + 3]) for j in range(5))
    return kv, norm, jnp.concatenate([b0, b1], 0), jnp.concatenate([d0, d1], 0), rows[16:18]


def three(row):
    hi = row.astype(BF).astype(F32)
    rest = row - hi
    mid = rest.astype(BF).astype(F32)
    return [hi, mid, rest - mid]


def run_copies(pairs, sems):
    copies = [pltpu.make_async_copy(a, b, sems.at[j]) for j, (a, b) in enumerate(pairs)]
    for copy in copies:
        copy.start()
    return copies


def pack_kernel(
    bias, decay, gate, value, output, steps, kv, norm, tokens, pack, ends, kv_v, norm_v, steps_v, sems
):
    copies = run_copies(
        (
            (kv, kv_v),
            (norm, norm_v),
            (steps, steps_v),
            (tokens.at[4080:4096], ends),
            (gate, pack.at[0:256, 0:128]),
            (value, pack.at[0:256, 128:256]),
            (output, pack.at[256:384]),
        ),
        sems,
    )
    for copy in copies[:3]:
        copy.wait()
    left = jnp.concatenate(three(kv_v[...]) + [jnp.zeros((4, 128), F32)], 0)
    rows = three(norm_v[...])
    for ref in (bias, decay):
        for j in range(2):
            rows = rows + three(jnp.full((1, 128), ref[j], F32))
    right = jnp.concatenate(rows + [jnp.zeros((1, 128), F32)], 0)
    below = jnp.concatenate([steps_v[...].astype(F32), jnp.zeros((14, 256), F32)], 0)
    pack[384:416, :] = jnp.concatenate([jnp.concatenate([left, right], 1), below], 0).astype(BF)
    for copy in copies[3:]:
        copy.wait()


def packed(bias, decay, gate, value, output, steps, kv, norm, tokens):
    return pl.pallas_call(
        pack_kernel,
        in_specs=[SMEM] * 2 + [HBM] * 7,
        out_specs=[VM] * 2,
        out_shape=[sds((416, 256), BF), sds((16, 256), BF)],
        scratch_shapes=[
            pltpu.VMEM((4, 128), F32),
            pltpu.VMEM((1, 128), F32),
            pltpu.VMEM((2, 256), BF),
            pltpu.SemaphoreType.DMA((7,)),
        ],
        compiler_params=few(4),
        name="pack",
    )(bias, decay, gate, value, output, steps, kv, norm, tokens)


def params_kernel(bias, decay, kv, ks, gain, steps, norm, taps, both, *refs):
    outs, kv_v, ks_v, sems = refs[:3], *refs[3:]
    copies = run_copies(
        ((kv, kv_v), (ks, ks_v), (gain, outs[0]), (steps, outs[1]), (norm, outs[2])), sems
    )
    for copy in copies:
        copy.wait()
    for j in range(4):
        cols = slice(j * 128, (j + 1) * 128)
        taps[j] = kv_v[:, cols] * 0.5
        taps[4 + j] = ks_v[:, cols] * 0.5
    rows = [jnp.full((1, 128), ref[j], F32) for ref in (bias, decay) for j in range(8)]
    both[...] = jnp.concatenate(rows, 0)


def coarse_params(bias, decay, kv, ks, gain, steps, norm):
    return pl.pallas_call(
        params_kernel,
        in_specs=[SMEM] * 2 + [HBM] * 5,
        out_specs=[VM] * 5,
        out_shape=[
            sds((8, 4, 128)), sds((16, 128)), sds((1, 1024)), sds((8, 1024), BF), sds((1, 512)),
        ],
        scratch_shapes=[
            pltpu.VMEM((4, 512), F32),
            pltpu.VMEM((4, 512), F32),
            pltpu.SemaphoreType.DMA((5,)),
        ],
        compiler_params=few(4),
        name="coarse_params",
    )(bias, decay, kv, ks, gain, steps, norm)


def state_chunk(x, rim, gain, pack, scans, ks, taps, cv, act):
    kv, _, bias, decay, steps = small_rows(pack)
    pad = jnp.zeros((6, 128), F32)
    bias = jnp.concatenate([bias, pad], 0)[:, 0:1]
    decay = jnp.concatenate([decay, pad], 0)[:, 0:1]
    steps = jnp.concatenate([steps, jnp.zeros((6, 256), F32)], 0).astype(BF)
    wv, wb = pack[0:256, 128:256], scans[:, 0:256]
    taps[0] = kv * 0.5
    taps[1] = ks[:, 0:128] * 0.5
    taps[2] = ks[:, 128:256] * 0.5
    normed = rms(x, gain[...])
    before = rms(rim, gain[...])
    project(before, wv, cv, 0, 0)
    project(before, wb, cv, 0, 1)
    project(normed, wv, cv, 16, 0)
    project(normed, wb, cv, 16, 1)
    convolve(cv, act, taps, 1024)
    raw = dot(steps, normed, NT)
    dt = softplus(raw + bias)
    logs = -dt * decay
    tri = upper()
    carry = jnp.zeros((8, 1), F32)
    pieces = []
    for b in range(4):
        piece = cumulate(logs[:, b * BLK : (b + 1) * BLK], tri) + carry
        carry = piece[:, BLK - 1 : BLK]
        pieces.append(piece)
    cum = jnp.concatenate(pieces, 1)
    tail = jnp.exp(carry - cum) * dt
    spread = dot(parts(tail), expander(128), TN)
    scaled = (act[0, 0:1024] * spread).astype(BF)
    local = dot(jnp.concatenate([act[1, 0:1024].astype(BF), act[2, 0:1024].astype(BF)], 1), scaled, TN)
    total = jnp.sum(
        jnp.where(head_sel(128), jnp.broadcast_to(carry, (8, 128)), 0.0), axis=0, keepdims=True
    )
    return local, total


def later_chunks_kernel(
    tokens, gain_h, pack, scans_h, ks_h,
    local, total, x0, mine, mine_rim, gain, scans, ks, xs, taps, cv, act, sems, x_sems,
):
    i = pl.program_id(0)
    start = pl.multiple_of(lax.axis_index(HEAD) * 1024, 1024)
    early = pl.multiple_of(jnp.maximum(start - 16, 0), 16)
    mine_pairs = (
        (tokens.at[0:1024], x0),
        (tokens.at[pl.ds(start, 1024)], mine),
        (tokens.at[pl.ds(early, 16)], mine_rim),
    )

    def chunk(j):
        begin_row = pl.multiple_of((j + 1) * 1024 - 16, 16)
        return pltpu.make_async_copy(tokens.at[pl.ds(begin_row, 1040)], xs.at[j], x_sems.at[j])

    @pl.when(i == 0)
    def _():
        chunk(0).start()
        copies = run_copies(((gain_h, gain), (scans_h, scans), (ks_h, ks)), sems)
        chunk(1).start()
        chunk(2).start()
        for j, (a, b) in enumerate(mine_pairs):
            pltpu.make_async_copy(a, b, sems.at[3 + j]).start()
        for copy in copies:
            copy.wait()

    chunk(i).wait()
    state, logs = state_chunk(xs[i, 16:1040], xs[i, 0:16], gain, pack, scans, ks, taps, cv, act)
    local[i] = state
    total[i] = jnp.broadcast_to(logs, (8, 128))

    @pl.when(i == 2)
    def _():
        for j, (a, b) in enumerate(mine_pairs):
            pltpu.make_async_copy(a, b, sems.at[3 + j]).wait()


def first_chunk_kernel(
    x, rim, gain, pack, scans, ks, later, later_total,
    local, total, whole, whole_total, message, taps, cv, act,
):
    state, logs = state_chunk(x[...], rim[...], gain, pack, scans, ks, taps, cv, act)
    local[...] = state
    total[...] = jnp.broadcast_to(logs, (8, 128))
    for j in range(3):
        piece = later_total[j, 0:1, :]
        state = state * jnp.exp(piece) + later[j]
        logs = logs + piece
    whole[...] = state
    whole_total[...] = jnp.broadcast_to(logs, (8, 128))
    message[0:256, :] = state.astype(BF)
    message[256:272, :] = decay_rows(logs)


def sds(shape, dtype=F32):
    return jax.ShapeDtypeStruct(shape, dtype)


def few(mib):
    return pltpu.CompilerParams(vmem_limit_bytes=mib << 20)


SMEM = pl.BlockSpec(memory_space=pltpu.SMEM)
VM = pl.BlockSpec(memory_space=pltpu.VMEM)
HBM = pl.BlockSpec(memory_space=pltpu.HBM)


def fine_states(tokens, ends_from, gain, pack, scans, ks):
    scratch = [
        pltpu.VMEM((3, 4, 128), F32),
        pltpu.VMEM((3, 1048, 128), F32),
        pltpu.VMEM((3, 1032, 128), F32),
    ]
    later, later_total, x0, *resident = pl.pallas_call(
        later_chunks_kernel,
        grid=(3,),
        in_specs=[HBM, HBM, VM, HBM, HBM],
        out_specs=[VM] * 8,
        out_shape=[
            sds((3, 256, 128)),
            sds((3, 8, 128)),
            sds((1024, 256), BF),
            sds((1024, 256), BF),
            sds((16, 256), BF),
            sds((1, 256)),
            sds((256, 512), BF),
            sds((4, 512)),
        ],
        scratch_shapes=[pltpu.VMEM((3, 1040, 256), BF)]
        + scratch
        + [pltpu.SemaphoreType.DMA((6,)), pltpu.SemaphoreType.DMA((3,))],
        compiler_params=few(16),
        name="later_chunks",
    )(tokens, gain, pack, scans, ks)
    _, _, gain, scans, ks = resident
    first = pl.pallas_call(
        first_chunk_kernel,
        in_specs=[VM] * 8,
        out_specs=[VM] * 5,
        out_shape=[
            sds((256, 128)),
            sds((8, 128)),
            sds((256, 128)),
            sds((8, 128)),
            sds((272, 128), BF),
        ],
        scratch_shapes=scratch,
        compiler_params=few(16),
        name="first_chunk",
    )(x0, ends_from, gain, pack, scans, ks, later, later_total)
    return later, later_total, resident, first


def combine(i, count, own, own_total, prior, prior_total, received):
    state = jnp.zeros_like(own)
    logs = jnp.zeros_like(own_total)
    zero = jnp.zeros((), F32)
    got = [(r[0:256, :].astype(F32), of_rows(r[256:272, :])) for r in received]
    for k in range(count - 1, 0, -1):
        s, l = got[k - 1]
        valid = i >= k
        state = jnp.where(valid, state * jnp.exp(l) + s, state)
        logs = jnp.where(valid, logs + l, logs)
    new_prior = state * jnp.exp(prior_total) + prior
    new_prior_total = logs + prior_total
    state = state * jnp.exp(own_total) + own
    logs = logs + own_total
    for m in range(1, count):
        s, l = got[count - m - 1]
        valid = i + m < count
        state = jnp.where(valid, state * jnp.exp(l) + s, state)
        logs = jnp.where(valid, logs + l, logs)
    return new_prior, new_prior_total, state, logs


def middle_kernel(axis, count, fresh, own, own_total, *refs):
    if fresh:
        prior, prior_total = jnp.zeros((256, 128), F32), jnp.zeros((1, 128), F32)
    else:
        prior, prior_total, refs = refs[0][...], refs[1][0:1, :], refs[2:]
    received, (np_ref, npt_ref, ns_ref, nst_ref, message) = refs[: count - 1], refs[count - 1 :]
    p, pt, s, st = combine(
        lax.axis_index(axis), count, own[...], own_total[0:1, :], prior, prior_total, received
    )
    np_ref[...] = p
    npt_ref[...] = jnp.broadcast_to(pt, (8, 128))
    ns_ref[...] = s
    nst_ref[...] = jnp.broadcast_to(st, (8, 128))
    message[0:256, :] = s.astype(BF)
    message[256:272, :] = decay_rows(st)


def middle_stage(axis, count, own, own_total, prior, received):
    return pl.pallas_call(
        lambda *refs: middle_kernel(axis, count, not prior, *refs),
        in_specs=[VM] * (2 + len(prior) + len(received)),
        out_specs=[VM] * 5,
        out_shape=[
            sds((256, 128)),
            sds((8, 128)),
            sds((256, 128)),
            sds((8, 128)),
            sds((272, 128), BF),
        ],
        compiler_params=few(4),
    )(own, own_total, *prior, *received)


def last_kernel(own, own_total, prior, prior_total, r1, r2, r3, l0, t0, later, later_total,
                o0, o1, o2, o3, sub):
    p, _, _, _ = combine(
        lax.axis_index("z"), 4, own[...], own_total[0:1, :], prior[...], prior_total[0:1, :],
        (r1, r2, r3),
    )
    sub[0] = p
    p = p * jnp.exp(t0[0:1, :]) + l0[...]
    sub[1] = p
    for j in range(2):
        p = p * jnp.exp(later_total[j, 0:1, :]) + later[j]
        sub[j + 2] = p
    h = lax.axis_index(HEAD)
    for k, out in enumerate((o0, o1, o2, o3)):
        out[...] = sub[h ^ k].astype(BF)


def last_stage(own, own_total, prior, received, l0, t0, later, later_total):
    return pl.pallas_call(
        last_kernel,
        in_specs=[VM] * 11,
        out_specs=[VM] * 4,
        out_shape=[sds((256, 128), BF)] * 4,
        scratch_shapes=[pltpu.VMEM((4, 256, 128), F32)],
        compiler_params=few(6),
        name="chain_last",
    )(own, own_total, *prior, *received, l0, t0, later, later_total)


def begin(before, wv, ws, cv, run, run_log):
    project(before, wv[...], cv, 0, 0)
    project(before, ws[...], cv, 0, 4)
    run[...] = jnp.zeros_like(run)
    run_log[...] = jnp.zeros_like(run_log)


def scan_block(
    normed, wg, wv, ws, wst, taps, bias, decay,
    lead, tail_out, maps_out, cv, act, sc, run, run_log,
):
    project(normed, wv[...], cv, 16, 0)
    project(normed, ws[...], cv, 16, 4)
    convolve(cv, act, taps, BLK)
    cv[:, 0:16, :] = cv[:, 256:272, :]
    raw = dot(wst[...], normed, NT)
    dt = softplus(raw + bias[...])
    logs = -dt * decay[...]
    cum = cumulate(logs, upper())
    last = cum[:, BLK - 1 : BLK]
    before_log = run_log[:, 0:1]
    stacked = jnp.concatenate(
        [jnp.exp(cum), jnp.exp(cum + before_log), jnp.exp(last - cum) * dt], 1
    )
    spread = dot(parts(stacked), expander(512), TN)
    run_log[...] = run_log[...] + last
    columns = dot(parts(cum), jnp.where(
        (iota((32, 128), 0) < 24) & (iota((32, 128), 0) % 8 == iota((32, 128), 1)), 1.0, 0.0
    ).astype(BF), TN)
    rows = cum - jnp.log(dt)
    in_map = jnp.concatenate([act[4, 0:BLK].astype(BF), act[5, 0:BLK].astype(BF)], 1)
    out_map = jnp.concatenate([act[6, 0:BLK].astype(BF), act[7, 0:BLK].astype(BF)], 1)
    maps_out[...] = out_map
    sc[...] = dot(out_map, in_map, NT)
    carried = dot(out_map, run[...].astype(BF))
    low_tri = iota((128, 128), 0) >= iota((128, 128), 1)
    lane_low = iota((BLK, 128), 1) < 64
    for p in range(4):
        cols = slice(p * 128, (p + 1) * 128)
        vals = act[p, 0:BLK]
        v0 = jnp.where(lane_low, vals, 0.0).astype(BF)
        v1 = jnp.where(lane_low, 0.0, vals).astype(BF)
        upper_w, lower_w = [], []
        for h in (2 * p, 2 * p + 1):
            c0, c1 = columns[0:128, h : h + 1], columns[128:256, h : h + 1]
            r0, r1 = rows[h : h + 1, 0:128], rows[h : h + 1, 128:256]
            upper_w.append(
                (sc[0:128, 0:128] * jnp.exp(jnp.where(low_tri, c0 - r0, -jnp.inf))).astype(BF)
            )
            lower_w.append((sc[128:256, 0:128] * jnp.exp(c1 - r0)).astype(BF))
            lower_w.append(
                (sc[128:256, 128:256] * jnp.exp(jnp.where(low_tri, c1 - r1, -jnp.inf))).astype(BF)
            )
        top = dot(
            jnp.concatenate(upper_w, 1), jnp.concatenate([v0[0:128], v1[0:128]], 0)
        )
        bottom = dot(jnp.concatenate(lower_w, 1), jnp.concatenate([v0, v1], 0))
        gate = silu(dot(normed, wg[:, cols]))
        lead[0:128, cols] = (top + spread[0:128, cols] * carried[0:128, cols]) * gate[0:128]
        lead[128:256, cols] = (
            bottom + spread[128:256, cols] * carried[128:256, cols]
        ) * gate[128:256]
        tail_out[:, cols] = spread[256:512, cols] * gate
        scaled = (vals * spread[512:768, cols]).astype(BF)
        run[:, cols] = run[:, cols] * spread[255:256, cols] + dot(in_map, scaled, TN)


SCAN_SCRATCH = [
    pltpu.VMEM((8, 280, 128), F32),
    pltpu.VMEM((8, BLK + 8, 128), F32),
    pltpu.VMEM((BLK, BLK), F32),
    pltpu.VMEM((256, 512), F32),
    pltpu.VMEM((8, 128), F32),
]


def fine_main_kernel(later, x, gain, ws, ks, p0, p1, p2, p3, *refs):
    (
        x0, x1, x2, lead, tail_out, maps_out, run, run_log, cv_end,
        wg, wv, wst, taps, bias, decay, cv, act, sc,
    ) = refs

    @pl.when(pl.program_id(0) == 0)
    def _():
        for j in range(4):
            taps[4 + j] = ks[:, j * 128 : (j + 1) * 128] * 0.5
        for j, p in enumerate((p0, p1, p2, p3)):
            cols = slice(j * 128, (j + 1) * 128)
            two = slice(2 * j, 2 * j + 2)
            wg[:, cols] = p[0:256, 0:128]
            wv[:, cols] = p[0:256, 128:256]
            kv, _, bias[two, :], decay[two, :], wst[two, :] = small_rows(p)
            taps[j] = kv * 0.5
        if later:
            run[...] = x0[...]
            run_log[...] = x1[...]
            cv[:, 0:16, :] = x2[...]
        else:
            rim = jnp.where(lax.axis_index(HEAD) == 0, x0[...].astype(F32), x1[...].astype(F32))
            begin(rms(rim, gain[...]), wv, ws, cv, run, run_log)

    scan_block(
        rms(x[...], gain[...]), wg, wv, ws, wst[...].astype(BF), taps, bias[:, 0:1], decay[:, 0:1],
        lead, tail_out, maps_out, cv, act, sc, run, run_log,
    )
    cv_end[...] = cv[:, 0:16, :]


def fine_main(x, gain, scans, ks, packs, extra, later):
    at = 2 if later else 0
    rows = [pl.BlockSpec((BLK, n), lambda i: (i, 0)) for n in (512, 512, 256)]
    return pl.pallas_call(
        lambda *refs: fine_main_kernel(later, *refs),
        grid=(2,),
        in_specs=[pl.BlockSpec((BLK, 256), lambda i: (at + i, 0))] + [VM] * 10,
        out_specs=rows + [VM] * 3,
        out_shape=[
            sds((512, 512)), sds((512, 512)), sds((512, 256), BF),
            sds((256, 512)), sds((8, 128)), sds((8, 16, 128)),
        ],
        scratch_shapes=[
            pltpu.VMEM((256, 512), BF),
            pltpu.VMEM((256, 512), BF),
            pltpu.VMEM((8, 256), F32),
            pltpu.VMEM((8, 4, 128), F32),
            pltpu.VMEM((8, 128), F32),
            pltpu.VMEM((8, 128), F32),
        ]
        + SCAN_SCRATCH[:3],
        compiler_params=few(16),
        name="fine_main_b" if later else "fine_main_a",
    )(x, gain, scans, ks, *packs, *extra)


def fine_close_kernel(
    lead_a, lead_b, tail_a, tail_b, maps_a, maps_b, x, s0, s1, s2, s3, p0, p1, p2, p3, merge,
    merged, end_rows, lead, tail, maps, hidden,
):
    i = pl.program_id(0)

    @pl.when(i < 2)
    def _():
        lead[...], tail[...], maps[...] = lead_a[...], tail_a[...], maps_a[...]

    @pl.when(i >= 2)
    def _():
        lead[...], tail[...], maps[...] = lead_b[...], tail_b[...], maps_b[...]

    gated = []
    for j, s in enumerate((s0, s1, s2, s3)):
        cols = slice(j * 128, (j + 1) * 128)
        gated.append(lead[:, cols] + tail[:, cols] * dot(maps[...], s[...]))
    squares = sum(jnp.sum(g * g, axis=1, keepdims=True) for g in gated)
    factor = lax.rsqrt(squares / 512.0 + EPSILON)
    out = x[...].astype(F32)
    total = None
    for g, p in zip(gated, (p0, p1, p2, p3)):
        norm = small_rows(p)[1]
        piece = dot((g * factor * norm).astype(BF), p[256:384, :])
        total = piece if total is None else total + piece
    start = pl.multiple_of(i * BLK, BLK)
    hidden[0, pl.ds(start, BLK), :] = rounded(out[:, 0:128] + total[:, 0:128])
    hidden[1, pl.ds(start, BLK), :] = rounded(out[:, 128:256] + total[:, 128:256])

    @pl.when(i == pl.num_programs(0) - 1)
    def _():
        total = None
        for odd in range(2):
            for half in range(2):
                rows = hidden[half, pl.ds(odd, 512, stride=2), :].reshape(8, 2, 32, 128)
                for line in range(2):
                    tile = rows[:, line].reshape(256, 128).astype(BF)
                    at = (2 * line + odd) * 256 + half * 128
                    piece = dot(tile, merge[at : at + 128, :])
                    total = piece if total is None else total + piece
        result = total.astype(BF)
        merged[...] = result
        end_rows[...] = result[240:256]


def fine_close(leads, tails, maps, x, states, packs, merge):
    def halves(width):
        return [
            pl.BlockSpec((BLK, width), lambda i: (jnp.minimum(i, 1), 0)),
            pl.BlockSpec((BLK, width), lambda i: (jnp.maximum(i - 2, 0), 0)),
        ]

    return pl.pallas_call(
        fine_close_kernel,
        grid=(4,),
        in_specs=halves(512)
        + halves(512)
        + halves(256)
        + [pl.BlockSpec((BLK, 256), lambda i: (i, 0))]
        + [VM] * 9,
        out_specs=[VM] * 2,
        scratch_shapes=[
            pltpu.VMEM((BLK, 512), F32),
            pltpu.VMEM((BLK, 512), F32),
            pltpu.VMEM((BLK, 256), BF),
            pltpu.VMEM((2, 1024, 128), F32),
        ],
        out_shape=[sds((256, 1024), BF), sds((16, 1024), BF)],
        compiler_params=few(16),
        name="fine_close",
    )(*leads, *tails, *maps, x, *states, *packs, merge)


def coarse_main_kernel(
    near, qa, qb, ra, rb, gain, wg, wv, ws, wst, taps, both, *refs
):
    if near:
        lead, tail_out, maps_out, share, run, run_log, ends = refs[:7]
    else:
        near_ends, near_run, near_log, lead, tail_out, maps_out, share, run, run_log, message = (
            refs[:10]
        )
    xs, sems, cv, act, sc = refs[-5:]
    i = pl.program_id(0)
    y, c = lax.axis_index("y"), lax.axis_index("c")
    h = 2 * y + c

    @pl.when(i == 0)
    def _():
        copies = run_copies(((qa, xs.at[c]), (qb, xs.at[1 - c])), sems)
        rim = ra[...].astype(F32) + rb[...].astype(F32)
        if not near:
            rim = jnp.where(y == 0, near_ends[...].astype(F32), rim)
        begin(rms(rim, gain[...]), wv, ws, cv, run, run_log)
        for copy in copies:
            copy.wait()
        if near:
            ends[...] = xs[1, 240:256, :]

    share[...] = xs[i, :, pl.ds(pl.multiple_of(h * 256, 256), 256)]
    scan_block(
        rms(xs[i], gain[...]), wg, wv, ws, wst[...], taps, both[0:8, 0:1], both[8:16, 0:1],
        lead, tail_out, maps_out, cv, act, sc, run, run_log,
    )

    if not near:

        @pl.when(i == 1)
        def _():
            first_log = jnp.where(y == 0, near_log[:, 0:1], run_log[:, 0:1])
            second_log = jnp.where(y == 0, run_log[:, 0:1], near_log[:, 0:1])
            extra = decay_rows(spread_row(first_log + second_log))
            row = jnp.exp(spread_row(second_log))
            for n in range(16):
                for half in range(2):
                    cols = slice(half * 256, (half + 1) * 256)
                    mine = run[n * 16 : (n + 1) * 16, cols]
                    other = near_run[n * 16 : (n + 1) * 16, cols]
                    total = jnp.where(
                        y == 0, other * row[:, cols] + mine, mine * row[:, cols] + other
                    )
                    message[2 * n + half, 0:16, :] = total.astype(BF)
                    message[2 * n + half, 16:32, :] = extra[:, cols]


def spread_row(column):
    return jnp.sum(
        jnp.where(head_sel(512), jnp.broadcast_to(column, (8, 512)), 0.0), axis=0, keepdims=True
    )


ANY = pl.BlockSpec(memory_space=pl.ANY)


def coarse_main(near, pieces, rims, weights, params, extra):
    taps, both, gain, wst, _ = params
    rows = [pl.BlockSpec((BLK, n), lambda i: (i, 0)) for n in (512, 512, 256, 256)]
    last = sds((16, 1024), BF) if near else sds((32, 32, 256), BF)
    return pl.pallas_call(
        lambda *refs: coarse_main_kernel(near, *refs),
        grid=(2,),
        in_specs=[ANY] * 2 + [VM] * (9 + len(extra)),
        out_specs=rows + [VM] * 3,
        out_shape=[
            sds((512, 512)),
            sds((512, 512)),
            sds((512, 256), BF),
            sds((512, 256), BF),
            sds((256, 512)),
            sds((8, 128)),
            last,
        ],
        scratch_shapes=[pltpu.VMEM((2, 256, 1024), BF), pltpu.SemaphoreType.DMA((2,))]
        + SCAN_SCRATCH[:3],
        compiler_params=few(16),
        name="coarse_main_near" if near else "coarse_main_far",
    )(*pieces, *rims, gain, *weights, wst, taps, both, *extra)


def prefix_kernel(got, out):
    state = jnp.zeros((16, 256), F32)
    for d in range(32):
        out[d] = state.astype(BF)
        state = state * jnp.exp(of_rows(got[d, 16:32, :])) + got[d, 0:16, :].astype(F32)


def prefix(got):
    return pl.pallas_call(
        prefix_kernel,
        in_specs=[VM],
        out_specs=VM,
        out_shape=sds((32, 16, 256), BF),
        compiler_params=few(4),
        name="prefix",
    )(got)


def coarse_close_kernel(
    near, lead, tail, maps, got, other_run, other_log, norm, wo, kk, ks, sk, ss, square_sums,
    state, sums,
):
    i = pl.program_id(0)
    y = lax.axis_index("y")
    h = 2 * y + lax.axis_index("c")

    @pl.when(i == 0)
    def _():
        row = jnp.exp(spread_row(other_log[:, 0:1]))
        later = (y == 1) if near else (y == 0)
        for n in range(16):
            for half in range(2):
                cols = slice(half * 256, (half + 1) * 256)
                came = got[2 * n + half].astype(F32)
                other = other_run[n * 16 : (n + 1) * 16, cols]
                came = jnp.where(later, came * row[:, cols] + other, came)
                state[n * 16 : (n + 1) * 16, cols] = came.astype(BF)

    gated = lead[...] + tail[...] * dot(maps[...], state[...])
    sq = gated * gated
    hi = sq.astype(BF)
    low = (sq - hi.astype(F32)).astype(BF)
    ones = jnp.ones((8, 512), BF)
    sums[i] = dot(ones, hi, NT) + dot(ones, low, NT)
    scaled = (gated * norm[...]).astype(BF)
    rows = pl.ds(pl.multiple_of(i * BLK, BLK), BLK)
    for k, out in enumerate((kk, sk, ks, ss)):
        at = pl.multiple_of((h ^ k) * 256, 256)
        out[rows, :] = dot(scaled, wo[:, pl.ds(at, 256)]).astype(BF)

    @pl.when(i == 1)
    def _():
        square_sums[...] = jnp.concatenate([sums[0], sums[1]], 1)
        ss[512:528, :] = sum_rows(sums[0, 0:1], sums[1, 0:1])


def sum_rows(a, b):
    return jnp.concatenate(three(a) + three(b) + [jnp.zeros((10, 256), F32)], 0).astype(BF)


def rows_sum(ref):
    rows = ref[512:528, :].astype(F32)
    return jnp.concatenate([of_rows(rows[0:3]), of_rows(rows[3:6])], 1)


def coarse_close(near, lead, tail, maps, got, other, norm, wo):
    rows = [pl.BlockSpec((BLK, n), lambda i: (i, 0)) for n in (512, 512, 256)]
    return pl.pallas_call(
        lambda *refs: coarse_close_kernel(near, *refs),
        grid=(2,),
        in_specs=rows + [VM] * 5,
        out_specs=[VM] * 5,
        out_shape=[sds((512, 256), BF)] * 3 + [sds((528, 256), BF), sds((8, 512))],
        scratch_shapes=[pltpu.VMEM((256, 512), BF), pltpu.VMEM((2, 8, 256), F32)],
        compiler_params=few(12),
        name="coarse_close_near" if near else "coarse_close_far",
    )(lead, tail, maps, got, *other, norm, wo)


def relay_kernel(ks, square_sums, came, out, sums):
    out[0:512, :] = (ks[...].astype(F32) + came[0:512, :].astype(F32)).astype(BF)
    total = square_sums[0:1, :] + rows_sum(came)
    out[512:528, :] = sum_rows(total[:, 0:256], total[:, 256:512])
    sums[...] = jnp.broadcast_to(total, (8, 512))


def relay(ks, square_sums, came):
    return pl.pallas_call(
        relay_kernel,
        in_specs=[VM] * 3,
        out_specs=[VM] * 2,
        out_shape=[sds((528, 256), BF), sds((8, 512))],
        compiler_params=few(4),
    )(ks, square_sums, came)


def final_kernel(sa, ka, ca, sum_a, far_a, sb, kb, cb, sum_b, far_b, out):
    y = lax.axis_index("y")
    pick = jnp.where(iota((32, 256), 0) % 8 == 0, 1.0, 0.0).astype(BF)
    sides = (y, sa, ka, ca, sum_a, far_a), (1 - y, sb, kb, cb, sum_b, far_b)
    for half, share, kk, sk, sums, far in sides:
        total = sums[...] + rows_sum(far)
        factor = lax.rsqrt(total / 2048.0 + EPSILON)
        for b in range(2):
            rows = slice(b * BLK, (b + 1) * BLK)
            spread = dot(parts(factor[:, rows]), pick, TN)
            total = kk[rows].astype(F32) + sk[rows].astype(F32) + far[rows].astype(F32)
            at = pl.multiple_of(half * 512 + b * BLK, BLK)
            out[pl.ds(at, BLK), :] = (share[rows].astype(F32) + total * spread).astype(BF)


def final(near, far):
    return pl.pallas_call(
        final_kernel,
        in_specs=[VM] * 10,
        out_specs=VM,
        out_shape=sds((1024, 256), BF),
        compiler_params=few(8),
        name="final",
    )(*near, *far)


def passed(x, axes, pairs):
    return lax.ppermute(x, axes, pairs)


def swapped(x, mask):
    return passed(x, HEAD, [(j, j ^ mask) for j in range(4)])


def round_of(x, axis):
    got = []
    for k in (1, 2, 3):
        got.append(passed(x, axis, [(j, (j + k) % 4) for j in range(4)]))
    return got


def shards(
    tokens, fine_gain, fine_gate, fine_value, fine_scans, fine_steps, fine_kernel, fine_taps,
    fine_bias, fine_decay, fine_norm, fine_output, merge_weight, coarse_gain, coarse_gate,
    coarse_value, coarse_scans, coarse_steps, coarse_kernel, coarse_taps, coarse_bias,
    coarse_decay, coarse_norm, coarse_output,
):
    pack, ends = packed(
        fine_bias, fine_decay, fine_gate, fine_value, fine_output, fine_steps.T, fine_kernel,
        fine_norm[None], tokens,
    )
    rim = passed(ends, SEQ, [(i, i + 1) for i in range(31)])
    packs = [pack] + [swapped(pack, m) for m in (1, 2, 3)]
    later, later_total, resident, (l0, t0, own, own_total, message) = fine_states(
        tokens, rim, fine_gain[None], pack, fine_scans, fine_taps
    )
    mine, mine_rim, gain, scans, ks = resident
    got = round_of(message, "x")
    first = fine_main(mine, gain, scans, ks, packs, (rim, mine_rim, t0), False)
    *prior, own, own_total, message = middle_stage("x", 4, own, own_total, (), got)
    got = [passed(message, "u", [(0, 1), (1, 0)])]
    params = coarse_params(
        coarse_bias, coarse_decay, coarse_kernel, coarse_taps, coarse_gain[None],
        coarse_steps.T, coarse_norm[None],
    )
    *prior, own, own_total, message = middle_stage("u", 2, own, own_total, prior, got)
    got = round_of(message, "z")
    second = fine_main(mine, gain, scans, ks, packs, first[3:], True)
    subs = last_stage(own, own_total, prior, got, l0, t0, later, later_total)
    states = [subs[0]] + [swapped(subs[m], m) for m in (1, 2, 3)]
    merged, end_rows = fine_close(
        (first[0], second[0]), (first[1], second[1]), (first[2], second[2]), mine, states, packs,
        merge_weight,
    )

    def rims(pairs):
        return passed(end_rows, ALL, pairs)

    rim_a = rims([(q, q + 1) for q in range(1, 127, 2)])
    rim_b = rims([(q, q + 2) for q in range(1, 126, 2)])
    rim_c = rims([(q, q + 3) for q in range(3, 125, 4)])
    rim_d = rims([(q, q + 4) for q in range(3, 124, 4)])
    across = swapped(merged, 2)
    beside = swapped(merged, 1)
    both = swapped(across, 1)
    weights = (coarse_gate, coarse_value, coarse_scans)
    near = coarse_main(True, (merged, beside), (rim_a, rim_b), weights, params, ())
    lead, tail, maps, share, run, run_log, near_ends = near
    far = coarse_main(
        False, (across, both), (rim_c, rim_d), weights, params, (near_ends, run, run_log)
    )
    lead_f, tail_f, maps_f, share_f, run_f, run_log_f, message = far
    got = lax.all_to_all(message, SEQ, split_axis=0, concat_axis=0, tiled=True)
    got = lax.all_to_all(prefix(got), SEQ, split_axis=0, concat_axis=0, tiled=True)
    norm = params[4]
    kk, ks, sk, ss, sums = coarse_close(
        True, lead, tail, maps, got, (run_f, run_log_f), norm, coarse_output
    )
    kk_f, ks_f, sk_f, ss_f, sums_f = coarse_close(
        False, lead_f, tail_f, maps_f, got, (run, run_log), norm, coarse_output
    )
    went, sums = relay(ks, sums, swapped(ss, 1))
    went = swapped(went, 2)
    went_f, sums_f = relay(ks_f, sums_f, swapped(ss_f, 1))
    went_f = swapped(went_f, 2)
    sk = swapped(sk, 1)
    sk_f = swapped(sk_f, 1)
    return final((share, kk, sk, sums, went_f), (share_f, kk_f, sk_f, sums_f, went))


def solution(mesh):
    finer = Mesh(mesh.devices.reshape(4, 2, 4, 2, 2), ALL)
    cols = P(None, HEAD)
    return jax.shard_map(
        shards,
        mesh=finer,
        in_specs=(
            P(SEQ, None), P(), cols, cols, P(), cols, cols, P(), P(HEAD), P(HEAD), P(HEAD),
            P(HEAD, None), P(), P(), cols, cols, P(), cols, cols, P(), P(HEAD), P(HEAD), P(HEAD),
            P(HEAD, None),
        ),
        out_specs=P(SEQ, HEAD),
        check_vma=False,
    )
```

time: 179 us -> 162 us (0.905)
  Pallas kernels: 57.4 us -> 46.8 us
  blocking collectives: 38.5 us -> 33.7 us
  starting transfers between devices: 36.5 us -> 39.3 us
  local copies, waits for them, and re-layouts: 10.7 us -> 8.48 us
  waiting for transfers between devices: 34.5 us -> 32.3 us
    pallas_call x9 -> x14, Pallas kernels: 56.3 us -> 46.3 us  [the longest x2 15.2 us: coarse_main(): pl.pallas_call(lambda *refs: coarse_main_kernel(near, *refs), grid=(2,),...]
    all_to_all x1, blocking collectives: 24.3 us -> 19.4 us  [shards(): got = lax.all_to_all(message, SEQ, split_axis=0, concat_axis=0, tiled=True)]
    ppermute x25 -> x27, starting transfers between devices: 36.5 us -> 39.3 us  [passed(): return lax.ppermute(x, axes, pairs)]
    ppermute x25 -> x27, waiting for transfers between devices: 34.5 us -> 32.3 us  [passed(): return lax.ppermute(x, axes, pairs)]
    unnamed x56 -> x50, local copies, waits for them, and re-layouts: 9.85 us -> 8.48 us
  transfers between devices with their start and end apart: 25 -> 27, of which waited for: 10 -> 11; matrix products, arithmetic and copies ran while one was open for 0% -> 0% of each run, Pallas kernels for 15% -> 17%
where the time goes in v2:
time: 162 us; the launch traced here: 161 us
  Pallas kernels  46.8 us (29%)
  starting transfers between devices  39.3 us (24%)
  blocking collectives  33.7 us (21%)
  waiting for transfers between devices  32.3 us (20%)
  local copies, waits for them, and re-layouts  8.48 us (5%)
    ppermute x27, starting transfers between devices, passed(): return lax.ppermute(x, axes, pairs)  39.3 us
    ppermute x27, waiting for transfers between devices, passed(): return lax.ppermute(x, axes, pairs)  32.3 us
    all_to_all x1, blocking collectives, shards(): got = lax.all_to_all(message, SEQ, split_axis=0, concat_axis=0, tiled=True)  19.4 us
    pallas_call x2, Pallas kernels, coarse_main(): pl.pallas_call(lambda *refs: coarse_main_kernel(near, *refs), grid=(2,),...  15.2 us
    all_to_all x1, blocking collectives, shards(): lax.all_to_all(prefix(got), SEQ, split_axis=0, concat_axis=0, tiled=True)  14.3 us
    pallas_call x2, Pallas kernels, fine_main(): pl.pallas_call(lambda *refs: fine_main_kernel(later, *refs), grid=(2,), i...  10.6 us
    unnamed x50, local copies, waits for them, and re-layouts  8.48 us
    pallas_call x1, Pallas kernels, fine_states(): pl.pallas_call(later_chunks_kernel, grid=(3,), in_specs=[HBM, HBM, VM, HB...  7.1 us
  transfers between devices with their start and end apart: 27, of which 11 were waited for; matrix products, arithmetic and copies ran while one was open for 0% of the time, Pallas kernels for 17%

profile of v2, /device:TPU:1, one launch (start us, length us, event | category | flops | bytes accessed | tf_op | source)
XLA Modules:
  0.0 161.2 jit_solution(1806355202294044295)
XLA Ops:
  0.0 1.6 copy-done
  1.6 0.8 copy-done.8
  2.5 0.8 copy-done.9
  3.3 0.8 copy-done.10
  4.1 0.7 copy-done.16
  4.8 0.7 copy-done.18
  5.5 0.7 copy-done.20
  6.1 0.7 copy-done.21
  6.8 0.7 copy-done.22
  7.5 0.8 pack.1
  8.2 3.9 %collective-permute-start.3 = (bf16[16,256]{1,0:T(8,128)(2,1)S(1)}, bf16[16,256]{1,0:T(8,128)(2,1)S(1)}, u32[]{:S(2)}, u32[]{:S(2)}) collective-permute-start(bf16[16,256]{1,0:T(8,128)(2,1)S(1)} %get-tuple-element.83), channel_id=1, source_target_pairs={{0,4},{4,8},{8,12},{12,16},{16,20},{20,24},{24,28},{28,32},{32,36}... | collective-permute-start | bytes 24584 | tf_op jit(solution)/shard_map/ppermute | solution.py:869
  12.2 0.9 copy-done.7
  13.1 7.1 %later_chunks.1 = (f32[3,256,128]{2,1,0:T(8,128)S(1)}, f32[3,8,128]{2,1,0:T(8,128)S(1)}, bf16[1024,256]{1,0:T(8,128)(2,1)S(1)}, bf16[1024,256]{1,0:T(8,128)(2,1)...) custom-call(bf16[4096,256]{1,0:T(8,128)(2,1)S(1)} %copy-done.1, ...), custom_call_target="tpu_custom_call" | custom-call | tf_op jit(solution)/shard_map/later_chunks/pallas_call | solution.py:328
  20.3 2.2 %first_chunk.1 = (f32[256,128]{1,0:T(8,128)S(1)}, f32[8,128]{1,0:T(8,128)S(1)}, f32[256,128]{1,0:T(8,128)S(1)}, f32[8,128]{1,0:T(8,128)S(1)}, bf16[272,128]{1,0:T(8,128)(2,1)S(1)}) custom-call(bf16[1024,256]{1,0:T(8,128)(2,1)S(1)} %get-tuple-element.85.x, bf16[16,256]{1,0:T(8,128)(2,1)S(1)} %collective-permute-done.3.rim.refs_8_, ...), custom_call_target="tpu_custom_call" | custom-call | tf_op jit(solution)/shard_map/first_chunk/pallas_call | solution.py:350
  22.5 4.2 %collective-permute-start.6 = (bf16[272,128]{1,0:T(8,128)(2,1)S(1)}, bf16[272,128]{1,0:T(8,128)(2,1)S(1)}, u32[]{:S(2)}, u32[]{:S(2)}) collective-permute-start(bf16[272,128]{1,0:T(8,128)(2,1)S(1)} %get-tuple-element.100), channel_id=1, source_target_pairs={{0,12},{4,0},{8,4},{12,8},{1,13},{5,1},{9,5},{13,9},{2,14},{6,2},{... | collective-permute-start | bytes 208904 | tf_op jit(solution)/shard_map/ppermute | solution.py:869
  26.7 0.7 collective-permute-start.4
  27.4 1.8 %collective-permute-start.2 = (bf16[416,256]{1,0:T(8,128)(2,1)S(1)}, bf16[416,256]{1,0:T(8,128)(2,1)S(1)}, u32[]{:S(2)}, u32[]{:S(2)}) collective-permute-start(bf16[416,256]{1,0:T(8,128)(2,1)S(1)} %get-tuple-element.78.pack.refs_4_.p0), channel_id=1, source_target_pairs={{0,3},{1,2},{2,1},{3,0},{4,7},{5,6},{6,5},{7,4},{8,11},{9,10},{10,... | collective-permute-start | bytes 638984 | tf_op jit(solution)/shard_map/ppermute | solution.py:869
  29.2 2.3 %collective-permute-done.5.refs_3_ = bf16[272,128]{1,0:T(8,128)(2,1)S(1)} collective-permute-done((bf16[272,128]{1,0:T(8,128)(2,1)S(1)}, bf16[272,128]{1,0:T(8,128)(2,1)S(1)}, u32[]{:S(2)}, u32[]{:S(2)}) %collective-permute-start.5) | collective-permute-done | bytes 69664 | tf_op jit(solution)/shard_map/ppermute | solution.py:869
  31.5 0.4 collective-permute-done.4.refs_2_
  31.8 0.1 shard_map.226
  32.0 1.8 %collective-permute-start.7 = (bf16[272,128]{1,0:T(8,128)(2,1)S(1)}, bf16[272,128]{1,0:T(8,128)(2,1)S(1)}, u32[]{:S(2)}, u32[]{:S(2)}) collective-permute-start(bf16[272,128]{1,0:T(8,128)(2,1)S(1)} %get-tuple-element.105), channel_id=1, source_target_pairs={{0,16},{16,0},{1,17},{17,1},{2,18},{18,2},{3,19},{19,3},{4,20},{20... | collective-permute-start | bytes 208904 | tf_op jit(solution)/shard_map/ppermute | solution.py:869
  33.7 1.0 collective-permute-start.1
  34.7 2.9 %collective-permute-start = (bf16[416,256]{1,0:T(8,128)(2,1)S(1)}, bf16[416,256]{1,0:T(8,128)(2,1)S(1)}, u32[]{:S(2)}, u32[]{:S(2)}) collective-permute-start(bf16[416,256]{1,0:T(8,128)(2,1)S(1)} %get-tuple-element.78.pack.refs_4_.p0), channel_id=1, source_target_pairs={{0,1},{1,0},{2,3},{3,2},{4,5},{5,4},{6,7},{7,6},{8,9},{9,8},{10,11... | collective-permute-start | bytes 638984 | tf_op jit(solution)/shard_map/ppermute | solution.py:869
  37.7 3.2 %collective-permute-start.10 = (bf16[272,128]{1,0:T(8,128)(2,1)S(1)}, bf16[272,128]{1,0:T(8,128)(2,1)S(1)}, u32[]{:S(2)}, u32[]{:S(2)}) collective-permute-start(bf16[272,128]{1,0:T(8,128)(2,1)S(1)} %get-tuple-element.110), channel_id=1, source_target_pairs={{0,96},{32,0},{64,32},{96,64},{1,97},{33,1},{65,33},{97,65},{2,98}... | collective-permute-start | bytes 208904 | tf_op jit(solution)/shard_map/ppermute | solution.py:869
  40.9 0.4 collective-permute-start.9
  41.3 1.0 collective-permute-done.10.r3
  42.3 0.6 collective-permute-start.8
  42.9 2.7 %collective-permute-done.9.r2 = bf16[272,128]{1,0:T(8,128)(2,1)S(1)} collective-permute-done((bf16[272,128]{1,0:T(8,128)(2,1)S(1)}, bf16[272,128]{1,0:T(8,128)(2,1)S(1)}, u32[]{:S(2)}, u32[]{:S(2)}) %collective-permute-start.9) | collective-permute-done | bytes 69664 | tf_op jit(solution)/shard_map/ppermute | solution.py:869
  45.6 1.4 collective-permute-done.8.r1
  47.0 0.1 chain_last.1
  47.2 5.8 %collective-permute-start.11 = (bf16[256,128]{1,0:T(8,128)(2,1)S(1)}, bf16[256,128]{1,0:T(8,128)(2,1)S(1)}, u32[]{:S(2)}, u32[]{:S(2)}) collective-permute-start(bf16[256,128]{1,0:T(8,128)(2,1)S(1)} %get-tuple-element.113), channel_id=1, source_target_pairs={{0,1},{1,0},{2,3},{3,2},{4,5},{5,4},{6,7},{7,6},{8,9},{9,8},{10,11... | collective-permute-start | bytes 196616 | tf_op jit(solution)/shard_map/ppermute | solution.py:869
  53.0 0.4 collective-permute-start.12
  53.4 1.3 collective-permute-start.13
  54.7 5.0 %fine_main_a.1 = (f32[512,512]{1,0:T(8,128)S(1)}, f32[512,512]{1,0:T(8,128)S(1)}, bf16[512,256]{1,0:T(8,128)(2,1)S(1)}, f32[256,512]{1,0:T(8,128)S(1)}, f32[8,128]{1,0:T(8,128)S(1)}, /*index=5*/f32[8,16,128]{2,1,0:T(8,128)S(1)}) custom-call(bf16[1024,256]{1,0:T(8,128)(2,1)S(1)} %get-tuple-element.79.refs_0_.x, f32[1,256]{1,0:T(1,128)S(1)} %get-tuple-element.80.gain.refs_1_, ...), custom_call_target="tpu_custom_call" | custom-call | tf_op jit(solution)/shard_map/fine_main_a/pallas_call | solution.py:563
  59.7 5.6 %fine_main_b.1 = (f32[512,512]{1,0:T(8,128)S(1)}, f32[512,512]{1,0:T(8,128)S(1)}, bf16[512,256]{1,0:T(8,128)(2,1)S(1)}, f32[256,512]{1,0:T(8,128)}, f32[8,128]{1,0:T(8,128)}, /*index=5*/f32[8,16,128]{2,1,0:T(8,128)}) custom-call(bf16[1024,256]{1,0:T(8,128)(2,1)S(1)} %get-tuple-element.79.refs_0_.x, f32[1,256]{1,0:T(1,128)S(1)} %get-tuple-element.80.gain.refs_1_, ...), custom_call_target="tpu_custom_call" | custom-call | tf_op jit(solution)/shard_map/fine_main_b/pallas_call | solution.py:563
  65.5 4.9 %fine_close.1 = (bf16[256,1024]{1,0:T(8,128)(2,1)S(1)}, bf16[16,1024]{1,0:T(8,128)(2,1)S(1)}) custom-call(f32[512,512]{1,0:T(8,128)S(1)} %get-tuple-element.89.lead_a, f32[512,512]{1,0:T(8,128)S(1)} %get-tuple-element.93.lead_b, f32[512,512]{1,0:T(8,128)S(1)} %get-tuple-element.94.tail_a, f32[512,512]{1,0:T(8,128)S(1)} %get-tuple-element.95.tail_b, ...), custom_call_target="tpu_custom_call" | custom-call | tf_op jit(solution)/shard_map/fine_close/pallas_call | solution.py:639
  70.4 0.5 collective-permute-start.17
  70.9 0.4 collective-permute-start.14
  71.3 12.5 %collective-permute-done.17.refs_0_ = bf16[256,1024]{1,0:T(8,128)(2,1)S(1)} collective-permute-done((bf16[256,1024]{1,0:T(8,128)(2,1)S(1)}, bf16[256,1024]{1,0:T(8,128)(2,1)S(1)}, u32[]{:S(2)}, u32[]{:S(2)}) %collective-permute-start.17) | collective-permute-done | bytes 524320 | tf_op jit(solution)/shard_map/ppermute | solution.py:869
  83.8 1.0 collective-permute-start.18
  84.8 2.3 %collective-permute-start.16 = (bf16[16,1024]{1,0:T(8,128)(2,1)S(1)}, bf16[16,1024]{1,0:T(8,128)(2,1)S(1)}, u32[]{:S(2)}, u32[]{:S(2)}) collective-permute-start(bf16[16,1024]{1,0:T(8,128)(2,1)S(1)} %get-tuple-element.117), channel_id=1, source_target_pairs={{1,3},{3,5},{5,7},{7,9},{9,11},{11,13},{13,15},{15,17},{17,19},{19... | collective-permute-start | bytes 98312 | tf_op jit(solution)/shard_map/ppermute | solution.py:869
  87.1 1.3 collective-permute-start.15
  88.4 0.7 collective-permute-start.20
  89.1 0.7 collective-permute-start.19
  89.8 0.7 coarse_params.1
  90.6 7.5 %coarse_main_near.1 = (f32[512,512]{1,0:T(8,128)S(1)}, f32[512,512]{1,0:T(8,128)S(1)}, bf16[512,256]{1,0:T(8,128)(2,1)S(1)}, bf16[512,256]{1,0:T(8,128)(2,1)S(1)...) custom-call(bf16[256,1024]{1,0:T(8,128)(2,1)S(1)} %get-tuple-element.116.refs_0_, ...), custom_call_target="tpu_custom_call" | custom-call | tf_op jit(solution)/shard_map/coarse_main_near/pallas_call | solution.py:725
  98.1 7.7 %coarse_main_far.1 = (f32[512,512]{1,0:T(8,128)S(1)}, f32[512,512]{1,0:T(8,128)S(1)}, bf16[512,256]{1,0:T(8,128)(2,1)S(1)}, bf16[512,256]{1,0:T(8,128)(2,1)S(1)}...) custom-call(bf16[256,1024]{1,0:T(8,128)(2,1)S(1)} %collective-permute-done.17.refs_0_, ...), custom_call_target="tpu_custom_call" | custom-call | tf_op jit(solution)/shard_map/coarse_main_far/pallas_call | solution.py:725
  105.8 19.4 %all_to_all.10.got = bf16[32,32,256]{2,1,0:T(8,128)(2,1)S(1)} all-to-all(bf16[32,32,256]{2,1,0:T(8,128)(2,1)S(1)} %get-tuple-element.129), channel_id=1, replica_groups=mesh['z'=4,'u'=2,'x'=4,'y'=2,'c'=2] {'z','u','x'}, dimensions={0} | all-to-all | bytes 1048576 | tf_op jit(solution)/shard_map/all_to_all | solution.py:934
  125.2 0.1 prefix.1
  125.3 14.3 %all_to_all.11.refs_3_ = bf16[32,16,256]{2,1,0:T(8,128)(2,1)S(1)} all-to-all(bf16[32,16,256]{2,1,0:T(8,128)(2,1)S(1)} %prefix.1), channel_id=1, replica_groups=mesh['z'=4,'u'=2,'x'=4,'y'=2,'c'=2] {'z','u','x'}, dimensions={0} | all-to-all | bytes 524288 | tf_op jit(solution)/shard_map/all_to_all | solution.py:935
  139.7 1.8 %coarse_close_far.1 = (bf16[512,256]{1,0:T(8,128)(2,1)S(1)}, bf16[512,256]{1,0:T(8,128)(2,1)S(1)}, bf16[512,256]{1,0:T(8,128)(2,1)S(1)}, bf16[528,256]{1,0:T(8,128)(2,1)S(1)}, f32[8,512]{1,0:T(8,128)S(1)}) custom-call(f32[512,512]{1,0:T(8,128)S(1)} %get-tuple-element.139.refs_0_, f32[512,512]{1,0:T(8,128)S(1)} %get-tuple-element.140.refs_1_, ...), custom_call_target="tpu_custom_call" | custom-call | tf_op jit(solution)/shard_map/coarse_close_far/pallas_call | solution.py:813
  141.4 3.1 %collective-permute-start.23 = (bf16[528,256]{1,0:T(8,128)(2,1)S(1)}, bf16[528,256]{1,0:T(8,128)(2,1)S(1)}, u32[]{:S(2)}, u32[]{:S(2)}) collective-permute-start(bf16[528,256]{1,0:T(8,128)(2,1)S(1)} %get-tuple-element.144), channel_id=1, source_target_pairs={{0,1},{1,0},{2,3},{3,2},{4,5},{5,4},{6,7},{7,6},{8,9},{9,8},{10,11... | collective-permute-start | bytes 811016 | tf_op jit(solution)/shard_map/ppermute | solution.py:869
  144.5 1.8 %coarse_close_near.1 = (bf16[512,256]{1,0:T(8,128)(2,1)S(1)}, bf16[512,256]{1,0:T(8,128)(2,1)S(1)}, bf16[512,256]{1,0:T(8,128)(2,1)S(1)}, bf16[528,256]{1,0:T(8,128)(2,1)S(1)}, f32[8,512]{1,0:T(8,128)S(1)}) custom-call(f32[512,512]{1,0:T(8,128)S(1)} %get-tuple-element.123.refs_0_, f32[512,512]{1,0:T(8,128)S(1)} %get-tuple-element.124.refs_1_, ...), custom_call_target="tpu_custom_call" | custom-call | tf_op jit(solution)/shard_map/coarse_close_near/pallas_call | solution.py:813
  146.2 0.1 collective-permute-start.22
  146.4 0.1 shard_map.229
  146.6 1.3 collective-permute-done.22.came
  147.9 0.1 shard_map.228
  148.0 0.2 collective-permute-start.26
  148.2 1.0 collective-permute-start.25
  149.2 1.2 collective-permute-done.25.cb
  150.4 0.4 collective-permute-done.21.ca
  150.8 3.4 %collective-permute-done.24.far_a = bf16[528,256]{1,0:T(8,128)(2,1)S(1)} collective-permute-done((bf16[528,256]{1,0:T(8,128)(2,1)S(1)}, bf16[528,256]{1,0:T(8,128)(2,1)S(1)}, u32[]{:S(2)}, u32[]{:S(2)}) %collective-permute-start.24) | collective-permute-done | bytes 270368 | tf_op jit(solution)/shard_map/ppermute | solution.py:869
  154.2 5.8 %collective-permute-done.26.far_b = bf16[528,256]{1,0:T(8,128)(2,1)S(1)} collective-permute-done((bf16[528,256]{1,0:T(8,128)(2,1)S(1)}, bf16[528,256]{1,0:T(8,128)(2,1)S(1)}, u32[]{:S(2)}, u32[]{:S(2)}) %collective-permute-start.26) | collective-permute-done | bytes 270368 | tf_op jit(solution)/shard_map/ppermute | solution.py:869
  159.9 1.2 final.1
  (60 shorter events, 0.3 us)
Async XLA Ops:
  0.0 12.2 %copy-start.19 = (f32[256]{0:T(256)S(1)}, f32[256]{0:T(256)}, u32[]{:S(2)}) copy-start(f32[256]{0:T(256)} %param.25) | copy-start | bytes 3076
  0.0 1.6 copy-start
  1.6 0.8 copy-start.8
  2.4 0.8 copy-start.9
  3.3 0.8 copy-start.10
  4.1 0.7 copy-start.16
  4.8 0.7 copy-start.18
  5.5 0.7 copy-start.20
  6.1 0.7 copy-start.21
  6.8 0.7 copy-start.22
  7.5 4.7 %copy-start.1 = (bf16[4096,256]{1,0:T(8,128)(2,1)S(1)}, bf16[4096,256]{1,0:T(8,128)(2,1)}, u32[]{:S(2)}) copy-start(bf16[4096,256]{1,0:T(8,128)(2,1)} %tokens.3) | copy-start | bytes 6291460
  7.5 4.7 %copy-start.12 = (f32[4,512]{1,0:T(4,128)S(1)}, f32[4,512]{1,0:T(4,128)}, u32[]{:S(2)}) copy-start(f32[4,512]{1,0:T(4,128)} %ks_h.1) | copy-start | bytes 24580
  8.2 12.0 %collective-permute-start.3 = (bf16[16,256]{1,0:T(8,128)(2,1)S(1)}, bf16[16,256]{1,0:T(8,128)(2,1)S(1)}, u32[]{:S(2)}, u32[]{:S(2)}) collective-permute-start(bf16[16,256]{1,0:T(8,128)(2,1)S(1)} %get-tuple-element.83), channel_id=1, source_target_pairs={{0,4},{4,8},{8,12},{12,16},{16,20},{20,24},{24,28},{28,32},{32,36}... | collective-permute-start | bytes 24584 | tf_op jit(solution)/shard_map/ppermute | solution.py:869
  12.2 1.0 copy-start.7
  22.5 6.6 %collective-permute-start.6 = (bf16[272,128]{1,0:T(8,128)(2,1)S(1)}, bf16[272,128]{1,0:T(8,128)(2,1)S(1)}, u32[]{:S(2)}, u32[]{:S(2)}) collective-permute-start(bf16[272,128]{1,0:T(8,128)(2,1)S(1)} %get-tuple-element.100), channel_id=1, source_target_pairs={{0,12},{4,0},{8,4},{12,8},{1,13},{5,1},{9,5},{13,9},{2,14},{6,2},{... | collective-permute-start | bytes 208904 | tf_op jit(solution)/shard_map/ppermute | solution.py:869
  26.7 4.8 %collective-permute-start.5 = (bf16[272,128]{1,0:T(8,128)(2,1)S(1)}, bf16[272,128]{1,0:T(8,128)(2,1)S(1)}, u32[]{:S(2)}, u32[]{:S(2)}) collective-permute-start(bf16[272,128]{1,0:T(8,128)(2,1)S(1)} %get-tuple-element.100), channel_id=1, source_target_pairs={{0,8},{4,12},{8,0},{12,4},{1,9},{5,13},{9,1},{13,5},{2,10},{6,14},... | collective-permute-start | bytes 208904 | tf_op jit(solution)/shard_map/ppermute | solution.py:869
  26.7 5.1 %collective-permute-start.4 = (bf16[272,128]{1,0:T(8,128)(2,1)S(1)}, bf16[272,128]{1,0:T(8,128)(2,1)S(1)}, u32[]{:S(2)}, u32[]{:S(2)}) collective-permute-start(bf16[272,128]{1,0:T(8,128)(2,1)S(1)} %get-tuple-element.100), channel_id=1, source_target_pairs={{0,4},{4,8},{8,12},{12,0},{1,5},{5,9},{9,13},{13,1},{2,6},{6,10},{... | collective-permute-start | bytes 208904 | tf_op jit(solution)/shard_map/ppermute | solution.py:869
  27.4 26.0 %collective-permute-start.2 = (bf16[416,256]{1,0:T(8,128)(2,1)S(1)}, bf16[416,256]{1,0:T(8,128)(2,1)S(1)}, u32[]{:S(2)}, u32[]{:S(2)}) collective-permute-start(bf16[416,256]{1,0:T(8,128)(2,1)S(1)} %get-tuple-element.78.pack.refs_4_.p0), channel_id=1, source_target_pairs={{0,3},{1,2},{2,1},{3,0},{4,7},{5,6},{6,5},{7,4},{8,11},{9,10},{10,... | collective-permute-start | bytes 638984 | tf_op jit(solution)/shard_map/ppermute | solution.py:869
  32.0 5.7 %collective-permute-start.7 = (bf16[272,128]{1,0:T(8,128)(2,1)S(1)}, bf16[272,128]{1,0:T(8,128)(2,1)S(1)}, u32[]{:S(2)}, u32[]{:S(2)}) collective-permute-start(bf16[272,128]{1,0:T(8,128)(2,1)S(1)} %get-tuple-element.105), channel_id=1, source_target_pairs={{0,16},{16,0},{1,17},{17,1},{2,18},{18,2},{3,19},{19,3},{4,20},{20... | collective-permute-start | bytes 208904 | tf_op jit(solution)/shard_map/ppermute | solution.py:869
  33.7 21.0 %collective-permute-start.1 = (bf16[416,256]{1,0:T(8,128)(2,1)S(1)}, bf16[416,256]{1,0:T(8,128)(2,1)S(1)}, u32[]{:S(2)}, u32[]{:S(2)}) collective-permute-start(bf16[416,256]{1,0:T(8,128)(2,1)S(1)} %get-tuple-element.78.pack.refs_4_.p0), channel_id=1, source_target_pairs={{0,2},{1,3},{2,0},{3,1},{4,6},{5,7},{6,4},{7,5},{8,10},{9,11},{10,... | collective-permute-start | bytes 638984 | tf_op jit(solution)/shard_map/ppermute | solution.py:869
  34.7 20.0 %collective-permute-start = (bf16[416,256]{1,0:T(8,128)(2,1)S(1)}, bf16[416,256]{1,0:T(8,128)(2,1)S(1)}, u32[]{:S(2)}, u32[]{:S(2)}) collective-permute-start(bf16[416,256]{1,0:T(8,128)(2,1)S(1)} %get-tuple-element.78.pack.refs_4_.p0), channel_id=1, source_target_pairs={{0,1},{1,0},{2,3},{3,2},{4,5},{5,4},{6,7},{7,6},{8,9},{9,8},{10,11... | collective-permute-start | bytes 638984 | tf_op jit(solution)/shard_map/ppermute | solution.py:869
  37.7 4.6 %collective-permute-start.10 = (bf16[272,128]{1,0:T(8,128)(2,1)S(1)}, bf16[272,128]{1,0:T(8,128)(2,1)S(1)}, u32[]{:S(2)}, u32[]{:S(2)}) collective-permute-start(bf16[272,128]{1,0:T(8,128)(2,1)S(1)} %get-tuple-element.110), channel_id=1, source_target_pairs={{0,96},{32,0},{64,32},{96,64},{1,97},{33,1},{65,33},{97,65},{2,98}... | collective-permute-start | bytes 208904 | tf_op jit(solution)/shard_map/ppermute | solution.py:869
  40.9 4.7 %collective-permute-start.9 = (bf16[272,128]{1,0:T(8,128)(2,1)S(1)}, bf16[272,128]{1,0:T(8,128)(2,1)S(1)}, u32[]{:S(2)}, u32[]{:S(2)}) collective-permute-start(bf16[272,128]{1,0:T(8,128)(2,1)S(1)} %get-tuple-element.110), channel_id=1, source_target_pairs={{0,64},{32,96},{64,0},{96,32},{1,65},{33,97},{65,1},{97,33},{2,66}... | collective-permute-start | bytes 208904 | tf_op jit(solution)/shard_map/ppermute | solution.py:869
  42.3 4.7 %collective-permute-start.8 = (bf16[272,128]{1,0:T(8,128)(2,1)S(1)}, bf16[272,128]{1,0:T(8,128)(2,1)S(1)}, u32[]{:S(2)}, u32[]{:S(2)}) collective-permute-start(bf16[272,128]{1,0:T(8,128)(2,1)S(1)} %get-tuple-element.110), channel_id=1, source_target_pairs={{0,32},{32,64},{64,96},{96,0},{1,33},{33,65},{65,97},{97,1},{2,34}... | collective-permute-start | bytes 208904 | tf_op jit(solution)/shard_map/ppermute | solution.py:869
  47.2 18.2 %copy-start.6 = (bf16[1024,1024]{1,0:T(8,128)(2,1)S(1)}, bf16[1024,1024]{1,0:T(8,128)(2,1)}, u32[]{:S(2)}) copy-start(bf16[1024,1024]{1,0:T(8,128)(2,1)} %merge.1) | copy-start | bytes 6291460
  47.2 18.2 %collective-permute-start.11 = (bf16[256,128]{1,0:T(8,128)(2,1)S(1)}, bf16[256,128]{1,0:T(8,128)(2,1)S(1)}, u32[]{:S(2)}, u32[]{:S(2)}) collective-permute-start(bf16[256,128]{1,0:T(8,128)(2,1)S(1)} %get-tuple-element.113), channel_id=1, source_target_pairs={{0,1},{1,0},{2,3},{3,2},{4,5},{5,4},{6,7},{7,6},{8,9},{9,8},{10,11... | collective-permute-start | bytes 196616 | tf_op jit(solution)/shard_map/ppermute | solution.py:869
  53.0 12.3 %collective-permute-start.12 = (bf16[256,128]{1,0:T(8,128)(2,1)S(1)}, bf16[256,128]{1,0:T(8,128)(2,1)S(1)}, u32[]{:S(2)}, u32[]{:S(2)}) collective-permute-start(bf16[256,128]{1,0:T(8,128)(2,1)S(1)} %get-tuple-element.114), channel_id=1, source_target_pairs={{0,2},{1,3},{2,0},{3,1},{4,6},{5,7},{6,4},{7,5},{8,10},{9,11},{10,... | collective-permute-start | bytes 196616 | tf_op jit(solution)/shard_map/ppermute | solution.py:869
  53.4 12.0 %collective-permute-start.13 = (bf16[256,128]{1,0:T(8,128)(2,1)S(1)}, bf16[256,128]{1,0:T(8,128)(2,1)S(1)}, u32[]{:S(2)}, u32[]{:S(2)}) collective-permute-start(bf16[256,128]{1,0:T(8,128)(2,1)S(1)} %get-tuple-element.115), channel_id=1, source_target_pairs={{0,3},{1,2},{2,1},{3,0},{4,7},{5,6},{6,5},{7,4},{8,11},{9,10},{10,... | collective-permute-start | bytes 196616 | tf_op jit(solution)/shard_map/ppermute | solution.py:869
  65.4 24.4 %copy-start.11 = (bf16[1024,8]{0,1:T(8,128)(2,1)S(1)}, bf16[1024,8]{0,1:T(8,128)(2,1)}, u32[]{:S(2)}) copy-start(bf16[1024,8]{0,1:T(8,128)(2,1)} %param.41) | copy-start | bytes 49156
  65.4 24.4 %copy-start.13 = (f32[4,512]{1,0:T(4,128)S(1)}, f32[4,512]{1,0:T(4,128)}, u32[]{:S(2)}) copy-start(f32[4,512]{1,0:T(4,128)} %kv.3) | copy-start | bytes 24580
  65.4 24.4 %copy-start.14 = (f32[4,512]{1,0:T(4,128)S(1)}, f32[4,512]{1,0:T(4,128)}, u32[]{:S(2)}) copy-start(f32[4,512]{1,0:T(4,128)} %ks.1) | copy-start | bytes 24580
  65.4 24.4 %copy-start.15 = (f32[1024]{0:T(1024)S(1)}, f32[1024]{0:T(1024)}, u32[]{:S(2)}) copy-start(f32[1024]{0:T(1024)} %param.37) | copy-start | bytes 12292
  65.4 24.4 %copy-start.17 = (f32[512]{0:T(512)S(1)}, f32[512]{0:T(512)}, u32[]{:S(2)}) copy-start(f32[512]{0:T(512)} %param.46) | copy-start | bytes 6148
  65.4 24.4 %copy-start.23 = (f32[8]{0:T(128)S(1)}, f32[8]{0:T(128)}, u32[]{:S(2)}) copy-start(f32[8]{0:T(128)} %bias.3) | copy-start | bytes 100
  65.4 24.4 %copy-start.24 = (f32[8]{0:T(128)S(1)}, f32[8]{0:T(128)}, u32[]{:S(2)}) copy-start(f32[8]{0:T(128)} %decay.3) | copy-start | bytes 100
  65.4 25.1 %copy-start.2 = (bf16[1024,512]{1,0:T(8,128)(2,1)S(1)}, bf16[1024,512]{1,0:T(8,128)(2,1)}, u32[]{:S(2)}) copy-start(bf16[1024,512]{1,0:T(8,128)(2,1)} %refs_5_.3) | copy-start | bytes 3145732
  65.5 25.1 %copy-start.3 = (bf16[1024,512]{1,0:T(8,128)(2,1)S(1)}, bf16[1024,512]{1,0:T(8,128)(2,1)}, u32[]{:S(2)}) copy-start(bf16[1024,512]{1,0:T(8,128)(2,1)} %refs_6_.3) | copy-start | bytes 3145732
  65.5 25.1 %copy-start.4 = (bf16[1024,512]{1,0:T(8,128)(2,1)S(1)}, bf16[1024,512]{1,0:T(8,128)(2,1)}, u32[]{:S(2)}) copy-start(bf16[1024,512]{1,0:T(8,128)(2,1)} %refs_7_.5) | copy-start | bytes 3145732
  70.4 13.4 %collective-permute-start.17 = (bf16[256,1024]{1,0:T(8,128)(2,1)S(1)}, bf16[256,1024]{1,0:T(8,128)(2,1)S(1)}, u32[]{:S(2)}, u32[]{:S(2)}) collective-permute-start(bf16[256,1024]{1,0:T(8,128)(2,1)S(1)} %get-tuple-element.116.refs_0_), channel_id=1, source_target_pairs={{0,2},{1,3},{2,0},{3,1},{4,6},{5,7},{6,4},{7,5},{8,10},{9,11},{10,... | collective-permute-start | bytes 1572872 | tf_op jit(solution)/shard_map/ppermute | solution.py:869
  70.9 19.6 %collective-permute-start.14 = (bf16[256,1024]{1,0:T(8,128)(2,1)S(1)}, bf16[256,1024]{1,0:T(8,128)(2,1)S(1)}, u32[]{:S(2)}, u32[]{:S(2)}) collective-permute-start(bf16[256,1024]{1,0:T(8,128)(2,1)S(1)} %get-tuple-element.116.refs_0_), channel_id=1, source_target_pairs={{0,1},{1,0},{2,3},{3,2},{4,5},{5,4},{6,7},{7,6},{8,9},{9,8},{10,11... | collective-permute-start | bytes 1572872 | tf_op jit(solution)/shard_map/ppermute | solution.py:869
  83.8 14.3 %collective-permute-start.18 = (bf16[256,1024]{1,0:T(8,128)(2,1)S(1)}, bf16[256,1024]{1,0:T(8,128)(2,1)S(1)}, u32[]{:S(2)}, u32[]{:S(2)}) collective-permute-start(bf16[256,1024]{1,0:T(8,128)(2,1)S(1)} %collective-permute-done.17.refs_0_), channel_id=1, source_target_pairs={{0,1},{1,0},{2,3},{3,2},{4,5},{5,4},{6,7},{7,6},{8,9},{9,8},{10,11... | collective-permute-start | bytes 1572872 | tf_op jit(solution)/shard_map/ppermute | solution.py:869
  84.8 4.3 %collective-permute-start.16 = (bf16[16,1024]{1,0:T(8,128)(2,1)S(1)}, bf16[16,1024]{1,0:T(8,128)(2,1)S(1)}, u32[]{:S(2)}, u32[]{:S(2)}) collective-permute-start(bf16[16,1024]{1,0:T(8,128)(2,1)S(1)} %get-tuple-element.117), channel_id=1, source_target_pairs={{1,3},{3,5},{5,7},{7,9},{9,11},{11,13},{13,15},{15,17},{17,19},{19... | collective-permute-start | bytes 98312 | tf_op jit(solution)/shard_map/ppermute | solution.py:869
  87.1 3.4 %collective-permute-start.15 = (bf16[16,1024]{1,0:T(8,128)(2,1)S(1)}, bf16[16,1024]{1,0:T(8,128)(2,1)S(1)}, u32[]{:S(2)}, u32[]{:S(2)}) collective-permute-start(bf16[16,1024]{1,0:T(8,128)(2,1)S(1)} %get-tuple-element.117), channel_id=1, source_target_pairs={{1,2},{3,4},{5,6},{7,8},{9,10},{11,12},{13,14},{15,16},{17,18},{19... | collective-permute-start | bytes 98312 | tf_op jit(solution)/shard_map/ppermute | solution.py:869
  88.4 9.6 %collective-permute-start.20 = (bf16[16,1024]{1,0:T(8,128)(2,1)S(1)}, bf16[16,1024]{1,0:T(8,128)(2,1)S(1)}, u32[]{:S(2)}, u32[]{:S(2)}) collective-permute-start(bf16[16,1024]{1,0:T(8,128)(2,1)S(1)} %get-tuple-element.117), channel_id=1, source_target_pairs={{3,7},{7,11},{11,15},{15,19},{19,23},{23,27},{27,31},{31,35},{35,3... | collective-permute-start | bytes 98312 | tf_op jit(solution)/shard_map/ppermute | solution.py:869
  89.1 9.0 %collective-permute-start.19 = (bf16[16,1024]{1,0:T(8,128)(2,1)S(1)}, bf16[16,1024]{1,0:T(8,128)(2,1)S(1)}, u32[]{:S(2)}, u32[]{:S(2)}) collective-permute-start(bf16[16,1024]{1,0:T(8,128)(2,1)S(1)} %get-tuple-element.117), channel_id=1, source_target_pairs={{3,6},{7,10},{11,14},{15,18},{19,22},{23,26},{27,30},{31,34},{35,3... | collective-permute-start | bytes 98312 | tf_op jit(solution)/shard_map/ppermute | solution.py:869
  105.8 33.9 %copy-start.5 = (bf16[512,1024]{1,0:T(8,128)(2,1)S(1)}, bf16[512,1024]{1,0:T(8,128)(2,1)}, u32[]{:S(2)}) copy-start(bf16[512,1024]{1,0:T(8,128)(2,1)} %refs_7_.7) | copy-start | bytes 3145732
  141.4 5.0 %collective-permute-start.23 = (bf16[528,256]{1,0:T(8,128)(2,1)S(1)}, bf16[528,256]{1,0:T(8,128)(2,1)S(1)}, u32[]{:S(2)}, u32[]{:S(2)}) collective-permute-start(bf16[528,256]{1,0:T(8,128)(2,1)S(1)} %get-tuple-element.144), channel_id=1, source_target_pairs={{0,1},{1,0},{2,3},{3,2},{4,5},{5,4},{6,7},{7,6},{8,9},{9,8},{10,11... | collective-permute-start | bytes 811016 | tf_op jit(solution)/shard_map/ppermute | solution.py:869
  146.2 1.6 %collective-permute-start.22 = (bf16[528,256]{1,0:T(8,128)(2,1)S(1)}, bf16[528,256]{1,0:T(8,128)(2,1)S(1)}, u32[]{:S(2)}, u32[]{:S(2)}) collective-permute-start(bf16[528,256]{1,0:T(8,128)(2,1)S(1)} %get-tuple-element.137), channel_id=1, source_target_pairs={{0,1},{1,0},{2,3},{3,2},{4,5},{5,4},{6,7},{7,6},{8,9},{9,8},{10,11... | collective-permute-start | bytes 811016 | tf_op jit(solution)/shard_map/ppermute | solution.py:869
  146.5 7.7 %collective-permute-start.24 = (bf16[528,256]{1,0:T(8,128)(2,1)S(1)}, bf16[528,256]{1,0:T(8,128)(2,1)S(1)}, u32[]{:S(2)}, u32[]{:S(2)}) collective-permute-start(bf16[528,256]{1,0:T(8,128)(2,1)S(1)} %get-tuple-element.145), channel_id=1, source_target_pairs={{0,2},{1,3},{2,0},{3,1},{4,6},{5,7},{6,4},{7,5},{8,10},{9,11},{10,... | collective-permute-start | bytes 811016 | tf_op jit(solution)/shard_map/ppermute | solution.py:869
  148.0 12.0 %collective-permute-start.26 = (bf16[528,256]{1,0:T(8,128)(2,1)S(1)}, bf16[528,256]{1,0:T(8,128)(2,1)S(1)}, u32[]{:S(2)}, u32[]{:S(2)}) collective-permute-start(bf16[528,256]{1,0:T(8,128)(2,1)S(1)} %get-tuple-element.150), channel_id=1, source_target_pairs={{0,2},{1,3},{2,0},{3,1},{4,6},{5,7},{6,4},{7,5},{8,10},{9,11},{10,... | collective-permute-start | bytes 811016 | tf_op jit(solution)/shard_map/ppermute | solution.py:869
  148.2 2.2 %collective-permute-start.25 = (bf16[512,256]{1,0:T(8,128)(2,1)S(1)}, bf16[512,256]{1,0:T(8,128)(2,1)S(1)}, u32[]{:S(2)}, u32[]{:S(2)}) collective-permute-start(bf16[512,256]{1,0:T(8,128)(2,1)S(1)} %get-tuple-element.148), channel_id=1, source_target_pairs={{0,1},{1,0},{2,3},{3,2},{4,5},{5,4},{6,7},{7,6},{8,9},{9,8},{10,11... | collective-permute-start | bytes 786440 | tf_op jit(solution)/shard_map/ppermute | solution.py:869
  149.2 1.5 collective-permute-start.21

commit v3 on v2

--- a/solution.py
+++ b/solution.py
@@ -176,7 +176,7 @@
         ],
         compiler_params=few(4),
         name="pack",
-    )(bias, decay, gate, value, output, steps, kv, norm, tokens)
+    )(bias, decay, *in_hbm(gate, value, output, steps, kv, norm, tokens))
 
 
 def params_kernel(bias, decay, kv, ks, gain, steps, norm, taps, both, *refs):
@@ -209,7 +209,7 @@
         ],
         compiler_params=few(4),
         name="coarse_params",
-    )(bias, decay, kv, ks, gain, steps, norm)
+    )(bias, decay, *in_hbm(kv, ks, gain, steps, norm))
 
 
 def state_chunk(x, rim, gain, pack, scans, ks, taps, cv, act):
@@ -310,6 +310,10 @@
     return jax.ShapeDtypeStruct(shape, dtype)
 
 
+def in_hbm(*arrays):
+    return [pltpu.with_memory_space_constraint(a, pltpu.HBM) for a in arrays]
+
+
 def few(mib):
     return pltpu.CompilerParams(vmem_limit_bytes=mib << 20)
 
@@ -345,7 +349,7 @@
         + [pltpu.SemaphoreType.DMA((6,)), pltpu.SemaphoreType.DMA((3,))],
         compiler_params=few(16),
         name="later_chunks",
-    )(tokens, gain, pack, scans, ks)
+    )(*in_hbm(tokens, gain), pack, *in_hbm(scans, ks))
     _, _, gain, scans, ks = resident
     first = pl.pallas_call(
         first_chunk_kernel,
@@ -458,10 +462,11 @@
 
 def scan_block(
     normed, wg, wv, ws, wst, taps, bias, decay,
-    lead, tail_out, maps_out, cv, act, sc, run, run_log,
+    lead, tail_out, maps_out, cv, act, sc, spread, scaled, run, run_log,
 ):
     project(normed, wv[...], cv, 16, 0)
     project(normed, ws[...], cv, 16, 4)
+    tail_out[...] = silu(dot(normed, wg[...]))
     convolve(cv, act, taps, BLK)
     cv[:, 0:16, :] = cv[:, 256:272, :]
     raw = dot(wst[...], normed, NT)
@@ -473,7 +478,7 @@
     stacked = jnp.concatenate(
         [jnp.exp(cum), jnp.exp(cum + before_log), jnp.exp(last - cum) * dt], 1
     )
-    spread = dot(parts(stacked), expander(512), TN)
+    spread[...] = dot(parts(stacked), expander(512), TN)
     run_log[...] = run_log[...] + last
     columns = dot(parts(cum), jnp.where(
         (iota((32, 128), 0) < 24) & (iota((32, 128), 0) % 8 == iota((32, 128), 1)), 1.0, 0.0
@@ -483,7 +488,7 @@
     out_map = jnp.concatenate([act[6, 0:BLK].astype(BF), act[7, 0:BLK].astype(BF)], 1)
     maps_out[...] = out_map
     sc[...] = dot(out_map, in_map, NT)
-    carried = dot(out_map, run[...].astype(BF))
+    lead[...] = spread[0:256, :] * dot(out_map, run[...].astype(BF))
     low_tri = iota((128, 128), 0) >= iota((128, 128), 1)
     lane_low = iota((BLK, 128), 1) < 64
     for p in range(4):
@@ -506,29 +511,27 @@
             jnp.concatenate(upper_w, 1), jnp.concatenate([v0[0:128], v1[0:128]], 0)
         )
         bottom = dot(jnp.concatenate(lower_w, 1), jnp.concatenate([v0, v1], 0))
-        gate = silu(dot(normed, wg[:, cols]))
-        lead[0:128, cols] = (top + spread[0:128, cols] * carried[0:128, cols]) * gate[0:128]
-        lead[128:256, cols] = (
-            bottom + spread[128:256, cols] * carried[128:256, cols]
-        ) * gate[128:256]
+        gate = tail_out[:, cols]
+        lead[0:128, cols] = (top + lead[0:128, cols]) * gate[0:128]
+        lead[128:256, cols] = (bottom + lead[128:256, cols]) * gate[128:256]
         tail_out[:, cols] = spread[256:512, cols] * gate
-        scaled = (vals * spread[512:768, cols]).astype(BF)
-        run[:, cols] = run[:, cols] * spread[255:256, cols] + dot(in_map, scaled, TN)
+        scaled[:, cols] = (vals * spread[512:768, cols]).astype(BF)
+    run[...] = run[...] * spread[255:256, :] + dot(in_map, scaled[...], TN)
 
 
 SCAN_SCRATCH = [
     pltpu.VMEM((8, 280, 128), F32),
     pltpu.VMEM((8, BLK + 8, 128), F32),
     pltpu.VMEM((BLK, BLK), F32),
-    pltpu.VMEM((256, 512), F32),
-    pltpu.VMEM((8, 128), F32),
+    pltpu.VMEM((768, 512), F32),
+    pltpu.VMEM((256, 512), BF),
 ]
 
 
 def fine_main_kernel(later, x, gain, ws, ks, p0, p1, p2, p3, *refs):
     (
         x0, x1, x2, lead, tail_out, maps_out, run, run_log, cv_end,
-        wg, wv, wst, taps, bias, decay, cv, act, sc,
+        wg, wv, wst, taps, bias, decay, cv, act, sc, spread, scaled,
     ) = refs
 
     @pl.when(pl.program_id(0) == 0)
@@ -552,7 +555,7 @@
 
     scan_block(
         rms(x[...], gain[...]), wg, wv, ws, wst[...].astype(BF), taps, bias[:, 0:1], decay[:, 0:1],
-        lead, tail_out, maps_out, cv, act, sc, run, run_log,
+        lead, tail_out, maps_out, cv, act, sc, spread, scaled, run, run_log,
     )
     cv_end[...] = cv[:, 0:16, :]
 
@@ -577,7 +580,7 @@
             pltpu.VMEM((8, 128), F32),
             pltpu.VMEM((8, 128), F32),
         ]
-        + SCAN_SCRATCH[:3],
+        + SCAN_SCRATCH,
         compiler_params=few(16),
         name="fine_main_b" if later else "fine_main_a",
     )(x, gain, scans, ks, *packs, *extra)
@@ -585,7 +588,7 @@
 
 def fine_close_kernel(
     lead_a, lead_b, tail_a, tail_b, maps_a, maps_b, x, s0, s1, s2, s3, p0, p1, p2, p3, merge,
-    merged, end_rows, lead, tail, maps, hidden,
+    merged, end_rows, lead, tail, maps, hidden, state, wo, norm,
 ):
     i = pl.program_id(0)
 
@@ -597,18 +600,18 @@
     def _():
         lead[...], tail[...], maps[...] = lead_b[...], tail_b[...], maps_b[...]
 
-    gated = []
-    for j, s in enumerate((s0, s1, s2, s3)):
-        cols = slice(j * 128, (j + 1) * 128)
-        gated.append(lead[:, cols] + tail[:, cols] * dot(maps[...], s[...]))
-    squares = sum(jnp.sum(g * g, axis=1, keepdims=True) for g in gated)
-    factor = lax.rsqrt(squares / 512.0 + EPSILON)
+    @pl.when(i == 0)
+    def _():
+        for j, (s, p) in enumerate(zip((s0, s1, s2, s3), (p0, p1, p2, p3))):
+            cols = slice(j * 128, (j + 1) * 128)
+            state[:, cols] = s[...]
+            wo[cols, :] = p[256:384, :]
+            norm[:, cols] = small_rows(p)[1]
+
+    gated = lead[...] + tail[...] * dot(maps[...], state[...])
+    factor = lax.rsqrt(jnp.sum(gated * gated, axis=1, keepdims=True) / 512.0 + EPSILON)
     out = x[...].astype(F32)
-    total = None
-    for g, p in zip(gated, (p0, p1, p2, p3)):
-        norm = small_rows(p)[1]
-        piece = dot((g * factor * norm).astype(BF), p[256:384, :])
-        total = piece if total is None else total + piece
+    total = dot((gated * factor * norm[...]).astype(BF), wo[...])
     start = pl.multiple_of(i * BLK, BLK)
     hidden[0, pl.ds(start, BLK), :] = rounded(out[:, 0:128] + total[:, 0:128])
     hidden[1, pl.ds(start, BLK), :] = rounded(out[:, 128:256] + total[:, 128:256])
@@ -617,13 +620,15 @@
     def _():
         total = None
         for odd in range(2):
-            for half in range(2):
-                rows = hidden[half, pl.ds(odd, 512, stride=2), :].reshape(8, 2, 32, 128)
-                for line in range(2):
-                    tile = rows[:, line].reshape(256, 128).astype(BF)
-                    at = (2 * line + odd) * 256 + half * 128
-                    piece = dot(tile, merge[at : at + 128, :])
-                    total = piece if total is None else total + piece
+            rows = [
+                hidden[half, pl.ds(odd, 512, stride=2), :].reshape(8, 2, 32, 128)
+                for half in range(2)
+            ]
+            for line in range(2):
+                tile = [r[:, line].reshape(256, 128).astype(BF) for r in rows]
+                at = (2 * line + odd) * 256
+                piece = dot(jnp.concatenate(tile, 1), merge[at : at + 256, :])
+                total = piece if total is None else total + piece
         result = total.astype(BF)
         merged[...] = result
         end_rows[...] = result[240:256]
@@ -650,6 +655,9 @@
             pltpu.VMEM((BLK, 512), F32),
             pltpu.VMEM((BLK, 256), BF),
             pltpu.VMEM((2, 1024, 128), F32),
+            pltpu.VMEM((256, 512), BF),
+            pltpu.VMEM((512, 256), BF),
+            pltpu.VMEM((1, 512), F32),
         ],
         out_shape=[sds((256, 1024), BF), sds((16, 1024), BF)],
         compiler_params=few(16),
@@ -657,56 +665,65 @@
     )(*leads, *tails, *maps, x, *states, *packs, merge)
 
 
-def coarse_main_kernel(
-    near, qa, qb, ra, rb, gain, wg, wv, ws, wst, taps, both, *refs
-):
-    if near:
-        lead, tail_out, maps_out, share, run, run_log, ends = refs[:7]
-    else:
-        near_ends, near_run, near_log, lead, tail_out, maps_out, share, run, run_log, message = (
-            refs[:10]
-        )
-    xs, sems, cv, act, sc = refs[-5:]
-    i = pl.program_id(0)
+def in_order(first, a, a_log, b, b_log):
+    lead_log = jnp.where(first, b_log, a_log)
+    row = jnp.exp(spread_row(lead_log))
+    return jnp.where(first, a, b) * row + jnp.where(first, b, a), a_log + b_log
+
+
+def coarse_main_kernel(kind, pieces, gain, wg, wv, ws, wst, taps, both, *refs):
+    qs, refs = refs[:pieces], refs[pieces:]
+    xs, sems, cv, act, sc, spread, scaled = refs[-7:]
     y, c = lax.axis_index("y"), lax.axis_index("c")
     h = 2 * y + c
+    if kind == "near":
+        ra, rb, lead, tail_out, maps_out, share, run, run_log, ends = refs[:-7]
+    elif kind == "far_1":
+        near_ends, re, lead, tail_out, maps_out, share, run, run_log, ends = refs[:-7]
+    else:
+        (
+            near_ends, ends_1, rd, near_run, near_log, run_1, run_log_1,
+            lead, tail_out, maps_out, share, run, run_log, far_run, far_log, message,
+        ) = refs[:-7]
+    i = pl.program_id(0)
 
     @pl.when(i == 0)
     def _():
-        copies = run_copies(((qa, xs.at[c]), (qb, xs.at[1 - c])), sems)
-        rim = ra[...].astype(F32) + rb[...].astype(F32)
-        if not near:
-            rim = jnp.where(y == 0, near_ends[...].astype(F32), rim)
+        if kind == "near":
+            copies = run_copies(((qs[0], xs.at[c]), (qs[1], xs.at[1 - c])), sems)
+            rim = ra[...].astype(F32) + rb[...].astype(F32)
+        else:
+            copies = run_copies(((qs[0], xs.at[0]),), sems)
+            rim = near_ends[...].astype(F32)
+            if kind == "far_1":
+                rim = jnp.where(h == 0, rim, re[...].astype(F32))
+            else:
+                rim = jnp.where(h == 1, rim, rd[...].astype(F32))
+                rim = jnp.where(c == 0, ends_1[...].astype(F32), rim)
         begin(rms(rim, gain[...]), wv, ws, cv, run, run_log)
         for copy in copies:
             copy.wait()
-        if near:
-            ends[...] = xs[1, 240:256, :]
+        if kind != "far_2":
+            ends[...] = xs[pieces - 1, 240:256, :]
 
     share[...] = xs[i, :, pl.ds(pl.multiple_of(h * 256, 256), 256)]
     scan_block(
         rms(xs[i], gain[...]), wg, wv, ws, wst[...], taps, both[0:8, 0:1], both[8:16, 0:1],
-        lead, tail_out, maps_out, cv, act, sc, run, run_log,
-    )
-
-    if not near:
-
-        @pl.when(i == 1)
-        def _():
-            first_log = jnp.where(y == 0, near_log[:, 0:1], run_log[:, 0:1])
-            second_log = jnp.where(y == 0, run_log[:, 0:1], near_log[:, 0:1])
-            extra = decay_rows(spread_row(first_log + second_log))
-            row = jnp.exp(spread_row(second_log))
-            for n in range(16):
-                for half in range(2):
-                    cols = slice(half * 256, (half + 1) * 256)
-                    mine = run[n * 16 : (n + 1) * 16, cols]
-                    other = near_run[n * 16 : (n + 1) * 16, cols]
-                    total = jnp.where(
-                        y == 0, other * row[:, cols] + mine, mine * row[:, cols] + other
-                    )
-                    message[2 * n + half, 0:16, :] = total.astype(BF)
-                    message[2 * n + half, 16:32, :] = extra[:, cols]
+        lead, tail_out, maps_out, cv, act, sc, spread, scaled, run, run_log,
+    )
+
+    if kind == "far_2":
+        log_1, log_2, log_n = run_log_1[:, 0:1], run_log[:, 0:1], near_log[:, 0:1]
+        far, log_f = in_order(c == 0, run_1[...], log_1, run[...], log_2)
+        far_run[...] = far
+        far_log[...] = jnp.broadcast_to(log_f, (8, 128))
+        total, log = in_order(y == 0, near_run[...], log_n, far, log_f)
+        extra = decay_rows(spread_row(log))[0:8]
+        for n in range(16):
+            for half in range(2):
+                cols = slice(half * 256, (half + 1) * 256)
+                message[2 * n + half, 0:16, :] = total[n * 16 : (n + 1) * 16, cols].astype(BF)
+                message[2 * n + half, 16:24, :] = extra[:, cols]
 
 
 def spread_row(column):
@@ -718,36 +735,39 @@
 ANY = pl.BlockSpec(memory_space=pl.ANY)
 
 
-def coarse_main(near, pieces, rims, weights, params, extra):
+def coarse_main(kind, pieces, weights, params, extra):
     taps, both, gain, wst, _ = params
+    blocks = len(pieces)
+    length = blocks * BLK
     rows = [pl.BlockSpec((BLK, n), lambda i: (i, 0)) for n in (512, 512, 256, 256)]
-    last = sds((16, 1024), BF) if near else sds((32, 32, 256), BF)
-    return pl.pallas_call(
-        lambda *refs: coarse_main_kernel(near, *refs),
-        grid=(2,),
-        in_specs=[ANY] * 2 + [VM] * (9 + len(extra)),
-        out_specs=rows + [VM] * 3,
+    last = [sds((16, 1024), BF)]
+    if kind == "far_2":
+        last = [sds((256, 512)), sds((8, 128)), sds((32, 24, 256), BF)]
+    return pl.pallas_call(
+        lambda *refs: coarse_main_kernel(kind, blocks, *refs),
+        grid=(blocks,),
+        in_specs=[VM] * 7 + [ANY] * blocks + [VM] * len(extra),
+        out_specs=rows + [VM] * (2 + len(last)),
         out_shape=[
-            sds((512, 512)),
-            sds((512, 512)),
-            sds((512, 256), BF),
-            sds((512, 256), BF),
+            sds((length, 512)),
+            sds((length, 512)),
+            sds((length, 256), BF),
+            sds((length, 256), BF),
             sds((256, 512)),
             sds((8, 128)),
-            last,
-        ],
-        scratch_shapes=[pltpu.VMEM((2, 256, 1024), BF), pltpu.SemaphoreType.DMA((2,))]
-        + SCAN_SCRATCH[:3],
+        ]
+        + last,
+        scratch_shapes=[pltpu.VMEM((blocks, 256, 1024), BF), pltpu.SemaphoreType.DMA((blocks,))]
+        + SCAN_SCRATCH,
         compiler_params=few(16),
-        name="coarse_main_near" if near else "coarse_main_far",
-    )(*pieces, *rims, gain, *weights, wst, taps, both, *extra)
+    )(gain, *weights, wst, taps, both, *pieces, *extra)
 
 
 def prefix_kernel(got, out):
     state = jnp.zeros((16, 256), F32)
     for d in range(32):
         out[d] = state.astype(BF)
-        state = state * jnp.exp(of_rows(got[d, 16:32, :])) + got[d, 0:16, :].astype(F32)
+        state = state * jnp.exp(of_rows(got[d, 16:24, :])) + got[d, 0:16, :].astype(F32)
 
 
 def prefix(got):
@@ -761,42 +781,83 @@
     )(got)
 
 
-def coarse_close_kernel(
-    near, lead, tail, maps, got, other_run, other_log, norm, wo, kk, ks, sk, ss, square_sums,
-    state, sums,
-):
-    i = pl.program_id(0)
-    y = lax.axis_index("y")
-    h = 2 * y + lax.axis_index("c")
-
-    @pl.when(i == 0)
-    def _():
-        row = jnp.exp(spread_row(other_log[:, 0:1]))
-        later = (y == 1) if near else (y == 0)
-        for n in range(16):
-            for half in range(2):
-                cols = slice(half * 256, (half + 1) * 256)
-                came = got[2 * n + half].astype(F32)
-                other = other_run[n * 16 : (n + 1) * 16, cols]
-                came = jnp.where(later, came * row[:, cols] + other, came)
-                state[n * 16 : (n + 1) * 16, cols] = came.astype(BF)
-
-    gated = lead[...] + tail[...] * dot(maps[...], state[...])
-    sq = gated * gated
-    hi = sq.astype(BF)
-    low = (sq - hi.astype(F32)).astype(BF)
+def coarse_close_kernel(near, *refs):
+    if near:
+        lead, tail, maps, got, far_run, far_log, norm, wo, *refs = refs
+    else:
+        leads, tails, mapss = refs[0:2], refs[2:4], refs[4:6]
+        got, near_run, near_log, run_1, log_1, run_2, log_2, norm, wo, *refs = refs[6:]
+    gn, ks, ss, square_sums, states, sums = refs
+    y, c = lax.axis_index("y"), lax.axis_index("c")
+    h = 2 * y + c
+    came = jnp.concatenate(
+        [jnp.concatenate([got[2 * n], got[2 * n + 1]], 1) for n in range(16)], 0
+    ).astype(F32)
+
+    def after(state, cond, run, log):
+        row = jnp.exp(spread_row(log[:, 0:1]))
+        return jnp.where(cond, state * row + run[...], state)
+
+    if near:
+        states[0] = after(came, y == 1, far_run, far_log).astype(BF)
+    else:
+        came = after(came, y == 0, near_run, near_log)
+        states[0] = after(came, c == 1, run_2, log_2).astype(BF)
+        states[1] = after(came, c == 0, run_1, log_1).astype(BF)
     ones = jnp.ones((8, 512), BF)
-    sums[i] = dot(ones, hi, NT) + dot(ones, low, NT)
-    scaled = (gated * norm[...]).astype(BF)
-    rows = pl.ds(pl.multiple_of(i * BLK, BLK), BLK)
-    for k, out in enumerate((kk, sk, ks, ss)):
-        at = pl.multiple_of((h ^ k) * 256, 256)
-        out[rows, :] = dot(scaled, wo[:, pl.ds(at, 256)]).astype(BF)
-
-    @pl.when(i == 1)
-    def _():
-        square_sums[...] = jnp.concatenate([sums[0], sums[1]], 1)
-        ss[512:528, :] = sum_rows(sums[0, 0:1], sums[1, 0:1])
+    for i in range(2):
+        if near:
+            rows = slice(i * BLK, (i + 1) * BLK)
+            gated = lead[rows] + tail[rows] * dot(maps[rows], states[0])
+            place = i
+        else:
+            gated = leads[i][...] + tails[i][...] * dot(mapss[i][...], states[i])
+            place = jnp.bitwise_xor(c, i)
+        sq = gated * gated
+        hi = sq.astype(BF)
+        low = (sq - hi.astype(F32)).astype(BF)
+        sums[place] = dot(ones, hi, NT) + dot(ones, low, NT)
+        scaled = (gated * norm[...]).astype(BF)
+        at = pl.ds(pl.multiple_of(place * BLK, BLK), BLK)
+        gn[at, :] = scaled
+        for k, out in ((2, ks), (3, ss)):
+            col = pl.multiple_of((h ^ k) * 256, 256)
+            out[at, :] = dot(scaled, wo[:, pl.ds(col, 256)]).astype(BF)
+    square_sums[...] = jnp.concatenate([sums[0], sums[1]], 1)
+    ss[512:528, :] = sum_rows(sums[0, 0:1], sums[1, 0:1])
+
+
+def coarse_close(near, *args):
+    return pl.pallas_call(
+        lambda *refs: coarse_close_kernel(near, *refs),
+        in_specs=[VM] * len(args),
+        out_specs=[VM] * 4,
+        out_shape=[
+            sds((512, 512), BF), sds((512, 256), BF), sds((528, 256), BF), sds((8, 512)),
+        ],
+        scratch_shapes=[pltpu.VMEM((2, 256, 512), BF), pltpu.VMEM((2, 8, 256), F32)],
+        compiler_params=few(12),
+        name="coarse_close_near" if near else "coarse_close_far",
+    )(*args)
+
+
+def close_rest_kernel(near, far, wo, kk, sk):
+    h = lax.axis_index(HEAD)
+    for k, out in enumerate((kk, sk)):
+        col = pl.multiple_of((h ^ k) * 256, 256)
+        for j, ref in enumerate((near, far)):
+            out[j * 512 : (j + 1) * 512, :] = dot(ref[...], wo[:, pl.ds(col, 256)]).astype(BF)
+
+
+def close_rest(near, far, wo):
+    return pl.pallas_call(
+        close_rest_kernel,
+        in_specs=[VM] * 3,
+        out_specs=[VM] * 2,
+        out_shape=[sds((1024, 256), BF)] * 2,
+        compiler_params=few(8),
+        name="close_rest",
+    )(near, far, wo)
 
 
 def sum_rows(a, b):
@@ -806,20 +867,6 @@
 def rows_sum(ref):
     rows = ref[512:528, :].astype(F32)
     return jnp.concatenate([of_rows(rows[0:3]), of_rows(rows[3:6])], 1)
-
-
-def coarse_close(near, lead, tail, maps, got, other, norm, wo):
-    rows = [pl.BlockSpec((BLK, n), lambda i: (i, 0)) for n in (512, 512, 256)]
-    return pl.pallas_call(
-        lambda *refs: coarse_close_kernel(near, *refs),
-        grid=(2,),
-        in_specs=rows + [VM] * 5,
-        out_specs=[VM] * 5,
-        out_shape=[sds((512, 256), BF)] * 3 + [sds((528, 256), BF), sds((8, 512))],
-        scratch_shapes=[pltpu.VMEM((256, 512), BF), pltpu.VMEM((2, 8, 256), F32)],
-        compiler_params=few(12),
-        name="coarse_close_near" if near else "coarse_close_far",
-    )(lead, tail, maps, got, *other, norm, wo)
 
 
 def relay_kernel(ks, square_sums, came, out, sums):
@@ -839,30 +886,34 @@
     )(ks, square_sums, came)
 
 
-def final_kernel(sa, ka, ca, sum_a, far_a, sb, kb, cb, sum_b, far_b, out):
-    y = lax.axis_index("y")
+def final_kernel(share, share_1, share_2, kk, sk, sum_a, far_a, sum_b, far_b, out):
+    y, c = lax.axis_index("y"), lax.axis_index("c")
     pick = jnp.where(iota((32, 256), 0) % 8 == 0, 1.0, 0.0).astype(BF)
-    sides = (y, sa, ka, ca, sum_a, far_a), (1 - y, sb, kb, cb, sum_b, far_b)
-    for half, share, kk, sk, sums, far in sides:
+    for side, (half, sums, far) in enumerate(((y, sum_a, far_a), (1 - y, sum_b, far_b))):
         total = sums[...] + rows_sum(far)
         factor = lax.rsqrt(total / 2048.0 + EPSILON)
         for b in range(2):
             rows = slice(b * BLK, (b + 1) * BLK)
+            here = slice(side * 512 + b * BLK, side * 512 + (b + 1) * BLK)
             spread = dot(parts(factor[:, rows]), pick, TN)
-            total = kk[rows].astype(F32) + sk[rows].astype(F32) + far[rows].astype(F32)
+            total = kk[here].astype(F32) + sk[here].astype(F32) + far[rows].astype(F32)
+            if side == 0:
+                own = share[rows].astype(F32)
+            else:
+                own = jnp.where(c == b, share_1[...].astype(F32), share_2[...].astype(F32))
             at = pl.multiple_of(half * 512 + b * BLK, BLK)
-            out[pl.ds(at, BLK), :] = (share[rows].astype(F32) + total * spread).astype(BF)
-
-
-def final(near, far):
+            out[pl.ds(at, BLK), :] = (own + total * spread).astype(BF)
+
+
+def final(*args):
     return pl.pallas_call(
         final_kernel,
-        in_specs=[VM] * 10,
+        in_specs=[VM] * 9,
         out_specs=VM,
         out_shape=sds((1024, 256), BF),
         compiler_params=few(8),
         name="final",
-    )(*near, *far)
+    )(*args)
 
 
 def passed(x, axes, pairs):
@@ -919,34 +970,43 @@
 
     rim_a = rims([(q, q + 1) for q in range(1, 127, 2)])
     rim_b = rims([(q, q + 2) for q in range(1, 126, 2)])
-    rim_c = rims([(q, q + 3) for q in range(3, 125, 4)])
     rim_d = rims([(q, q + 4) for q in range(3, 124, 4)])
+    rim_e = rims(
+        [(q, q - 1) for q in range(2, 128, 4)]
+        + [(q, q + 3) for q in range(0, 128, 4)]
+        + [(q, q + 3) for q in range(3, 124, 4)],
+    )
     across = swapped(merged, 2)
     beside = swapped(merged, 1)
     both = swapped(across, 1)
     weights = (coarse_gate, coarse_value, coarse_scans)
-    near = coarse_main(True, (merged, beside), (rim_a, rim_b), weights, params, ())
-    lead, tail, maps, share, run, run_log, near_ends = near
-    far = coarse_main(
-        False, (across, both), (rim_c, rim_d), weights, params, (near_ends, run, run_log)
-    )
-    lead_f, tail_f, maps_f, share_f, run_f, run_log_f, message = far
+    lead, tail, maps, share, run, run_log, near_ends = coarse_main(
+        "near", (merged, beside), weights, params, (rim_a, rim_b)
+    )
+    lead_1, tail_1, maps_1, share_1, run_1, run_log_1, ends_1 = coarse_main(
+        "far_1", (across,), weights, params, (near_ends, rim_e)
+    )
+    lead_2, tail_2, maps_2, share_2, run_2, run_log_2, run_f, run_log_f, message = coarse_main(
+        "far_2", (both,), weights, params,
+        (near_ends, ends_1, rim_d, run, run_log, run_1, run_log_1),
+    )
     got = lax.all_to_all(message, SEQ, split_axis=0, concat_axis=0, tiled=True)
     got = lax.all_to_all(prefix(got), SEQ, split_axis=0, concat_axis=0, tiled=True)
     norm = params[4]
-    kk, ks, sk, ss, sums = coarse_close(
-        True, lead, tail, maps, got, (run_f, run_log_f), norm, coarse_output
-    )
-    kk_f, ks_f, sk_f, ss_f, sums_f = coarse_close(
-        False, lead_f, tail_f, maps_f, got, (run, run_log), norm, coarse_output
+    gn, ks, ss, sums = coarse_close(
+        True, lead, tail, maps, got, run_f, run_log_f, norm, coarse_output
+    )
+    gn_f, ks_f, ss_f, sums_f = coarse_close(
+        False, lead_1, lead_2, tail_1, tail_2, maps_1, maps_2, got, run, run_log,
+        run_1, run_log_1, run_2, run_log_2, norm, coarse_output,
     )
     went, sums = relay(ks, sums, swapped(ss, 1))
     went = swapped(went, 2)
     went_f, sums_f = relay(ks_f, sums_f, swapped(ss_f, 1))
     went_f = swapped(went_f, 2)
+    kk, sk = close_rest(gn, gn_f, coarse_output)
     sk = swapped(sk, 1)
-    sk_f = swapped(sk_f, 1)
-    return final((share, kk, sk, sums, went_f), (share_f, kk_f, sk_f, sums_f, went))
+    return final(share, share_1, share_2, kk, sk, sums, went_f, sums_f, went)
 
 
 def solution(mesh):

time: 162 us -> 157 us (0.969)
  local copies, waits for them, and re-layouts: 8.48 us -> 1.35 us
  starting transfers between devices: 39.3 us -> 43.7 us
  blocking collectives: 33.7 us -> 30.7 us
    unnamed x50 -> x18, local copies, waits for them, and re-layouts: 8.48 us -> 1.35 us
    ppermute x27 -> x26, starting transfers between devices: 39.3 us -> 43.7 us  [passed(): return lax.ppermute(x, axes, pairs)]
    all_to_all x1, blocking collectives: 19.4 us -> 17.6 us  [shards(): got = lax.all_to_all(message, SEQ, split_axis=0, concat_axis=0, tiled=True)]
    pallas_call x5 -> x7, Pallas kernels: 19.9 us -> 19.6 us  [the longest x3 15.1 us: coarse_main(): pl.pallas_call(lambda *refs: coarse_main_kernel(kind, blocks, *refs), gri...]
    ppermute x27 -> x26, waiting for transfers between devices: 32.3 us -> 32.5 us  [passed(): return lax.ppermute(x, axes, pairs)]
  transfers between devices with their start and end apart: 27 -> 26, of which waited for: 11 -> 8; matrix products, arithmetic and copies ran while one was open for 0% -> 0% of each run, Pallas kernels for 17% -> 22%
where the time goes in v3:
time: 157 us
  Pallas kernels  48 us (31%)
  starting transfers between devices  43.7 us (28%)
  waiting for transfers between devices  32.5 us (21%)
  blocking collectives  30.7 us (20%)
    ppermute x26, starting transfers between devices, passed(): return lax.ppermute(x, axes, pairs)  43.7 us
    ppermute x26, waiting for transfers between devices, passed(): return lax.ppermute(x, axes, pairs)  32.5 us
    all_to_all x1, blocking collectives, shards(): got = lax.all_to_all(message, SEQ, split_axis=0, concat_axis=0, tiled=True)  17.6 us
    pallas_call x3, Pallas kernels, coarse_main(): pl.pallas_call(lambda *refs: coarse_main_kernel(kind, blocks, *refs), gri...  15.1 us
    all_to_all x1, blocking collectives, shards(): lax.all_to_all(prefix(got), SEQ, split_axis=0, concat_axis=0, tiled=True)  13.2 us
    pallas_call x2, Pallas kernels, fine_main(): pl.pallas_call(lambda *refs: fine_main_kernel(later, *refs), grid=(2,), i...  11.1 us
    pallas_call x1, Pallas kernels, fine_states(): pl.pallas_call(later_chunks_kernel, grid=(3,), in_specs=[HBM, HBM, VM, HB...  8 us
    pallas_call x1, Pallas kernels, fine_close(): pl.pallas_call(fine_close_kernel, grid=(4,), in_specs=halves(512) + halve...  3.46 us
  transfers between devices with their start and end apart: 26, of which 8 were waited for; matrix products, arithmetic and copies ran while one was open for 0% of the time, Pallas kernels for 22%

profile of v3, /device:TPU:1, one launch (start us, length us, event | category | flops | bytes accessed | tf_op | source)
XLA Modules:
  0.0 156.7 jit_solution(12565834819385038332)
XLA Ops:
  0.0 0.7 copy-done.5
  0.7 0.7 copy-done.6
  1.3 1.6 %pack.1 = (bf16[416,256]{1,0:T(8,128)(2,1)S(1)}, bf16[16,256]{1,0:T(8,128)(2,1)S(1)}) custom-call(f32[2]{0:T(128)S(1)} %copy-done.5, f32[2]{0:T(128)S(1)} %copy-done.6, bf16[256,128]{1,0:T(8,128)(2,1)} %gate.1, bf16[256,128]{1,0:T(8,128)(2,1)} %value.1, bf16[128,256]{1,0:T(8,128)(2,1)} %output.1, bf16[2,256]{1,0:T(2,128)(2,1)} %bitcast.9, f32[4,128]{1,0:T(4,128)} %kv.3, ...), custom_call_target="tpu_custom_call" | custom-call | tf_op jit(solution)/shard_map/pack/pallas_call | solution.py:166
  2.9 3.9 %collective-permute-start.3 = (bf16[16,256]{1,0:T(8,128)(2,1)S(1)}, bf16[16,256]{1,0:T(8,128)(2,1)S(1)}, u32[]{:S(2)}, u32[]{:S(2)}) collective-permute-start(bf16[16,256]{1,0:T(8,128)(2,1)S(1)} %get-tuple-element.96), channel_id=1, source_target_pairs={{0,4},{4,8},{8,12},{12,16},{16,20},{20,24},{24,28},{28,32},{32,36}... | collective-permute-start | bytes 24584 | tf_op jit(solution)/shard_map/ppermute | solution.py:920
  6.8 8.0 %later_chunks.1 = (f32[3,256,128]{2,1,0:T(8,128)S(1)}, f32[3,8,128]{2,1,0:T(8,128)S(1)}, bf16[1024,256]{1,0:T(8,128)(2,1)S(1)}, bf16[1024,256]{1,0:T(8,128)(2,1)...) custom-call(bf16[4096,256]{1,0:T(8,128)(2,1)} %tokens.3, ...), custom_call_target="tpu_custom_call" | custom-call | tf_op jit(solution)/shard_map/later_chunks/pallas_call | solution.py:332
  14.8 2.2 %first_chunk.1 = (f32[256,128]{1,0:T(8,128)S(1)}, f32[8,128]{1,0:T(8,128)S(1)}, f32[256,128]{1,0:T(8,128)S(1)}, f32[8,128]{1,0:T(8,128)S(1)}, bf16[272,128]{1,0:T(8,128)(2,1)S(1)}) custom-call(bf16[1024,256]{1,0:T(8,128)(2,1)S(1)} %get-tuple-element.98.x, bf16[16,256]{1,0:T(8,128)(2,1)S(1)} %collective-permute-done.3.rim.refs_8_, ...), custom_call_target="tpu_custom_call" | custom-call | tf_op jit(solution)/shard_map/first_chunk/pallas_call | solution.py:354
  17.1 4.2 %collective-permute-start.6 = (bf16[272,128]{1,0:T(8,128)(2,1)S(1)}, bf16[272,128]{1,0:T(8,128)(2,1)S(1)}, u32[]{:S(2)}, u32[]{:S(2)}) collective-permute-start(bf16[272,128]{1,0:T(8,128)(2,1)S(1)} %get-tuple-element.113), channel_id=1, source_target_pairs={{0,12},{4,0},{8,4},{12,8},{1,13},{5,1},{9,5},{13,9},{2,14},{6,2},{... | collective-permute-start | bytes 208904 | tf_op jit(solution)/shard_map/ppermute | solution.py:920
  21.3 0.7 collective-permute-start.4
  21.9 1.8 %collective-permute-start.2 = (bf16[416,256]{1,0:T(8,128)(2,1)S(1)}, bf16[416,256]{1,0:T(8,128)(2,1)S(1)}, u32[]{:S(2)}, u32[]{:S(2)}) collective-permute-start(bf16[416,256]{1,0:T(8,128)(2,1)S(1)} %get-tuple-element.91.pack.refs_4_.p0), channel_id=1, source_target_pairs={{0,3},{1,2},{2,1},{3,0},{4,7},{5,6},{6,5},{7,4},{8,11},{9,10},{10,... | collective-permute-start | bytes 638984 | tf_op jit(solution)/shard_map/ppermute | solution.py:920
  23.7 2.3 %collective-permute-done.5.refs_3_ = bf16[272,128]{1,0:T(8,128)(2,1)S(1)} collective-permute-done((bf16[272,128]{1,0:T(8,128)(2,1)S(1)}, bf16[272,128]{1,0:T(8,128)(2,1)S(1)}, u32[]{:S(2)}, u32[]{:S(2)}) %collective-permute-start.5) | collective-permute-done | bytes 69664 | tf_op jit(solution)/shard_map/ppermute | solution.py:920
  26.0 0.4 collective-permute-done.4.refs_2_
  26.4 0.1 shard_map.226
  26.5 1.8 %collective-permute-start.7 = (bf16[272,128]{1,0:T(8,128)(2,1)S(1)}, bf16[272,128]{1,0:T(8,128)(2,1)S(1)}, u32[]{:S(2)}, u32[]{:S(2)}) collective-permute-start(bf16[272,128]{1,0:T(8,128)(2,1)S(1)} %get-tuple-element.118), channel_id=1, source_target_pairs={{0,16},{16,0},{1,17},{17,1},{2,18},{18,2},{3,19},{19,3},{4,20},{20... | collective-permute-start | bytes 208904 | tf_op jit(solution)/shard_map/ppermute | solution.py:920
  28.3 1.0 collective-permute-start.1
  29.3 3.0 %collective-permute-start = (bf16[416,256]{1,0:T(8,128)(2,1)S(1)}, bf16[416,256]{1,0:T(8,128)(2,1)S(1)}, u32[]{:S(2)}, u32[]{:S(2)}) collective-permute-start(bf16[416,256]{1,0:T(8,128)(2,1)S(1)} %get-tuple-element.91.pack.refs_4_.p0), channel_id=1, source_target_pairs={{0,1},{1,0},{2,3},{3,2},{4,5},{5,4},{6,7},{7,6},{8,9},{9,8},{10,11... | collective-permute-start | bytes 638984 | tf_op jit(solution)/shard_map/ppermute | solution.py:920
  32.3 0.1 shard_map.227
  32.4 3.2 %collective-permute-start.10 = (bf16[272,128]{1,0:T(8,128)(2,1)S(1)}, bf16[272,128]{1,0:T(8,128)(2,1)S(1)}, u32[]{:S(2)}, u32[]{:S(2)}) collective-permute-start(bf16[272,128]{1,0:T(8,128)(2,1)S(1)} %get-tuple-element.123), channel_id=1, source_target_pairs={{0,96},{32,0},{64,32},{96,64},{1,97},{33,1},{65,33},{97,65},{2,98}... | collective-permute-start | bytes 208904 | tf_op jit(solution)/shard_map/ppermute | solution.py:920
  35.5 0.4 collective-permute-start.9
  35.9 1.0 collective-permute-done.10.r3
  36.9 0.6 collective-permute-start.8
  37.5 2.7 %collective-permute-done.9.r2 = bf16[272,128]{1,0:T(8,128)(2,1)S(1)} collective-permute-done((bf16[272,128]{1,0:T(8,128)(2,1)S(1)}, bf16[272,128]{1,0:T(8,128)(2,1)S(1)}, u32[]{:S(2)}, u32[]{:S(2)}) %collective-permute-start.9) | collective-permute-done | bytes 69664 | tf_op jit(solution)/shard_map/ppermute | solution.py:920
  40.2 1.4 collective-permute-done.8.r1
  41.6 0.1 chain_last.1
  41.8 0.0 copy-start.4
  41.8 5.8 %collective-permute-start.11 = (bf16[256,128]{1,0:T(8,128)(2,1)S(1)}, bf16[256,128]{1,0:T(8,128)(2,1)S(1)}, u32[]{:S(2)}, u32[]{:S(2)}) collective-permute-start(bf16[256,128]{1,0:T(8,128)(2,1)S(1)} %get-tuple-element.126), channel_id=1, source_target_pairs={{0,1},{1,0},{2,3},{3,2},{4,5},{5,4},{6,7},{7,6},{8,9},{9,8},{10,11... | collective-permute-start | bytes 196616 | tf_op jit(solution)/shard_map/ppermute | solution.py:920
  47.6 0.4 collective-permute-start.12
  48.0 1.3 collective-permute-start.13
  49.3 5.2 %fine_main_a.1 = (f32[512,512]{1,0:T(8,128)S(1)}, f32[512,512]{1,0:T(8,128)S(1)}, bf16[512,256]{1,0:T(8,128)(2,1)S(1)}, f32[256,512]{1,0:T(8,128)S(1)}, f32[8,128]{1,0:T(8,128)S(1)}, /*index=5*/f32[8,16,128]{2,1,0:T(8,128)S(1)}) custom-call(bf16[1024,256]{1,0:T(8,128)(2,1)S(1)} %get-tuple-element.92.refs_0_.x, f32[1,256]{1,0:T(1,128)S(1)} %get-tuple-element.93.gain.refs_1_, ...), custom_call_target="tpu_custom_call" | custom-call | tf_op jit(solution)/shard_map/fine_main_a/pallas_call | solution.py:566
  54.6 5.8 %fine_main_b.1 = (f32[512,512]{1,0:T(8,128)S(1)}, f32[512,512]{1,0:T(8,128)S(1)}, bf16[512,256]{1,0:T(8,128)(2,1)S(1)}, f32[256,512]{1,0:T(8,128)}, f32[8,128]{1,0:T(8,128)}, /*index=5*/f32[8,16,128]{2,1,0:T(8,128)}) custom-call(bf16[1024,256]{1,0:T(8,128)(2,1)S(1)} %get-tuple-element.92.refs_0_.x, f32[1,256]{1,0:T(1,128)S(1)} %get-tuple-element.93.gain.refs_1_, ...), custom_call_target="tpu_custom_call" | custom-call | tf_op jit(solution)/shard_map/fine_main_b/pallas_call | solution.py:566
  60.4 0.0 copy-start.7
  60.4 0.0 copy-start.8
  60.4 0.0 copy-start
  60.5 0.0 copy-start.1
  60.5 3.5 %fine_close.1 = (bf16[256,1024]{1,0:T(8,128)(2,1)S(1)}, bf16[16,1024]{1,0:T(8,128)(2,1)S(1)}) custom-call(f32[512,512]{1,0:T(8,128)S(1)} %get-tuple-element.102.lead_a, f32[512,512]{1,0:T(8,128)S(1)} %get-tuple-element.106.lead_b, f32[512,512]{1,0:T(8,128)S(1)} %get-tuple-element.107.tail_a, f32[512,512]{1,0:T(8,128)S(1)} %get-tuple-element.108.tail_b, ...), custom_call_target="tpu_custom_call" | custom-call | tf_op jit(solution)/shard_map/fine_close/pallas_call | solution.py:644
  64.0 0.7 collective-permute-start.17
  64.6 0.4 collective-permute-start.14
  65.0 12.5 %collective-permute-done.17.refs_7_ = bf16[256,1024]{1,0:T(8,128)(2,1)S(1)} collective-permute-done((bf16[256,1024]{1,0:T(8,128)(2,1)S(1)}, bf16[256,1024]{1,0:T(8,128)(2,1)S(1)}, u32[]{:S(2)}, u32[]{:S(2)}) %collective-permute-start.17) | collective-permute-done | bytes 524320 | tf_op jit(solution)/shard_map/ppermute | solution.py:920
  77.5 1.0 collective-permute-start.19
  78.6 2.3 %collective-permute-start.16 = (bf16[16,1024]{1,0:T(8,128)(2,1)S(1)}, bf16[16,1024]{1,0:T(8,128)(2,1)S(1)}, u32[]{:S(2)}, u32[]{:S(2)}) collective-permute-start(bf16[16,1024]{1,0:T(8,128)(2,1)S(1)} %get-tuple-element.130), channel_id=1, source_target_pairs={{1,3},{3,5},{5,7},{7,9},{9,11},{11,13},{13,15},{15,17},{17,19},{19... | collective-permute-start | bytes 98312 | tf_op jit(solution)/shard_map/ppermute | solution.py:920
  80.9 1.3 collective-permute-start.15
  82.2 1.3 collective-permute-start.18
  83.5 0.7 collective-permute-start.20
  84.2 1.4 coarse_params.1
  85.6 7.2 %shard_map.228 = (f32[512,512]{1,0:T(8,128)S(1)}, f32[512,512]{1,0:T(8,128)S(1)}, bf16[512,256]{1,0:T(8,128)(2,1)S(1)}, bf16[512,256]{1,0:T(8,128)(2,1)S(1)}, f3...) custom-call(f32[1,1024]{1,0:T(1,128)S(1)} %get-tuple-element.87.refs_0_, ...), custom_call_target="tpu_custom_call" | custom-call | tf_op jit(solution)/shard_map/pallas_call | solution.py:746
  92.8 3.8 %shard_map.229 = (f32[256,512]{1,0:T(8,128)S(1)}, f32[256,512]{1,0:T(8,128)S(1)}, bf16[256,256]{1,0:T(8,128)(2,1)S(1)}, bf16[256,256]{1,0:T(8,128)(2,1)S(1)}, f3...) custom-call(f32[1,1024]{1,0:T(1,128)S(1)} %get-tuple-element.87.refs_0_, ...), custom_call_target="tpu_custom_call" | custom-call | tf_op jit(solution)/shard_map/pallas_call | solution.py:746
  96.7 4.0 %shard_map.230 = (f32[256,512]{1,0:T(8,128)S(1)}, f32[256,512]{1,0:T(8,128)S(1)}, bf16[256,256]{1,0:T(8,128)(2,1)S(1)}, bf16[256,256]{1,0:T(8,128)(2,1)S(1)}, f3...) custom-call(f32[1,1024]{1,0:T(1,128)S(1)} %get-tuple-element.87.refs, ...), custom_call_target="tpu_custom_call" | custom-call | tf_op jit(solution)/shard_map/pallas_call | solution.py:746
  100.7 0.0 copy-start.3
  100.7 17.6 %all_to_all.10.got = bf16[32,24,256]{2,1,0:T(8,128)(2,1)S(1)} all-to-all(bf16[32,24,256]{2,1,0:T(8,128)(2,1)S(1)} %get-tuple-element.143), channel_id=1, replica_groups=mesh['z'=4,'u'=2,'x'=4,'y'=2,'c'=2] {'z','u','x'}, dimensions={0} | all-to-all | bytes 786432 | tf_op jit(solution)/shard_map/all_to_all | solution.py:993
  118.3 0.1 prefix.1
  118.4 13.2 %all_to_all.11.refs_3_.refs_6_ = bf16[32,16,256]{2,1,0:T(8,128)(2,1)S(1)} all-to-all(bf16[32,16,256]{2,1,0:T(8,128)(2,1)S(1)} %prefix.1), channel_id=1, replica_groups=mesh['z'=4,'u'=2,'x'=4,'y'=2,'c'=2] {'z','u','x'}, dimensions={0} | all-to-all | bytes 524288 | tf_op jit(solution)/shard_map/all_to_all | solution.py:994
  131.6 1.3 coarse_close_far.1
  133.0 5.9 %collective-permute-start.23 = (bf16[528,256]{1,0:T(8,128)(2,1)S(1)}, bf16[528,256]{1,0:T(8,128)(2,1)S(1)}, u32[]{:S(2)}, u32[]{:S(2)}) collective-permute-start(bf16[528,256]{1,0:T(8,128)(2,1)S(1)} %get-tuple-element.165), channel_id=1, source_target_pairs={{0,1},{1,0},{2,3},{3,2},{4,5},{5,4},{6,7},{7,6},{8,9},{9,8},{10,11... | collective-permute-start | bytes 811016 | tf_op jit(solution)/shard_map/ppermute | solution.py:920
  138.8 1.2 coarse_close_near.1
  140.1 0.1 collective-permute-start.22
  140.2 0.7 close_rest.1
  140.9 0.6 collective-permute-start.21
  141.4 0.1 shard_map.232
  141.5 0.1 collective-permute-start.24
  141.6 0.0 collective-permute-done.22.came
  141.7 0.1 shard_map.231
  141.8 1.5 collective-permute-start.25
  143.3 6.4 %collective-permute-done.24.far_a = bf16[528,256]{1,0:T(8,128)(2,1)S(1)} collective-permute-done((bf16[528,256]{1,0:T(8,128)(2,1)S(1)}, bf16[528,256]{1,0:T(8,128)(2,1)S(1)}, u32[]{:S(2)}, u32[]{:S(2)}) %collective-permute-start.24) | collective-permute-done | bytes 270368 | tf_op jit(solution)/shard_map/ppermute | solution.py:920
  149.6 5.8 %collective-permute-done.25.far_b = bf16[528,256]{1,0:T(8,128)(2,1)S(1)} collective-permute-done((bf16[528,256]{1,0:T(8,128)(2,1)S(1)}, bf16[528,256]{1,0:T(8,128)(2,1)S(1)}, u32[]{:S(2)}, u32[]{:S(2)}) %collective-permute-start.25) | collective-permute-done | bytes 270368 | tf_op jit(solution)/shard_map/ppermute | solution.py:920
  155.4 1.3 final.1
  (28 shorter events, 0.1 us)
Async XLA Ops:
  0.0 0.7 copy-start.5
  0.7 0.7 copy-start.6
  2.9 12.0 %collective-permute-start.3 = (bf16[16,256]{1,0:T(8,128)(2,1)S(1)}, bf16[16,256]{1,0:T(8,128)(2,1)S(1)}, u32[]{:S(2)}, u32[]{:S(2)}) collective-permute-start(bf16[16,256]{1,0:T(8,128)(2,1)S(1)} %get-tuple-element.96), channel_id=1, source_target_pairs={{0,4},{4,8},{8,12},{12,16},{16,20},{20,24},{24,28},{28,32},{32,36}... | collective-permute-start | bytes 24584 | tf_op jit(solution)/shard_map/ppermute | solution.py:920
  17.1 6.7 %collective-permute-start.6 = (bf16[272,128]{1,0:T(8,128)(2,1)S(1)}, bf16[272,128]{1,0:T(8,128)(2,1)S(1)}, u32[]{:S(2)}, u32[]{:S(2)}) collective-permute-start(bf16[272,128]{1,0:T(8,128)(2,1)S(1)} %get-tuple-element.113), channel_id=1, source_target_pairs={{0,12},{4,0},{8,4},{12,8},{1,13},{5,1},{9,5},{13,9},{2,14},{6,2},{... | collective-permute-start | bytes 208904 | tf_op jit(solution)/shard_map/ppermute | solution.py:920
  21.3 4.8 %collective-permute-start.5 = (bf16[272,128]{1,0:T(8,128)(2,1)S(1)}, bf16[272,128]{1,0:T(8,128)(2,1)S(1)}, u32[]{:S(2)}, u32[]{:S(2)}) collective-permute-start(bf16[272,128]{1,0:T(8,128)(2,1)S(1)} %get-tuple-element.113), channel_id=1, source_target_pairs={{0,8},{4,12},{8,0},{12,4},{1,9},{5,13},{9,1},{13,5},{2,10},{6,14},... | collective-permute-start | bytes 208904 | tf_op jit(solution)/shard_map/ppermute | solution.py:920
  21.3 5.1 %collective-permute-start.4 = (bf16[272,128]{1,0:T(8,128)(2,1)S(1)}, bf16[272,128]{1,0:T(8,128)(2,1)S(1)}, u32[]{:S(2)}, u32[]{:S(2)}) collective-permute-start(bf16[272,128]{1,0:T(8,128)(2,1)S(1)} %get-tuple-element.113), channel_id=1, source_target_pairs={{0,4},{4,8},{8,12},{12,0},{1,5},{5,9},{9,13},{13,1},{2,6},{6,10},{... | collective-permute-start | bytes 208904 | tf_op jit(solution)/shard_map/ppermute | solution.py:920
  21.9 26.0 %collective-permute-start.2 = (bf16[416,256]{1,0:T(8,128)(2,1)S(1)}, bf16[416,256]{1,0:T(8,128)(2,1)S(1)}, u32[]{:S(2)}, u32[]{:S(2)}) collective-permute-start(bf16[416,256]{1,0:T(8,128)(2,1)S(1)} %get-tuple-element.91.pack.refs_4_.p0), channel_id=1, source_target_pairs={{0,3},{1,2},{2,1},{3,0},{4,7},{5,6},{6,5},{7,4},{8,11},{9,10},{10,... | collective-permute-start | bytes 638984 | tf_op jit(solution)/shard_map/ppermute | solution.py:920
  26.5 5.7 %collective-permute-start.7 = (bf16[272,128]{1,0:T(8,128)(2,1)S(1)}, bf16[272,128]{1,0:T(8,128)(2,1)S(1)}, u32[]{:S(2)}, u32[]{:S(2)}) collective-permute-start(bf16[272,128]{1,0:T(8,128)(2,1)S(1)} %get-tuple-element.118), channel_id=1, source_target_pairs={{0,16},{16,0},{1,17},{17,1},{2,18},{18,2},{3,19},{19,3},{4,20},{20... | collective-permute-start | bytes 208904 | tf_op jit(solution)/shard_map/ppermute | solution.py:920
  28.3 21.0 %collective-permute-start.1 = (bf16[416,256]{1,0:T(8,128)(2,1)S(1)}, bf16[416,256]{1,0:T(8,128)(2,1)S(1)}, u32[]{:S(2)}, u32[]{:S(2)}) collective-permute-start(bf16[416,256]{1,0:T(8,128)(2,1)S(1)} %get-tuple-element.91.pack.refs_4_.p0), channel_id=1, source_target_pairs={{0,2},{1,3},{2,0},{3,1},{4,6},{5,7},{6,4},{7,5},{8,10},{9,11},{10,... | collective-permute-start | bytes 638984 | tf_op jit(solution)/shard_map/ppermute | solution.py:920
  29.3 20.0 %collective-permute-start = (bf16[416,256]{1,0:T(8,128)(2,1)S(1)}, bf16[416,256]{1,0:T(8,128)(2,1)S(1)}, u32[]{:S(2)}, u32[]{:S(2)}) collective-permute-start(bf16[416,256]{1,0:T(8,128)(2,1)S(1)} %get-tuple-element.91.pack.refs_4_.p0), channel_id=1, source_target_pairs={{0,1},{1,0},{2,3},{3,2},{4,5},{5,4},{6,7},{7,6},{8,9},{9,8},{10,11... | collective-permute-start | bytes 638984 | tf_op jit(solution)/shard_map/ppermute | solution.py:920
  32.4 4.6 %collective-permute-start.10 = (bf16[272,128]{1,0:T(8,128)(2,1)S(1)}, bf16[272,128]{1,0:T(8,128)(2,1)S(1)}, u32[]{:S(2)}, u32[]{:S(2)}) collective-permute-start(bf16[272,128]{1,0:T(8,128)(2,1)S(1)} %get-tuple-element.123), channel_id=1, source_target_pairs={{0,96},{32,0},{64,32},{96,64},{1,97},{33,1},{65,33},{97,65},{2,98}... | collective-permute-start | bytes 208904 | tf_op jit(solution)/shard_map/ppermute | solution.py:920
  35.5 4.7 %collective-permute-start.9 = (bf16[272,128]{1,0:T(8,128)(2,1)S(1)}, bf16[272,128]{1,0:T(8,128)(2,1)S(1)}, u32[]{:S(2)}, u32[]{:S(2)}) collective-permute-start(bf16[272,128]{1,0:T(8,128)(2,1)S(1)} %get-tuple-element.123), channel_id=1, source_target_pairs={{0,64},{32,96},{64,0},{96,32},{1,65},{33,97},{65,1},{97,33},{2,66}... | collective-permute-start | bytes 208904 | tf_op jit(solution)/shard_map/ppermute | solution.py:920
  36.9 4.7 %collective-permute-start.8 = (bf16[272,128]{1,0:T(8,128)(2,1)S(1)}, bf16[272,128]{1,0:T(8,128)(2,1)S(1)}, u32[]{:S(2)}, u32[]{:S(2)}) collective-permute-start(bf16[272,128]{1,0:T(8,128)(2,1)S(1)} %get-tuple-element.123), channel_id=1, source_target_pairs={{0,32},{32,64},{64,96},{96,0},{1,33},{33,65},{65,97},{97,1},{2,34}... | collective-permute-start | bytes 208904 | tf_op jit(solution)/shard_map/ppermute | solution.py:920
  41.8 18.7 %copy-start.4 = (bf16[1024,1024]{1,0:T(8,128)(2,1)S(1)}, bf16[1024,1024]{1,0:T(8,128)(2,1)}, u32[]{:S(2)}) copy-start(bf16[1024,1024]{1,0:T(8,128)(2,1)} %merge.1) | copy-start | bytes 6291460
  41.8 18.6 %collective-permute-start.11 = (bf16[256,128]{1,0:T(8,128)(2,1)S(1)}, bf16[256,128]{1,0:T(8,128)(2,1)S(1)}, u32[]{:S(2)}, u32[]{:S(2)}) collective-permute-start(bf16[256,128]{1,0:T(8,128)(2,1)S(1)} %get-tuple-element.126), channel_id=1, source_target_pairs={{0,1},{1,0},{2,3},{3,2},{4,5},{5,4},{6,7},{7,6},{8,9},{9,8},{10,11... | collective-permute-start | bytes 196616 | tf_op jit(solution)/shard_map/ppermute | solution.py:920
  47.6 12.8 %collective-permute-start.12 = (bf16[256,128]{1,0:T(8,128)(2,1)S(1)}, bf16[256,128]{1,0:T(8,128)(2,1)S(1)}, u32[]{:S(2)}, u32[]{:S(2)}) collective-permute-start(bf16[256,128]{1,0:T(8,128)(2,1)S(1)} %get-tuple-element.127), channel_id=1, source_target_pairs={{0,2},{1,3},{2,0},{3,1},{4,6},{5,7},{6,4},{7,5},{8,10},{9,11},{10,... | collective-permute-start | bytes 196616 | tf_op jit(solution)/shard_map/ppermute | solution.py:920
  48.0 12.4 %collective-permute-start.13 = (bf16[256,128]{1,0:T(8,128)(2,1)S(1)}, bf16[256,128]{1,0:T(8,128)(2,1)S(1)}, u32[]{:S(2)}, u32[]{:S(2)}) collective-permute-start(bf16[256,128]{1,0:T(8,128)(2,1)S(1)} %get-tuple-element.128), channel_id=1, source_target_pairs={{0,3},{1,2},{2,1},{3,0},{4,7},{5,6},{6,5},{7,4},{8,11},{9,10},{10,... | collective-permute-start | bytes 196616 | tf_op jit(solution)/shard_map/ppermute | solution.py:920
  60.4 23.7 %copy-start.7 = (f32[8]{0:T(128)S(1)}, f32[8]{0:T(128)}, u32[]{:S(2)}) copy-start(f32[8]{0:T(128)} %bias.2) | copy-start | bytes 100
  60.4 23.7 %copy-start.8 = (f32[8]{0:T(128)S(1)}, f32[8]{0:T(128)}, u32[]{:S(2)}) copy-start(f32[8]{0:T(128)} %decay.2) | copy-start | bytes 100
  60.4 25.1 %copy-start = (bf16[1024,512]{1,0:T(8,128)(2,1)S(1)}, bf16[1024,512]{1,0:T(8,128)(2,1)}, u32[]{:S(2)}) copy-start(bf16[1024,512]{1,0:T(8,128)(2,1)} %refs_1_.5) | copy-start | bytes 3145732
  60.5 25.1 %copy-start.1 = (bf16[1024,512]{1,0:T(8,128)(2,1)S(1)}, bf16[1024,512]{1,0:T(8,128)(2,1)}, u32[]{:S(2)}) copy-start(bf16[1024,512]{1,0:T(8,128)(2,1)} %refs_2_.5) | copy-start | bytes 3145732
  60.5 25.1 %copy-start.2 = (bf16[1024,512]{1,0:T(8,128)(2,1)S(1)}, bf16[1024,512]{1,0:T(8,128)(2,1)}, u32[]{:S(2)}) copy-start(bf16[1024,512]{1,0:T(8,128)(2,1)} %refs_3_.5) | copy-start | bytes 3145732
  64.0 13.6 %collective-permute-start.17 = (bf16[256,1024]{1,0:T(8,128)(2,1)S(1)}, bf16[256,1024]{1,0:T(8,128)(2,1)S(1)}, u32[]{:S(2)}, u32[]{:S(2)}) collective-permute-start(bf16[256,1024]{1,0:T(8,128)(2,1)S(1)} %get-tuple-element.129.refs_7_), channel_id=1, source_target_pairs={{0,2},{1,3},{2,0},{3,1},{4,6},{5,7},{6,4},{7,5},{8,10},{9,11},{10,... | collective-permute-start | bytes 1572872 | tf_op jit(solution)/shard_map/ppermute | solution.py:920
  64.6 20.9 %collective-permute-start.14 = (bf16[256,1024]{1,0:T(8,128)(2,1)S(1)}, bf16[256,1024]{1,0:T(8,128)(2,1)S(1)}, u32[]{:S(2)}, u32[]{:S(2)}) collective-permute-start(bf16[256,1024]{1,0:T(8,128)(2,1)S(1)} %get-tuple-element.129.refs_7_), channel_id=1, source_target_pairs={{0,1},{1,0},{2,3},{3,2},{4,5},{5,4},{6,7},{7,6},{8,9},{9,8},{10,11... | collective-permute-start | bytes 1572872 | tf_op jit(solution)/shard_map/ppermute | solution.py:920
  77.5 19.1 %collective-permute-start.19 = (bf16[256,1024]{1,0:T(8,128)(2,1)S(1)}, bf16[256,1024]{1,0:T(8,128)(2,1)S(1)}, u32[]{:S(2)}, u32[]{:S(2)}) collective-permute-start(bf16[256,1024]{1,0:T(8,128)(2,1)S(1)} %collective-permute-done.17.refs_7_), channel_id=1, source_target_pairs={{0,1},{1,0},{2,3},{3,2},{4,5},{5,4},{6,7},{7,6},{8,9},{9,8},{10,11... | collective-permute-start | bytes 1572872 | tf_op jit(solution)/shard_map/ppermute | solution.py:920
  78.6 4.9 %collective-permute-start.16 = (bf16[16,1024]{1,0:T(8,128)(2,1)S(1)}, bf16[16,1024]{1,0:T(8,128)(2,1)S(1)}, u32[]{:S(2)}, u32[]{:S(2)}) collective-permute-start(bf16[16,1024]{1,0:T(8,128)(2,1)S(1)} %get-tuple-element.130), channel_id=1, source_target_pairs={{1,3},{3,5},{5,7},{7,9},{9,11},{11,13},{13,15},{15,17},{17,19},{19... | collective-permute-start | bytes 98312 | tf_op jit(solution)/shard_map/ppermute | solution.py:920
  80.9 4.7 %collective-permute-start.15 = (bf16[16,1024]{1,0:T(8,128)(2,1)S(1)}, bf16[16,1024]{1,0:T(8,128)(2,1)S(1)}, u32[]{:S(2)}, u32[]{:S(2)}) collective-permute-start(bf16[16,1024]{1,0:T(8,128)(2,1)S(1)} %get-tuple-element.130), channel_id=1, source_target_pairs={{1,2},{3,4},{5,6},{7,8},{9,10},{11,12},{13,14},{15,16},{17,18},{19... | collective-permute-start | bytes 98312 | tf_op jit(solution)/shard_map/ppermute | solution.py:920
  82.2 10.7 %collective-permute-start.18 = (bf16[16,1024]{1,0:T(8,128)(2,1)S(1)}, bf16[16,1024]{1,0:T(8,128)(2,1)S(1)}, u32[]{:S(2)}, u32[]{:S(2)}) collective-permute-start(bf16[16,1024]{1,0:T(8,128)(2,1)S(1)} %get-tuple-element.130), channel_id=1, source_target_pairs={{2,1},{6,5},{10,9},{14,13},{18,17},{22,21},{26,25},{30,29},{34,33}... | collective-permute-start | bytes 98312 | tf_op jit(solution)/shard_map/ppermute | solution.py:920
  83.5 13.2 %collective-permute-start.20 = (bf16[16,1024]{1,0:T(8,128)(2,1)S(1)}, bf16[16,1024]{1,0:T(8,128)(2,1)S(1)}, u32[]{:S(2)}, u32[]{:S(2)}) collective-permute-start(bf16[16,1024]{1,0:T(8,128)(2,1)S(1)} %get-tuple-element.130), channel_id=1, source_target_pairs={{3,7},{7,11},{11,15},{15,19},{19,23},{23,27},{27,31},{31,35},{35,3... | collective-permute-start | bytes 98312 | tf_op jit(solution)/shard_map/ppermute | solution.py:920
  100.7 30.9 %copy-start.3 = (bf16[512,1024]{1,0:T(8,128)(2,1)S(1)}, bf16[512,1024]{1,0:T(8,128)(2,1)}, u32[]{:S(2)}) copy-start(bf16[512,1024]{1,0:T(8,128)(2,1)} %wo.1) | copy-start | bytes 3145732
  133.0 8.5 %collective-permute-start.23 = (bf16[528,256]{1,0:T(8,128)(2,1)S(1)}, bf16[528,256]{1,0:T(8,128)(2,1)S(1)}, u32[]{:S(2)}, u32[]{:S(2)}) collective-permute-start(bf16[528,256]{1,0:T(8,128)(2,1)S(1)} %get-tuple-element.165), channel_id=1, source_target_pairs={{0,1},{1,0},{2,3},{3,2},{4,5},{5,4},{6,7},{7,6},{8,9},{9,8},{10,11... | collective-permute-start | bytes 811016 | tf_op jit(solution)/shard_map/ppermute | solution.py:920
  140.1 1.6 %collective-permute-start.22 = (bf16[528,256]{1,0:T(8,128)(2,1)S(1)}, bf16[528,256]{1,0:T(8,128)(2,1)S(1)}, u32[]{:S(2)}, u32[]{:S(2)}) collective-permute-start(bf16[528,256]{1,0:T(8,128)(2,1)S(1)} %get-tuple-element.161), channel_id=1, source_target_pairs={{0,1},{1,0},{2,3},{3,2},{4,5},{5,4},{6,7},{7,6},{8,9},{9,8},{10,11... | collective-permute-start | bytes 811016 | tf_op jit(solution)/shard_map/ppermute | solution.py:920
  140.9 2.4 %collective-permute-start.21 = (bf16[1024,256]{1,0:T(8,128)(2,1)S(1)}, bf16[1024,256]{1,0:T(8,128)(2,1)S(1)}, u32[]{:S(2)}, u32[]{:S(2)}) collective-permute-start(bf16[1024,256]{1,0:T(8,128)(2,1)S(1)} %get-tuple-element.158), channel_id=1, source_target_pairs={{0,1},{1,0},{2,3},{3,2},{4,5},{5,4},{6,7},{7,6},{8,9},{9,8},{10,11... | collective-permute-start | bytes 1572872 | tf_op jit(solution)/shard_map/ppermute | solution.py:920
  141.5 8.1 %collective-permute-start.24 = (bf16[528,256]{1,0:T(8,128)(2,1)S(1)}, bf16[528,256]{1,0:T(8,128)(2,1)S(1)}, u32[]{:S(2)}, u32[]{:S(2)}) collective-permute-start(bf16[528,256]{1,0:T(8,128)(2,1)S(1)} %get-tuple-element.166), channel_id=1, source_target_pairs={{0,2},{1,3},{2,0},{3,1},{4,6},{5,7},{6,4},{7,5},{8,10},{9,11},{10,... | collective-permute-start | bytes 811016 | tf_op jit(solution)/shard_map/ppermute | solution.py:920
  141.8 13.7 %collective-permute-start.25 = (bf16[528,256]{1,0:T(8,128)(2,1)S(1)}, bf16[528,256]{1,0:T(8,128)(2,1)S(1)}, u32[]{:S(2)}, u32[]{:S(2)}) collective-permute-start(bf16[528,256]{1,0:T(8,128)(2,1)S(1)} %get-tuple-element.168), channel_id=1, source_target_pairs={{0,2},{1,3},{2,0},{3,1},{4,6},{5,7},{6,4},{7,5},{8,10},{9,11},{10,... | collective-permute-start | bytes 811016 | tf_op jit(solution)/shard_map/ppermute | solution.py:920

commit v4 on v3

--- a/solution.py
+++ b/solution.py
@@ -87,7 +87,7 @@
 def convolve(cv, act, half_taps, length):
     apart = spaced(length)
 
-    def slab(c, carry):
+    def slab(c):
         taps = half_taps[c]
         rows = [cv[c, pl.ds(13 + i, 8, stride=apart), :] for i in range(3)]
         for i in range(apart):
@@ -96,9 +96,9 @@
             for k in range(1, 4):
                 h = h + rows[i + k] * taps[k : k + 1]
             act[c, pl.ds(i, 8, stride=apart), :] = h + h * jnp.tanh(h)
-        return carry
-
-    lax.fori_loop(0, cv.shape[0], slab, 0)
+
+    for c in range(cv.shape[0]):
+        slab(c)
 
 
 def project(rows, weights, cv, start, slab):
@@ -134,13 +134,16 @@
 
 
 def pack_kernel(
-    bias, decay, gate, value, output, steps, kv, norm, tokens, pack, ends, kv_v, norm_v, steps_v, sems
+    bias, decay, gate, value, output, steps, kv, norm, tokens,
+    pack, ends, kv_v, norm_v, steps_v, bias_v, decay_v, sems,
 ):
     copies = run_copies(
         (
             (kv, kv_v),
             (norm, norm_v),
             (steps, steps_v),
+            (bias, bias_v),
+            (decay, decay_v),
             (tokens.at[4080:4096], ends),
             (gate, pack.at[0:256, 0:128]),
             (value, pack.at[0:256, 128:256]),
@@ -148,41 +151,47 @@
         ),
         sems,
     )
-    for copy in copies[:3]:
+    for copy in copies[:5]:
         copy.wait()
     left = jnp.concatenate(three(kv_v[...]) + [jnp.zeros((4, 128), F32)], 0)
     rows = three(norm_v[...])
-    for ref in (bias, decay):
+    for ref in (bias_v, decay_v):
         for j in range(2):
-            rows = rows + three(jnp.full((1, 128), ref[j], F32))
+            rows = rows + three(jnp.broadcast_to(ref[:, j : j + 1], (1, 128)))
     right = jnp.concatenate(rows + [jnp.zeros((1, 128), F32)], 0)
     below = jnp.concatenate([steps_v[...].astype(F32), jnp.zeros((14, 256), F32)], 0)
     pack[384:416, :] = jnp.concatenate([jnp.concatenate([left, right], 1), below], 0).astype(BF)
-    for copy in copies[3:]:
+    for copy in copies[5:]:
         copy.wait()
 
 
 def packed(bias, decay, gate, value, output, steps, kv, norm, tokens):
     return pl.pallas_call(
         pack_kernel,
-        in_specs=[SMEM] * 2 + [HBM] * 7,
+        in_specs=[HBM] * 9,
         out_specs=[VM] * 2,
         out_shape=[sds((416, 256), BF), sds((16, 256), BF)],
         scratch_shapes=[
             pltpu.VMEM((4, 128), F32),
             pltpu.VMEM((1, 128), F32),
             pltpu.VMEM((2, 256), BF),
-            pltpu.SemaphoreType.DMA((7,)),
+            pltpu.VMEM((1, 2), F32),
+            pltpu.VMEM((1, 2), F32),
+            pltpu.SemaphoreType.DMA((9,)),
         ],
         compiler_params=few(4),
         name="pack",
-    )(bias, decay, *in_hbm(gate, value, output, steps, kv, norm, tokens))
+    )(*in_hbm(bias, decay, gate, value, output, steps, kv, norm, tokens))
 
 
 def params_kernel(bias, decay, kv, ks, gain, steps, norm, taps, both, *refs):
-    outs, kv_v, ks_v, sems = refs[:3], *refs[3:]
+    outs, kv_v, ks_v, bias_v, decay_v, sems = refs[:3], *refs[3:]
     copies = run_copies(
-        ((kv, kv_v), (ks, ks_v), (gain, outs[0]), (steps, outs[1]), (norm, outs[2])), sems
+        (
+            (kv, kv_v), (ks, ks_v), (bias, bias_v), (decay, decay_v),
+            (gain, outs[0]), (steps, outs[1]), (norm, outs[2]),
+        ),
+        sems,
     )
     for copy in copies:
         copy.wait()
@@ -190,14 +199,16 @@
         cols = slice(j * 128, (j + 1) * 128)
         taps[j] = kv_v[:, cols] * 0.5
         taps[4 + j] = ks_v[:, cols] * 0.5
-    rows = [jnp.full((1, 128), ref[j], F32) for ref in (bias, decay) for j in range(8)]
+    rows = [
+        jnp.broadcast_to(ref[:, j : j + 1], (1, 128)) for ref in (bias_v, decay_v) for j in range(8)
+    ]
     both[...] = jnp.concatenate(rows, 0)
 
 
 def coarse_params(bias, decay, kv, ks, gain, steps, norm):
     return pl.pallas_call(
         params_kernel,
-        in_specs=[SMEM] * 2 + [HBM] * 5,
+        in_specs=[HBM] * 7,
         out_specs=[VM] * 5,
         out_shape=[
             sds((8, 4, 128)), sds((16, 128)), sds((1, 1024)), sds((8, 1024), BF), sds((1, 512)),
@@ -205,11 +216,13 @@
         scratch_shapes=[
             pltpu.VMEM((4, 512), F32),
             pltpu.VMEM((4, 512), F32),
-            pltpu.SemaphoreType.DMA((5,)),
+            pltpu.VMEM((1, 8), F32),
+            pltpu.VMEM((1, 8), F32),
+            pltpu.SemaphoreType.DMA((7,)),
         ],
         compiler_params=few(4),
         name="coarse_params",
-    )(bias, decay, *in_hbm(kv, ks, gain, steps, norm))
+    )(*in_hbm(bias, decay, kv, ks, gain, steps, norm))
 
 
 def state_chunk(x, rim, gain, pack, scans, ks, taps, cv, act):
@@ -318,7 +331,6 @@
     return pltpu.CompilerParams(vmem_limit_bytes=mib << 20)
 
 
-SMEM = pl.BlockSpec(memory_space=pltpu.SMEM)
 VM = pl.BlockSpec(memory_space=pltpu.VMEM)
 HBM = pl.BlockSpec(memory_space=pltpu.HBM)
 
@@ -691,7 +703,7 @@
     def _():
         if kind == "near":
             copies = run_copies(((qs[0], xs.at[c]), (qs[1], xs.at[1 - c])), sems)
-            rim = ra[...].astype(F32) + rb[...].astype(F32)
+            rim = jnp.where(c == 0, ra[...].astype(F32), rb[...].astype(F32))
         else:
             copies = run_copies(((qs[0], xs.at[0]),), sems)
             rim = near_ends[...].astype(F32)
@@ -938,7 +950,7 @@
     coarse_decay, coarse_norm, coarse_output,
 ):
     pack, ends = packed(
-        fine_bias, fine_decay, fine_gate, fine_value, fine_output, fine_steps.T, fine_kernel,
+        fine_bias[None], fine_decay[None], fine_gate, fine_value, fine_output, fine_steps.T, fine_kernel,
         fine_norm[None], tokens,
     )
     rim = passed(ends, SEQ, [(i, i + 1) for i in range(31)])
@@ -952,7 +964,7 @@
     *prior, own, own_total, message = middle_stage("x", 4, own, own_total, (), got)
     got = [passed(message, "u", [(0, 1), (1, 0)])]
     params = coarse_params(
-        coarse_bias, coarse_decay, coarse_kernel, coarse_taps, coarse_gain[None],
+        coarse_bias[None], coarse_decay[None], coarse_kernel, coarse_taps, coarse_gain[None],
         coarse_steps.T, coarse_norm[None],
     )
     *prior, own, own_total, message = middle_stage("u", 2, own, own_total, prior, got)
@@ -969,7 +981,7 @@
         return passed(end_rows, ALL, pairs)
 
     rim_a = rims([(q, q + 1) for q in range(1, 127, 2)])
-    rim_b = rims([(q, q + 2) for q in range(1, 126, 2)])
+    rim_b = swapped(rim_a, 1)
     rim_d = rims([(q, q + 4) for q in range(3, 124, 4)])
     rim_e = rims(
         [(q, q - 1) for q in range(2, 128, 4)]

time: 157 us -> 152 us (0.968)
  Pallas kernels: 48 us -> 43.3 us
  blocking collectives: 30.7 us -> 33.6 us
  starting transfers between devices: 43.7 us -> 41.1 us
    ppermute x26, starting transfers between devices: 43.7 us -> 41.1 us  [passed(): return lax.ppermute(x, axes, pairs)]
    all_to_all x1, blocking collectives: 17.6 us -> 19.7 us  [shards(): got = lax.all_to_all(message, SEQ, split_axis=0, concat_axis=0, tiled=True)]
    pallas_call x3, Pallas kernels: 15.1 us -> 13.3 us  [coarse_main(): pl.pallas_call(lambda *refs: coarse_main_kernel(kind, blocks, *refs), gri...]
  transfers between devices with their start and end apart: 26 -> 26, of which waited for: 8 -> 9; matrix products, arithmetic and copies ran while one was open for 0% -> 0% of each run, Pallas kernels for 22% -> 20%
where the time goes in v4:
time: 152 us
  Pallas kernels  43.3 us (28%)
  starting transfers between devices  41.1 us (27%)
  waiting for transfers between devices  33.6 us (22%)
  blocking collectives  33.6 us (22%)
    ppermute x26, starting transfers between devices, passed(): return lax.ppermute(x, axes, pairs)  41.1 us
    ppermute x26, waiting for transfers between devices, passed(): return lax.ppermute(x, axes, pairs)  33.6 us
    all_to_all x1, blocking collectives, shards(): got = lax.all_to_all(message, SEQ, split_axis=0, concat_axis=0, tiled=True)  19.7 us
    all_to_all x1, blocking collectives, shards(): lax.all_to_all(prefix(got), SEQ, split_axis=0, concat_axis=0, tiled=True)  13.9 us
    pallas_call x3, Pallas kernels, coarse_main(): pl.pallas_call(lambda *refs: coarse_main_kernel(kind, blocks, *refs), gri...  13.3 us
    pallas_call x2, Pallas kernels, fine_main(): pl.pallas_call(lambda *refs: fine_main_kernel(later, *refs), grid=(2,), i...  9.6 us
    pallas_call x1, Pallas kernels, fine_states(): pl.pallas_call(later_chunks_kernel, grid=(3,), in_specs=[HBM, HBM, VM, HB...  7.69 us
    pallas_call x1, Pallas kernels, fine_close(): pl.pallas_call(fine_close_kernel, grid=(4,), in_specs=halves(512) + halve...  3.46 us
  transfers between devices with their start and end apart: 26, of which 9 were waited for; matrix products, arithmetic and copies ran while one was open for 0% of the time, Pallas kernels for 20%

profile of v4, /device:TPU:1, one launch (start us, length us, event | category | flops | bytes accessed | tf_op | source)
XLA Modules:
  0.0 151.9 jit_solution(11913527902973774019)
XLA Ops:
  0.0 1.1 pack.1
  1.1 3.9 %collective-permute-start.3 = (bf16[16,256]{1,0:T(8,128)(2,1)S(1)}, bf16[16,256]{1,0:T(8,128)(2,1)S(1)}, u32[]{:S(2)}, u32[]{:S(2)}) collective-permute-start(bf16[16,256]{1,0:T(8,128)(2,1)S(1)} %get-tuple-element.96), channel_id=1, source_target_pairs={{0,4},{4,8},{8,12},{12,16},{16,20},{20,24},{24,28},{28,32},{32,36}... | collective-permute-start | bytes 24584 | tf_op jit(solution)/shard_map/ppermute | solution.py:932
  5.0 7.7 %later_chunks.1 = (f32[3,256,128]{2,1,0:T(8,128)S(1)}, f32[3,8,128]{2,1,0:T(8,128)S(1)}, bf16[1024,256]{1,0:T(8,128)(2,1)S(1)}, bf16[1024,256]{1,0:T(8,128)(2,1)...) custom-call(bf16[4096,256]{1,0:T(8,128)(2,1)} %tokens.3, ...), custom_call_target="tpu_custom_call" | custom-call | tf_op jit(solution)/shard_map/later_chunks/pallas_call | solution.py:344
  12.7 2.0 %first_chunk.1 = (f32[256,128]{1,0:T(8,128)S(1)}, f32[8,128]{1,0:T(8,128)S(1)}, f32[256,128]{1,0:T(8,128)S(1)}, f32[8,128]{1,0:T(8,128)S(1)}, bf16[272,128]{1,0:T(8,128)(2,1)S(1)}) custom-call(bf16[1024,256]{1,0:T(8,128)(2,1)S(1)} %get-tuple-element.98.x, bf16[16,256]{1,0:T(8,128)(2,1)S(1)} %collective-permute-done.3.rim.refs_8_, ...), custom_call_target="tpu_custom_call" | custom-call | tf_op jit(solution)/shard_map/first_chunk/pallas_call | solution.py:366
  14.8 4.2 %collective-permute-start.6 = (bf16[272,128]{1,0:T(8,128)(2,1)S(1)}, bf16[272,128]{1,0:T(8,128)(2,1)S(1)}, u32[]{:S(2)}, u32[]{:S(2)}) collective-permute-start(bf16[272,128]{1,0:T(8,128)(2,1)S(1)} %get-tuple-element.113), channel_id=1, source_target_pairs={{0,12},{4,0},{8,4},{12,8},{1,13},{5,1},{9,5},{13,9},{2,14},{6,2},{... | collective-permute-start | bytes 208904 | tf_op jit(solution)/shard_map/ppermute | solution.py:932
  19.0 0.7 collective-permute-start.4
  19.6 1.8 %collective-permute-start.2 = (bf16[416,256]{1,0:T(8,128)(2,1)S(1)}, bf16[416,256]{1,0:T(8,128)(2,1)S(1)}, u32[]{:S(2)}, u32[]{:S(2)}) collective-permute-start(bf16[416,256]{1,0:T(8,128)(2,1)S(1)} %get-tuple-element.91.pack.refs_4_.p0), channel_id=1, source_target_pairs={{0,3},{1,2},{2,1},{3,0},{4,7},{5,6},{6,5},{7,4},{8,11},{9,10},{10,... | collective-permute-start | bytes 638984 | tf_op jit(solution)/shard_map/ppermute | solution.py:932
  21.4 2.3 %collective-permute-done.5.refs_3_ = bf16[272,128]{1,0:T(8,128)(2,1)S(1)} collective-permute-done((bf16[272,128]{1,0:T(8,128)(2,1)S(1)}, bf16[272,128]{1,0:T(8,128)(2,1)S(1)}, u32[]{:S(2)}, u32[]{:S(2)}) %collective-permute-start.5) | collective-permute-done | bytes 69664 | tf_op jit(solution)/shard_map/ppermute | solution.py:932
  23.7 0.4 collective-permute-done.4.refs_2_
  24.1 0.1 shard_map.226
  24.2 1.8 %collective-permute-start.7 = (bf16[272,128]{1,0:T(8,128)(2,1)S(1)}, bf16[272,128]{1,0:T(8,128)(2,1)S(1)}, u32[]{:S(2)}, u32[]{:S(2)}) collective-permute-start(bf16[272,128]{1,0:T(8,128)(2,1)S(1)} %get-tuple-element.118), channel_id=1, source_target_pairs={{0,16},{16,0},{1,17},{17,1},{2,18},{18,2},{3,19},{19,3},{4,20},{20... | collective-permute-start | bytes 208904 | tf_op jit(solution)/shard_map/ppermute | solution.py:932
  26.0 1.0 collective-permute-start.1
  27.0 2.9 %collective-permute-start = (bf16[416,256]{1,0:T(8,128)(2,1)S(1)}, bf16[416,256]{1,0:T(8,128)(2,1)S(1)}, u32[]{:S(2)}, u32[]{:S(2)}) collective-permute-start(bf16[416,256]{1,0:T(8,128)(2,1)S(1)} %get-tuple-element.91.pack.refs_4_.p0), channel_id=1, source_target_pairs={{0,1},{1,0},{2,3},{3,2},{4,5},{5,4},{6,7},{7,6},{8,9},{9,8},{10,11... | collective-permute-start | bytes 638984 | tf_op jit(solution)/shard_map/ppermute | solution.py:932
  30.0 0.0 collective-permute-done.7.refs_4_
  30.0 0.1 shard_map.227
  30.1 3.2 %collective-permute-start.10 = (bf16[272,128]{1,0:T(8,128)(2,1)S(1)}, bf16[272,128]{1,0:T(8,128)(2,1)S(1)}, u32[]{:S(2)}, u32[]{:S(2)}) collective-permute-start(bf16[272,128]{1,0:T(8,128)(2,1)S(1)} %get-tuple-element.123), channel_id=1, source_target_pairs={{0,96},{32,0},{64,32},{96,64},{1,97},{33,1},{65,33},{97,65},{2,98}... | collective-permute-start | bytes 208904 | tf_op jit(solution)/shard_map/ppermute | solution.py:932
  33.2 0.4 collective-permute-start.9
  33.6 1.0 collective-permute-done.10.r3
  34.6 0.6 collective-permute-start.8
  35.2 2.7 %collective-permute-done.9.r2 = bf16[272,128]{1,0:T(8,128)(2,1)S(1)} collective-permute-done((bf16[272,128]{1,0:T(8,128)(2,1)S(1)}, bf16[272,128]{1,0:T(8,128)(2,1)S(1)}, u32[]{:S(2)}, u32[]{:S(2)}) %collective-permute-start.9) | collective-permute-done | bytes 69664 | tf_op jit(solution)/shard_map/ppermute | solution.py:932
  37.9 1.4 collective-permute-done.8.r1
  39.3 0.1 chain_last.1
  39.4 0.0 copy-start.4
  39.5 5.8 %collective-permute-start.11 = (bf16[256,128]{1,0:T(8,128)(2,1)S(1)}, bf16[256,128]{1,0:T(8,128)(2,1)S(1)}, u32[]{:S(2)}, u32[]{:S(2)}) collective-permute-start(bf16[256,128]{1,0:T(8,128)(2,1)S(1)} %get-tuple-element.126), channel_id=1, source_target_pairs={{0,1},{1,0},{2,3},{3,2},{4,5},{5,4},{6,7},{7,6},{8,9},{9,8},{10,11... | collective-permute-start | bytes 196616 | tf_op jit(solution)/shard_map/ppermute | solution.py:932
  45.3 0.4 collective-permute-start.12
  45.7 0.0 collective-permute-done.2.refs_7_.p3
  45.7 1.3 collective-permute-start.13
  47.0 4.4 %fine_main_a.1 = (f32[512,512]{1,0:T(8,128)S(1)}, f32[512,512]{1,0:T(8,128)S(1)}, bf16[512,256]{1,0:T(8,128)(2,1)S(1)}, f32[256,512]{1,0:T(8,128)S(1)}, f32[8,128]{1,0:T(8,128)S(1)}, /*index=5*/f32[8,16,128]{2,1,0:T(8,128)S(1)}) custom-call(bf16[1024,256]{1,0:T(8,128)(2,1)S(1)} %get-tuple-element.92.refs_0_.x, f32[1,256]{1,0:T(1,128)S(1)} %get-tuple-element.93.gain.refs_1_, ...), custom_call_target="tpu_custom_call" | custom-call | tf_op jit(solution)/shard_map/fine_main_a/pallas_call | solution.py:578
  51.5 5.2 %fine_main_b.1 = (f32[512,512]{1,0:T(8,128)S(1)}, f32[512,512]{1,0:T(8,128)S(1)}, bf16[512,256]{1,0:T(8,128)(2,1)S(1)}, f32[256,512]{1,0:T(8,128)}, f32[8,128]{1,0:T(8,128)}, /*index=5*/f32[8,16,128]{2,1,0:T(8,128)}) custom-call(bf16[1024,256]{1,0:T(8,128)(2,1)S(1)} %get-tuple-element.92.refs_0_.x, f32[1,256]{1,0:T(1,128)S(1)} %get-tuple-element.93.gain.refs_1_, ...), custom_call_target="tpu_custom_call" | custom-call | tf_op jit(solution)/shard_map/fine_main_b/pallas_call | solution.py:578
  56.6 0.0 collective-permute-done.11.s1
  56.6 0.0 collective-permute-done.12.s2
  56.7 0.0 copy-start
  56.7 0.0 copy-start.1
  56.7 0.0 copy-start.2
  56.7 3.5 %fine_close.1 = (bf16[256,1024]{1,0:T(8,128)(2,1)S(1)}, bf16[16,1024]{1,0:T(8,128)(2,1)S(1)}) custom-call(f32[512,512]{1,0:T(8,128)S(1)} %get-tuple-element.102.lead_a, f32[512,512]{1,0:T(8,128)S(1)} %get-tuple-element.106.lead_b, f32[512,512]{1,0:T(8,128)S(1)} %get-tuple-element.107.tail_a, f32[512,512]{1,0:T(8,128)S(1)} %get-tuple-element.108.tail_b, ...), custom_call_target="tpu_custom_call" | custom-call | tf_op jit(solution)/shard_map/fine_close/pallas_call | solution.py:656
  60.2 0.5 collective-permute-start.17
  60.6 0.4 collective-permute-start.14
  61.1 12.5 %collective-permute-done.17.refs_7_ = bf16[256,1024]{1,0:T(8,128)(2,1)S(1)} collective-permute-done((bf16[256,1024]{1,0:T(8,128)(2,1)S(1)}, bf16[256,1024]{1,0:T(8,128)(2,1)S(1)}, u32[]{:S(2)}, u32[]{:S(2)}) %collective-permute-start.17) | collective-permute-done | bytes 524320 | tf_op jit(solution)/shard_map/ppermute | solution.py:932
  73.6 1.0 collective-permute-start.19
  74.6 2.2 %collective-permute-start.15 = (bf16[16,1024]{1,0:T(8,128)(2,1)S(1)}, bf16[16,1024]{1,0:T(8,128)(2,1)S(1)}, u32[]{:S(2)}, u32[]{:S(2)}) collective-permute-start(bf16[16,1024]{1,0:T(8,128)(2,1)S(1)} %get-tuple-element.130), channel_id=1, source_target_pairs={{1,2},{3,4},{5,6},{7,8},{9,10},{11,12},{13,14},{15,16},{17,18},{19... | collective-permute-start | bytes 98312 | tf_op jit(solution)/shard_map/ppermute | solution.py:932
  76.8 1.0 collective-permute-done.15.refs_9_
  77.8 1.3 collective-permute-start.18
  79.1 0.9 collective-permute-start.20
  80.0 1.0 coarse_params.1
  81.0 6.3 %shard_map.228 = (f32[512,512]{1,0:T(8,128)S(1)}, f32[512,512]{1,0:T(8,128)S(1)}, bf16[512,256]{1,0:T(8,128)(2,1)S(1)}, bf16[512,256]{1,0:T(8,128)(2,1)S(1)}, f3...) custom-call(f32[1,1024]{1,0:T(1,128)S(1)} %get-tuple-element.87.refs_0_, ...), custom_call_target="tpu_custom_call" | custom-call | tf_op jit(solution)/shard_map/pallas_call | solution.py:758
  87.3 3.4 %shard_map.229 = (f32[256,512]{1,0:T(8,128)S(1)}, f32[256,512]{1,0:T(8,128)S(1)}, bf16[256,256]{1,0:T(8,128)(2,1)S(1)}, bf16[256,256]{1,0:T(8,128)(2,1)S(1)}, f3...) custom-call(f32[1,1024]{1,0:T(1,128)S(1)} %get-tuple-element.87.refs_0_, ...), custom_call_target="tpu_custom_call" | custom-call | tf_op jit(solution)/shard_map/pallas_call | solution.py:758
  90.8 3.5 %shard_map.230 = (f32[256,512]{1,0:T(8,128)S(1)}, f32[256,512]{1,0:T(8,128)S(1)}, bf16[256,256]{1,0:T(8,128)(2,1)S(1)}, bf16[256,256]{1,0:T(8,128)(2,1)S(1)}, f3...) custom-call(f32[1,1024]{1,0:T(1,128)S(1)} %get-tuple-element.87.refs, ...), custom_call_target="tpu_custom_call" | custom-call | tf_op jit(solution)/shard_map/pallas_call | solution.py:758
  94.3 0.0 copy-start.3
  94.3 19.7 %all_to_all.10.got = bf16[32,24,256]{2,1,0:T(8,128)(2,1)S(1)} all-to-all(bf16[32,24,256]{2,1,0:T(8,128)(2,1)S(1)} %get-tuple-element.143), channel_id=1, replica_groups=mesh['z'=4,'u'=2,'x'=4,'y'=2,'c'=2] {'z','u','x'}, dimensions={0} | all-to-all | bytes 786432 | tf_op jit(solution)/shard_map/all_to_all | solution.py:1005
  114.0 0.1 prefix.1
  114.2 13.9 %all_to_all.11.refs_3_.refs_6_ = bf16[32,16,256]{2,1,0:T(8,128)(2,1)S(1)} all-to-all(bf16[32,16,256]{2,1,0:T(8,128)(2,1)S(1)} %prefix.1), channel_id=1, replica_groups=mesh['z'=4,'u'=2,'x'=4,'y'=2,'c'=2] {'z','u','x'}, dimensions={0} | all-to-all | bytes 524288 | tf_op jit(solution)/shard_map/all_to_all | solution.py:1006
  128.0 1.3 coarse_close_far.1
  129.4 3.5 %collective-permute-start.23 = (bf16[528,256]{1,0:T(8,128)(2,1)S(1)}, bf16[528,256]{1,0:T(8,128)(2,1)S(1)}, u32[]{:S(2)}, u32[]{:S(2)}) collective-permute-start(bf16[528,256]{1,0:T(8,128)(2,1)S(1)} %get-tuple-element.165), channel_id=1, source_target_pairs={{0,1},{1,0},{2,3},{3,2},{4,5},{5,4},{6,7},{7,6},{8,9},{9,8},{10,11... | collective-permute-start | bytes 811016 | tf_op jit(solution)/shard_map/ppermute | solution.py:932
  132.9 1.2 coarse_close_near.1
  134.1 0.1 collective-permute-start.22
  134.2 0.7 close_rest.1
  134.9 0.6 collective-permute-start.21
  135.5 0.1 shard_map.232
  135.6 2.5 %collective-permute-start.24 = (bf16[528,256]{1,0:T(8,128)(2,1)S(1)}, bf16[528,256]{1,0:T(8,128)(2,1)S(1)}, u32[]{:S(2)}, u32[]{:S(2)}) collective-permute-start(bf16[528,256]{1,0:T(8,128)(2,1)S(1)} %get-tuple-element.166), channel_id=1, source_target_pairs={{0,2},{1,3},{2,0},{3,1},{4,6},{5,7},{6,4},{7,5},{8,10},{9,11},{10,... | collective-permute-start | bytes 811016 | tf_op jit(solution)/shard_map/ppermute | solution.py:932
  138.1 0.1 shard_map.231
  138.2 0.1 collective-permute-start.25
  138.3 6.5 %collective-permute-done.24.far_a = bf16[528,256]{1,0:T(8,128)(2,1)S(1)} collective-permute-done((bf16[528,256]{1,0:T(8,128)(2,1)S(1)}, bf16[528,256]{1,0:T(8,128)(2,1)S(1)}, u32[]{:S(2)}, u32[]{:S(2)}) %collective-permute-start.24) | collective-permute-done | bytes 270368 | tf_op jit(solution)/shard_map/ppermute | solution.py:932
  144.8 5.8 %collective-permute-done.25.far_b = bf16[528,256]{1,0:T(8,128)(2,1)S(1)} collective-permute-done((bf16[528,256]{1,0:T(8,128)(2,1)S(1)}, bf16[528,256]{1,0:T(8,128)(2,1)S(1)}, u32[]{:S(2)}, u32[]{:S(2)}) %collective-permute-start.25) | collective-permute-done | bytes 270368 | tf_op jit(solution)/shard_map/ppermute | solution.py:932
  150.6 1.3 final.1
  (20 shorter events, 0.0 us)
Async XLA Ops:
  1.1 11.6 %collective-permute-start.3 = (bf16[16,256]{1,0:T(8,128)(2,1)S(1)}, bf16[16,256]{1,0:T(8,128)(2,1)S(1)}, u32[]{:S(2)}, u32[]{:S(2)}) collective-permute-start(bf16[16,256]{1,0:T(8,128)(2,1)S(1)} %get-tuple-element.96), channel_id=1, source_target_pairs={{0,4},{4,8},{8,12},{12,16},{16,20},{20,24},{24,28},{28,32},{32,36}... | collective-permute-start | bytes 24584 | tf_op jit(solution)/shard_map/ppermute | solution.py:932
  14.8 6.7 %collective-permute-start.6 = (bf16[272,128]{1,0:T(8,128)(2,1)S(1)}, bf16[272,128]{1,0:T(8,128)(2,1)S(1)}, u32[]{:S(2)}, u32[]{:S(2)}) collective-permute-start(bf16[272,128]{1,0:T(8,128)(2,1)S(1)} %get-tuple-element.113), channel_id=1, source_target_pairs={{0,12},{4,0},{8,4},{12,8},{1,13},{5,1},{9,5},{13,9},{2,14},{6,2},{... | collective-permute-start | bytes 208904 | tf_op jit(solution)/shard_map/ppermute | solution.py:932
  19.0 4.8 %collective-permute-start.5 = (bf16[272,128]{1,0:T(8,128)(2,1)S(1)}, bf16[272,128]{1,0:T(8,128)(2,1)S(1)}, u32[]{:S(2)}, u32[]{:S(2)}) collective-permute-start(bf16[272,128]{1,0:T(8,128)(2,1)S(1)} %get-tuple-element.113), channel_id=1, source_target_pairs={{0,8},{4,12},{8,0},{12,4},{1,9},{5,13},{9,1},{13,5},{2,10},{6,14},... | collective-permute-start | bytes 208904 | tf_op jit(solution)/shard_map/ppermute | solution.py:932
  19.0 5.1 %collective-permute-start.4 = (bf16[272,128]{1,0:T(8,128)(2,1)S(1)}, bf16[272,128]{1,0:T(8,128)(2,1)S(1)}, u32[]{:S(2)}, u32[]{:S(2)}) collective-permute-start(bf16[272,128]{1,0:T(8,128)(2,1)S(1)} %get-tuple-element.113), channel_id=1, source_target_pairs={{0,4},{4,8},{8,12},{12,0},{1,5},{5,9},{9,13},{13,1},{2,6},{6,10},{... | collective-permute-start | bytes 208904 | tf_op jit(solution)/shard_map/ppermute | solution.py:932
  19.6 26.0 %collective-permute-start.2 = (bf16[416,256]{1,0:T(8,128)(2,1)S(1)}, bf16[416,256]{1,0:T(8,128)(2,1)S(1)}, u32[]{:S(2)}, u32[]{:S(2)}) collective-permute-start(bf16[416,256]{1,0:T(8,128)(2,1)S(1)} %get-tuple-element.91.pack.refs_4_.p0), channel_id=1, source_target_pairs={{0,3},{1,2},{2,1},{3,0},{4,7},{5,6},{6,5},{7,4},{8,11},{9,10},{10,... | collective-permute-start | bytes 638984 | tf_op jit(solution)/shard_map/ppermute | solution.py:932
  24.2 5.7 %collective-permute-start.7 = (bf16[272,128]{1,0:T(8,128)(2,1)S(1)}, bf16[272,128]{1,0:T(8,128)(2,1)S(1)}, u32[]{:S(2)}, u32[]{:S(2)}) collective-permute-start(bf16[272,128]{1,0:T(8,128)(2,1)S(1)} %get-tuple-element.118), channel_id=1, source_target_pairs={{0,16},{16,0},{1,17},{17,1},{2,18},{18,2},{3,19},{19,3},{4,20},{20... | collective-permute-start | bytes 208904 | tf_op jit(solution)/shard_map/ppermute | solution.py:932
  26.0 21.0 %collective-permute-start.1 = (bf16[416,256]{1,0:T(8,128)(2,1)S(1)}, bf16[416,256]{1,0:T(8,128)(2,1)S(1)}, u32[]{:S(2)}, u32[]{:S(2)}) collective-permute-start(bf16[416,256]{1,0:T(8,128)(2,1)S(1)} %get-tuple-element.91.pack.refs_4_.p0), channel_id=1, source_target_pairs={{0,2},{1,3},{2,0},{3,1},{4,6},{5,7},{6,4},{7,5},{8,10},{9,11},{10,... | collective-permute-start | bytes 638984 | tf_op jit(solution)/shard_map/ppermute | solution.py:932
  27.0 20.0 %collective-permute-start = (bf16[416,256]{1,0:T(8,128)(2,1)S(1)}, bf16[416,256]{1,0:T(8,128)(2,1)S(1)}, u32[]{:S(2)}, u32[]{:S(2)}) collective-permute-start(bf16[416,256]{1,0:T(8,128)(2,1)S(1)} %get-tuple-element.91.pack.refs_4_.p0), channel_id=1, source_target_pairs={{0,1},{1,0},{2,3},{3,2},{4,5},{5,4},{6,7},{7,6},{8,9},{9,8},{10,11... | collective-permute-start | bytes 638984 | tf_op jit(solution)/shard_map/ppermute | solution.py:932
  30.1 4.6 %collective-permute-start.10 = (bf16[272,128]{1,0:T(8,128)(2,1)S(1)}, bf16[272,128]{1,0:T(8,128)(2,1)S(1)}, u32[]{:S(2)}, u32[]{:S(2)}) collective-permute-start(bf16[272,128]{1,0:T(8,128)(2,1)S(1)} %get-tuple-element.123), channel_id=1, source_target_pairs={{0,96},{32,0},{64,32},{96,64},{1,97},{33,1},{65,33},{97,65},{2,98}... | collective-permute-start | bytes 208904 | tf_op jit(solution)/shard_map/ppermute | solution.py:932
  33.2 4.7 %collective-permute-start.9 = (bf16[272,128]{1,0:T(8,128)(2,1)S(1)}, bf16[272,128]{1,0:T(8,128)(2,1)S(1)}, u32[]{:S(2)}, u32[]{:S(2)}) collective-permute-start(bf16[272,128]{1,0:T(8,128)(2,1)S(1)} %get-tuple-element.123), channel_id=1, source_target_pairs={{0,64},{32,96},{64,0},{96,32},{1,65},{33,97},{65,1},{97,33},{2,66}... | collective-permute-start | bytes 208904 | tf_op jit(solution)/shard_map/ppermute | solution.py:932
  34.6 4.7 %collective-permute-start.8 = (bf16[272,128]{1,0:T(8,128)(2,1)S(1)}, bf16[272,128]{1,0:T(8,128)(2,1)S(1)}, u32[]{:S(2)}, u32[]{:S(2)}) collective-permute-start(bf16[272,128]{1,0:T(8,128)(2,1)S(1)} %get-tuple-element.123), channel_id=1, source_target_pairs={{0,32},{32,64},{64,96},{96,0},{1,33},{33,65},{65,97},{97,1},{2,34}... | collective-permute-start | bytes 208904 | tf_op jit(solution)/shard_map/ppermute | solution.py:932
  39.4 17.2 %copy-start.4 = (bf16[1024,1024]{1,0:T(8,128)(2,1)S(1)}, bf16[1024,1024]{1,0:T(8,128)(2,1)}, u32[]{:S(2)}) copy-start(bf16[1024,1024]{1,0:T(8,128)(2,1)} %merge.1) | copy-start | bytes 6291460
  39.5 17.2 %collective-permute-start.11 = (bf16[256,128]{1,0:T(8,128)(2,1)S(1)}, bf16[256,128]{1,0:T(8,128)(2,1)S(1)}, u32[]{:S(2)}, u32[]{:S(2)}) collective-permute-start(bf16[256,128]{1,0:T(8,128)(2,1)S(1)} %get-tuple-element.126), channel_id=1, source_target_pairs={{0,1},{1,0},{2,3},{3,2},{4,5},{5,4},{6,7},{7,6},{8,9},{9,8},{10,11... | collective-permute-start | bytes 196616 | tf_op jit(solution)/shard_map/ppermute | solution.py:932
  45.3 11.4 %collective-permute-start.12 = (bf16[256,128]{1,0:T(8,128)(2,1)S(1)}, bf16[256,128]{1,0:T(8,128)(2,1)S(1)}, u32[]{:S(2)}, u32[]{:S(2)}) collective-permute-start(bf16[256,128]{1,0:T(8,128)(2,1)S(1)} %get-tuple-element.127), channel_id=1, source_target_pairs={{0,2},{1,3},{2,0},{3,1},{4,6},{5,7},{6,4},{7,5},{8,10},{9,11},{10,... | collective-permute-start | bytes 196616 | tf_op jit(solution)/shard_map/ppermute | solution.py:932
  45.7 11.0 %collective-permute-start.13 = (bf16[256,128]{1,0:T(8,128)(2,1)S(1)}, bf16[256,128]{1,0:T(8,128)(2,1)S(1)}, u32[]{:S(2)}, u32[]{:S(2)}) collective-permute-start(bf16[256,128]{1,0:T(8,128)(2,1)S(1)} %get-tuple-element.128), channel_id=1, source_target_pairs={{0,3},{1,2},{2,1},{3,0},{4,7},{5,6},{6,5},{7,4},{8,11},{9,10},{10,... | collective-permute-start | bytes 196616 | tf_op jit(solution)/shard_map/ppermute | solution.py:932
  56.7 24.3 %copy-start = (bf16[1024,512]{1,0:T(8,128)(2,1)S(1)}, bf16[1024,512]{1,0:T(8,128)(2,1)}, u32[]{:S(2)}) copy-start(bf16[1024,512]{1,0:T(8,128)(2,1)} %refs_1_.5) | copy-start | bytes 3145732
  56.7 24.3 %copy-start.1 = (bf16[1024,512]{1,0:T(8,128)(2,1)S(1)}, bf16[1024,512]{1,0:T(8,128)(2,1)}, u32[]{:S(2)}) copy-start(bf16[1024,512]{1,0:T(8,128)(2,1)} %refs_2_.5) | copy-start | bytes 3145732
  56.7 24.3 %copy-start.2 = (bf16[1024,512]{1,0:T(8,128)(2,1)S(1)}, bf16[1024,512]{1,0:T(8,128)(2,1)}, u32[]{:S(2)}) copy-start(bf16[1024,512]{1,0:T(8,128)(2,1)} %refs_3_.5) | copy-start | bytes 3145732
  60.2 13.4 %collective-permute-start.17 = (bf16[256,1024]{1,0:T(8,128)(2,1)S(1)}, bf16[256,1024]{1,0:T(8,128)(2,1)S(1)}, u32[]{:S(2)}, u32[]{:S(2)}) collective-permute-start(bf16[256,1024]{1,0:T(8,128)(2,1)S(1)} %get-tuple-element.129.refs_7_), channel_id=1, source_target_pairs={{0,2},{1,3},{2,0},{3,1},{4,6},{5,7},{6,4},{7,5},{8,10},{9,11},{10,... | collective-permute-start | bytes 1572872 | tf_op jit(solution)/shard_map/ppermute | solution.py:932
  60.6 20.3 %collective-permute-start.14 = (bf16[256,1024]{1,0:T(8,128)(2,1)S(1)}, bf16[256,1024]{1,0:T(8,128)(2,1)S(1)}, u32[]{:S(2)}, u32[]{:S(2)}) collective-permute-start(bf16[256,1024]{1,0:T(8,128)(2,1)S(1)} %get-tuple-element.129.refs_7_), channel_id=1, source_target_pairs={{0,1},{1,0},{2,3},{3,2},{4,5},{5,4},{6,7},{7,6},{8,9},{9,8},{10,11... | collective-permute-start | bytes 1572872 | tf_op jit(solution)/shard_map/ppermute | solution.py:932
  73.6 17.2 %collective-permute-start.19 = (bf16[256,1024]{1,0:T(8,128)(2,1)S(1)}, bf16[256,1024]{1,0:T(8,128)(2,1)S(1)}, u32[]{:S(2)}, u32[]{:S(2)}) collective-permute-start(bf16[256,1024]{1,0:T(8,128)(2,1)S(1)} %collective-permute-done.17.refs_7_), channel_id=1, source_target_pairs={{0,1},{1,0},{2,3},{3,2},{4,5},{5,4},{6,7},{7,6},{8,9},{9,8},{10,11... | collective-permute-start | bytes 1572872 | tf_op jit(solution)/shard_map/ppermute | solution.py:932
  74.6 3.2 %collective-permute-start.15 = (bf16[16,1024]{1,0:T(8,128)(2,1)S(1)}, bf16[16,1024]{1,0:T(8,128)(2,1)S(1)}, u32[]{:S(2)}, u32[]{:S(2)}) collective-permute-start(bf16[16,1024]{1,0:T(8,128)(2,1)S(1)} %get-tuple-element.130), channel_id=1, source_target_pairs={{1,2},{3,4},{5,6},{7,8},{9,10},{11,12},{13,14},{15,16},{17,18},{19... | collective-permute-start | bytes 98312 | tf_op jit(solution)/shard_map/ppermute | solution.py:932
  77.8 3.2 %collective-permute-start.16 = (bf16[16,1024]{1,0:T(8,128)(2,1)S(1)}, bf16[16,1024]{1,0:T(8,128)(2,1)S(1)}, u32[]{:S(2)}, u32[]{:S(2)}) collective-permute-start(bf16[16,1024]{1,0:T(8,128)(2,1)S(1)} %collective-permute-done.15.refs_9_), channel_id=1, source_target_pairs={{0,1},{1,0},{2,3},{3,2},{4,5},{5,4},{6,7},{7,6},{8,9},{9,8},{10,11... | collective-permute-start | bytes 98312 | tf_op jit(solution)/shard_map/ppermute | solution.py:932
  77.8 9.5 %collective-permute-start.18 = (bf16[16,1024]{1,0:T(8,128)(2,1)S(1)}, bf16[16,1024]{1,0:T(8,128)(2,1)S(1)}, u32[]{:S(2)}, u32[]{:S(2)}) collective-permute-start(bf16[16,1024]{1,0:T(8,128)(2,1)S(1)} %get-tuple-element.130), channel_id=1, source_target_pairs={{2,1},{6,5},{10,9},{14,13},{18,17},{22,21},{26,25},{30,29},{34,33}... | collective-permute-start | bytes 98312 | tf_op jit(solution)/shard_map/ppermute | solution.py:932
  79.1 11.7 %collective-permute-start.20 = (bf16[16,1024]{1,0:T(8,128)(2,1)S(1)}, bf16[16,1024]{1,0:T(8,128)(2,1)S(1)}, u32[]{:S(2)}, u32[]{:S(2)}) collective-permute-start(bf16[16,1024]{1,0:T(8,128)(2,1)S(1)} %get-tuple-element.130), channel_id=1, source_target_pairs={{3,7},{7,11},{11,15},{15,19},{19,23},{23,27},{27,31},{31,35},{35,3... | collective-permute-start | bytes 98312 | tf_op jit(solution)/shard_map/ppermute | solution.py:932
  94.3 33.7 %copy-start.3 = (bf16[512,1024]{1,0:T(8,128)(2,1)S(1)}, bf16[512,1024]{1,0:T(8,128)(2,1)}, u32[]{:S(2)}) copy-start(bf16[512,1024]{1,0:T(8,128)(2,1)} %wo.1) | copy-start | bytes 3145732
  129.4 6.1 %collective-permute-start.23 = (bf16[528,256]{1,0:T(8,128)(2,1)S(1)}, bf16[528,256]{1,0:T(8,128)(2,1)S(1)}, u32[]{:S(2)}, u32[]{:S(2)}) collective-permute-start(bf16[528,256]{1,0:T(8,128)(2,1)S(1)} %get-tuple-element.165), channel_id=1, source_target_pairs={{0,1},{1,0},{2,3},{3,2},{4,5},{5,4},{6,7},{7,6},{8,9},{9,8},{10,11... | collective-permute-start | bytes 811016 | tf_op jit(solution)/shard_map/ppermute | solution.py:932
  134.1 4.0 %collective-permute-start.22 = (bf16[528,256]{1,0:T(8,128)(2,1)S(1)}, bf16[528,256]{1,0:T(8,128)(2,1)S(1)}, u32[]{:S(2)}, u32[]{:S(2)}) collective-permute-start(bf16[528,256]{1,0:T(8,128)(2,1)S(1)} %get-tuple-element.161), channel_id=1, source_target_pairs={{0,1},{1,0},{2,3},{3,2},{4,5},{5,4},{6,7},{7,6},{8,9},{9,8},{10,11... | collective-permute-start | bytes 811016 | tf_op jit(solution)/shard_map/ppermute | solution.py:932
  134.9 3.4 %collective-permute-start.21 = (bf16[1024,256]{1,0:T(8,128)(2,1)S(1)}, bf16[1024,256]{1,0:T(8,128)(2,1)S(1)}, u32[]{:S(2)}, u32[]{:S(2)}) collective-permute-start(bf16[1024,256]{1,0:T(8,128)(2,1)S(1)} %get-tuple-element.158), channel_id=1, source_target_pairs={{0,1},{1,0},{2,3},{3,2},{4,5},{5,4},{6,7},{7,6},{8,9},{9,8},{10,11... | collective-permute-start | bytes 1572872 | tf_op jit(solution)/shard_map/ppermute | solution.py:932
  135.6 9.2 %collective-permute-start.24 = (bf16[528,256]{1,0:T(8,128)(2,1)S(1)}, bf16[528,256]{1,0:T(8,128)(2,1)S(1)}, u32[]{:S(2)}, u32[]{:S(2)}) collective-permute-start(bf16[528,256]{1,0:T(8,128)(2,1)S(1)} %get-tuple-element.166), channel_id=1, source_target_pairs={{0,2},{1,3},{2,0},{3,1},{4,6},{5,7},{6,4},{7,5},{8,10},{9,11},{10,... | collective-permute-start | bytes 811016 | tf_op jit(solution)/shard_map/ppermute | solution.py:932
  138.2 12.4 %collective-permute-start.25 = (bf16[528,256]{1,0:T(8,128)(2,1)S(1)}, bf16[528,256]{1,0:T(8,128)(2,1)S(1)}, u32[]{:S(2)}, u32[]{:S(2)}) collective-permute-start(bf16[528,256]{1,0:T(8,128)(2,1)S(1)} %get-tuple-element.168), channel_id=1, source_target_pairs={{0,2},{1,3},{2,0},{3,1},{4,6},{5,7},{6,4},{7,5},{8,10},{9,11},{10,... | collective-permute-start | bytes 811016 | tf_op jit(solution)/shard_map/ppermute | solution.py:932

commit v5 on v4

--- a/solution.py
+++ b/solution.py
@@ -689,12 +689,12 @@
     y, c = lax.axis_index("y"), lax.axis_index("c")
     h = 2 * y + c
     if kind == "near":
-        ra, rb, lead, tail_out, maps_out, share, run, run_log, ends = refs[:-7]
+        ra, rb, lead, tail_out, maps_out, share, run, run_log = refs[:-7]
     elif kind == "far_1":
-        near_ends, re, lead, tail_out, maps_out, share, run, run_log, ends = refs[:-7]
+        re, lead, tail_out, maps_out, share, run, run_log, ends = refs[:-7]
     else:
         (
-            near_ends, ends_1, rd, near_run, near_log, run_1, run_log_1,
+            ends_1, rd, near_run, near_log, run_1, run_log_1,
             lead, tail_out, maps_out, share, run, run_log, far_run, far_log, message,
         ) = refs[:-7]
     i = pl.program_id(0)
@@ -706,17 +706,14 @@
             rim = jnp.where(c == 0, ra[...].astype(F32), rb[...].astype(F32))
         else:
             copies = run_copies(((qs[0], xs.at[0]),), sems)
-            rim = near_ends[...].astype(F32)
-            if kind == "far_1":
-                rim = jnp.where(h == 0, rim, re[...].astype(F32))
-            else:
-                rim = jnp.where(h == 1, rim, rd[...].astype(F32))
+            rim = re[...].astype(F32) if kind == "far_1" else rd[...].astype(F32)
+            if kind == "far_2":
                 rim = jnp.where(c == 0, ends_1[...].astype(F32), rim)
         begin(rms(rim, gain[...]), wv, ws, cv, run, run_log)
         for copy in copies:
             copy.wait()
-        if kind != "far_2":
-            ends[...] = xs[pieces - 1, 240:256, :]
+        if kind == "far_1":
+            ends[...] = xs[0, 240:256, :]
 
     share[...] = xs[i, :, pl.ds(pl.multiple_of(h * 256, 256), 256)]
     scan_block(
@@ -752,8 +749,10 @@
     blocks = len(pieces)
     length = blocks * BLK
     rows = [pl.BlockSpec((BLK, n), lambda i: (i, 0)) for n in (512, 512, 256, 256)]
-    last = [sds((16, 1024), BF)]
-    if kind == "far_2":
+    last = []
+    if kind == "far_1":
+        last = [sds((16, 1024), BF)]
+    elif kind == "far_2":
         last = [sds((256, 512)), sds((8, 128)), sds((32, 24, 256), BF)]
     return pl.pallas_call(
         lambda *refs: coarse_main_kernel(kind, blocks, *refs),
@@ -773,6 +772,23 @@
         + SCAN_SCRATCH,
         compiler_params=few(16),
     )(gain, *weights, wst, taps, both, *pieces, *extra)
+
+
+def own_rim_kernel(came, beside, out):
+    out[...] = jnp.where(
+        lax.axis_index("c") == 0, came[...].astype(F32), beside[240:256, :].astype(F32)
+    ).astype(BF)
+
+
+def own_rim(came, beside):
+    return pl.pallas_call(
+        own_rim_kernel,
+        in_specs=[VM] * 2,
+        out_specs=VM,
+        out_shape=sds((16, 1024), BF),
+        compiler_params=few(4),
+        name="own_rim",
+    )(came, beside)
 
 
 def prefix_kernel(got, out):
@@ -977,30 +993,23 @@
         merge_weight,
     )
 
-    def rims(pairs):
-        return passed(end_rows, ALL, pairs)
-
-    rim_a = rims([(q, q + 1) for q in range(1, 127, 2)])
-    rim_b = swapped(rim_a, 1)
-    rim_d = rims([(q, q + 4) for q in range(3, 124, 4)])
-    rim_e = rims(
-        [(q, q - 1) for q in range(2, 128, 4)]
-        + [(q, q + 3) for q in range(0, 128, 4)]
-        + [(q, q + 3) for q in range(3, 124, 4)],
-    )
+    rim_a = passed(end_rows, ALL, [(q, q + 1) for q in range(1, 127, 2)])
     across = swapped(merged, 2)
     beside = swapped(merged, 1)
+    rim_b = swapped(rim_a, 1)
+    rim_y = swapped(own_rim(rim_a, beside), 2)
+    rim_yc = swapped(rim_y, 1)
     both = swapped(across, 1)
     weights = (coarse_gate, coarse_value, coarse_scans)
-    lead, tail, maps, share, run, run_log, near_ends = coarse_main(
+    lead, tail, maps, share, run, run_log = coarse_main(
         "near", (merged, beside), weights, params, (rim_a, rim_b)
     )
     lead_1, tail_1, maps_1, share_1, run_1, run_log_1, ends_1 = coarse_main(
-        "far_1", (across,), weights, params, (near_ends, rim_e)
+        "far_1", (across,), weights, params, (rim_y,)
     )
     lead_2, tail_2, maps_2, share_2, run_2, run_log_2, run_f, run_log_f, message = coarse_main(
         "far_2", (both,), weights, params,
-        (near_ends, ends_1, rim_d, run, run_log, run_1, run_log_1),
+        (ends_1, rim_yc, run, run_log, run_1, run_log_1),
     )
     got = lax.all_to_all(message, SEQ, split_axis=0, concat_axis=0, tiled=True)
     got = lax.all_to_all(prefix(got), SEQ, split_axis=0, concat_axis=0, tiled=True)

time: 152 us -> 153 us (level)
  transfers between devices with their start and end apart: 26 -> 26, of which waited for: 9 -> 10; matrix products, arithmetic and copies ran while one was open for 0% -> 0% of each run, Pallas kernels for 20% -> 20%
where the time goes in v5:
time: 153 us; the launch traced here: 152 us
  Pallas kernels  43.3 us (28%)
  starting transfers between devices  41.7 us (27%)
  waiting for transfers between devices  33.6 us (22%)
  blocking collectives  33.6 us (22%)
    ppermute x26, starting transfers between devices, passed(): return lax.ppermute(x, axes, pairs)  41.7 us
    ppermute x26, waiting for transfers between devices, passed(): return lax.ppermute(x, axes, pairs)  33.6 us
    all_to_all x1, blocking collectives, shards(): got = lax.all_to_all(message, SEQ, split_axis=0, concat_axis=0, tiled=True)  19.7 us
    all_to_all x1, blocking collectives, shards(): lax.all_to_all(prefix(got), SEQ, split_axis=0, concat_axis=0, tiled=True)  13.9 us
    pallas_call x3, Pallas kernels, coarse_main(): pl.pallas_call(lambda *refs: coarse_main_kernel(kind, blocks, *refs), gri...  13.2 us
    pallas_call x2, Pallas kernels, fine_main(): pl.pallas_call(lambda *refs: fine_main_kernel(later, *refs), grid=(2,), i...  9.6 us
    pallas_call x1, Pallas kernels, fine_states(): pl.pallas_call(later_chunks_kernel, grid=(3,), in_specs=[HBM, HBM, VM, HB...  7.69 us
    pallas_call x1, Pallas kernels, fine_close(): pl.pallas_call(fine_close_kernel, grid=(4,), in_specs=halves(512) + halve...  3.46 us
  transfers between devices with their start and end apart: 26, of which 10 were waited for; matrix products, arithmetic and copies ran while one was open for 0% of the time, Pallas kernels for 20%

profile of v5, /device:TPU:1, one launch (start us, length us, event | category | flops | bytes accessed | tf_op | source)
XLA Modules:
  0.0 152.5 jit_solution(1824791155632956316)
XLA Ops:
  0.0 1.1 pack.1
  1.1 3.9 %collective-permute-start.3 = (bf16[16,256]{1,0:T(8,128)(2,1)S(1)}, bf16[16,256]{1,0:T(8,128)(2,1)S(1)}, u32[]{:S(2)}, u32[]{:S(2)}) collective-permute-start(bf16[16,256]{1,0:T(8,128)(2,1)S(1)} %get-tuple-element.95), channel_id=1, source_target_pairs={{0,4},{4,8},{8,12},{12,16},{16,20},{20,24},{24,28},{28,32},{32,36}... | collective-permute-start | bytes 24584 | tf_op jit(solution)/shard_map/ppermute | solution.py:948
  5.0 7.7 %later_chunks.1 = (f32[3,256,128]{2,1,0:T(8,128)S(1)}, f32[3,8,128]{2,1,0:T(8,128)S(1)}, bf16[1024,256]{1,0:T(8,128)(2,1)S(1)}, bf16[1024,256]{1,0:T(8,128)(2,1)...) custom-call(bf16[4096,256]{1,0:T(8,128)(2,1)} %tokens.3, ...), custom_call_target="tpu_custom_call" | custom-call | tf_op jit(solution)/shard_map/later_chunks/pallas_call | solution.py:344
  12.7 2.0 %first_chunk.1 = (f32[256,128]{1,0:T(8,128)S(1)}, f32[8,128]{1,0:T(8,128)S(1)}, f32[256,128]{1,0:T(8,128)S(1)}, f32[8,128]{1,0:T(8,128)S(1)}, bf16[272,128]{1,0:T(8,128)(2,1)S(1)}) custom-call(bf16[1024,256]{1,0:T(8,128)(2,1)S(1)} %get-tuple-element.97.x, bf16[16,256]{1,0:T(8,128)(2,1)S(1)} %collective-permute-done.3.rim.refs_8_, ...), custom_call_target="tpu_custom_call" | custom-call | tf_op jit(solution)/shard_map/first_chunk/pallas_call | solution.py:366
  14.8 4.2 %collective-permute-start.6 = (bf16[272,128]{1,0:T(8,128)(2,1)S(1)}, bf16[272,128]{1,0:T(8,128)(2,1)S(1)}, u32[]{:S(2)}, u32[]{:S(2)}) collective-permute-start(bf16[272,128]{1,0:T(8,128)(2,1)S(1)} %get-tuple-element.112), channel_id=1, source_target_pairs={{0,12},{4,0},{8,4},{12,8},{1,13},{5,1},{9,5},{13,9},{2,14},{6,2},{... | collective-permute-start | bytes 208904 | tf_op jit(solution)/shard_map/ppermute | solution.py:948
  19.0 0.7 collective-permute-start.4
  19.6 1.8 %collective-permute-start.2 = (bf16[416,256]{1,0:T(8,128)(2,1)S(1)}, bf16[416,256]{1,0:T(8,128)(2,1)S(1)}, u32[]{:S(2)}, u32[]{:S(2)}) collective-permute-start(bf16[416,256]{1,0:T(8,128)(2,1)S(1)} %get-tuple-element.90.pack.refs_4_.p0), channel_id=1, source_target_pairs={{0,3},{1,2},{2,1},{3,0},{4,7},{5,6},{6,5},{7,4},{8,11},{9,10},{10,... | collective-permute-start | bytes 638984 | tf_op jit(solution)/shard_map/ppermute | solution.py:948
  21.4 2.3 %collective-permute-done.5.refs_3_ = bf16[272,128]{1,0:T(8,128)(2,1)S(1)} collective-permute-done((bf16[272,128]{1,0:T(8,128)(2,1)S(1)}, bf16[272,128]{1,0:T(8,128)(2,1)S(1)}, u32[]{:S(2)}, u32[]{:S(2)}) %collective-permute-start.5) | collective-permute-done | bytes 69664 | tf_op jit(solution)/shard_map/ppermute | solution.py:948
  23.7 0.4 collective-permute-done.4.refs_2_
  24.1 0.1 shard_map.226
  24.2 1.8 %collective-permute-start.7 = (bf16[272,128]{1,0:T(8,128)(2,1)S(1)}, bf16[272,128]{1,0:T(8,128)(2,1)S(1)}, u32[]{:S(2)}, u32[]{:S(2)}) collective-permute-start(bf16[272,128]{1,0:T(8,128)(2,1)S(1)} %get-tuple-element.117), channel_id=1, source_target_pairs={{0,16},{16,0},{1,17},{17,1},{2,18},{18,2},{3,19},{19,3},{4,20},{20... | collective-permute-start | bytes 208904 | tf_op jit(solution)/shard_map/ppermute | solution.py:948
  26.0 1.0 collective-permute-start.1
  27.0 2.9 %collective-permute-start = (bf16[416,256]{1,0:T(8,128)(2,1)S(1)}, bf16[416,256]{1,0:T(8,128)(2,1)S(1)}, u32[]{:S(2)}, u32[]{:S(2)}) collective-permute-start(bf16[416,256]{1,0:T(8,128)(2,1)S(1)} %get-tuple-element.90.pack.refs_4_.p0), channel_id=1, source_target_pairs={{0,1},{1,0},{2,3},{3,2},{4,5},{5,4},{6,7},{7,6},{8,9},{9,8},{10,11... | collective-permute-start | bytes 638984 | tf_op jit(solution)/shard_map/ppermute | solution.py:948
  30.0 0.0 collective-permute-done.7.refs_4_
  30.0 0.1 shard_map.227
  30.1 3.2 %collective-permute-start.10 = (bf16[272,128]{1,0:T(8,128)(2,1)S(1)}, bf16[272,128]{1,0:T(8,128)(2,1)S(1)}, u32[]{:S(2)}, u32[]{:S(2)}) collective-permute-start(bf16[272,128]{1,0:T(8,128)(2,1)S(1)} %get-tuple-element.122), channel_id=1, source_target_pairs={{0,96},{32,0},{64,32},{96,64},{1,97},{33,1},{65,33},{97,65},{2,98}... | collective-permute-start | bytes 208904 | tf_op jit(solution)/shard_map/ppermute | solution.py:948
  33.2 0.4 collective-permute-start.9
  33.6 1.0 collective-permute-done.10.r3
  34.6 0.6 collective-permute-start.8
  35.2 2.7 %collective-permute-done.9.r2 = bf16[272,128]{1,0:T(8,128)(2,1)S(1)} collective-permute-done((bf16[272,128]{1,0:T(8,128)(2,1)S(1)}, bf16[272,128]{1,0:T(8,128)(2,1)S(1)}, u32[]{:S(2)}, u32[]{:S(2)}) %collective-permute-start.9) | collective-permute-done | bytes 69664 | tf_op jit(solution)/shard_map/ppermute | solution.py:948
  37.9 1.4 collective-permute-done.8.r1
  39.3 0.1 chain_last.1
  39.4 0.0 copy-start.4
  39.5 5.8 %collective-permute-start.11 = (bf16[256,128]{1,0:T(8,128)(2,1)S(1)}, bf16[256,128]{1,0:T(8,128)(2,1)S(1)}, u32[]{:S(2)}, u32[]{:S(2)}) collective-permute-start(bf16[256,128]{1,0:T(8,128)(2,1)S(1)} %get-tuple-element.125), channel_id=1, source_target_pairs={{0,1},{1,0},{2,3},{3,2},{4,5},{5,4},{6,7},{7,6},{8,9},{9,8},{10,11... | collective-permute-start | bytes 196616 | tf_op jit(solution)/shard_map/ppermute | solution.py:948
  45.3 0.4 collective-permute-start.12
  45.7 1.3 collective-permute-start.13
  47.0 4.4 %fine_main_a.1 = (f32[512,512]{1,0:T(8,128)S(1)}, f32[512,512]{1,0:T(8,128)S(1)}, bf16[512,256]{1,0:T(8,128)(2,1)S(1)}, f32[256,512]{1,0:T(8,128)S(1)}, f32[8,128]{1,0:T(8,128)S(1)}, /*index=5*/f32[8,16,128]{2,1,0:T(8,128)S(1)}) custom-call(bf16[1024,256]{1,0:T(8,128)(2,1)S(1)} %get-tuple-element.91.refs_0_.x, f32[1,256]{1,0:T(1,128)S(1)} %get-tuple-element.92.gain.refs_1_, ...), custom_call_target="tpu_custom_call" | custom-call | tf_op jit(solution)/shard_map/fine_main_a/pallas_call | solution.py:578
  51.5 5.2 %fine_main_b.1 = (f32[512,512]{1,0:T(8,128)S(1)}, f32[512,512]{1,0:T(8,128)S(1)}, bf16[512,256]{1,0:T(8,128)(2,1)S(1)}, f32[256,512]{1,0:T(8,128)}, f32[8,128]{1,0:T(8,128)}, /*index=5*/f32[8,16,128]{2,1,0:T(8,128)}) custom-call(bf16[1024,256]{1,0:T(8,128)(2,1)S(1)} %get-tuple-element.91.refs_0_.x, f32[1,256]{1,0:T(1,128)S(1)} %get-tuple-element.92.gain.refs_1_, ...), custom_call_target="tpu_custom_call" | custom-call | tf_op jit(solution)/shard_map/fine_main_b/pallas_call | solution.py:578
  56.7 0.0 copy-start
  56.7 0.0 copy-start.1
  56.7 0.0 copy-start.2
  56.7 3.5 %fine_close.1 = (bf16[256,1024]{1,0:T(8,128)(2,1)S(1)}, bf16[16,1024]{1,0:T(8,128)(2,1)S(1)}) custom-call(f32[512,512]{1,0:T(8,128)S(1)} %get-tuple-element.101.lead_a, f32[512,512]{1,0:T(8,128)S(1)} %get-tuple-element.105.lead_b, f32[512,512]{1,0:T(8,128)S(1)} %get-tuple-element.106.tail_a, f32[512,512]{1,0:T(8,128)S(1)} %get-tuple-element.107.tail_b, ...), custom_call_target="tpu_custom_call" | custom-call | tf_op jit(solution)/shard_map/fine_close/pallas_call | solution.py:656
  60.2 0.5 collective-permute-start.17
  60.6 0.4 collective-permute-start.14
  61.1 12.5 %collective-permute-done.17.refs_7_ = bf16[256,1024]{1,0:T(8,128)(2,1)S(1)} collective-permute-done((bf16[256,1024]{1,0:T(8,128)(2,1)S(1)}, bf16[256,1024]{1,0:T(8,128)(2,1)S(1)}, u32[]{:S(2)}, u32[]{:S(2)}) %collective-permute-start.17) | collective-permute-done | bytes 524320 | tf_op jit(solution)/shard_map/ppermute | solution.py:948
  73.6 1.0 collective-permute-start.19
  74.6 2.2 %collective-permute-start.15 = (bf16[16,1024]{1,0:T(8,128)(2,1)S(1)}, bf16[16,1024]{1,0:T(8,128)(2,1)S(1)}, u32[]{:S(2)}, u32[]{:S(2)}) collective-permute-start(bf16[16,1024]{1,0:T(8,128)(2,1)S(1)} %get-tuple-element.129), channel_id=1, source_target_pairs={{1,2},{3,4},{5,6},{7,8},{9,10},{11,12},{13,14},{15,16},{17,18},{19... | collective-permute-start | bytes 98312 | tf_op jit(solution)/shard_map/ppermute | solution.py:948
  76.8 1.0 collective-permute-done.15.refs_9_.came
  77.8 0.1 collective-permute-start.18
  77.9 2.7 %collective-permute-start.16 = (bf16[16,1024]{1,0:T(8,128)(2,1)S(1)}, bf16[16,1024]{1,0:T(8,128)(2,1)S(1)}, u32[]{:S(2)}, u32[]{:S(2)}) collective-permute-start(bf16[16,1024]{1,0:T(8,128)(2,1)S(1)} %collective-permute-done.15.refs_9_.came), channel_id=1, source_target_pairs={{0,1},{1,0},{2,3},{3,2},{4,5},{5,4},{6,7},{7,6},{8,9},{9,8},{10,11... | collective-permute-start | bytes 98312 | tf_op jit(solution)/shard_map/ppermute | solution.py:948
  80.6 0.1 collective-permute-done.18.refs_8_
  80.6 1.8 %collective-permute-start.20 = (bf16[16,1024]{1,0:T(8,128)(2,1)S(1)}, bf16[16,1024]{1,0:T(8,128)(2,1)S(1)}, u32[]{:S(2)}, u32[]{:S(2)}) collective-permute-start(bf16[16,1024]{1,0:T(8,128)(2,1)S(1)} %collective-permute-done.18.refs_8_), channel_id=1, source_target_pairs={{0,1},{1,0},{2,3},{3,2},{4,5},{5,4},{6,7},{7,6},{8,9},{9,8},{10,11... | collective-permute-start | bytes 98312 | tf_op jit(solution)/shard_map/ppermute | solution.py:948
  82.5 1.0 coarse_params.1
  83.5 6.3 %shard_map.228 = (f32[512,512]{1,0:T(8,128)S(1)}, f32[512,512]{1,0:T(8,128)S(1)}, bf16[512,256]{1,0:T(8,128)(2,1)S(1)}, bf16[512,256]{1,0:T(8,128)(2,1)S(1)}, f3...) custom-call(f32[1,1024]{1,0:T(1,128)S(1)} %get-tuple-element.86.refs_0_, bf16[1024,512]{1,0:T(8,128)(2,1)S(1)} %copy-done, ...), custom_call_target="tpu_custom_call" | custom-call | tf_op jit(solution)/shard_map/pallas_call | solution.py:757
  89.8 3.4 %shard_map.229 = (f32[256,512]{1,0:T(8,128)S(1)}, f32[256,512]{1,0:T(8,128)S(1)}, bf16[256,256]{1,0:T(8,128)(2,1)S(1)}, bf16[256,256]{1,0:T(8,128)(2,1)S(1)}, f3...) custom-call(f32[1,1024]{1,0:T(1,128)S(1)} %get-tuple-element.86.refs_0_, ...), custom_call_target="tpu_custom_call" | custom-call | tf_op jit(solution)/shard_map/pallas_call | solution.py:757
  93.2 3.6 %shard_map.230 = (f32[256,512]{1,0:T(8,128)S(1)}, f32[256,512]{1,0:T(8,128)S(1)}, bf16[256,256]{1,0:T(8,128)(2,1)S(1)}, bf16[256,256]{1,0:T(8,128)(2,1)S(1)}, f3...) custom-call(f32[1,1024]{1,0:T(1,128)S(1)} %get-tuple-element.86.refs, ...), custom_call_target="tpu_custom_call" | custom-call | tf_op jit(solution)/shard_map/pallas_call | solution.py:757
  96.8 0.0 copy-start.3
  96.8 19.7 %all_to_all.10.got = bf16[32,24,256]{2,1,0:T(8,128)(2,1)S(1)} all-to-all(bf16[32,24,256]{2,1,0:T(8,128)(2,1)S(1)} %get-tuple-element.141), channel_id=1, replica_groups=mesh['z'=4,'u'=2,'x'=4,'y'=2,'c'=2] {'z','u','x'}, dimensions={0} | all-to-all | bytes 786432 | tf_op jit(solution)/shard_map/all_to_all | solution.py:1014
  116.4 0.1 prefix.1
  116.6 13.9 %all_to_all.11.refs_3_.refs_6_ = bf16[32,16,256]{2,1,0:T(8,128)(2,1)S(1)} all-to-all(bf16[32,16,256]{2,1,0:T(8,128)(2,1)S(1)} %prefix.1), channel_id=1, replica_groups=mesh['z'=4,'u'=2,'x'=4,'y'=2,'c'=2] {'z','u','x'}, dimensions={0} | all-to-all | bytes 524288 | tf_op jit(solution)/shard_map/all_to_all | solution.py:1015
  130.5 1.3 coarse_close_far.1
  131.9 2.8 %collective-permute-start.23 = (bf16[528,256]{1,0:T(8,128)(2,1)S(1)}, bf16[528,256]{1,0:T(8,128)(2,1)S(1)}, u32[]{:S(2)}, u32[]{:S(2)}) collective-permute-start(bf16[528,256]{1,0:T(8,128)(2,1)S(1)} %get-tuple-element.163), channel_id=1, source_target_pairs={{0,1},{1,0},{2,3},{3,2},{4,5},{5,4},{6,7},{7,6},{8,9},{9,8},{10,11... | collective-permute-start | bytes 811016 | tf_op jit(solution)/shard_map/ppermute | solution.py:948
  134.6 1.2 coarse_close_near.1
  135.9 0.1 collective-permute-start.22
  136.0 0.7 close_rest.1
  136.7 0.6 collective-permute-start.21
  137.2 0.1 shard_map.232
  137.3 0.1 collective-permute-start.24
  137.4 0.0 collective-permute-done.22.came
  137.5 0.1 shard_map.231
  137.6 1.5 collective-permute-start.25
  139.1 6.4 %collective-permute-done.24.far_a = bf16[528,256]{1,0:T(8,128)(2,1)S(1)} collective-permute-done((bf16[528,256]{1,0:T(8,128)(2,1)S(1)}, bf16[528,256]{1,0:T(8,128)(2,1)S(1)}, u32[]{:S(2)}, u32[]{:S(2)}) %collective-permute-start.24) | collective-permute-done | bytes 270368 | tf_op jit(solution)/shard_map/ppermute | solution.py:948
  145.4 5.8 %collective-permute-done.25.far_b = bf16[528,256]{1,0:T(8,128)(2,1)S(1)} collective-permute-done((bf16[528,256]{1,0:T(8,128)(2,1)S(1)}, bf16[528,256]{1,0:T(8,128)(2,1)S(1)}, u32[]{:S(2)}, u32[]{:S(2)}) %collective-permute-start.25) | collective-permute-done | bytes 270368 | tf_op jit(solution)/shard_map/ppermute | solution.py:948
  151.2 1.3 final.1
  (21 shorter events, 0.1 us)
Async XLA Ops:
  1.1 11.6 %collective-permute-start.3 = (bf16[16,256]{1,0:T(8,128)(2,1)S(1)}, bf16[16,256]{1,0:T(8,128)(2,1)S(1)}, u32[]{:S(2)}, u32[]{:S(2)}) collective-permute-start(bf16[16,256]{1,0:T(8,128)(2,1)S(1)} %get-tuple-element.95), channel_id=1, source_target_pairs={{0,4},{4,8},{8,12},{12,16},{16,20},{20,24},{24,28},{28,32},{32,36}... | collective-permute-start | bytes 24584 | tf_op jit(solution)/shard_map/ppermute | solution.py:948
  14.8 6.7 %collective-permute-start.6 = (bf16[272,128]{1,0:T(8,128)(2,1)S(1)}, bf16[272,128]{1,0:T(8,128)(2,1)S(1)}, u32[]{:S(2)}, u32[]{:S(2)}) collective-permute-start(bf16[272,128]{1,0:T(8,128)(2,1)S(1)} %get-tuple-element.112), channel_id=1, source_target_pairs={{0,12},{4,0},{8,4},{12,8},{1,13},{5,1},{9,5},{13,9},{2,14},{6,2},{... | collective-permute-start | bytes 208904 | tf_op jit(solution)/shard_map/ppermute | solution.py:948
  19.0 4.8 %collective-permute-start.5 = (bf16[272,128]{1,0:T(8,128)(2,1)S(1)}, bf16[272,128]{1,0:T(8,128)(2,1)S(1)}, u32[]{:S(2)}, u32[]{:S(2)}) collective-permute-start(bf16[272,128]{1,0:T(8,128)(2,1)S(1)} %get-tuple-element.112), channel_id=1, source_target_pairs={{0,8},{4,12},{8,0},{12,4},{1,9},{5,13},{9,1},{13,5},{2,10},{6,14},... | collective-permute-start | bytes 208904 | tf_op jit(solution)/shard_map/ppermute | solution.py:948
  19.0 5.1 %collective-permute-start.4 = (bf16[272,128]{1,0:T(8,128)(2,1)S(1)}, bf16[272,128]{1,0:T(8,128)(2,1)S(1)}, u32[]{:S(2)}, u32[]{:S(2)}) collective-permute-start(bf16[272,128]{1,0:T(8,128)(2,1)S(1)} %get-tuple-element.112), channel_id=1, source_target_pairs={{0,4},{4,8},{8,12},{12,0},{1,5},{5,9},{9,13},{13,1},{2,6},{6,10},{... | collective-permute-start | bytes 208904 | tf_op jit(solution)/shard_map/ppermute | solution.py:948
  19.6 26.0 %collective-permute-start.2 = (bf16[416,256]{1,0:T(8,128)(2,1)S(1)}, bf16[416,256]{1,0:T(8,128)(2,1)S(1)}, u32[]{:S(2)}, u32[]{:S(2)}) collective-permute-start(bf16[416,256]{1,0:T(8,128)(2,1)S(1)} %get-tuple-element.90.pack.refs_4_.p0), channel_id=1, source_target_pairs={{0,3},{1,2},{2,1},{3,0},{4,7},{5,6},{6,5},{7,4},{8,11},{9,10},{10,... | collective-permute-start | bytes 638984 | tf_op jit(solution)/shard_map/ppermute | solution.py:948
  24.2 5.7 %collective-permute-start.7 = (bf16[272,128]{1,0:T(8,128)(2,1)S(1)}, bf16[272,128]{1,0:T(8,128)(2,1)S(1)}, u32[]{:S(2)}, u32[]{:S(2)}) collective-permute-start(bf16[272,128]{1,0:T(8,128)(2,1)S(1)} %get-tuple-element.117), channel_id=1, source_target_pairs={{0,16},{16,0},{1,17},{17,1},{2,18},{18,2},{3,19},{19,3},{4,20},{20... | collective-permute-start | bytes 208904 | tf_op jit(solution)/shard_map/ppermute | solution.py:948
  26.0 21.0 %collective-permute-start.1 = (bf16[416,256]{1,0:T(8,128)(2,1)S(1)}, bf16[416,256]{1,0:T(8,128)(2,1)S(1)}, u32[]{:S(2)}, u32[]{:S(2)}) collective-permute-start(bf16[416,256]{1,0:T(8,128)(2,1)S(1)} %get-tuple-element.90.pack.refs_4_.p0), channel_id=1, source_target_pairs={{0,2},{1,3},{2,0},{3,1},{4,6},{5,7},{6,4},{7,5},{8,10},{9,11},{10,... | collective-permute-start | bytes 638984 | tf_op jit(solution)/shard_map/ppermute | solution.py:948
  27.0 20.0 %collective-permute-start = (bf16[416,256]{1,0:T(8,128)(2,1)S(1)}, bf16[416,256]{1,0:T(8,128)(2,1)S(1)}, u32[]{:S(2)}, u32[]{:S(2)}) collective-permute-start(bf16[416,256]{1,0:T(8,128)(2,1)S(1)} %get-tuple-element.90.pack.refs_4_.p0), channel_id=1, source_target_pairs={{0,1},{1,0},{2,3},{3,2},{4,5},{5,4},{6,7},{7,6},{8,9},{9,8},{10,11... | collective-permute-start | bytes 638984 | tf_op jit(solution)/shard_map/ppermute | solution.py:948
  30.1 4.6 %collective-permute-start.10 = (bf16[272,128]{1,0:T(8,128)(2,1)S(1)}, bf16[272,128]{1,0:T(8,128)(2,1)S(1)}, u32[]{:S(2)}, u32[]{:S(2)}) collective-permute-start(bf16[272,128]{1,0:T(8,128)(2,1)S(1)} %get-tuple-element.122), channel_id=1, source_target_pairs={{0,96},{32,0},{64,32},{96,64},{1,97},{33,1},{65,33},{97,65},{2,98}... | collective-permute-start | bytes 208904 | tf_op jit(solution)/shard_map/ppermute | solution.py:948
  33.2 4.7 %collective-permute-start.9 = (bf16[272,128]{1,0:T(8,128)(2,1)S(1)}, bf16[272,128]{1,0:T(8,128)(2,1)S(1)}, u32[]{:S(2)}, u32[]{:S(2)}) collective-permute-start(bf16[272,128]{1,0:T(8,128)(2,1)S(1)} %get-tuple-element.122), channel_id=1, source_target_pairs={{0,64},{32,96},{64,0},{96,32},{1,65},{33,97},{65,1},{97,33},{2,66}... | collective-permute-start | bytes 208904 | tf_op jit(solution)/shard_map/ppermute | solution.py:948
  34.6 4.7 %collective-permute-start.8 = (bf16[272,128]{1,0:T(8,128)(2,1)S(1)}, bf16[272,128]{1,0:T(8,128)(2,1)S(1)}, u32[]{:S(2)}, u32[]{:S(2)}) collective-permute-start(bf16[272,128]{1,0:T(8,128)(2,1)S(1)} %get-tuple-element.122), channel_id=1, source_target_pairs={{0,32},{32,64},{64,96},{96,0},{1,33},{33,65},{65,97},{97,1},{2,34}... | collective-permute-start | bytes 208904 | tf_op jit(solution)/shard_map/ppermute | solution.py:948
  39.4 17.2 %copy-start.4 = (bf16[1024,1024]{1,0:T(8,128)(2,1)S(1)}, bf16[1024,1024]{1,0:T(8,128)(2,1)}, u32[]{:S(2)}) copy-start(bf16[1024,1024]{1,0:T(8,128)(2,1)} %merge.1) | copy-start | bytes 6291460
  39.5 17.2 %collective-permute-start.11 = (bf16[256,128]{1,0:T(8,128)(2,1)S(1)}, bf16[256,128]{1,0:T(8,128)(2,1)S(1)}, u32[]{:S(2)}, u32[]{:S(2)}) collective-permute-start(bf16[256,128]{1,0:T(8,128)(2,1)S(1)} %get-tuple-element.125), channel_id=1, source_target_pairs={{0,1},{1,0},{2,3},{3,2},{4,5},{5,4},{6,7},{7,6},{8,9},{9,8},{10,11... | collective-permute-start | bytes 196616 | tf_op jit(solution)/shard_map/ppermute | solution.py:948
  45.3 11.4 %collective-permute-start.12 = (bf16[256,128]{1,0:T(8,128)(2,1)S(1)}, bf16[256,128]{1,0:T(8,128)(2,1)S(1)}, u32[]{:S(2)}, u32[]{:S(2)}) collective-permute-start(bf16[256,128]{1,0:T(8,128)(2,1)S(1)} %get-tuple-element.126), channel_id=1, source_target_pairs={{0,2},{1,3},{2,0},{3,1},{4,6},{5,7},{6,4},{7,5},{8,10},{9,11},{10,... | collective-permute-start | bytes 196616 | tf_op jit(solution)/shard_map/ppermute | solution.py:948
  45.7 11.0 %collective-permute-start.13 = (bf16[256,128]{1,0:T(8,128)(2,1)S(1)}, bf16[256,128]{1,0:T(8,128)(2,1)S(1)}, u32[]{:S(2)}, u32[]{:S(2)}) collective-permute-start(bf16[256,128]{1,0:T(8,128)(2,1)S(1)} %get-tuple-element.127), channel_id=1, source_target_pairs={{0,3},{1,2},{2,1},{3,0},{4,7},{5,6},{6,5},{7,4},{8,11},{9,10},{10,... | collective-permute-start | bytes 196616 | tf_op jit(solution)/shard_map/ppermute | solution.py:948
  56.7 26.8 %copy-start = (bf16[1024,512]{1,0:T(8,128)(2,1)S(1)}, bf16[1024,512]{1,0:T(8,128)(2,1)}, u32[]{:S(2)}) copy-start(bf16[1024,512]{1,0:T(8,128)(2,1)} %refs_1_.5) | copy-start | bytes 3145732
  56.7 26.8 %copy-start.1 = (bf16[1024,512]{1,0:T(8,128)(2,1)S(1)}, bf16[1024,512]{1,0:T(8,128)(2,1)}, u32[]{:S(2)}) copy-start(bf16[1024,512]{1,0:T(8,128)(2,1)} %refs_2_.5) | copy-start | bytes 3145732
  56.7 26.8 %copy-start.2 = (bf16[1024,512]{1,0:T(8,128)(2,1)S(1)}, bf16[1024,512]{1,0:T(8,128)(2,1)}, u32[]{:S(2)}) copy-start(bf16[1024,512]{1,0:T(8,128)(2,1)} %refs_3_.5) | copy-start | bytes 3145732
  60.2 13.4 %collective-permute-start.17 = (bf16[256,1024]{1,0:T(8,128)(2,1)S(1)}, bf16[256,1024]{1,0:T(8,128)(2,1)S(1)}, u32[]{:S(2)}, u32[]{:S(2)}) collective-permute-start(bf16[256,1024]{1,0:T(8,128)(2,1)S(1)} %get-tuple-element.128.refs_7_), channel_id=1, source_target_pairs={{0,2},{1,3},{2,0},{3,1},{4,6},{5,7},{6,4},{7,5},{8,10},{9,11},{10,... | collective-permute-start | bytes 1572872 | tf_op jit(solution)/shard_map/ppermute | solution.py:948
  60.6 17.1 %collective-permute-start.14 = (bf16[256,1024]{1,0:T(8,128)(2,1)S(1)}, bf16[256,1024]{1,0:T(8,128)(2,1)S(1)}, u32[]{:S(2)}, u32[]{:S(2)}) collective-permute-start(bf16[256,1024]{1,0:T(8,128)(2,1)S(1)} %get-tuple-element.128.refs_7_), channel_id=1, source_target_pairs={{0,1},{1,0},{2,3},{3,2},{4,5},{5,4},{6,7},{7,6},{8,9},{9,8},{10,11... | collective-permute-start | bytes 1572872 | tf_op jit(solution)/shard_map/ppermute | solution.py:948
  73.6 19.6 %collective-permute-start.19 = (bf16[256,1024]{1,0:T(8,128)(2,1)S(1)}, bf16[256,1024]{1,0:T(8,128)(2,1)S(1)}, u32[]{:S(2)}, u32[]{:S(2)}) collective-permute-start(bf16[256,1024]{1,0:T(8,128)(2,1)S(1)} %collective-permute-done.17.refs_7_), channel_id=1, source_target_pairs={{0,1},{1,0},{2,3},{3,2},{4,5},{5,4},{6,7},{7,6},{8,9},{9,8},{10,11... | collective-permute-start | bytes 1572872 | tf_op jit(solution)/shard_map/ppermute | solution.py:948
  74.6 3.2 %collective-permute-start.15 = (bf16[16,1024]{1,0:T(8,128)(2,1)S(1)}, bf16[16,1024]{1,0:T(8,128)(2,1)S(1)}, u32[]{:S(2)}, u32[]{:S(2)}) collective-permute-start(bf16[16,1024]{1,0:T(8,128)(2,1)S(1)} %get-tuple-element.129), channel_id=1, source_target_pairs={{1,2},{3,4},{5,6},{7,8},{9,10},{11,12},{13,14},{15,16},{17,18},{19... | collective-permute-start | bytes 98312 | tf_op jit(solution)/shard_map/ppermute | solution.py:948
  77.8 2.8 %collective-permute-start.18 = (bf16[16,1024]{1,0:T(8,128)(2,1)S(1)}, bf16[16,1024]{1,0:T(8,128)(2,1)S(1)}, u32[]{:S(2)}, u32[]{:S(2)}) collective-permute-start(bf16[16,1024]{1,0:T(8,128)(2,1)S(1)} %own_rim.1), channel_id=1, source_target_pairs={{0,2},{1,3},{2,0},{3,1},{4,6},{5,7},{6,4},{7,5},{8,10},{9,11},{10,... | collective-permute-start | bytes 98312 | tf_op jit(solution)/shard_map/ppermute | solution.py:948
  77.9 5.6 %collective-permute-start.16 = (bf16[16,1024]{1,0:T(8,128)(2,1)S(1)}, bf16[16,1024]{1,0:T(8,128)(2,1)S(1)}, u32[]{:S(2)}, u32[]{:S(2)}) collective-permute-start(bf16[16,1024]{1,0:T(8,128)(2,1)S(1)} %collective-permute-done.15.refs_9_.came), channel_id=1, source_target_pairs={{0,1},{1,0},{2,3},{3,2},{4,5},{5,4},{6,7},{7,6},{8,9},{9,8},{10,11... | collective-permute-start | bytes 98312 | tf_op jit(solution)/shard_map/ppermute | solution.py:948
  80.6 12.5 %collective-permute-start.20 = (bf16[16,1024]{1,0:T(8,128)(2,1)S(1)}, bf16[16,1024]{1,0:T(8,128)(2,1)S(1)}, u32[]{:S(2)}, u32[]{:S(2)}) collective-permute-start(bf16[16,1024]{1,0:T(8,128)(2,1)S(1)} %collective-permute-done.18.refs_8_), channel_id=1, source_target_pairs={{0,1},{1,0},{2,3},{3,2},{4,5},{5,4},{6,7},{7,6},{8,9},{9,8},{10,11... | collective-permute-start | bytes 98312 | tf_op jit(solution)/shard_map/ppermute | solution.py:948
  96.8 33.8 %copy-start.3 = (bf16[512,1024]{1,0:T(8,128)(2,1)S(1)}, bf16[512,1024]{1,0:T(8,128)(2,1)}, u32[]{:S(2)}) copy-start(bf16[512,1024]{1,0:T(8,128)(2,1)} %wo.1) | copy-start | bytes 3145732
  131.9 5.4 %collective-permute-start.23 = (bf16[528,256]{1,0:T(8,128)(2,1)S(1)}, bf16[528,256]{1,0:T(8,128)(2,1)S(1)}, u32[]{:S(2)}, u32[]{:S(2)}) collective-permute-start(bf16[528,256]{1,0:T(8,128)(2,1)S(1)} %get-tuple-element.163), channel_id=1, source_target_pairs={{0,1},{1,0},{2,3},{3,2},{4,5},{5,4},{6,7},{7,6},{8,9},{9,8},{10,11... | collective-permute-start | bytes 811016 | tf_op jit(solution)/shard_map/ppermute | solution.py:948
  135.9 1.6 %collective-permute-start.22 = (bf16[528,256]{1,0:T(8,128)(2,1)S(1)}, bf16[528,256]{1,0:T(8,128)(2,1)S(1)}, u32[]{:S(2)}, u32[]{:S(2)}) collective-permute-start(bf16[528,256]{1,0:T(8,128)(2,1)S(1)} %get-tuple-element.159), channel_id=1, source_target_pairs={{0,1},{1,0},{2,3},{3,2},{4,5},{5,4},{6,7},{7,6},{8,9},{9,8},{10,11... | collective-permute-start | bytes 811016 | tf_op jit(solution)/shard_map/ppermute | solution.py:948
  136.7 2.4 %collective-permute-start.21 = (bf16[1024,256]{1,0:T(8,128)(2,1)S(1)}, bf16[1024,256]{1,0:T(8,128)(2,1)S(1)}, u32[]{:S(2)}, u32[]{:S(2)}) collective-permute-start(bf16[1024,256]{1,0:T(8,128)(2,1)S(1)} %get-tuple-element.156), channel_id=1, source_target_pairs={{0,1},{1,0},{2,3},{3,2},{4,5},{5,4},{6,7},{7,6},{8,9},{9,8},{10,11... | collective-permute-start | bytes 1572872 | tf_op jit(solution)/shard_map/ppermute | solution.py:948
  137.3 8.1 %collective-permute-start.24 = (bf16[528,256]{1,0:T(8,128)(2,1)S(1)}, bf16[528,256]{1,0:T(8,128)(2,1)S(1)}, u32[]{:S(2)}, u32[]{:S(2)}) collective-permute-start(bf16[528,256]{1,0:T(8,128)(2,1)S(1)} %get-tuple-element.164), channel_id=1, source_target_pairs={{0,2},{1,3},{2,0},{3,1},{4,6},{5,7},{6,4},{7,5},{8,10},{9,11},{10,... | collective-permute-start | bytes 811016 | tf_op jit(solution)/shard_map/ppermute | solution.py:948
  137.6 13.6 %collective-permute-start.25 = (bf16[528,256]{1,0:T(8,128)(2,1)S(1)}, bf16[528,256]{1,0:T(8,128)(2,1)S(1)}, u32[]{:S(2)}, u32[]{:S(2)}) collective-permute-start(bf16[528,256]{1,0:T(8,128)(2,1)S(1)} %get-tuple-element.166), channel_id=1, source_target_pairs={{0,2},{1,3},{2,0},{3,1},{4,6},{5,7},{6,4},{7,5},{8,10},{9,11},{10,... | collective-permute-start | bytes 811016 | tf_op jit(solution)/shard_map/ppermute | solution.py:948

commit v6 on v5

--- a/solution.py
+++ b/solution.py
@@ -134,8 +134,8 @@
 
 
 def pack_kernel(
-    bias, decay, gate, value, output, steps, kv, norm, tokens,
-    pack, ends, kv_v, norm_v, steps_v, bias_v, decay_v, sems,
+    bias, decay, gate, value, output, steps, kv, norm, tokens, gain, scans, ks,
+    pack, ends, chunk, gain_v, scans_v, ks_v, kv_v, norm_v, steps_v, bias_v, decay_v, sems,
 ):
     copies = run_copies(
         (
@@ -148,6 +148,10 @@
             (gate, pack.at[0:256, 0:128]),
             (value, pack.at[0:256, 128:256]),
             (output, pack.at[256:384]),
+            (tokens.at[1008:2048], chunk),
+            (gain, gain_v),
+            (scans, scans_v),
+            (ks, ks_v),
         ),
         sems,
     )
@@ -165,23 +169,30 @@
         copy.wait()
 
 
-def packed(bias, decay, gate, value, output, steps, kv, norm, tokens):
+def packed(*args):
     return pl.pallas_call(
         pack_kernel,
-        in_specs=[HBM] * 9,
-        out_specs=[VM] * 2,
-        out_shape=[sds((416, 256), BF), sds((16, 256), BF)],
+        in_specs=[HBM] * 12,
+        out_specs=[VM] * 6,
+        out_shape=[
+            sds((416, 256), BF),
+            sds((16, 256), BF),
+            sds((1040, 256), BF),
+            sds((1, 256)),
+            sds((256, 512), BF),
+            sds((4, 512)),
+        ],
         scratch_shapes=[
             pltpu.VMEM((4, 128), F32),
             pltpu.VMEM((1, 128), F32),
             pltpu.VMEM((2, 256), BF),
             pltpu.VMEM((1, 2), F32),
             pltpu.VMEM((1, 2), F32),
-            pltpu.SemaphoreType.DMA((9,)),
+            pltpu.SemaphoreType.DMA((13,)),
         ],
         compiler_params=few(4),
         name="pack",
-    )(*in_hbm(bias, decay, gate, value, output, steps, kv, norm, tokens))
+    )(*in_hbm(*args))
 
 
 def params_kernel(bias, decay, kv, ks, gain, steps, norm, taps, both, *refs):
@@ -225,7 +236,7 @@
     )(*in_hbm(bias, decay, kv, ks, gain, steps, norm))
 
 
-def state_chunk(x, rim, gain, pack, scans, ks, taps, cv, act):
+def state_chunk(x, gain, pack, scans, ks, taps, cv, act):
     kv, _, bias, decay, steps = small_rows(pack)
     pad = jnp.zeros((6, 128), F32)
     bias = jnp.concatenate([bias, pad], 0)[:, 0:1]
@@ -236,13 +247,10 @@
     taps[1] = ks[:, 0:128] * 0.5
     taps[2] = ks[:, 128:256] * 0.5
     normed = rms(x, gain[...])
-    before = rms(rim, gain[...])
-    project(before, wv, cv, 0, 0)
-    project(before, wb, cv, 0, 1)
-    project(normed, wv, cv, 16, 0)
-    project(normed, wb, cv, 16, 1)
+    project(normed, wv, cv, 0, 0)
+    project(normed, wb, cv, 0, 1)
+    raw = dot(steps, normed[16:1040], NT)
     convolve(cv, act, taps, 1024)
-    raw = dot(steps, normed, NT)
     dt = softplus(raw + bias)
     logs = -dt * decay
     tri = upper()
@@ -256,7 +264,8 @@
     tail = jnp.exp(carry - cum) * dt
     spread = dot(parts(tail), expander(128), TN)
     scaled = (act[0, 0:1024] * spread).astype(BF)
-    local = dot(jnp.concatenate([act[1, 0:1024].astype(BF), act[2, 0:1024].astype(BF)], 1), scaled, TN)
+    maps = jnp.concatenate([act[1, 0:1024].astype(BF), act[2, 0:1024].astype(BF)], 1)
+    local = dot(scaled, maps, TN).T
     total = jnp.sum(
         jnp.where(head_sel(128), jnp.broadcast_to(carry, (8, 128)), 0.0), axis=0, keepdims=True
     )
@@ -264,8 +273,8 @@
 
 
 def later_chunks_kernel(
-    tokens, gain_h, pack, scans_h, ks_h,
-    local, total, x0, mine, mine_rim, gain, scans, ks, xs, taps, cv, act, sems, x_sems,
+    tokens, chunk_0, gain, pack, scans, ks,
+    local, total, x0, mine, mine_rim, xs, taps, cv, act, sems, x_sems,
 ):
     i = pl.program_id(0)
     start = pl.multiple_of(lax.axis_index(HEAD) * 1024, 1024)
@@ -282,31 +291,32 @@
 
     @pl.when(i == 0)
     def _():
-        chunk(0).start()
-        copies = run_copies(((gain_h, gain), (scans_h, scans), (ks_h, ks)), sems)
         chunk(1).start()
         chunk(2).start()
         for j, (a, b) in enumerate(mine_pairs):
-            pltpu.make_async_copy(a, b, sems.at[3 + j]).start()
-        for copy in copies:
-            copy.wait()
-
-    chunk(i).wait()
-    state, logs = state_chunk(xs[i, 16:1040], xs[i, 0:16], gain, pack, scans, ks, taps, cv, act)
+            pltpu.make_async_copy(a, b, sems.at[j]).start()
+        xs[0] = chunk_0[...]
+
+    @pl.when(i > 0)
+    def _():
+        chunk(i).wait()
+
+    state, logs = state_chunk(xs[i], gain, pack, scans, ks, taps, cv, act)
     local[i] = state
     total[i] = jnp.broadcast_to(logs, (8, 128))
 
     @pl.when(i == 2)
     def _():
         for j, (a, b) in enumerate(mine_pairs):
-            pltpu.make_async_copy(a, b, sems.at[3 + j]).wait()
+            pltpu.make_async_copy(a, b, sems.at[j]).wait()
 
 
 def first_chunk_kernel(
     x, rim, gain, pack, scans, ks, later, later_total,
     local, total, whole, whole_total, message, taps, cv, act,
 ):
-    state, logs = state_chunk(x[...], rim[...], gain, pack, scans, ks, taps, cv, act)
+    rows = jnp.concatenate([rim[...], x[...]], 0)
+    state, logs = state_chunk(rows, gain, pack, scans, ks, taps, cv, act)
     local[...] = state
     total[...] = jnp.broadcast_to(logs, (8, 128))
     for j in range(3):
@@ -335,34 +345,30 @@
 HBM = pl.BlockSpec(memory_space=pltpu.HBM)
 
 
-def fine_states(tokens, ends_from, gain, pack, scans, ks):
+def fine_states(tokens, chunk, ends_from, gain, pack, scans, ks):
     scratch = [
         pltpu.VMEM((3, 4, 128), F32),
         pltpu.VMEM((3, 1048, 128), F32),
         pltpu.VMEM((3, 1032, 128), F32),
     ]
-    later, later_total, x0, *resident = pl.pallas_call(
+    later, later_total, x0, *mine = pl.pallas_call(
         later_chunks_kernel,
         grid=(3,),
-        in_specs=[HBM, HBM, VM, HBM, HBM],
-        out_specs=[VM] * 8,
+        in_specs=[HBM] + [VM] * 5,
+        out_specs=[VM] * 5,
         out_shape=[
             sds((3, 256, 128)),
             sds((3, 8, 128)),
             sds((1024, 256), BF),
             sds((1024, 256), BF),
             sds((16, 256), BF),
-            sds((1, 256)),
-            sds((256, 512), BF),
-            sds((4, 512)),
         ],
         scratch_shapes=[pltpu.VMEM((3, 1040, 256), BF)]
         + scratch
-        + [pltpu.SemaphoreType.DMA((6,)), pltpu.SemaphoreType.DMA((3,))],
+        + [pltpu.SemaphoreType.DMA((3,)), pltpu.SemaphoreType.DMA((3,))],
         compiler_params=few(16),
         name="later_chunks",
-    )(*in_hbm(tokens, gain), pack, *in_hbm(scans, ks))
-    _, _, gain, scans, ks = resident
+    )(*in_hbm(tokens), chunk, gain, pack, scans, ks)
     first = pl.pallas_call(
         first_chunk_kernel,
         in_specs=[VM] * 8,
@@ -378,7 +384,7 @@
         compiler_params=few(16),
         name="first_chunk",
     )(x0, ends_from, gain, pack, scans, ks, later, later_total)
-    return later, later_total, resident, first
+    return later, later_total, mine, first
 
 
 def combine(i, count, own, own_total, prior, prior_total, received):
@@ -465,33 +471,28 @@
     )(own, own_total, *prior, *received, l0, t0, later, later_total)
 
 
-def begin(before, wv, ws, cv, run, run_log):
-    project(before, wv[...], cv, 0, 0)
-    project(before, ws[...], cv, 0, 4)
-    run[...] = jnp.zeros_like(run)
-    run_log[...] = jnp.zeros_like(run_log)
-
-
 def scan_block(
-    normed, wg, wv, ws, wst, taps, bias, decay,
+    fresh, normed, wg, wv, ws, wst, taps, bias, decay,
     lead, tail_out, maps_out, cv, act, sc, spread, scaled, run, run_log,
 ):
-    project(normed, wv[...], cv, 16, 0)
-    project(normed, ws[...], cv, 16, 4)
+    project(normed, wv[...], cv, 0, 0)
+    project(normed, ws[...], cv, 0, 4)
+    normed = normed[16:272]
     tail_out[...] = silu(dot(normed, wg[...]))
     convolve(cv, act, taps, BLK)
-    cv[:, 0:16, :] = cv[:, 256:272, :]
     raw = dot(wst[...], normed, NT)
     dt = softplus(raw + bias[...])
     logs = -dt * decay[...]
     cum = cumulate(logs, upper())
     last = cum[:, BLK - 1 : BLK]
-    before_log = run_log[:, 0:1]
-    stacked = jnp.concatenate(
-        [jnp.exp(cum), jnp.exp(cum + before_log), jnp.exp(last - cum) * dt], 1
-    )
-    spread[...] = dot(parts(stacked), expander(512), TN)
-    run_log[...] = run_log[...] + last
+    stacked = [jnp.exp(cum), jnp.exp(last - cum) * dt]
+    if fresh:
+        run_log[...] = jnp.broadcast_to(last, (8, 128))
+    else:
+        stacked = [jnp.exp(cum + run_log[:, 0:1])] + stacked
+        run_log[...] = run_log[...] + last
+    first = 256 * (len(stacked) - 2)
+    spread[0 : first + 512, :] = dot(parts(jnp.concatenate(stacked, 1)), expander(512), TN)
     columns = dot(parts(cum), jnp.where(
         (iota((32, 128), 0) < 24) & (iota((32, 128), 0) % 8 == iota((32, 128), 1)), 1.0, 0.0
     ).astype(BF), TN)
@@ -500,7 +501,8 @@
     out_map = jnp.concatenate([act[6, 0:BLK].astype(BF), act[7, 0:BLK].astype(BF)], 1)
     maps_out[...] = out_map
     sc[...] = dot(out_map, in_map, NT)
-    lead[...] = spread[0:256, :] * dot(out_map, run[...].astype(BF))
+    if not fresh:
+        lead[...] = spread[256:512, :] * dot(out_map, run[...].astype(BF))
     low_tri = iota((128, 128), 0) >= iota((128, 128), 1)
     lane_low = iota((BLK, 128), 1) < 64
     for p in range(4):
@@ -524,11 +526,15 @@
         )
         bottom = dot(jnp.concatenate(lower_w, 1), jnp.concatenate([v0, v1], 0))
         gate = tail_out[:, cols]
-        lead[0:128, cols] = (top + lead[0:128, cols]) * gate[0:128]
-        lead[128:256, cols] = (bottom + lead[128:256, cols]) * gate[128:256]
-        tail_out[:, cols] = spread[256:512, cols] * gate
-        scaled[:, cols] = (vals * spread[512:768, cols]).astype(BF)
-    run[...] = run[...] * spread[255:256, :] + dot(in_map, scaled[...], TN)
+        if not fresh:
+            top = top + lead[0:128, cols]
+            bottom = bottom + lead[128:256, cols]
+        lead[0:128, cols] = top * gate[0:128]
+        lead[128:256, cols] = bottom * gate[128:256]
+        tail_out[:, cols] = spread[0:256, cols] * gate
+        scaled[:, cols] = (vals * spread[first + 256 : first + 512, cols]).astype(BF)
+    local = dot(in_map, scaled[...], TN)
+    run[...] = local if fresh else run[...] * spread[511:512, :] + local
 
 
 SCAN_SCRATCH = [
@@ -540,14 +546,24 @@
 ]
 
 
-def fine_main_kernel(later, x, gain, ws, ks, p0, p1, p2, p3, *refs):
-    (
-        x0, x1, x2, lead, tail_out, maps_out, run, run_log, cv_end,
-        wg, wv, wst, taps, bias, decay, cv, act, sc, spread, scaled,
-    ) = refs
-
-    @pl.when(pl.program_id(0) == 0)
+def fine_main_kernel(at, mine, gain, ws, *refs):
+    later = at > 0
+    if later:
+        x0, x1, wg, wv, wst, taps, bias, decay, lead, tail_out, maps_out, run, run_log = refs[:13]
+    else:
+        ks, p0, p1, p2, p3, x0, x1, lead, tail_out, maps_out, run, run_log = refs[:12]
+        wg, wv, wst, taps, bias, decay = refs[12:18]
+    cv, act, sc, spread, scaled = refs[-5:]
+    i = pl.program_id(0)
+
+    @pl.when(i == 0)
     def _():
+        if later:
+            run[...] = x0[...]
+            run_log[...] = x1[...]
+            return
+        run[...] = jnp.zeros_like(run)
+        run_log[...] = jnp.zeros_like(run_log)
         for j in range(4):
             taps[4 + j] = ks[:, j * 128 : (j + 1) * 128] * 0.5
         for j, p in enumerate((p0, p1, p2, p3)):
@@ -557,49 +573,45 @@
             wv[:, cols] = p[0:256, 128:256]
             kv, _, bias[two, :], decay[two, :], wst[two, :] = small_rows(p)
             taps[j] = kv * 0.5
-        if later:
-            run[...] = x0[...]
-            run_log[...] = x1[...]
-            cv[:, 0:16, :] = x2[...]
-        else:
-            rim = jnp.where(lax.axis_index(HEAD) == 0, x0[...].astype(F32), x1[...].astype(F32))
-            begin(rms(rim, gain[...]), wv, ws, cv, run, run_log)
-
+
+    start = pl.multiple_of((i + at) * BLK, BLK)
+    rim = mine[pl.ds(pl.multiple_of(jnp.maximum(start - 16, 0), 16), 16), :].astype(F32)
+    if not later:
+        edge = jnp.where(lax.axis_index(HEAD) == 0, x0[...].astype(F32), x1[...].astype(F32))
+        rim = jnp.where(i == 0, edge, rim)
+    x = jnp.concatenate([rim, mine[pl.ds(start, BLK), :].astype(F32)], 0)
     scan_block(
-        rms(x[...], gain[...]), wg, wv, ws, wst[...].astype(BF), taps, bias[:, 0:1], decay[:, 0:1],
-        lead, tail_out, maps_out, cv, act, sc, spread, scaled, run, run_log,
-    )
-    cv_end[...] = cv[:, 0:16, :]
-
-
-def fine_main(x, gain, scans, ks, packs, extra, later):
-    at = 2 if later else 0
+        False, rms(x, gain[...]), wg, wv, ws, wst[...].astype(BF), taps, bias[:, 0:1],
+        decay[:, 0:1], lead, tail_out, maps_out, cv, act, sc, spread, scaled, run, run_log,
+    )
+
+
+def fine_main(at, blocks, *args):
+    length = blocks * BLK
     rows = [pl.BlockSpec((BLK, n), lambda i: (i, 0)) for n in (512, 512, 256)]
-    return pl.pallas_call(
-        lambda *refs: fine_main_kernel(later, *refs),
-        grid=(2,),
-        in_specs=[pl.BlockSpec((BLK, 256), lambda i: (at + i, 0))] + [VM] * 10,
-        out_specs=rows + [VM] * 3,
+    weights = []
+    if at == 0:
+        weights = [
+            sds((256, 512), BF), sds((256, 512), BF), sds((8, 256)), sds((8, 4, 128)),
+            sds((8, 128)), sds((8, 128)),
+        ]
+    return pl.pallas_call(
+        lambda *refs: fine_main_kernel(at, *refs),
+        grid=(blocks,),
+        in_specs=[VM] * len(args),
+        out_specs=rows + [VM] * (2 + len(weights)),
         out_shape=[
-            sds((512, 512)), sds((512, 512)), sds((512, 256), BF),
-            sds((256, 512)), sds((8, 128)), sds((8, 16, 128)),
-        ],
-        scratch_shapes=[
-            pltpu.VMEM((256, 512), BF),
-            pltpu.VMEM((256, 512), BF),
-            pltpu.VMEM((8, 256), F32),
-            pltpu.VMEM((8, 4, 128), F32),
-            pltpu.VMEM((8, 128), F32),
-            pltpu.VMEM((8, 128), F32),
+            sds((length, 512)), sds((length, 512)), sds((length, 256), BF),
+            sds((256, 512)), sds((8, 128)),
         ]
-        + SCAN_SCRATCH,
+        + weights,
+        scratch_shapes=SCAN_SCRATCH,
         compiler_params=few(16),
-        name="fine_main_b" if later else "fine_main_a",
-    )(x, gain, scans, ks, *packs, *extra)
+    )(*args)
 
 
 def fine_close_kernel(
-    lead_a, lead_b, tail_a, tail_b, maps_a, maps_b, x, s0, s1, s2, s3, p0, p1, p2, p3, merge,
+    lead_a, lead_b, lead_c, tail_a, tail_b, tail_c, maps_a, maps_b, maps_c, x, s0, s1, s2, s3, p0, p1, p2, p3, merge,
     merged, end_rows, lead, tail, maps, hidden, state, wo, norm,
 ):
     i = pl.program_id(0)
@@ -608,9 +620,13 @@
     def _():
         lead[...], tail[...], maps[...] = lead_a[...], tail_a[...], maps_a[...]
 
-    @pl.when(i >= 2)
+    @pl.when(i == 2)
     def _():
         lead[...], tail[...], maps[...] = lead_b[...], tail_b[...], maps_b[...]
+
+    @pl.when(i == 3)
+    def _():
+        lead[...], tail[...], maps[...] = lead_c[...], tail_c[...], maps_c[...]
 
     @pl.when(i == 0)
     def _():
@@ -650,7 +666,8 @@
     def halves(width):
         return [
             pl.BlockSpec((BLK, width), lambda i: (jnp.minimum(i, 1), 0)),
-            pl.BlockSpec((BLK, width), lambda i: (jnp.maximum(i - 2, 0), 0)),
+            pl.BlockSpec((BLK, width), lambda i: (0, 0)),
+            pl.BlockSpec((BLK, width), lambda i: (0, 0)),
         ]
 
     return pl.pallas_call(
@@ -685,18 +702,18 @@
 
 def coarse_main_kernel(kind, pieces, gain, wg, wv, ws, wst, taps, both, *refs):
     qs, refs = refs[:pieces], refs[pieces:]
-    xs, sems, cv, act, sc, spread, scaled = refs[-7:]
+    xs, sems, rims, cv, act, sc, spread, scaled = refs[-8:]
     y, c = lax.axis_index("y"), lax.axis_index("c")
     h = 2 * y + c
     if kind == "near":
-        ra, rb, lead, tail_out, maps_out, share, run, run_log = refs[:-7]
+        ra, rb, lead, tail_out, maps_out, share, run, run_log = refs[:-8]
     elif kind == "far_1":
-        re, lead, tail_out, maps_out, share, run, run_log, ends = refs[:-7]
+        re, lead, tail_out, maps_out, share, run, run_log, ends = refs[:-8]
     else:
         (
             ends_1, rd, near_run, near_log, run_1, run_log_1,
             lead, tail_out, maps_out, share, run, run_log, far_run, far_log, message,
-        ) = refs[:-7]
+        ) = refs[:-8]
     i = pl.program_id(0)
 
     @pl.when(i == 0)
@@ -709,16 +726,23 @@
             rim = re[...].astype(F32) if kind == "far_1" else rd[...].astype(F32)
             if kind == "far_2":
                 rim = jnp.where(c == 0, ends_1[...].astype(F32), rim)
-        begin(rms(rim, gain[...]), wv, ws, cv, run, run_log)
+        rims[...] = rim
+        if kind == "near":
+            run[...] = jnp.zeros_like(run)
+            run_log[...] = jnp.zeros_like(run_log)
         for copy in copies:
             copy.wait()
         if kind == "far_1":
             ends[...] = xs[0, 240:256, :]
 
     share[...] = xs[i, :, pl.ds(pl.multiple_of(h * 256, 256), 256)]
+    rim = rims[...]
+    if kind == "near":
+        rim = jnp.where(i == 0, rim, xs[0, 240:256, :].astype(F32))
+    x = jnp.concatenate([rim, xs[i].astype(F32)], 0)
     scan_block(
-        rms(xs[i], gain[...]), wg, wv, ws, wst[...], taps, both[0:8, 0:1], both[8:16, 0:1],
-        lead, tail_out, maps_out, cv, act, sc, spread, scaled, run, run_log,
+        kind != "near", rms(x, gain[...]), wg, wv, ws, wst[...], taps, both[0:8, 0:1],
+        both[8:16, 0:1], lead, tail_out, maps_out, cv, act, sc, spread, scaled, run, run_log,
     )
 
     if kind == "far_2":
@@ -768,7 +792,11 @@
             sds((8, 128)),
         ]
         + last,
-        scratch_shapes=[pltpu.VMEM((blocks, 256, 1024), BF), pltpu.SemaphoreType.DMA((blocks,))]
+        scratch_shapes=[
+            pltpu.VMEM((blocks, 256, 1024), BF),
+            pltpu.SemaphoreType.DMA((blocks,)),
+            pltpu.VMEM((16, 1024), F32),
+        ]
         + SCAN_SCRATCH,
         compiler_params=few(16),
     )(gain, *weights, wst, taps, both, *pieces, *extra)
@@ -965,31 +993,31 @@
     coarse_value, coarse_scans, coarse_steps, coarse_kernel, coarse_taps, coarse_bias,
     coarse_decay, coarse_norm, coarse_output,
 ):
-    pack, ends = packed(
-        fine_bias[None], fine_decay[None], fine_gate, fine_value, fine_output, fine_steps.T, fine_kernel,
-        fine_norm[None], tokens,
+    pack, ends, chunk, gain, scans, ks = packed(
+        fine_bias[None], fine_decay[None], fine_gate, fine_value, fine_output, fine_steps.T,
+        fine_kernel, fine_norm[None], tokens, fine_gain[None], fine_scans, fine_taps,
     )
     rim = passed(ends, SEQ, [(i, i + 1) for i in range(31)])
     packs = [pack] + [swapped(pack, m) for m in (1, 2, 3)]
-    later, later_total, resident, (l0, t0, own, own_total, message) = fine_states(
-        tokens, rim, fine_gain[None], pack, fine_scans, fine_taps
-    )
-    mine, mine_rim, gain, scans, ks = resident
+    later, later_total, (mine, mine_rim), (l0, t0, own, own_total, message) = fine_states(
+        tokens, chunk, rim, gain, pack, scans, ks
+    )
     got = round_of(message, "x")
-    first = fine_main(mine, gain, scans, ks, packs, (rim, mine_rim, t0), False)
+    first = fine_main(0, 2, mine, gain, scans, ks, *packs, rim, mine_rim)
     *prior, own, own_total, message = middle_stage("x", 4, own, own_total, (), got)
     got = [passed(message, "u", [(0, 1), (1, 0)])]
     params = coarse_params(
         coarse_bias[None], coarse_decay[None], coarse_kernel, coarse_taps, coarse_gain[None],
         coarse_steps.T, coarse_norm[None],
     )
+    second = fine_main(2, 1, mine, gain, scans, *first[3:])
     *prior, own, own_total, message = middle_stage("u", 2, own, own_total, prior, got)
     got = round_of(message, "z")
-    second = fine_main(mine, gain, scans, ks, packs, first[3:], True)
+    third = fine_main(3, 1, mine, gain, scans, *second[3:], *first[5:])
     subs = last_stage(own, own_total, prior, got, l0, t0, later, later_total)
     states = [subs[0]] + [swapped(subs[m], m) for m in (1, 2, 3)]
     merged, end_rows = fine_close(
-        (first[0], second[0]), (first[1], second[1]), (first[2], second[2]), mine, states, packs,
+        *([call[j] for call in (first, second, third)] for j in range(3)), mine, states, packs,
         merge_weight,
     )
 

time: 153 us -> 150 us (0.980)
  Pallas kernels: 43.3 us -> 40.2 us
    pallas_call x3, Pallas kernels: 13.2 us -> 11.5 us  [coarse_main(): pl.pallas_call(lambda *refs: coarse_main_kernel(kind, blocks, *refs), gri...]
    pallas_call x4 -> x5, Pallas kernels: 18.4 us -> 16.9 us  [the longest x3 9.07 us: fine_main(): pl.pallas_call(lambda *refs: fine_main_kernel(at, *refs), grid=(blocks,),...]
  transfers between devices with their start and end apart: 26 -> 26, of which waited for: 10 -> 10; matrix products, arithmetic and copies ran while one was open for 0% -> 0% of each run, Pallas kernels for 20% -> 18%
where the time goes in v6:
time: 150 us; the launch traced here: 149 us
  starting transfers between devices  41.7 us (28%)
  Pallas kernels  40.2 us (27%)
  waiting for transfers between devices  33.6 us (22%)
  blocking collectives  33.6 us (22%)
    ppermute x26, starting transfers between devices, passed(): return lax.ppermute(x, axes, pairs)  41.7 us
    ppermute x26, waiting for transfers between devices, passed(): return lax.ppermute(x, axes, pairs)  33.6 us
    all_to_all x1, blocking collectives, shards(): got = lax.all_to_all(message, SEQ, split_axis=0, concat_axis=0, tiled=True)  19.7 us
    all_to_all x1, blocking collectives, shards(): lax.all_to_all(prefix(got), SEQ, split_axis=0, concat_axis=0, tiled=True)  13.9 us
    pallas_call x3, Pallas kernels, coarse_main(): pl.pallas_call(lambda *refs: coarse_main_kernel(kind, blocks, *refs), gri...  11.5 us
    pallas_call x3, Pallas kernels, fine_main(): pl.pallas_call(lambda *refs: fine_main_kernel(at, *refs), grid=(blocks,),...  9.07 us
    pallas_call x1, Pallas kernels, fine_states(): pl.pallas_call(later_chunks_kernel, grid=(3,), in_specs=[HBM] + [VM] * 5,...  6.44 us
    pallas_call x1, Pallas kernels, fine_close(): pl.pallas_call(fine_close_kernel, grid=(4,), in_specs=halves(512) + halve...  3.48 us
  transfers between devices with their start and end apart: 26, of which 10 were waited for; matrix products, arithmetic and copies ran while one was open for 0% of the time, Pallas kernels for 18%

profile of v6, /device:TPU:1, one launch (start us, length us, event | category | flops | bytes accessed | tf_op | source)
XLA Modules:
  0.0 149.4 jit_solution(8539077433477506982)
XLA Ops:
  0.0 1.4 pack.1
  1.4 3.9 %collective-permute-start.3 = (bf16[16,256]{1,0:T(8,128)(2,1)S(1)}, bf16[16,256]{1,0:T(8,128)(2,1)S(1)}, u32[]{:S(2)}, u32[]{:S(2)}) collective-permute-start(bf16[16,256]{1,0:T(8,128)(2,1)S(1)} %get-tuple-element.107), channel_id=1, source_target_pairs={{0,4},{4,8},{8,12},{12,16},{16,20},{20,24},{24,28},{28,32},{32,36}... | collective-permute-start | bytes 24584 | tf_op jit(solution)/shard_map/ppermute | solution.py:976
  5.4 6.4 %later_chunks.1 = (f32[3,256,128]{2,1,0:T(8,128)S(1)}, f32[3,8,128]{2,1,0:T(8,128)S(1)}, bf16[1024,256]{1,0:T(8,128)(2,1)S(1)}, bf16[1024,256]{1,0:T(8,128)(2,1)S(1)}, bf16[16,256]{1,0:T(8,128)(2,1)S(1)}) custom-call(bf16[4096,256]{1,0:T(8,128)(2,1)} %tokens.3, bf16[1040,256]{1,0:T(8,128)(2,1)S(1)} %get-tuple-element.101.chunk_0, ...), custom_call_target="tpu_custom_call" | custom-call | tf_op jit(solution)/shard_map/later_chunks/pallas_call | solution.py:354
  11.8 2.1 %first_chunk.1 = (f32[256,128]{1,0:T(8,128)S(1)}, f32[8,128]{1,0:T(8,128)S(1)}, f32[256,128]{1,0:T(8,128)S(1)}, f32[8,128]{1,0:T(8,128)S(1)}, bf16[272,128]{1,0:T(8,128)(2,1)S(1)}) custom-call(bf16[1024,256]{1,0:T(8,128)(2,1)S(1)} %get-tuple-element.128.x, bf16[16,256]{1,0:T(8,128)(2,1)S(1)} %collective-permute-done.3.refs_8_.rim, ...), custom_call_target="tpu_custom_call" | custom-call | tf_op jit(solution)/shard_map/first_chunk/pallas_call | solution.py:372
  13.9 4.2 %collective-permute-start.6 = (bf16[272,128]{1,0:T(8,128)(2,1)S(1)}, bf16[272,128]{1,0:T(8,128)(2,1)S(1)}, u32[]{:S(2)}, u32[]{:S(2)}) collective-permute-start(bf16[272,128]{1,0:T(8,128)(2,1)S(1)} %get-tuple-element.133), channel_id=1, source_target_pairs={{0,12},{4,0},{8,4},{12,8},{1,13},{5,1},{9,5},{13,9},{2,14},{6,2},{... | collective-permute-start | bytes 208904 | tf_op jit(solution)/shard_map/ppermute | solution.py:976
  18.1 0.7 collective-permute-start.4
  18.7 1.8 %collective-permute-start.2 = (bf16[416,256]{1,0:T(8,128)(2,1)S(1)}, bf16[416,256]{1,0:T(8,128)(2,1)S(1)}, u32[]{:S(2)}, u32[]{:S(2)}) collective-permute-start(bf16[416,256]{1,0:T(8,128)(2,1)S(1)} %get-tuple-element.103.pack.refs_4_.p0), channel_id=1, source_target_pairs={{0,3},{1,2},{2,1},{3,0},{4,7},{5,6},{6,5},{7,4},{8,11},{9,10},{10,... | collective-permute-start | bytes 638984 | tf_op jit(solution)/shard_map/ppermute | solution.py:976
  20.5 2.3 %collective-permute-done.5.refs_3_ = bf16[272,128]{1,0:T(8,128)(2,1)S(1)} collective-permute-done((bf16[272,128]{1,0:T(8,128)(2,1)S(1)}, bf16[272,128]{1,0:T(8,128)(2,1)S(1)}, u32[]{:S(2)}, u32[]{:S(2)}) %collective-permute-start.5) | collective-permute-done | bytes 69664 | tf_op jit(solution)/shard_map/ppermute | solution.py:976
  22.8 0.4 collective-permute-done.4.refs_2_
  23.2 0.1 shard_map.229
  23.3 1.8 %collective-permute-start.7 = (bf16[272,128]{1,0:T(8,128)(2,1)S(1)}, bf16[272,128]{1,0:T(8,128)(2,1)S(1)}, u32[]{:S(2)}, u32[]{:S(2)}) collective-permute-start(bf16[272,128]{1,0:T(8,128)(2,1)S(1)} %get-tuple-element.138), channel_id=1, source_target_pairs={{0,16},{16,0},{1,17},{17,1},{2,18},{18,2},{3,19},{19,3},{4,20},{20... | collective-permute-start | bytes 208904 | tf_op jit(solution)/shard_map/ppermute | solution.py:976
  25.1 1.0 collective-permute-start.1
  26.1 2.9 %collective-permute-start = (bf16[416,256]{1,0:T(8,128)(2,1)S(1)}, bf16[416,256]{1,0:T(8,128)(2,1)S(1)}, u32[]{:S(2)}, u32[]{:S(2)}) collective-permute-start(bf16[416,256]{1,0:T(8,128)(2,1)S(1)} %get-tuple-element.103.pack.refs_4_.p0), channel_id=1, source_target_pairs={{0,1},{1,0},{2,3},{3,2},{4,5},{5,4},{6,7},{7,6},{8,9},{9,8},{10,11... | collective-permute-start | bytes 638984 | tf_op jit(solution)/shard_map/ppermute | solution.py:976
  29.1 0.1 shard_map.230
  29.1 3.2 %collective-permute-start.10 = (bf16[272,128]{1,0:T(8,128)(2,1)S(1)}, bf16[272,128]{1,0:T(8,128)(2,1)S(1)}, u32[]{:S(2)}, u32[]{:S(2)}) collective-permute-start(bf16[272,128]{1,0:T(8,128)(2,1)S(1)} %get-tuple-element.143), channel_id=1, source_target_pairs={{0,96},{32,0},{64,32},{96,64},{1,97},{33,1},{65,33},{97,65},{2,98}... | collective-permute-start | bytes 208904 | tf_op jit(solution)/shard_map/ppermute | solution.py:976
  32.3 0.4 collective-permute-start.9
  32.7 1.0 collective-permute-done.10.r3
  33.7 0.6 collective-permute-start.8
  34.3 2.7 %collective-permute-done.9.r2 = bf16[272,128]{1,0:T(8,128)(2,1)S(1)} collective-permute-done((bf16[272,128]{1,0:T(8,128)(2,1)S(1)}, bf16[272,128]{1,0:T(8,128)(2,1)S(1)}, u32[]{:S(2)}, u32[]{:S(2)}) %collective-permute-start.9) | collective-permute-done | bytes 69664 | tf_op jit(solution)/shard_map/ppermute | solution.py:976
  37.0 1.4 collective-permute-done.8.r1
  38.4 0.1 chain_last.1
  38.5 5.8 %collective-permute-start.11 = (bf16[256,128]{1,0:T(8,128)(2,1)S(1)}, bf16[256,128]{1,0:T(8,128)(2,1)S(1)}, u32[]{:S(2)}, u32[]{:S(2)}) collective-permute-start(bf16[256,128]{1,0:T(8,128)(2,1)S(1)} %get-tuple-element.147), channel_id=1, source_target_pairs={{0,1},{1,0},{2,3},{3,2},{4,5},{5,4},{6,7},{7,6},{8,9},{9,8},{10,11... | collective-permute-start | bytes 196616 | tf_op jit(solution)/shard_map/ppermute | solution.py:976
  44.3 0.4 collective-permute-start.12
  44.7 1.3 collective-permute-start.13
  46.1 4.2 %shard_map.226 = (f32[512,512]{1,0:T(8,128)S(1)}, f32[512,512]{1,0:T(8,128)S(1)}, bf16[512,256]{1,0:T(8,128)(2,1)S(1)}, f32[256,512]{1,0:T(8,128)S(1)}, f32[8,12...) custom-call(bf16[1024,256]{1,0:T(8,128)(2,1)S(1)} %get-tuple-element, ...), custom_call_target="tpu_custom_call" | custom-call | tf_op jit(solution)/shard_map/pallas_call | solution.py:598
  50.3 0.0 copy-start.4
  50.3 2.0 %shard_map.227 = (f32[256,512]{1,0:T(8,128)S(1)}, f32[256,512]{1,0:T(8,128)S(1)}, bf16[256,256]{1,0:T(8,128)(2,1)S(1)}, f32[256,512]{1,0:T(8,128)S(1)}, f32[8,128]{1,0:T(8,128)S(1)}) custom-call(bf16[1024,256]{1,0:T(8,128)(2,1)S(1)} %get-tuple-element.106.refs_0_.x, f32[1,256]{1,0:T(1,128)S(1)} %get-tuple-element.102.gain.refs_1_, ...), custom_call_target="tpu_custom_call" | custom-call | tf_op jit(solution)/shard_map/pallas_call | solution.py:598
  52.3 2.8 %shard_map.228 = (f32[256,512]{1,0:T(8,128)S(1)}, f32[256,512]{1,0:T(8,128)S(1)}, bf16[256,256]{1,0:T(8,128)(2,1)S(1)}, f32[256,512]{1,0:T(8,128)}, f32[8,128]{1,0:T(8,128)}) custom-call(bf16[1024,256]{1,0:T(8,128)(2,1)S(1)} %get-tuple-element.106.refs_0_.x, f32[1,256]{1,0:T(1,128)S(1)} %get-tuple-element.102.gain.refs_1_, ...), custom_call_target="tpu_custom_call" | custom-call | tf_op jit(solution)/shard_map/pallas_call | solution.py:598
  55.2 0.0 copy-start
  55.2 0.0 copy-start.1
  55.2 0.0 copy-start.2
  55.2 3.5 %fine_close.1 = (bf16[256,1024]{1,0:T(8,128)(2,1)S(1)}, bf16[16,1024]{1,0:T(8,128)(2,1)S(1)}) custom-call(f32[512,512]{1,0:T(8,128)S(1)} %get-tuple-element.109.lead_a, f32[256,512]{1,0:T(8,128)S(1)} %get-tuple-element.118.lead_b, f32[256,512]{1,0:T(8,128)S(1)} %get-tuple-element.121.lead_c, f32[512,512]{1,0:T(8,128)S(1)} %get-tuple-element.122.tail_a, ...), custom_call_target="tpu_custom_call" | custom-call | tf_op jit(solution)/shard_map/fine_close/pallas_call | solution.py:673
  58.7 0.5 collective-permute-start.17
  59.2 0.4 collective-permute-start.14
  59.6 12.5 %collective-permute-done.17.refs_7_ = bf16[256,1024]{1,0:T(8,128)(2,1)S(1)} collective-permute-done((bf16[256,1024]{1,0:T(8,128)(2,1)S(1)}, bf16[256,1024]{1,0:T(8,128)(2,1)S(1)}, u32[]{:S(2)}, u32[]{:S(2)}) %collective-permute-start.17) | collective-permute-done | bytes 524320 | tf_op jit(solution)/shard_map/ppermute | solution.py:976
  72.2 1.0 collective-permute-start.19
  73.1 2.2 %collective-permute-start.15 = (bf16[16,1024]{1,0:T(8,128)(2,1)S(1)}, bf16[16,1024]{1,0:T(8,128)(2,1)S(1)}, u32[]{:S(2)}, u32[]{:S(2)}) collective-permute-start(bf16[16,1024]{1,0:T(8,128)(2,1)S(1)} %get-tuple-element.151), channel_id=1, source_target_pairs={{1,2},{3,4},{5,6},{7,8},{9,10},{11,12},{13,14},{15,16},{17,18},{19... | collective-permute-start | bytes 98312 | tf_op jit(solution)/shard_map/ppermute | solution.py:976
  75.3 1.0 collective-permute-done.15.refs_9_.came
  76.4 0.1 collective-permute-start.18
  76.5 2.7 %collective-permute-start.16 = (bf16[16,1024]{1,0:T(8,128)(2,1)S(1)}, bf16[16,1024]{1,0:T(8,128)(2,1)S(1)}, u32[]{:S(2)}, u32[]{:S(2)}) collective-permute-start(bf16[16,1024]{1,0:T(8,128)(2,1)S(1)} %collective-permute-done.15.refs_9_.came), channel_id=1, source_target_pairs={{0,1},{1,0},{2,3},{3,2},{4,5},{5,4},{6,7},{7,6},{8,9},{9,8},{10,11... | collective-permute-start | bytes 98312 | tf_op jit(solution)/shard_map/ppermute | solution.py:976
  79.2 0.1 collective-permute-done.18.refs_8_
  79.2 1.8 %collective-permute-start.20 = (bf16[16,1024]{1,0:T(8,128)(2,1)S(1)}, bf16[16,1024]{1,0:T(8,128)(2,1)S(1)}, u32[]{:S(2)}, u32[]{:S(2)}) collective-permute-start(bf16[16,1024]{1,0:T(8,128)(2,1)S(1)} %collective-permute-done.18.refs_8_), channel_id=1, source_target_pairs={{0,1},{1,0},{2,3},{3,2},{4,5},{5,4},{6,7},{7,6},{8,9},{9,8},{10,11... | collective-permute-start | bytes 98312 | tf_op jit(solution)/shard_map/ppermute | solution.py:976
  81.0 1.0 coarse_params.1
  82.0 5.9 %shard_map.231 = (f32[512,512]{1,0:T(8,128)S(1)}, f32[512,512]{1,0:T(8,128)S(1)}, bf16[512,256]{1,0:T(8,128)(2,1)S(1)}, bf16[512,256]{1,0:T(8,128)(2,1)S(1)}, f3...) custom-call(f32[1,1024]{1,0:T(1,128)S(1)} %get-tuple-element.97.refs_0_, bf16[1024,512]{1,0:T(8,128)(2,1)S(1)} %copy-done, ...), custom_call_target="tpu_custom_call" | custom-call | tf_op jit(solution)/shard_map/pallas_call | solution.py:781
  88.0 2.8 %shard_map.232 = (f32[256,512]{1,0:T(8,128)S(1)}, f32[256,512]{1,0:T(8,128)S(1)}, bf16[256,256]{1,0:T(8,128)(2,1)S(1)}, bf16[256,256]{1,0:T(8,128)(2,1)S(1)}, f3...) custom-call(f32[1,1024]{1,0:T(1,128)S(1)} %get-tuple-element.97.refs_0_, ...), custom_call_target="tpu_custom_call" | custom-call | tf_op jit(solution)/shard_map/pallas_call | solution.py:781
  90.7 2.9 %shard_map.233 = (f32[256,512]{1,0:T(8,128)S(1)}, f32[256,512]{1,0:T(8,128)S(1)}, bf16[256,256]{1,0:T(8,128)(2,1)S(1)}, bf16[256,256]{1,0:T(8,128)(2,1)S(1)}, f3...) custom-call(f32[1,1024]{1,0:T(1,128)S(1)} %get-tuple-element.97.refs, ...), custom_call_target="tpu_custom_call" | custom-call | tf_op jit(solution)/shard_map/pallas_call | solution.py:781
  93.6 0.0 copy-start.3
  93.6 19.7 %all_to_all.10.got = bf16[32,24,256]{2,1,0:T(8,128)(2,1)S(1)} all-to-all(bf16[32,24,256]{2,1,0:T(8,128)(2,1)S(1)} %get-tuple-element.163), channel_id=1, replica_groups=mesh['z'=4,'u'=2,'x'=4,'y'=2,'c'=2] {'z','u','x'}, dimensions={0} | all-to-all | bytes 786432 | tf_op jit(solution)/shard_map/all_to_all | solution.py:1042
  113.3 0.1 prefix.1
  113.4 13.9 %all_to_all.11.refs_3_.refs_6_ = bf16[32,16,256]{2,1,0:T(8,128)(2,1)S(1)} all-to-all(bf16[32,16,256]{2,1,0:T(8,128)(2,1)S(1)} %prefix.1), channel_id=1, replica_groups=mesh['z'=4,'u'=2,'x'=4,'y'=2,'c'=2] {'z','u','x'}, dimensions={0} | all-to-all | bytes 524288 | tf_op jit(solution)/shard_map/all_to_all | solution.py:1043
  127.4 1.3 coarse_close_far.1
  128.7 2.8 %collective-permute-start.23 = (bf16[528,256]{1,0:T(8,128)(2,1)S(1)}, bf16[528,256]{1,0:T(8,128)(2,1)S(1)}, u32[]{:S(2)}, u32[]{:S(2)}) collective-permute-start(bf16[528,256]{1,0:T(8,128)(2,1)S(1)} %get-tuple-element.185), channel_id=1, source_target_pairs={{0,1},{1,0},{2,3},{3,2},{4,5},{5,4},{6,7},{7,6},{8,9},{9,8},{10,11... | collective-permute-start | bytes 811016 | tf_op jit(solution)/shard_map/ppermute | solution.py:976
  131.5 1.2 coarse_close_near.1
  132.7 0.1 collective-permute-start.22
  132.8 0.7 close_rest.1
  133.5 0.6 collective-permute-start.21
  134.1 0.1 shard_map.235
  134.2 0.1 collective-permute-start.24
  134.3 0.0 collective-permute-done.22.came
  134.3 0.1 shard_map.234
  134.4 1.5 collective-permute-start.25
  135.9 6.4 %collective-permute-done.24.far_a = bf16[528,256]{1,0:T(8,128)(2,1)S(1)} collective-permute-done((bf16[528,256]{1,0:T(8,128)(2,1)S(1)}, bf16[528,256]{1,0:T(8,128)(2,1)S(1)}, u32[]{:S(2)}, u32[]{:S(2)}) %collective-permute-start.24) | collective-permute-done | bytes 270368 | tf_op jit(solution)/shard_map/ppermute | solution.py:976
  142.3 5.8 %collective-permute-done.25.far_b = bf16[528,256]{1,0:T(8,128)(2,1)S(1)} collective-permute-done((bf16[528,256]{1,0:T(8,128)(2,1)S(1)}, bf16[528,256]{1,0:T(8,128)(2,1)S(1)}, u32[]{:S(2)}, u32[]{:S(2)}) %collective-permute-start.25) | collective-permute-done | bytes 270368 | tf_op jit(solution)/shard_map/ppermute | solution.py:976
  148.1 1.3 final.1
  (22 shorter events, 0.1 us)
Async XLA Ops:
  1.4 10.4 %collective-permute-start.3 = (bf16[16,256]{1,0:T(8,128)(2,1)S(1)}, bf16[16,256]{1,0:T(8,128)(2,1)S(1)}, u32[]{:S(2)}, u32[]{:S(2)}) collective-permute-start(bf16[16,256]{1,0:T(8,128)(2,1)S(1)} %get-tuple-element.107), channel_id=1, source_target_pairs={{0,4},{4,8},{8,12},{12,16},{16,20},{20,24},{24,28},{28,32},{32,36}... | collective-permute-start | bytes 24584 | tf_op jit(solution)/shard_map/ppermute | solution.py:976
  13.9 6.6 %collective-permute-start.6 = (bf16[272,128]{1,0:T(8,128)(2,1)S(1)}, bf16[272,128]{1,0:T(8,128)(2,1)S(1)}, u32[]{:S(2)}, u32[]{:S(2)}) collective-permute-start(bf16[272,128]{1,0:T(8,128)(2,1)S(1)} %get-tuple-element.133), channel_id=1, source_target_pairs={{0,12},{4,0},{8,4},{12,8},{1,13},{5,1},{9,5},{13,9},{2,14},{6,2},{... | collective-permute-start | bytes 208904 | tf_op jit(solution)/shard_map/ppermute | solution.py:976
  18.1 4.8 %collective-permute-start.5 = (bf16[272,128]{1,0:T(8,128)(2,1)S(1)}, bf16[272,128]{1,0:T(8,128)(2,1)S(1)}, u32[]{:S(2)}, u32[]{:S(2)}) collective-permute-start(bf16[272,128]{1,0:T(8,128)(2,1)S(1)} %get-tuple-element.133), channel_id=1, source_target_pairs={{0,8},{4,12},{8,0},{12,4},{1,9},{5,13},{9,1},{13,5},{2,10},{6,14},... | collective-permute-start | bytes 208904 | tf_op jit(solution)/shard_map/ppermute | solution.py:976
  18.1 5.1 %collective-permute-start.4 = (bf16[272,128]{1,0:T(8,128)(2,1)S(1)}, bf16[272,128]{1,0:T(8,128)(2,1)S(1)}, u32[]{:S(2)}, u32[]{:S(2)}) collective-permute-start(bf16[272,128]{1,0:T(8,128)(2,1)S(1)} %get-tuple-element.133), channel_id=1, source_target_pairs={{0,4},{4,8},{8,12},{12,0},{1,5},{5,9},{9,13},{13,1},{2,6},{6,10},{... | collective-permute-start | bytes 208904 | tf_op jit(solution)/shard_map/ppermute | solution.py:976
  18.7 26.0 %collective-permute-start.2 = (bf16[416,256]{1,0:T(8,128)(2,1)S(1)}, bf16[416,256]{1,0:T(8,128)(2,1)S(1)}, u32[]{:S(2)}, u32[]{:S(2)}) collective-permute-start(bf16[416,256]{1,0:T(8,128)(2,1)S(1)} %get-tuple-element.103.pack.refs_4_.p0), channel_id=1, source_target_pairs={{0,3},{1,2},{2,1},{3,0},{4,7},{5,6},{6,5},{7,4},{8,11},{9,10},{10,... | collective-permute-start | bytes 638984 | tf_op jit(solution)/shard_map/ppermute | solution.py:976
  23.3 5.7 %collective-permute-start.7 = (bf16[272,128]{1,0:T(8,128)(2,1)S(1)}, bf16[272,128]{1,0:T(8,128)(2,1)S(1)}, u32[]{:S(2)}, u32[]{:S(2)}) collective-permute-start(bf16[272,128]{1,0:T(8,128)(2,1)S(1)} %get-tuple-element.138), channel_id=1, source_target_pairs={{0,16},{16,0},{1,17},{17,1},{2,18},{18,2},{3,19},{19,3},{4,20},{20... | collective-permute-start | bytes 208904 | tf_op jit(solution)/shard_map/ppermute | solution.py:976
  25.1 21.0 %collective-permute-start.1 = (bf16[416,256]{1,0:T(8,128)(2,1)S(1)}, bf16[416,256]{1,0:T(8,128)(2,1)S(1)}, u32[]{:S(2)}, u32[]{:S(2)}) collective-permute-start(bf16[416,256]{1,0:T(8,128)(2,1)S(1)} %get-tuple-element.103.pack.refs_4_.p0), channel_id=1, source_target_pairs={{0,2},{1,3},{2,0},{3,1},{4,6},{5,7},{6,4},{7,5},{8,10},{9,11},{10,... | collective-permute-start | bytes 638984 | tf_op jit(solution)/shard_map/ppermute | solution.py:976
  26.1 20.0 %collective-permute-start = (bf16[416,256]{1,0:T(8,128)(2,1)S(1)}, bf16[416,256]{1,0:T(8,128)(2,1)S(1)}, u32[]{:S(2)}, u32[]{:S(2)}) collective-permute-start(bf16[416,256]{1,0:T(8,128)(2,1)S(1)} %get-tuple-element.103.pack.refs_4_.p0), channel_id=1, source_target_pairs={{0,1},{1,0},{2,3},{3,2},{4,5},{5,4},{6,7},{7,6},{8,9},{9,8},{10,11... | collective-permute-start | bytes 638984 | tf_op jit(solution)/shard_map/ppermute | solution.py:976
  29.1 4.6 %collective-permute-start.10 = (bf16[272,128]{1,0:T(8,128)(2,1)S(1)}, bf16[272,128]{1,0:T(8,128)(2,1)S(1)}, u32[]{:S(2)}, u32[]{:S(2)}) collective-permute-start(bf16[272,128]{1,0:T(8,128)(2,1)S(1)} %get-tuple-element.143), channel_id=1, source_target_pairs={{0,96},{32,0},{64,32},{96,64},{1,97},{33,1},{65,33},{97,65},{2,98}... | collective-permute-start | bytes 208904 | tf_op jit(solution)/shard_map/ppermute | solution.py:976
  32.3 4.7 %collective-permute-start.9 = (bf16[272,128]{1,0:T(8,128)(2,1)S(1)}, bf16[272,128]{1,0:T(8,128)(2,1)S(1)}, u32[]{:S(2)}, u32[]{:S(2)}) collective-permute-start(bf16[272,128]{1,0:T(8,128)(2,1)S(1)} %get-tuple-element.143), channel_id=1, source_target_pairs={{0,64},{32,96},{64,0},{96,32},{1,65},{33,97},{65,1},{97,33},{2,66}... | collective-permute-start | bytes 208904 | tf_op jit(solution)/shard_map/ppermute | solution.py:976
  33.7 4.7 %collective-permute-start.8 = (bf16[272,128]{1,0:T(8,128)(2,1)S(1)}, bf16[272,128]{1,0:T(8,128)(2,1)S(1)}, u32[]{:S(2)}, u32[]{:S(2)}) collective-permute-start(bf16[272,128]{1,0:T(8,128)(2,1)S(1)} %get-tuple-element.143), channel_id=1, source_target_pairs={{0,32},{32,64},{64,96},{96,0},{1,33},{33,65},{65,97},{97,1},{2,34}... | collective-permute-start | bytes 208904 | tf_op jit(solution)/shard_map/ppermute | solution.py:976
  38.5 16.6 %collective-permute-start.11 = (bf16[256,128]{1,0:T(8,128)(2,1)S(1)}, bf16[256,128]{1,0:T(8,128)(2,1)S(1)}, u32[]{:S(2)}, u32[]{:S(2)}) collective-permute-start(bf16[256,128]{1,0:T(8,128)(2,1)S(1)} %get-tuple-element.147), channel_id=1, source_target_pairs={{0,1},{1,0},{2,3},{3,2},{4,5},{5,4},{6,7},{7,6},{8,9},{9,8},{10,11... | collective-permute-start | bytes 196616 | tf_op jit(solution)/shard_map/ppermute | solution.py:976
  44.3 10.8 %collective-permute-start.12 = (bf16[256,128]{1,0:T(8,128)(2,1)S(1)}, bf16[256,128]{1,0:T(8,128)(2,1)S(1)}, u32[]{:S(2)}, u32[]{:S(2)}) collective-permute-start(bf16[256,128]{1,0:T(8,128)(2,1)S(1)} %get-tuple-element.148), channel_id=1, source_target_pairs={{0,2},{1,3},{2,0},{3,1},{4,6},{5,7},{6,4},{7,5},{8,10},{9,11},{10,... | collective-permute-start | bytes 196616 | tf_op jit(solution)/shard_map/ppermute | solution.py:976
  44.7 10.4 %collective-permute-start.13 = (bf16[256,128]{1,0:T(8,128)(2,1)S(1)}, bf16[256,128]{1,0:T(8,128)(2,1)S(1)}, u32[]{:S(2)}, u32[]{:S(2)}) collective-permute-start(bf16[256,128]{1,0:T(8,128)(2,1)S(1)} %get-tuple-element.149), channel_id=1, source_target_pairs={{0,3},{1,2},{2,1},{3,0},{4,7},{5,6},{6,5},{7,4},{8,11},{9,10},{10,... | collective-permute-start | bytes 196616 | tf_op jit(solution)/shard_map/ppermute | solution.py:976
  50.3 4.9 %copy-start.4 = (bf16[1024,1024]{1,0:T(8,128)(2,1)S(1)}, bf16[1024,1024]{1,0:T(8,128)(2,1)}, u32[]{:S(2)}) copy-start(bf16[1024,1024]{1,0:T(8,128)(2,1)} %merge.1) | copy-start | bytes 6291460
  55.2 26.8 %copy-start = (bf16[1024,512]{1,0:T(8,128)(2,1)S(1)}, bf16[1024,512]{1,0:T(8,128)(2,1)}, u32[]{:S(2)}) copy-start(bf16[1024,512]{1,0:T(8,128)(2,1)} %refs_1_.5) | copy-start | bytes 3145732
  55.2 26.8 %copy-start.1 = (bf16[1024,512]{1,0:T(8,128)(2,1)S(1)}, bf16[1024,512]{1,0:T(8,128)(2,1)}, u32[]{:S(2)}) copy-start(bf16[1024,512]{1,0:T(8,128)(2,1)} %refs_2_.5) | copy-start | bytes 3145732
  55.2 26.8 %copy-start.2 = (bf16[1024,512]{1,0:T(8,128)(2,1)S(1)}, bf16[1024,512]{1,0:T(8,128)(2,1)}, u32[]{:S(2)}) copy-start(bf16[1024,512]{1,0:T(8,128)(2,1)} %refs_3_.5) | copy-start | bytes 3145732
  58.7 13.4 %collective-permute-start.17 = (bf16[256,1024]{1,0:T(8,128)(2,1)S(1)}, bf16[256,1024]{1,0:T(8,128)(2,1)S(1)}, u32[]{:S(2)}, u32[]{:S(2)}) collective-permute-start(bf16[256,1024]{1,0:T(8,128)(2,1)S(1)} %get-tuple-element.150.refs_7_), channel_id=1, source_target_pairs={{0,2},{1,3},{2,0},{3,1},{4,6},{5,7},{6,4},{7,5},{8,10},{9,11},{10,... | collective-permute-start | bytes 1572872 | tf_op jit(solution)/shard_map/ppermute | solution.py:976
  59.2 17.1 %collective-permute-start.14 = (bf16[256,1024]{1,0:T(8,128)(2,1)S(1)}, bf16[256,1024]{1,0:T(8,128)(2,1)S(1)}, u32[]{:S(2)}, u32[]{:S(2)}) collective-permute-start(bf16[256,1024]{1,0:T(8,128)(2,1)S(1)} %get-tuple-element.150.refs_7_), channel_id=1, source_target_pairs={{0,1},{1,0},{2,3},{3,2},{4,5},{5,4},{6,7},{7,6},{8,9},{9,8},{10,11... | collective-permute-start | bytes 1572872 | tf_op jit(solution)/shard_map/ppermute | solution.py:976
  72.2 18.6 %collective-permute-start.19 = (bf16[256,1024]{1,0:T(8,128)(2,1)S(1)}, bf16[256,1024]{1,0:T(8,128)(2,1)S(1)}, u32[]{:S(2)}, u32[]{:S(2)}) collective-permute-start(bf16[256,1024]{1,0:T(8,128)(2,1)S(1)} %collective-permute-done.17.refs_7_), channel_id=1, source_target_pairs={{0,1},{1,0},{2,3},{3,2},{4,5},{5,4},{6,7},{7,6},{8,9},{9,8},{10,11... | collective-permute-start | bytes 1572872 | tf_op jit(solution)/shard_map/ppermute | solution.py:976
  73.1 3.2 %collective-permute-start.15 = (bf16[16,1024]{1,0:T(8,128)(2,1)S(1)}, bf16[16,1024]{1,0:T(8,128)(2,1)S(1)}, u32[]{:S(2)}, u32[]{:S(2)}) collective-permute-start(bf16[16,1024]{1,0:T(8,128)(2,1)S(1)} %get-tuple-element.151), channel_id=1, source_target_pairs={{1,2},{3,4},{5,6},{7,8},{9,10},{11,12},{13,14},{15,16},{17,18},{19... | collective-permute-start | bytes 98312 | tf_op jit(solution)/shard_map/ppermute | solution.py:976
  76.4 2.8 %collective-permute-start.18 = (bf16[16,1024]{1,0:T(8,128)(2,1)S(1)}, bf16[16,1024]{1,0:T(8,128)(2,1)S(1)}, u32[]{:S(2)}, u32[]{:S(2)}) collective-permute-start(bf16[16,1024]{1,0:T(8,128)(2,1)S(1)} %own_rim.1), channel_id=1, source_target_pairs={{0,2},{1,3},{2,0},{3,1},{4,6},{5,7},{6,4},{7,5},{8,10},{9,11},{10,... | collective-permute-start | bytes 98312 | tf_op jit(solution)/shard_map/ppermute | solution.py:976
  76.5 5.6 %collective-permute-start.16 = (bf16[16,1024]{1,0:T(8,128)(2,1)S(1)}, bf16[16,1024]{1,0:T(8,128)(2,1)S(1)}, u32[]{:S(2)}, u32[]{:S(2)}) collective-permute-start(bf16[16,1024]{1,0:T(8,128)(2,1)S(1)} %collective-permute-done.15.refs_9_.came), channel_id=1, source_target_pairs={{0,1},{1,0},{2,3},{3,2},{4,5},{5,4},{6,7},{7,6},{8,9},{9,8},{10,11... | collective-permute-start | bytes 98312 | tf_op jit(solution)/shard_map/ppermute | solution.py:976
  79.2 11.5 %collective-permute-start.20 = (bf16[16,1024]{1,0:T(8,128)(2,1)S(1)}, bf16[16,1024]{1,0:T(8,128)(2,1)S(1)}, u32[]{:S(2)}, u32[]{:S(2)}) collective-permute-start(bf16[16,1024]{1,0:T(8,128)(2,1)S(1)} %collective-permute-done.18.refs_8_), channel_id=1, source_target_pairs={{0,1},{1,0},{2,3},{3,2},{4,5},{5,4},{6,7},{7,6},{8,9},{9,8},{10,11... | collective-permute-start | bytes 98312 | tf_op jit(solution)/shard_map/ppermute | solution.py:976
  93.6 33.8 %copy-start.3 = (bf16[512,1024]{1,0:T(8,128)(2,1)S(1)}, bf16[512,1024]{1,0:T(8,128)(2,1)}, u32[]{:S(2)}) copy-start(bf16[512,1024]{1,0:T(8,128)(2,1)} %wo.1) | copy-start | bytes 3145732
  128.7 5.4 %collective-permute-start.23 = (bf16[528,256]{1,0:T(8,128)(2,1)S(1)}, bf16[528,256]{1,0:T(8,128)(2,1)S(1)}, u32[]{:S(2)}, u32[]{:S(2)}) collective-permute-start(bf16[528,256]{1,0:T(8,128)(2,1)S(1)} %get-tuple-element.185), channel_id=1, source_target_pairs={{0,1},{1,0},{2,3},{3,2},{4,5},{5,4},{6,7},{7,6},{8,9},{9,8},{10,11... | collective-permute-start | bytes 811016 | tf_op jit(solution)/shard_map/ppermute | solution.py:976
  132.7 1.6 %collective-permute-start.22 = (bf16[528,256]{1,0:T(8,128)(2,1)S(1)}, bf16[528,256]{1,0:T(8,128)(2,1)S(1)}, u32[]{:S(2)}, u32[]{:S(2)}) collective-permute-start(bf16[528,256]{1,0:T(8,128)(2,1)S(1)} %get-tuple-element.181), channel_id=1, source_target_pairs={{0,1},{1,0},{2,3},{3,2},{4,5},{5,4},{6,7},{7,6},{8,9},{9,8},{10,11... | collective-permute-start | bytes 811016 | tf_op jit(solution)/shard_map/ppermute | solution.py:976
  133.5 2.4 %collective-permute-start.21 = (bf16[1024,256]{1,0:T(8,128)(2,1)S(1)}, bf16[1024,256]{1,0:T(8,128)(2,1)S(1)}, u32[]{:S(2)}, u32[]{:S(2)}) collective-permute-start(bf16[1024,256]{1,0:T(8,128)(2,1)S(1)} %get-tuple-element.178), channel_id=1, source_target_pairs={{0,1},{1,0},{2,3},{3,2},{4,5},{5,4},{6,7},{7,6},{8,9},{9,8},{10,11... | collective-permute-start | bytes 1572872 | tf_op jit(solution)/shard_map/ppermute | solution.py:976
  134.2 8.1 %collective-permute-start.24 = (bf16[528,256]{1,0:T(8,128)(2,1)S(1)}, bf16[528,256]{1,0:T(8,128)(2,1)S(1)}, u32[]{:S(2)}, u32[]{:S(2)}) collective-permute-start(bf16[528,256]{1,0:T(8,128)(2,1)S(1)} %get-tuple-element.186), channel_id=1, source_target_pairs={{0,2},{1,3},{2,0},{3,1},{4,6},{5,7},{6,4},{7,5},{8,10},{9,11},{10,... | collective-permute-start | bytes 811016 | tf_op jit(solution)/shard_map/ppermute | solution.py:976
  134.4 13.7 %collective-permute-start.25 = (bf16[528,256]{1,0:T(8,128)(2,1)S(1)}, bf16[528,256]{1,0:T(8,128)(2,1)S(1)}, u32[]{:S(2)}, u32[]{:S(2)}) collective-permute-start(bf16[528,256]{1,0:T(8,128)(2,1)S(1)} %get-tuple-element.188), channel_id=1, source_target_pairs={{0,2},{1,3},{2,0},{3,1},{4,6},{5,7},{6,4},{7,5},{8,10},{9,11},{10,... | collective-permute-start | bytes 811016 | tf_op jit(solution)/shard_map/ppermute | solution.py:976

commit v7 on v6

--- a/solution.py
+++ b/solution.py
@@ -311,11 +311,15 @@
             pltpu.make_async_copy(a, b, sems.at[j]).wait()
 
 
+def since_start(rows):
+    return jnp.where(lax.axis_index(SEQ) == 0, 0.0, rows[...].astype(F32))
+
+
 def first_chunk_kernel(
     x, rim, gain, pack, scans, ks, later, later_total,
     local, total, whole, whole_total, message, taps, cv, act,
 ):
-    rows = jnp.concatenate([rim[...], x[...]], 0)
+    rows = jnp.concatenate([since_start(rim), x[...].astype(F32)], 0)
     state, logs = state_chunk(rows, gain, pack, scans, ks, taps, cv, act)
     local[...] = state
     total[...] = jnp.broadcast_to(logs, (8, 128))
@@ -577,7 +581,7 @@
     start = pl.multiple_of((i + at) * BLK, BLK)
     rim = mine[pl.ds(pl.multiple_of(jnp.maximum(start - 16, 0), 16), 16), :].astype(F32)
     if not later:
-        edge = jnp.where(lax.axis_index(HEAD) == 0, x0[...].astype(F32), x1[...].astype(F32))
+        edge = jnp.where(lax.axis_index(HEAD) == 0, since_start(x0), x1[...].astype(F32))
         rim = jnp.where(i == 0, edge, rim)
     x = jnp.concatenate([rim, mine[pl.ds(start, BLK), :].astype(F32)], 0)
     scan_block(
@@ -610,79 +614,46 @@
     )(*args)
 
 
-def fine_close_kernel(
-    lead_a, lead_b, lead_c, tail_a, tail_b, tail_c, maps_a, maps_b, maps_c, x, s0, s1, s2, s3, p0, p1, p2, p3, merge,
-    merged, end_rows, lead, tail, maps, hidden, state, wo, norm,
-):
-    i = pl.program_id(0)
-
-    @pl.when(i < 2)
-    def _():
-        lead[...], tail[...], maps[...] = lead_a[...], tail_a[...], maps_a[...]
-
-    @pl.when(i == 2)
-    def _():
-        lead[...], tail[...], maps[...] = lead_b[...], tail_b[...], maps_b[...]
-
-    @pl.when(i == 3)
-    def _():
-        lead[...], tail[...], maps[...] = lead_c[...], tail_c[...], maps_c[...]
-
-    @pl.when(i == 0)
-    def _():
-        for j, (s, p) in enumerate(zip((s0, s1, s2, s3), (p0, p1, p2, p3))):
-            cols = slice(j * 128, (j + 1) * 128)
-            state[:, cols] = s[...]
-            wo[cols, :] = p[256:384, :]
-            norm[:, cols] = small_rows(p)[1]
-
-    gated = lead[...] + tail[...] * dot(maps[...], state[...])
-    factor = lax.rsqrt(jnp.sum(gated * gated, axis=1, keepdims=True) / 512.0 + EPSILON)
-    out = x[...].astype(F32)
-    total = dot((gated * factor * norm[...]).astype(BF), wo[...])
-    start = pl.multiple_of(i * BLK, BLK)
-    hidden[0, pl.ds(start, BLK), :] = rounded(out[:, 0:128] + total[:, 0:128])
-    hidden[1, pl.ds(start, BLK), :] = rounded(out[:, 128:256] + total[:, 128:256])
-
-    @pl.when(i == pl.num_programs(0) - 1)
-    def _():
-        total = None
-        for odd in range(2):
-            rows = [
-                hidden[half, pl.ds(odd, 512, stride=2), :].reshape(8, 2, 32, 128)
-                for half in range(2)
-            ]
-            for line in range(2):
-                tile = [r[:, line].reshape(256, 128).astype(BF) for r in rows]
-                at = (2 * line + odd) * 256
-                piece = dot(jnp.concatenate(tile, 1), merge[at : at + 256, :])
-                total = piece if total is None else total + piece
-        result = total.astype(BF)
-        merged[...] = result
-        end_rows[...] = result[240:256]
+def fine_close_kernel(*refs):
+    leads, tails, mapss, x, states, packs = (
+        refs[0:3], refs[3:6], refs[6:9], refs[9], refs[10:14], refs[14:18]
+    )
+    merge, merged, end_rows, hidden, state, wo, norm = refs[18:]
+    for j, (s, p) in enumerate(zip(states, packs)):
+        cols = slice(j * 128, (j + 1) * 128)
+        state[:, cols] = s[...]
+        wo[cols, :] = p[256:384, :]
+        norm[:, cols] = small_rows(p)[1]
+    for i, (call, at) in enumerate(((0, 0), (0, 1), (1, 0), (2, 0))):
+        part = slice(at * BLK, (at + 1) * BLK)
+        rows = slice(i * BLK, (i + 1) * BLK)
+        gated = leads[call][part] + tails[call][part] * dot(mapss[call][part], state[...])
+        factor = lax.rsqrt(jnp.sum(gated * gated, axis=1, keepdims=True) / 512.0 + EPSILON)
+        total = dot((gated * factor * norm[...]).astype(BF), wo[...])
+        out = x[rows].astype(F32) + total
+        hidden[0, rows, :] = rounded(out[:, 0:128])
+        hidden[1, rows, :] = rounded(out[:, 128:256])
+    total = None
+    for odd in range(2):
+        rows = [
+            hidden[half, pl.ds(odd, 512, stride=2), :].reshape(8, 2, 32, 128) for half in range(2)
+        ]
+        for line in range(2):
+            tile = [r[:, line].reshape(256, 128).astype(BF) for r in rows]
+            at = (2 * line + odd) * 256
+            piece = dot(jnp.concatenate(tile, 1), merge[at : at + 256, :])
+            total = piece if total is None else total + piece
+    result = total.astype(BF)
+    merged[...] = result
+    end_rows[...] = result[240:256]
 
 
 def fine_close(leads, tails, maps, x, states, packs, merge):
-    def halves(width):
-        return [
-            pl.BlockSpec((BLK, width), lambda i: (jnp.minimum(i, 1), 0)),
-            pl.BlockSpec((BLK, width), lambda i: (0, 0)),
-            pl.BlockSpec((BLK, width), lambda i: (0, 0)),
-        ]
-
     return pl.pallas_call(
         fine_close_kernel,
-        grid=(4,),
-        in_specs=halves(512)
-        + halves(512)
-        + halves(256)
-        + [pl.BlockSpec((BLK, 256), lambda i: (i, 0))]
-        + [VM] * 9,
+        in_specs=[VM] * 19,
         out_specs=[VM] * 2,
         scratch_shapes=[
-            pltpu.VMEM((BLK, 512), F32),
-            pltpu.VMEM((BLK, 512), F32),
-            pltpu.VMEM((BLK, 256), BF),
             pltpu.VMEM((2, 1024, 128), F32),
             pltpu.VMEM((256, 512), BF),
             pltpu.VMEM((512, 256), BF),
@@ -698,6 +669,11 @@
     lead_log = jnp.where(first, b_log, a_log)
     row = jnp.exp(spread_row(lead_log))
     return jnp.where(first, a, b) * row + jnp.where(first, b, a), a_log + b_log
+
+
+def chip_start(rows):
+    first = lax.axis_index(("z", "u", "x", "y")) == 0
+    return jnp.where(first, 0.0, rows[...].astype(F32))
 
 
 def coarse_main_kernel(kind, pieces, gain, wg, wv, ws, wst, taps, both, *refs):
@@ -720,7 +696,7 @@
     def _():
         if kind == "near":
             copies = run_copies(((qs[0], xs.at[c]), (qs[1], xs.at[1 - c])), sems)
-            rim = jnp.where(c == 0, ra[...].astype(F32), rb[...].astype(F32))
+            rim = jnp.where(c == 0, chip_start(ra), chip_start(rb))
         else:
             copies = run_copies(((qs[0], xs.at[0]),), sems)
             rim = re[...].astype(F32) if kind == "far_1" else rd[...].astype(F32)
@@ -804,7 +780,7 @@
 
 def own_rim_kernel(came, beside, out):
     out[...] = jnp.where(
-        lax.axis_index("c") == 0, came[...].astype(F32), beside[240:256, :].astype(F32)
+        lax.axis_index("c") == 0, chip_start(came), beside[240:256, :].astype(F32)
     ).astype(BF)
 
 
@@ -997,7 +973,7 @@
         fine_bias[None], fine_decay[None], fine_gate, fine_value, fine_output, fine_steps.T,
         fine_kernel, fine_norm[None], tokens, fine_gain[None], fine_scans, fine_taps,
     )
-    rim = passed(ends, SEQ, [(i, i + 1) for i in range(31)])
+    rim = passed(ends, SEQ, [(i, (i + 1) % 32) for i in range(32)])
     packs = [pack] + [swapped(pack, m) for m in (1, 2, 3)]
     later, later_total, (mine, mine_rim), (l0, t0, own, own_total, message) = fine_states(
         tokens, chunk, rim, gain, pack, scans, ks
@@ -1021,7 +997,7 @@
         merge_weight,
     )
 
-    rim_a = passed(end_rows, ALL, [(q, q + 1) for q in range(1, 127, 2)])
+    rim_a = passed(end_rows, ALL, [(q, (q - 1 + 2 * (q % 2)) % 128) for q in range(128)])
     across = swapped(merged, 2)
     beside = swapped(merged, 1)
     rim_b = swapped(rim_a, 1)

time: 150 us -> 146 us (0.973)
  blocking collectives: 33.6 us -> 27.8 us
  waiting for transfers between devices: 33.6 us -> 37.5 us
    all_to_all x1, blocking collectives: 19.7 us -> 13.9 us  [shards(): got = lax.all_to_all(message, SEQ, split_axis=0, concat_axis=0, tiled=True)]
    ppermute x26, waiting for transfers between devices: 33.6 us -> 37.5 us  [passed(): return lax.ppermute(x, axes, pairs)]
  transfers between devices with their start and end apart: 26 -> 26, of which waited for: 10 -> 10; matrix products, arithmetic and copies ran while one was open for 0% -> 0% of each run, Pallas kernels for 18% -> 19%
where the time goes in v7:
time: 146 us
  starting transfers between devices  40.9 us (28%)
  Pallas kernels  39 us (27%)
  waiting for transfers between devices  37.5 us (26%)
  blocking collectives  27.8 us (19%)
    ppermute x26, starting transfers between devices, passed(): return lax.ppermute(x, axes, pairs)  40.9 us
    ppermute x26, waiting for transfers between devices, passed(): return lax.ppermute(x, axes, pairs)  37.5 us
    all_to_all x1, blocking collectives, shards(): got = lax.all_to_all(message, SEQ, split_axis=0, concat_axis=0, tiled=True)  13.9 us
    all_to_all x1, blocking collectives, shards(): lax.all_to_all(prefix(got), SEQ, split_axis=0, concat_axis=0, tiled=True)  13.8 us
    pallas_call x3, Pallas kernels, coarse_main(): pl.pallas_call(lambda *refs: coarse_main_kernel(kind, blocks, *refs), gri...  11.5 us
    pallas_call x3, Pallas kernels, fine_main(): pl.pallas_call(lambda *refs: fine_main_kernel(at, *refs), grid=(blocks,),...  9.08 us
    pallas_call x1, Pallas kernels, fine_states(): pl.pallas_call(later_chunks_kernel, grid=(3,), in_specs=[HBM] + [VM] * 5,...  6.42 us
  transfers between devices with their start and end apart: 26, of which 10 were waited for; matrix products, arithmetic and copies ran while one was open for 0% of the time, Pallas kernels for 19%

profile of v7, /device:TPU:1, one launch (start us, length us, event | category | flops | bytes accessed | tf_op | source)
XLA Modules:
  0.0 145.5 jit_solution(18258908565888937919)
XLA Ops:
  0.0 1.4 pack.1
  1.4 2.1 %collective-permute-start.3 = (bf16[16,256]{1,0:T(8,128)(2,1)S(1)}, bf16[16,256]{1,0:T(8,128)(2,1)S(1)}, u32[]{:S(2)}, u32[]{:S(2)}) collective-permute-start(bf16[16,256]{1,0:T(8,128)(2,1)S(1)} %get-tuple-element.107), channel_id=1, source_target_pairs={{0,4},{4,8},{8,12},{12,16},{16,20},{20,24},{24,28},{28,32},{32,36}... | collective-permute-start | bytes 24584 | tf_op jit(solution)/shard_map/ppermute | solution.py:952
  3.5 6.4 %later_chunks.1 = (f32[3,256,128]{2,1,0:T(8,128)S(1)}, f32[3,8,128]{2,1,0:T(8,128)S(1)}, bf16[1024,256]{1,0:T(8,128)(2,1)S(1)}, bf16[1024,256]{1,0:T(8,128)(2,1)S(1)}, bf16[16,256]{1,0:T(8,128)(2,1)S(1)}) custom-call(bf16[4096,256]{1,0:T(8,128)(2,1)} %tokens.3, bf16[1040,256]{1,0:T(8,128)(2,1)S(1)} %get-tuple-element.101.chunk_0, ...), custom_call_target="tpu_custom_call" | custom-call | tf_op jit(solution)/shard_map/later_chunks/pallas_call | solution.py:358
  9.9 2.0 %collective-permute-done.3.refs_8_.rim = bf16[16,256]{1,0:T(8,128)(2,1)S(1)} collective-permute-done((bf16[16,256]{1,0:T(8,128)(2,1)S(1)}, bf16[16,256]{1,0:T(8,128)(2,1)S(1)}, u32[]{:S(2)}, u32[]{:S(2)}) %collective-permute-start.3) | collective-permute-done | bytes 8224 | tf_op jit(solution)/shard_map/ppermute | solution.py:952
  11.9 2.1 %first_chunk.1 = (f32[256,128]{1,0:T(8,128)S(1)}, f32[8,128]{1,0:T(8,128)S(1)}, f32[256,128]{1,0:T(8,128)S(1)}, f32[8,128]{1,0:T(8,128)S(1)}, bf16[272,128]{1,0:T(8,128)(2,1)S(1)}) custom-call(bf16[1024,256]{1,0:T(8,128)(2,1)S(1)} %get-tuple-element.128.x, bf16[16,256]{1,0:T(8,128)(2,1)S(1)} %collective-permute-done.3.refs_8_.rim, ...), custom_call_target="tpu_custom_call" | custom-call | tf_op jit(solution)/shard_map/first_chunk/pallas_call | solution.py:376
  14.0 2.2 %collective-permute-start.6 = (bf16[272,128]{1,0:T(8,128)(2,1)S(1)}, bf16[272,128]{1,0:T(8,128)(2,1)S(1)}, u32[]{:S(2)}, u32[]{:S(2)}) collective-permute-start(bf16[272,128]{1,0:T(8,128)(2,1)S(1)} %get-tuple-element.133), channel_id=1, source_target_pairs={{0,12},{4,0},{8,4},{12,8},{1,13},{5,1},{9,5},{13,9},{2,14},{6,2},{... | collective-permute-start | bytes 208904 | tf_op jit(solution)/shard_map/ppermute | solution.py:952
  16.2 0.7 collective-permute-start.4
  16.9 1.8 %collective-permute-start.2 = (bf16[416,256]{1,0:T(8,128)(2,1)S(1)}, bf16[416,256]{1,0:T(8,128)(2,1)S(1)}, u32[]{:S(2)}, u32[]{:S(2)}) collective-permute-start(bf16[416,256]{1,0:T(8,128)(2,1)S(1)} %get-tuple-element.103.pack.refs_4_.refs_14_), channel_id=1, source_target_pairs={{0,3},{1,2},{2,1},{3,0},{4,7},{5,6},{6,5},{7,4},{8,11},{9,10},{10,... | collective-permute-start | bytes 638984 | tf_op jit(solution)/shard_map/ppermute | solution.py:952
  18.7 2.3 %collective-permute-done.5.refs_3_ = bf16[272,128]{1,0:T(8,128)(2,1)S(1)} collective-permute-done((bf16[272,128]{1,0:T(8,128)(2,1)S(1)}, bf16[272,128]{1,0:T(8,128)(2,1)S(1)}, u32[]{:S(2)}, u32[]{:S(2)}) %collective-permute-start.5) | collective-permute-done | bytes 69664 | tf_op jit(solution)/shard_map/ppermute | solution.py:952
  21.0 0.4 collective-permute-done.4.refs_2_
  21.3 0.1 shard_map.229
  21.5 1.8 %collective-permute-start.7 = (bf16[272,128]{1,0:T(8,128)(2,1)S(1)}, bf16[272,128]{1,0:T(8,128)(2,1)S(1)}, u32[]{:S(2)}, u32[]{:S(2)}) collective-permute-start(bf16[272,128]{1,0:T(8,128)(2,1)S(1)} %get-tuple-element.138), channel_id=1, source_target_pairs={{0,16},{16,0},{1,17},{17,1},{2,18},{18,2},{3,19},{19,3},{4,20},{20... | collective-permute-start | bytes 208904 | tf_op jit(solution)/shard_map/ppermute | solution.py:952
  23.3 1.0 collective-permute-start.1
  24.3 2.9 %collective-permute-start = (bf16[416,256]{1,0:T(8,128)(2,1)S(1)}, bf16[416,256]{1,0:T(8,128)(2,1)S(1)}, u32[]{:S(2)}, u32[]{:S(2)}) collective-permute-start(bf16[416,256]{1,0:T(8,128)(2,1)S(1)} %get-tuple-element.103.pack.refs_4_.refs_14_), channel_id=1, source_target_pairs={{0,1},{1,0},{2,3},{3,2},{4,5},{5,4},{6,7},{7,6},{8,9},{9,8},{10,11... | collective-permute-start | bytes 638984 | tf_op jit(solution)/shard_map/ppermute | solution.py:952
  27.2 0.0 collective-permute-done.7.refs_4_
  27.2 0.1 shard_map.230
  27.3 3.2 %collective-permute-start.10 = (bf16[272,128]{1,0:T(8,128)(2,1)S(1)}, bf16[272,128]{1,0:T(8,128)(2,1)S(1)}, u32[]{:S(2)}, u32[]{:S(2)}) collective-permute-start(bf16[272,128]{1,0:T(8,128)(2,1)S(1)} %get-tuple-element.143), channel_id=1, source_target_pairs={{0,96},{32,0},{64,32},{96,64},{1,97},{33,1},{65,33},{97,65},{2,98}... | collective-permute-start | bytes 208904 | tf_op jit(solution)/shard_map/ppermute | solution.py:952
  30.5 0.3 collective-permute-start.9
  30.8 1.0 collective-permute-done.10.r3
  31.8 0.6 collective-permute-start.8
  32.4 2.7 %collective-permute-done.9.r2 = bf16[272,128]{1,0:T(8,128)(2,1)S(1)} collective-permute-done((bf16[272,128]{1,0:T(8,128)(2,1)S(1)}, bf16[272,128]{1,0:T(8,128)(2,1)S(1)}, u32[]{:S(2)}, u32[]{:S(2)}) %collective-permute-start.9) | collective-permute-done | bytes 69664 | tf_op jit(solution)/shard_map/ppermute | solution.py:952
  35.1 1.4 collective-permute-done.8.r1
  36.5 0.1 chain_last.1
  36.7 5.8 %collective-permute-start.11 = (bf16[256,128]{1,0:T(8,128)(2,1)S(1)}, bf16[256,128]{1,0:T(8,128)(2,1)S(1)}, u32[]{:S(2)}, u32[]{:S(2)}) collective-permute-start(bf16[256,128]{1,0:T(8,128)(2,1)S(1)} %get-tuple-element.147), channel_id=1, source_target_pairs={{0,1},{1,0},{2,3},{3,2},{4,5},{5,4},{6,7},{7,6},{8,9},{9,8},{10,11... | collective-permute-start | bytes 196616 | tf_op jit(solution)/shard_map/ppermute | solution.py:952
  42.5 0.4 collective-permute-start.12
  42.9 1.3 collective-permute-start.13
  44.2 4.2 %shard_map.226 = (f32[512,512]{1,0:T(8,128)S(1)}, f32[512,512]{1,0:T(8,128)S(1)}, bf16[512,256]{1,0:T(8,128)(2,1)S(1)}, f32[256,512]{1,0:T(8,128)S(1)}, f32[8,12...) custom-call(bf16[1024,256]{1,0:T(8,128)(2,1)S(1)} %get-tuple-element, ...), custom_call_target="tpu_custom_call" | custom-call | tf_op jit(solution)/shard_map/pallas_call | solution.py:602
  48.5 0.0 copy-start.4
  48.5 2.0 %shard_map.227 = (f32[256,512]{1,0:T(8,128)S(1)}, f32[256,512]{1,0:T(8,128)S(1)}, bf16[256,256]{1,0:T(8,128)(2,1)S(1)}, f32[256,512]{1,0:T(8,128)S(1)}, f32[8,128]{1,0:T(8,128)S(1)}) custom-call(bf16[1024,256]{1,0:T(8,128)(2,1)S(1)} %get-tuple-element.106.refs_0_.refs_9_, f32[1,256]{1,0:T(1,128)S(1)} %get-tuple-element.102.gain.refs_1_, ...), custom_call_target="tpu_custom_call" | custom-call | tf_op jit(solution)/shard_map/pallas_call | solution.py:602
  50.5 2.8 %shard_map.228 = (f32[256,512]{1,0:T(8,128)S(1)}, f32[256,512]{1,0:T(8,128)S(1)}, bf16[256,256]{1,0:T(8,128)(2,1)S(1)}, f32[256,512]{1,0:T(8,128)}, f32[8,128]{1,0:T(8,128)}) custom-call(bf16[1024,256]{1,0:T(8,128)(2,1)S(1)} %get-tuple-element.106.refs_0_.refs_9_, f32[1,256]{1,0:T(1,128)S(1)} %get-tuple-element.102.gain.refs_1_, ...), custom_call_target="tpu_custom_call" | custom-call | tf_op jit(solution)/shard_map/pallas_call | solution.py:602
  53.4 0.0 copy-start
  53.4 0.0 copy-start.1
  53.4 0.0 copy-start.2
  53.4 2.3 %fine_close.1 = (bf16[256,1024]{1,0:T(8,128)(2,1)S(1)}, bf16[16,1024]{1,0:T(8,128)(2,1)S(1)}) custom-call(f32[512,512]{1,0:T(8,128)S(1)} %get-tuple-element.109.refs_0_, f32[256,512]{1,0:T(8,128)S(1)} %get-tuple-element.118.refs_1_, f32[256,512]{1,0:T(8,128)S(1)} %get-tuple-element.121.refs_2_, f32[512,512]{1,0:T(8,128)S(1)} %get-tuple-element.122.refs_3_, ...), custom_call_target="tpu_custom_call" | custom-call | tf_op jit(solution)/shard_map/fine_close/pallas_call | solution.py:652
  55.7 0.5 collective-permute-start.17
  56.2 0.4 collective-permute-start.14
  56.6 12.5 %collective-permute-done.17.refs_7_ = bf16[256,1024]{1,0:T(8,128)(2,1)S(1)} collective-permute-done((bf16[256,1024]{1,0:T(8,128)(2,1)S(1)}, bf16[256,1024]{1,0:T(8,128)(2,1)S(1)}, u32[]{:S(2)}, u32[]{:S(2)}) %collective-permute-start.17) | collective-permute-done | bytes 524320 | tf_op jit(solution)/shard_map/ppermute | solution.py:952
  69.2 1.0 collective-permute-start.19
  70.2 0.3 collective-permute-start.15
  70.4 3.1 %collective-permute-done.15.refs_9_.came = bf16[16,1024]{1,0:T(8,128)(2,1)S(1)} collective-permute-done((bf16[16,1024]{1,0:T(8,128)(2,1)S(1)}, bf16[16,1024]{1,0:T(8,128)(2,1)S(1)}, u32[]{:S(2)}, u32[]{:S(2)}) %collective-permute-start.15) | collective-permute-done | bytes 32800 | tf_op jit(solution)/shard_map/ppermute | solution.py:952
  73.5 1.4 collective-permute-start.18
  74.9 4.2 %collective-permute-start.16 = (bf16[16,1024]{1,0:T(8,128)(2,1)S(1)}, bf16[16,1024]{1,0:T(8,128)(2,1)S(1)}, u32[]{:S(2)}, u32[]{:S(2)}) collective-permute-start(bf16[16,1024]{1,0:T(8,128)(2,1)S(1)} %collective-permute-done.15.refs_9_.came), channel_id=1, source_target_pairs={{0,1},{1,0},{2,3},{3,2},{4,5},{5,4},{6,7},{7,6},{8,9},{9,8},{10,11... | collective-permute-start | bytes 98312 | tf_op jit(solution)/shard_map/ppermute | solution.py:952
  79.1 3.8 %collective-permute-start.20 = (bf16[16,1024]{1,0:T(8,128)(2,1)S(1)}, bf16[16,1024]{1,0:T(8,128)(2,1)S(1)}, u32[]{:S(2)}, u32[]{:S(2)}) collective-permute-start(bf16[16,1024]{1,0:T(8,128)(2,1)S(1)} %collective-permute-done.18.refs_8_), channel_id=1, source_target_pairs={{0,1},{1,0},{2,3},{3,2},{4,5},{5,4},{6,7},{7,6},{8,9},{9,8},{10,11... | collective-permute-start | bytes 98312 | tf_op jit(solution)/shard_map/ppermute | solution.py:952
  83.0 1.0 coarse_params.1
  84.0 5.9 %shard_map.231 = (f32[512,512]{1,0:T(8,128)S(1)}, f32[512,512]{1,0:T(8,128)S(1)}, bf16[512,256]{1,0:T(8,128)(2,1)S(1)}, bf16[512,256]{1,0:T(8,128)(2,1)S(1)}, f3...) custom-call(f32[1,1024]{1,0:T(1,128)S(1)} %get-tuple-element.97.refs_0_, bf16[1024,512]{1,0:T(8,128)(2,1)S(1)} %copy-done, ...), custom_call_target="tpu_custom_call" | custom-call | tf_op jit(solution)/shard_map/pallas_call | solution.py:757
  89.9 2.8 %shard_map.232 = (f32[256,512]{1,0:T(8,128)S(1)}, f32[256,512]{1,0:T(8,128)S(1)}, bf16[256,256]{1,0:T(8,128)(2,1)S(1)}, bf16[256,256]{1,0:T(8,128)(2,1)S(1)}, f3...) custom-call(f32[1,1024]{1,0:T(1,128)S(1)} %get-tuple-element.97.refs_0_, ...), custom_call_target="tpu_custom_call" | custom-call | tf_op jit(solution)/shard_map/pallas_call | solution.py:757
  92.7 2.9 %shard_map.233 = (f32[256,512]{1,0:T(8,128)S(1)}, f32[256,512]{1,0:T(8,128)S(1)}, bf16[256,256]{1,0:T(8,128)(2,1)S(1)}, bf16[256,256]{1,0:T(8,128)(2,1)S(1)}, f3...) custom-call(f32[1,1024]{1,0:T(1,128)S(1)} %get-tuple-element.97.refs, ...), custom_call_target="tpu_custom_call" | custom-call | tf_op jit(solution)/shard_map/pallas_call | solution.py:757
  95.5 0.0 copy-start.3
  95.6 13.9 %all_to_all.10.got = bf16[32,24,256]{2,1,0:T(8,128)(2,1)S(1)} all-to-all(bf16[32,24,256]{2,1,0:T(8,128)(2,1)S(1)} %get-tuple-element.163), channel_id=1, replica_groups=mesh['z'=4,'u'=2,'x'=4,'y'=2,'c'=2] {'z','u','x'}, dimensions={0} | all-to-all | bytes 786432 | tf_op jit(solution)/shard_map/all_to_all | solution.py:1018
  109.5 0.1 prefix.1
  109.6 13.8 %all_to_all.11.refs_3_.refs_6_ = bf16[32,16,256]{2,1,0:T(8,128)(2,1)S(1)} all-to-all(bf16[32,16,256]{2,1,0:T(8,128)(2,1)S(1)} %prefix.1), channel_id=1, replica_groups=mesh['z'=4,'u'=2,'x'=4,'y'=2,'c'=2] {'z','u','x'}, dimensions={0} | all-to-all | bytes 524288 | tf_op jit(solution)/shard_map/all_to_all | solution.py:1019
  123.5 1.3 coarse_close_far.1
  124.8 2.8 %collective-permute-start.23 = (bf16[528,256]{1,0:T(8,128)(2,1)S(1)}, bf16[528,256]{1,0:T(8,128)(2,1)S(1)}, u32[]{:S(2)}, u32[]{:S(2)}) collective-permute-start(bf16[528,256]{1,0:T(8,128)(2,1)S(1)} %get-tuple-element.185), channel_id=1, source_target_pairs={{0,1},{1,0},{2,3},{3,2},{4,5},{5,4},{6,7},{7,6},{8,9},{9,8},{10,11... | collective-permute-start | bytes 811016 | tf_op jit(solution)/shard_map/ppermute | solution.py:952
  127.7 1.2 coarse_close_near.1
  128.9 0.1 collective-permute-start.22
  129.0 0.7 close_rest.1
  129.7 0.6 collective-permute-start.21
  130.3 0.1 shard_map.235
  130.4 0.4 collective-permute-start.24
  130.8 0.1 shard_map.234
  130.9 1.2 collective-permute-start.25
  132.1 6.4 %collective-permute-done.24.far_a = bf16[528,256]{1,0:T(8,128)(2,1)S(1)} collective-permute-done((bf16[528,256]{1,0:T(8,128)(2,1)S(1)}, bf16[528,256]{1,0:T(8,128)(2,1)S(1)}, u32[]{:S(2)}, u32[]{:S(2)}) %collective-permute-start.24) | collective-permute-done | bytes 270368 | tf_op jit(solution)/shard_map/ppermute | solution.py:952
  138.5 5.8 %collective-permute-done.25.far_b = bf16[528,256]{1,0:T(8,128)(2,1)S(1)} collective-permute-done((bf16[528,256]{1,0:T(8,128)(2,1)S(1)}, bf16[528,256]{1,0:T(8,128)(2,1)S(1)}, u32[]{:S(2)}, u32[]{:S(2)}) %collective-permute-start.25) | collective-permute-done | bytes 270368 | tf_op jit(solution)/shard_map/ppermute | solution.py:952
  144.2 1.3 final.1
  (22 shorter events, 0.1 us)
Async XLA Ops:
  1.4 10.5 %collective-permute-start.3 = (bf16[16,256]{1,0:T(8,128)(2,1)S(1)}, bf16[16,256]{1,0:T(8,128)(2,1)S(1)}, u32[]{:S(2)}, u32[]{:S(2)}) collective-permute-start(bf16[16,256]{1,0:T(8,128)(2,1)S(1)} %get-tuple-element.107), channel_id=1, source_target_pairs={{0,4},{4,8},{8,12},{12,16},{16,20},{20,24},{24,28},{28,32},{32,36}... | collective-permute-start | bytes 24584 | tf_op jit(solution)/shard_map/ppermute | solution.py:952
  14.0 4.7 %collective-permute-start.6 = (bf16[272,128]{1,0:T(8,128)(2,1)S(1)}, bf16[272,128]{1,0:T(8,128)(2,1)S(1)}, u32[]{:S(2)}, u32[]{:S(2)}) collective-permute-start(bf16[272,128]{1,0:T(8,128)(2,1)S(1)} %get-tuple-element.133), channel_id=1, source_target_pairs={{0,12},{4,0},{8,4},{12,8},{1,13},{5,1},{9,5},{13,9},{2,14},{6,2},{... | collective-permute-start | bytes 208904 | tf_op jit(solution)/shard_map/ppermute | solution.py:952
  16.2 4.8 %collective-permute-start.5 = (bf16[272,128]{1,0:T(8,128)(2,1)S(1)}, bf16[272,128]{1,0:T(8,128)(2,1)S(1)}, u32[]{:S(2)}, u32[]{:S(2)}) collective-permute-start(bf16[272,128]{1,0:T(8,128)(2,1)S(1)} %get-tuple-element.133), channel_id=1, source_target_pairs={{0,8},{4,12},{8,0},{12,4},{1,9},{5,13},{9,1},{13,5},{2,10},{6,14},... | collective-permute-start | bytes 208904 | tf_op jit(solution)/shard_map/ppermute | solution.py:952
  16.2 5.1 %collective-permute-start.4 = (bf16[272,128]{1,0:T(8,128)(2,1)S(1)}, bf16[272,128]{1,0:T(8,128)(2,1)S(1)}, u32[]{:S(2)}, u32[]{:S(2)}) collective-permute-start(bf16[272,128]{1,0:T(8,128)(2,1)S(1)} %get-tuple-element.133), channel_id=1, source_target_pairs={{0,4},{4,8},{8,12},{12,0},{1,5},{5,9},{9,13},{13,1},{2,6},{6,10},{... | collective-permute-start | bytes 208904 | tf_op jit(solution)/shard_map/ppermute | solution.py:952
  16.9 26.0 %collective-permute-start.2 = (bf16[416,256]{1,0:T(8,128)(2,1)S(1)}, bf16[416,256]{1,0:T(8,128)(2,1)S(1)}, u32[]{:S(2)}, u32[]{:S(2)}) collective-permute-start(bf16[416,256]{1,0:T(8,128)(2,1)S(1)} %get-tuple-element.103.pack.refs_4_.refs_14_), channel_id=1, source_target_pairs={{0,3},{1,2},{2,1},{3,0},{4,7},{5,6},{6,5},{7,4},{8,11},{9,10},{10,... | collective-permute-start | bytes 638984 | tf_op jit(solution)/shard_map/ppermute | solution.py:952
  21.5 5.7 %collective-permute-start.7 = (bf16[272,128]{1,0:T(8,128)(2,1)S(1)}, bf16[272,128]{1,0:T(8,128)(2,1)S(1)}, u32[]{:S(2)}, u32[]{:S(2)}) collective-permute-start(bf16[272,128]{1,0:T(8,128)(2,1)S(1)} %get-tuple-element.138), channel_id=1, source_target_pairs={{0,16},{16,0},{1,17},{17,1},{2,18},{18,2},{3,19},{19,3},{4,20},{20... | collective-permute-start | bytes 208904 | tf_op jit(solution)/shard_map/ppermute | solution.py:952
  23.3 21.0 %collective-permute-start.1 = (bf16[416,256]{1,0:T(8,128)(2,1)S(1)}, bf16[416,256]{1,0:T(8,128)(2,1)S(1)}, u32[]{:S(2)}, u32[]{:S(2)}) collective-permute-start(bf16[416,256]{1,0:T(8,128)(2,1)S(1)} %get-tuple-element.103.pack.refs_4_.refs_14_), channel_id=1, source_target_pairs={{0,2},{1,3},{2,0},{3,1},{4,6},{5,7},{6,4},{7,5},{8,10},{9,11},{10,... | collective-permute-start | bytes 638984 | tf_op jit(solution)/shard_map/ppermute | solution.py:952
  24.3 20.0 %collective-permute-start = (bf16[416,256]{1,0:T(8,128)(2,1)S(1)}, bf16[416,256]{1,0:T(8,128)(2,1)S(1)}, u32[]{:S(2)}, u32[]{:S(2)}) collective-permute-start(bf16[416,256]{1,0:T(8,128)(2,1)S(1)} %get-tuple-element.103.pack.refs_4_.refs_14_), channel_id=1, source_target_pairs={{0,1},{1,0},{2,3},{3,2},{4,5},{5,4},{6,7},{7,6},{8,9},{9,8},{10,11... | collective-permute-start | bytes 638984 | tf_op jit(solution)/shard_map/ppermute | solution.py:952
  27.3 4.6 %collective-permute-start.10 = (bf16[272,128]{1,0:T(8,128)(2,1)S(1)}, bf16[272,128]{1,0:T(8,128)(2,1)S(1)}, u32[]{:S(2)}, u32[]{:S(2)}) collective-permute-start(bf16[272,128]{1,0:T(8,128)(2,1)S(1)} %get-tuple-element.143), channel_id=1, source_target_pairs={{0,96},{32,0},{64,32},{96,64},{1,97},{33,1},{65,33},{97,65},{2,98}... | collective-permute-start | bytes 208904 | tf_op jit(solution)/shard_map/ppermute | solution.py:952
  30.5 4.7 %collective-permute-start.9 = (bf16[272,128]{1,0:T(8,128)(2,1)S(1)}, bf16[272,128]{1,0:T(8,128)(2,1)S(1)}, u32[]{:S(2)}, u32[]{:S(2)}) collective-permute-start(bf16[272,128]{1,0:T(8,128)(2,1)S(1)} %get-tuple-element.143), channel_id=1, source_target_pairs={{0,64},{32,96},{64,0},{96,32},{1,65},{33,97},{65,1},{97,33},{2,66}... | collective-permute-start | bytes 208904 | tf_op jit(solution)/shard_map/ppermute | solution.py:952
  31.8 4.7 %collective-permute-start.8 = (bf16[272,128]{1,0:T(8,128)(2,1)S(1)}, bf16[272,128]{1,0:T(8,128)(2,1)S(1)}, u32[]{:S(2)}, u32[]{:S(2)}) collective-permute-start(bf16[272,128]{1,0:T(8,128)(2,1)S(1)} %get-tuple-element.143), channel_id=1, source_target_pairs={{0,32},{32,64},{64,96},{96,0},{1,33},{33,65},{65,97},{97,1},{2,34}... | collective-permute-start | bytes 208904 | tf_op jit(solution)/shard_map/ppermute | solution.py:952
  36.7 16.7 %collective-permute-start.11 = (bf16[256,128]{1,0:T(8,128)(2,1)S(1)}, bf16[256,128]{1,0:T(8,128)(2,1)S(1)}, u32[]{:S(2)}, u32[]{:S(2)}) collective-permute-start(bf16[256,128]{1,0:T(8,128)(2,1)S(1)} %get-tuple-element.147), channel_id=1, source_target_pairs={{0,1},{1,0},{2,3},{3,2},{4,5},{5,4},{6,7},{7,6},{8,9},{9,8},{10,11... | collective-permute-start | bytes 196616 | tf_op jit(solution)/shard_map/ppermute | solution.py:952
  42.5 10.9 %collective-permute-start.12 = (bf16[256,128]{1,0:T(8,128)(2,1)S(1)}, bf16[256,128]{1,0:T(8,128)(2,1)S(1)}, u32[]{:S(2)}, u32[]{:S(2)}) collective-permute-start(bf16[256,128]{1,0:T(8,128)(2,1)S(1)} %get-tuple-element.148), channel_id=1, source_target_pairs={{0,2},{1,3},{2,0},{3,1},{4,6},{5,7},{6,4},{7,5},{8,10},{9,11},{10,... | collective-permute-start | bytes 196616 | tf_op jit(solution)/shard_map/ppermute | solution.py:952
  42.9 10.5 %collective-permute-start.13 = (bf16[256,128]{1,0:T(8,128)(2,1)S(1)}, bf16[256,128]{1,0:T(8,128)(2,1)S(1)}, u32[]{:S(2)}, u32[]{:S(2)}) collective-permute-start(bf16[256,128]{1,0:T(8,128)(2,1)S(1)} %get-tuple-element.149), channel_id=1, source_target_pairs={{0,3},{1,2},{2,1},{3,0},{4,7},{5,6},{6,5},{7,4},{8,11},{9,10},{10,... | collective-permute-start | bytes 196616 | tf_op jit(solution)/shard_map/ppermute | solution.py:952
  48.5 4.9 %copy-start.4 = (bf16[1024,1024]{1,0:T(8,128)(2,1)S(1)}, bf16[1024,1024]{1,0:T(8,128)(2,1)}, u32[]{:S(2)}) copy-start(bf16[1024,1024]{1,0:T(8,128)(2,1)} %refs_18_.1) | copy-start | bytes 6291460
  53.4 30.6 %copy-start = (bf16[1024,512]{1,0:T(8,128)(2,1)S(1)}, bf16[1024,512]{1,0:T(8,128)(2,1)}, u32[]{:S(2)}) copy-start(bf16[1024,512]{1,0:T(8,128)(2,1)} %refs_1_.5) | copy-start | bytes 3145732
  53.4 30.6 %copy-start.1 = (bf16[1024,512]{1,0:T(8,128)(2,1)S(1)}, bf16[1024,512]{1,0:T(8,128)(2,1)}, u32[]{:S(2)}) copy-start(bf16[1024,512]{1,0:T(8,128)(2,1)} %refs_2_.5) | copy-start | bytes 3145732
  53.4 30.6 %copy-start.2 = (bf16[1024,512]{1,0:T(8,128)(2,1)S(1)}, bf16[1024,512]{1,0:T(8,128)(2,1)}, u32[]{:S(2)}) copy-start(bf16[1024,512]{1,0:T(8,128)(2,1)} %refs_3_.5) | copy-start | bytes 3145732
  55.7 13.4 %collective-permute-start.17 = (bf16[256,1024]{1,0:T(8,128)(2,1)S(1)}, bf16[256,1024]{1,0:T(8,128)(2,1)S(1)}, u32[]{:S(2)}, u32[]{:S(2)}) collective-permute-start(bf16[256,1024]{1,0:T(8,128)(2,1)S(1)} %get-tuple-element.150.refs_7_), channel_id=1, source_target_pairs={{0,2},{1,3},{2,0},{3,1},{4,6},{5,7},{6,4},{7,5},{8,10},{9,11},{10,... | collective-permute-start | bytes 1572872 | tf_op jit(solution)/shard_map/ppermute | solution.py:952
  56.2 17.3 %collective-permute-start.14 = (bf16[256,1024]{1,0:T(8,128)(2,1)S(1)}, bf16[256,1024]{1,0:T(8,128)(2,1)S(1)}, u32[]{:S(2)}, u32[]{:S(2)}) collective-permute-start(bf16[256,1024]{1,0:T(8,128)(2,1)S(1)} %get-tuple-element.150.refs_7_), channel_id=1, source_target_pairs={{0,1},{1,0},{2,3},{3,2},{4,5},{5,4},{6,7},{7,6},{8,9},{9,8},{10,11... | collective-permute-start | bytes 1572872 | tf_op jit(solution)/shard_map/ppermute | solution.py:952
  69.2 23.5 %collective-permute-start.19 = (bf16[256,1024]{1,0:T(8,128)(2,1)S(1)}, bf16[256,1024]{1,0:T(8,128)(2,1)S(1)}, u32[]{:S(2)}, u32[]{:S(2)}) collective-permute-start(bf16[256,1024]{1,0:T(8,128)(2,1)S(1)} %collective-permute-done.17.refs_7_), channel_id=1, source_target_pairs={{0,1},{1,0},{2,3},{3,2},{4,5},{5,4},{6,7},{7,6},{8,9},{9,8},{10,11... | collective-permute-start | bytes 1572872 | tf_op jit(solution)/shard_map/ppermute | solution.py:952
  70.2 3.3 %collective-permute-start.15 = (bf16[16,1024]{1,0:T(8,128)(2,1)S(1)}, bf16[16,1024]{1,0:T(8,128)(2,1)S(1)}, u32[]{:S(2)}, u32[]{:S(2)}) collective-permute-start(bf16[16,1024]{1,0:T(8,128)(2,1)S(1)} %get-tuple-element.151), channel_id=1, source_target_pairs={{0,127},{1,2},{2,1},{3,4},{4,3},{5,6},{6,5},{7,8},{8,7},{9,10},{10... | collective-permute-start | bytes 98312 | tf_op jit(solution)/shard_map/ppermute | solution.py:952
  73.5 5.6 %collective-permute-start.18 = (bf16[16,1024]{1,0:T(8,128)(2,1)S(1)}, bf16[16,1024]{1,0:T(8,128)(2,1)S(1)}, u32[]{:S(2)}, u32[]{:S(2)}) collective-permute-start(bf16[16,1024]{1,0:T(8,128)(2,1)S(1)} %own_rim.1), channel_id=1, source_target_pairs={{0,2},{1,3},{2,0},{3,1},{4,6},{5,7},{6,4},{7,5},{8,10},{9,11},{10,... | collective-permute-start | bytes 98312 | tf_op jit(solution)/shard_map/ppermute | solution.py:952
  74.9 9.0 %collective-permute-start.16 = (bf16[16,1024]{1,0:T(8,128)(2,1)S(1)}, bf16[16,1024]{1,0:T(8,128)(2,1)S(1)}, u32[]{:S(2)}, u32[]{:S(2)}) collective-permute-start(bf16[16,1024]{1,0:T(8,128)(2,1)S(1)} %collective-permute-done.15.refs_9_.came), channel_id=1, source_target_pairs={{0,1},{1,0},{2,3},{3,2},{4,5},{5,4},{6,7},{7,6},{8,9},{9,8},{10,11... | collective-permute-start | bytes 98312 | tf_op jit(solution)/shard_map/ppermute | solution.py:952
  79.1 13.5 %collective-permute-start.20 = (bf16[16,1024]{1,0:T(8,128)(2,1)S(1)}, bf16[16,1024]{1,0:T(8,128)(2,1)S(1)}, u32[]{:S(2)}, u32[]{:S(2)}) collective-permute-start(bf16[16,1024]{1,0:T(8,128)(2,1)S(1)} %collective-permute-done.18.refs_8_), channel_id=1, source_target_pairs={{0,1},{1,0},{2,3},{3,2},{4,5},{5,4},{6,7},{7,6},{8,9},{9,8},{10,11... | collective-permute-start | bytes 98312 | tf_op jit(solution)/shard_map/ppermute | solution.py:952
  95.5 27.9 %copy-start.3 = (bf16[512,1024]{1,0:T(8,128)(2,1)S(1)}, bf16[512,1024]{1,0:T(8,128)(2,1)}, u32[]{:S(2)}) copy-start(bf16[512,1024]{1,0:T(8,128)(2,1)} %wo.1) | copy-start | bytes 3145732
  124.8 5.5 %collective-permute-start.23 = (bf16[528,256]{1,0:T(8,128)(2,1)S(1)}, bf16[528,256]{1,0:T(8,128)(2,1)S(1)}, u32[]{:S(2)}, u32[]{:S(2)}) collective-permute-start(bf16[528,256]{1,0:T(8,128)(2,1)S(1)} %get-tuple-element.185), channel_id=1, source_target_pairs={{0,1},{1,0},{2,3},{3,2},{4,5},{5,4},{6,7},{7,6},{8,9},{9,8},{10,11... | collective-permute-start | bytes 811016 | tf_op jit(solution)/shard_map/ppermute | solution.py:952
  128.9 1.9 %collective-permute-start.22 = (bf16[528,256]{1,0:T(8,128)(2,1)S(1)}, bf16[528,256]{1,0:T(8,128)(2,1)S(1)}, u32[]{:S(2)}, u32[]{:S(2)}) collective-permute-start(bf16[528,256]{1,0:T(8,128)(2,1)S(1)} %get-tuple-element.181), channel_id=1, source_target_pairs={{0,1},{1,0},{2,3},{3,2},{4,5},{5,4},{6,7},{7,6},{8,9},{9,8},{10,11... | collective-permute-start | bytes 811016 | tf_op jit(solution)/shard_map/ppermute | solution.py:952
  129.7 2.4 %collective-permute-start.21 = (bf16[1024,256]{1,0:T(8,128)(2,1)S(1)}, bf16[1024,256]{1,0:T(8,128)(2,1)S(1)}, u32[]{:S(2)}, u32[]{:S(2)}) collective-permute-start(bf16[1024,256]{1,0:T(8,128)(2,1)S(1)} %get-tuple-element.178), channel_id=1, source_target_pairs={{0,1},{1,0},{2,3},{3,2},{4,5},{5,4},{6,7},{7,6},{8,9},{9,8},{10,11... | collective-permute-start | bytes 1572872 | tf_op jit(solution)/shard_map/ppermute | solution.py:952
  130.4 8.1 %collective-permute-start.24 = (bf16[528,256]{1,0:T(8,128)(2,1)S(1)}, bf16[528,256]{1,0:T(8,128)(2,1)S(1)}, u32[]{:S(2)}, u32[]{:S(2)}) collective-permute-start(bf16[528,256]{1,0:T(8,128)(2,1)S(1)} %get-tuple-element.186), channel_id=1, source_target_pairs={{0,2},{1,3},{2,0},{3,1},{4,6},{5,7},{6,4},{7,5},{8,10},{9,11},{10,... | collective-permute-start | bytes 811016 | tf_op jit(solution)/shard_map/ppermute | solution.py:952
  130.9 13.3 %collective-permute-start.25 = (bf16[528,256]{1,0:T(8,128)(2,1)S(1)}, bf16[528,256]{1,0:T(8,128)(2,1)S(1)}, u32[]{:S(2)}, u32[]{:S(2)}) collective-permute-start(bf16[528,256]{1,0:T(8,128)(2,1)S(1)} %get-tuple-element.188), channel_id=1, source_target_pairs={{0,2},{1,3},{2,0},{3,1},{4,6},{5,7},{6,4},{7,5},{8,10},{9,11},{10,... | collective-permute-start | bytes 811016 | tf_op jit(solution)/shard_map/ppermute | solution.py:952

commit v8 on v7

--- a/solution.py
+++ b/solution.py
@@ -593,7 +593,8 @@
 def fine_main(at, blocks, *args):
     length = blocks * BLK
     rows = [pl.BlockSpec((BLK, n), lambda i: (i, 0)) for n in (512, 512, 256)]
-    weights = []
+    weights, carried = [], [sds((256, 512)), sds((8, 128))]
+    last = at + blocks == 4
     if at == 0:
         weights = [
             sds((256, 512), BF), sds((256, 512), BF), sds((8, 256)), sds((8, 4, 128)),
@@ -603,13 +604,10 @@
         lambda *refs: fine_main_kernel(at, *refs),
         grid=(blocks,),
         in_specs=[VM] * len(args),
-        out_specs=rows + [VM] * (2 + len(weights)),
-        out_shape=[
-            sds((length, 512)), sds((length, 512)), sds((length, 256), BF),
-            sds((256, 512)), sds((8, 128)),
-        ]
-        + weights,
-        scratch_shapes=SCAN_SCRATCH,
+        out_specs=rows + [VM] * (0 if last else 2 + len(weights)),
+        out_shape=[sds((length, 512)), sds((length, 512)), sds((length, 256), BF)]
+        + ([] if last else carried + weights),
+        scratch_shapes=[pltpu.VMEM(c.shape, F32) for c in carried if last] + SCAN_SCRATCH,
         compiler_params=few(16),
     )(*args)
 
@@ -918,33 +916,39 @@
     )(ks, square_sums, came)
 
 
-def final_kernel(share, share_1, share_2, kk, sk, sum_a, far_a, sum_b, far_b, out):
+def final_kernel(side, *refs):
+    shares, (kk, sk, sums, far), refs = refs[: side + 1], refs[side + 1 : side + 5], refs[side + 5 :]
+    out, rows_v, sem = refs[-3:]
     y, c = lax.axis_index("y"), lax.axis_index("c")
     pick = jnp.where(iota((32, 256), 0) % 8 == 0, 1.0, 0.0).astype(BF)
-    for side, (half, sums, far) in enumerate(((y, sum_a, far_a), (1 - y, sum_b, far_b))):
-        total = sums[...] + rows_sum(far)
-        factor = lax.rsqrt(total / 2048.0 + EPSILON)
-        for b in range(2):
-            rows = slice(b * BLK, (b + 1) * BLK)
-            here = slice(side * 512 + b * BLK, side * 512 + (b + 1) * BLK)
-            spread = dot(parts(factor[:, rows]), pick, TN)
-            total = kk[here].astype(F32) + sk[here].astype(F32) + far[rows].astype(F32)
-            if side == 0:
-                own = share[rows].astype(F32)
-            else:
-                own = jnp.where(c == b, share_1[...].astype(F32), share_2[...].astype(F32))
-            at = pl.multiple_of(half * 512 + b * BLK, BLK)
-            out[pl.ds(at, BLK), :] = (own + total * spread).astype(BF)
-
-
-def final(*args):
-    return pl.pallas_call(
-        final_kernel,
-        in_specs=[VM] * 9,
-        out_specs=VM,
-        out_shape=sds((1024, 256), BF),
-        compiler_params=few(8),
-        name="final",
+    factor = lax.rsqrt((sums[...] + rows_sum(far)) / 2048.0 + EPSILON)
+    for b in range(2):
+        rows = slice(b * BLK, (b + 1) * BLK)
+        here = slice(side * 512 + b * BLK, side * 512 + (b + 1) * BLK)
+        spread = dot(parts(factor[:, rows]), pick, TN)
+        total = kk[here].astype(F32) + sk[here].astype(F32) + far[rows].astype(F32)
+        if side == 0:
+            own = shares[0][rows].astype(F32)
+        else:
+            own = jnp.where(c == b, shares[0][...].astype(F32), shares[1][...].astype(F32))
+        rows_v[rows, :] = (own + total * spread).astype(BF)
+    half = y if side == 0 else 1 - y
+    at = pl.multiple_of(half * 512, 512)
+    copy = pltpu.make_async_copy(rows_v, out.at[pl.ds(at, 512)], sem)
+    copy.start()
+    copy.wait()
+
+
+def final(side, *args):
+    into = len(args) - (side + 5)
+    return pl.pallas_call(
+        lambda *refs: final_kernel(side, *refs),
+        in_specs=[VM] * (side + 5) + [HBM] * into,
+        out_specs=HBM,
+        out_shape=pltpu.HBM((1024, 256), BF),
+        input_output_aliases={side + 5: 0} if into else {},
+        scratch_shapes=[pltpu.VMEM((512, 256), BF), pltpu.SemaphoreType.DMA],
+        compiler_params=few(6),
     )(*args)
 
 
@@ -1031,7 +1035,8 @@
     went_f = swapped(went_f, 2)
     kk, sk = close_rest(gn, gn_f, coarse_output)
     sk = swapped(sk, 1)
-    return final(share, share_1, share_2, kk, sk, sums, went_f, sums_f, went)
+    out = final(1, share_1, share_2, kk, sk, sums_f, went)
+    return final(0, share, kk, sk, sums, went_f, out)
 
 
 def solution(mesh):

time: 146 us -> 145 us (level)
  no operation moved by 1% of the time
where the time goes in v8:
time: 145 us
  starting transfers between devices  40.9 us (28%)
  Pallas kernels  38.9 us (27%)
  waiting for transfers between devices  36.5 us (25%)
  blocking collectives  27.8 us (19%)
    ppermute x26, starting transfers between devices, passed(): return lax.ppermute(x, axes, pairs)  40.9 us
    ppermute x26, waiting for transfers between devices, passed(): return lax.ppermute(x, axes, pairs)  36.5 us
    all_to_all x1, blocking collectives, shards(): got = lax.all_to_all(message, SEQ, split_axis=0, concat_axis=0, tiled=True)  13.9 us
    all_to_all x1, blocking collectives, shards(): lax.all_to_all(prefix(got), SEQ, split_axis=0, concat_axis=0, tiled=True)  13.9 us
    pallas_call x3, Pallas kernels, coarse_main(): pl.pallas_call(lambda *refs: coarse_main_kernel(kind, blocks, *refs), gri...  11.5 us
    pallas_call x3, Pallas kernels, fine_main(): pl.pallas_call(lambda *refs: fine_main_kernel(at, *refs), grid=(blocks,),...  8.22 us
    pallas_call x1, Pallas kernels, fine_states(): pl.pallas_call(later_chunks_kernel, grid=(3,), in_specs=[HBM] + [VM] * 5,...  6.42 us
  transfers between devices with their start and end apart: 26, of which 10 were waited for; matrix products, arithmetic and copies ran while one was open for 0% of the time, Pallas kernels for 19%

profile of v8, /device:TPU:1, one launch (start us, length us, event | category | flops | bytes accessed | tf_op | source)
XLA Modules:
  0.0 144.6 jit_solution(1171126143361480634)
XLA Ops:
  0.0 1.4 pack.1
  1.4 2.1 %collective-permute-start.3 = (bf16[16,256]{1,0:T(8,128)(2,1)S(1)}, bf16[16,256]{1,0:T(8,128)(2,1)S(1)}, u32[]{:S(2)}, u32[]{:S(2)}) collective-permute-start(bf16[16,256]{1,0:T(8,128)(2,1)S(1)} %get-tuple-element.107), channel_id=1, source_target_pairs={{0,4},{4,8},{8,12},{12,16},{16,20},{20,24},{24,28},{28,32},{32,36}... | collective-permute-start | bytes 24584 | tf_op jit(solution)/shard_map/ppermute | solution.py:956
  3.5 6.4 %later_chunks.1 = (f32[3,256,128]{2,1,0:T(8,128)S(1)}, f32[3,8,128]{2,1,0:T(8,128)S(1)}, bf16[1024,256]{1,0:T(8,128)(2,1)S(1)}, bf16[1024,256]{1,0:T(8,128)(2,1)S(1)}, bf16[16,256]{1,0:T(8,128)(2,1)S(1)}) custom-call(bf16[4096,256]{1,0:T(8,128)(2,1)} %tokens.3, bf16[1040,256]{1,0:T(8,128)(2,1)S(1)} %get-tuple-element.101.chunk_0, ...), custom_call_target="tpu_custom_call" | custom-call | tf_op jit(solution)/shard_map/later_chunks/pallas_call | solution.py:358
  9.9 2.0 %collective-permute-done.3.refs_8_.rim = bf16[16,256]{1,0:T(8,128)(2,1)S(1)} collective-permute-done((bf16[16,256]{1,0:T(8,128)(2,1)S(1)}, bf16[16,256]{1,0:T(8,128)(2,1)S(1)}, u32[]{:S(2)}, u32[]{:S(2)}) %collective-permute-start.3) | collective-permute-done | bytes 8224 | tf_op jit(solution)/shard_map/ppermute | solution.py:956
  11.9 2.1 %first_chunk.1 = (f32[256,128]{1,0:T(8,128)S(1)}, f32[8,128]{1,0:T(8,128)S(1)}, f32[256,128]{1,0:T(8,128)S(1)}, f32[8,128]{1,0:T(8,128)S(1)}, bf16[272,128]{1,0:T(8,128)(2,1)S(1)}) custom-call(bf16[1024,256]{1,0:T(8,128)(2,1)S(1)} %get-tuple-element.128.x, bf16[16,256]{1,0:T(8,128)(2,1)S(1)} %collective-permute-done.3.refs_8_.rim, ...), custom_call_target="tpu_custom_call" | custom-call | tf_op jit(solution)/shard_map/first_chunk/pallas_call | solution.py:376
  14.0 2.2 %collective-permute-start.6 = (bf16[272,128]{1,0:T(8,128)(2,1)S(1)}, bf16[272,128]{1,0:T(8,128)(2,1)S(1)}, u32[]{:S(2)}, u32[]{:S(2)}) collective-permute-start(bf16[272,128]{1,0:T(8,128)(2,1)S(1)} %get-tuple-element.133), channel_id=1, source_target_pairs={{0,12},{4,0},{8,4},{12,8},{1,13},{5,1},{9,5},{13,9},{2,14},{6,2},{... | collective-permute-start | bytes 208904 | tf_op jit(solution)/shard_map/ppermute | solution.py:956
  16.2 0.7 collective-permute-start.4
  16.9 1.8 %collective-permute-start.2 = (bf16[416,256]{1,0:T(8,128)(2,1)S(1)}, bf16[416,256]{1,0:T(8,128)(2,1)S(1)}, u32[]{:S(2)}, u32[]{:S(2)}) collective-permute-start(bf16[416,256]{1,0:T(8,128)(2,1)S(1)} %get-tuple-element.103.pack.refs_4_.refs_14_), channel_id=1, source_target_pairs={{0,3},{1,2},{2,1},{3,0},{4,7},{5,6},{6,5},{7,4},{8,11},{9,10},{10,... | collective-permute-start | bytes 638984 | tf_op jit(solution)/shard_map/ppermute | solution.py:956
  18.7 2.3 %collective-permute-done.5.refs_3_ = bf16[272,128]{1,0:T(8,128)(2,1)S(1)} collective-permute-done((bf16[272,128]{1,0:T(8,128)(2,1)S(1)}, bf16[272,128]{1,0:T(8,128)(2,1)S(1)}, u32[]{:S(2)}, u32[]{:S(2)}) %collective-permute-start.5) | collective-permute-done | bytes 69664 | tf_op jit(solution)/shard_map/ppermute | solution.py:956
  21.0 0.4 collective-permute-done.4.refs_2_
  21.3 0.1 shard_map.229
  21.5 1.8 %collective-permute-start.7 = (bf16[272,128]{1,0:T(8,128)(2,1)S(1)}, bf16[272,128]{1,0:T(8,128)(2,1)S(1)}, u32[]{:S(2)}, u32[]{:S(2)}) collective-permute-start(bf16[272,128]{1,0:T(8,128)(2,1)S(1)} %get-tuple-element.138), channel_id=1, source_target_pairs={{0,16},{16,0},{1,17},{17,1},{2,18},{18,2},{3,19},{19,3},{4,20},{20... | collective-permute-start | bytes 208904 | tf_op jit(solution)/shard_map/ppermute | solution.py:956
  23.3 1.0 collective-permute-start.1
  24.3 2.9 %collective-permute-start = (bf16[416,256]{1,0:T(8,128)(2,1)S(1)}, bf16[416,256]{1,0:T(8,128)(2,1)S(1)}, u32[]{:S(2)}, u32[]{:S(2)}) collective-permute-start(bf16[416,256]{1,0:T(8,128)(2,1)S(1)} %get-tuple-element.103.pack.refs_4_.refs_14_), channel_id=1, source_target_pairs={{0,1},{1,0},{2,3},{3,2},{4,5},{5,4},{6,7},{7,6},{8,9},{9,8},{10,11... | collective-permute-start | bytes 638984 | tf_op jit(solution)/shard_map/ppermute | solution.py:956
  27.2 0.1 shard_map.230
  27.3 3.2 %collective-permute-start.10 = (bf16[272,128]{1,0:T(8,128)(2,1)S(1)}, bf16[272,128]{1,0:T(8,128)(2,1)S(1)}, u32[]{:S(2)}, u32[]{:S(2)}) collective-permute-start(bf16[272,128]{1,0:T(8,128)(2,1)S(1)} %get-tuple-element.143), channel_id=1, source_target_pairs={{0,96},{32,0},{64,32},{96,64},{1,97},{33,1},{65,33},{97,65},{2,98}... | collective-permute-start | bytes 208904 | tf_op jit(solution)/shard_map/ppermute | solution.py:956
  30.5 0.3 collective-permute-start.9
  30.8 1.0 collective-permute-done.10.r3
  31.8 0.6 collective-permute-start.8
  32.4 2.7 %collective-permute-done.9.r2 = bf16[272,128]{1,0:T(8,128)(2,1)S(1)} collective-permute-done((bf16[272,128]{1,0:T(8,128)(2,1)S(1)}, bf16[272,128]{1,0:T(8,128)(2,1)S(1)}, u32[]{:S(2)}, u32[]{:S(2)}) %collective-permute-start.9) | collective-permute-done | bytes 69664 | tf_op jit(solution)/shard_map/ppermute | solution.py:956
  35.1 1.4 collective-permute-done.8.r1
  36.5 0.1 chain_last.1
  36.7 5.8 %collective-permute-start.11 = (bf16[256,128]{1,0:T(8,128)(2,1)S(1)}, bf16[256,128]{1,0:T(8,128)(2,1)S(1)}, u32[]{:S(2)}, u32[]{:S(2)}) collective-permute-start(bf16[256,128]{1,0:T(8,128)(2,1)S(1)} %get-tuple-element.147), channel_id=1, source_target_pairs={{0,1},{1,0},{2,3},{3,2},{4,5},{5,4},{6,7},{7,6},{8,9},{9,8},{10,11... | collective-permute-start | bytes 196616 | tf_op jit(solution)/shard_map/ppermute | solution.py:956
  42.5 0.4 collective-permute-start.12
  42.9 1.3 collective-permute-start.13
  44.2 4.2 %shard_map.226 = (f32[512,512]{1,0:T(8,128)S(1)}, f32[512,512]{1,0:T(8,128)S(1)}, bf16[512,256]{1,0:T(8,128)(2,1)S(1)}, f32[256,512]{1,0:T(8,128)S(1)}, f32[8,12...) custom-call(bf16[1024,256]{1,0:T(8,128)(2,1)S(1)} %get-tuple-element, ...), custom_call_target="tpu_custom_call" | custom-call | tf_op jit(solution)/shard_map/pallas_call | solution.py:603
  48.5 0.0 copy-start.4
  48.5 2.0 %shard_map.227 = (f32[256,512]{1,0:T(8,128)S(1)}, f32[256,512]{1,0:T(8,128)S(1)}, bf16[256,256]{1,0:T(8,128)(2,1)S(1)}, f32[256,512]{1,0:T(8,128)S(1)}, f32[8,128]{1,0:T(8,128)S(1)}) custom-call(bf16[1024,256]{1,0:T(8,128)(2,1)S(1)} %get-tuple-element.106.refs_0_.refs_9_, f32[1,256]{1,0:T(1,128)S(1)} %get-tuple-element.102.gain.refs_1_, ...), custom_call_target="tpu_custom_call" | custom-call | tf_op jit(solution)/shard_map/pallas_call | solution.py:603
  50.5 2.0 %shard_map.228 = (f32[256,512]{1,0:T(8,128)S(1)}, f32[256,512]{1,0:T(8,128)S(1)}, bf16[256,256]{1,0:T(8,128)(2,1)S(1)}) custom-call(bf16[1024,256]{1,0:T(8,128)(2,1)S(1)} %get-tuple-element.106.refs_0_.refs_9_, f32[1,256]{1,0:T(1,128)S(1)} %get-tuple-element.102.gain.refs_1_, bf16[256,512]{1,0:T(8,128)(2,1)S(1)} %get-tuple-element.104.scans.refs_2_, ...), custom_call_target="tpu_custom_call" | custom-call | tf_op jit(solution)/shard_map/pallas_call | solution.py:603
  52.5 0.0 copy-start
  52.6 0.0 copy-start.1
  52.6 0.0 copy-start.2
  52.6 2.3 %fine_close.1 = (bf16[256,1024]{1,0:T(8,128)(2,1)S(1)}, bf16[16,1024]{1,0:T(8,128)(2,1)S(1)}) custom-call(f32[512,512]{1,0:T(8,128)S(1)} %get-tuple-element.109.refs_0_, f32[256,512]{1,0:T(8,128)S(1)} %get-tuple-element.118.refs_1_, f32[256,512]{1,0:T(8,128)S(1)} %get-tuple-element.121.refs_2_, f32[512,512]{1,0:T(8,128)S(1)} %get-tuple-element.122.refs_3_, ...), custom_call_target="tpu_custom_call" | custom-call | tf_op jit(solution)/shard_map/fine_close/pallas_call | solution.py:650
  54.9 0.5 collective-permute-start.17
  55.4 0.4 collective-permute-start.14
  55.8 12.5 %collective-permute-done.17.refs_7_ = bf16[256,1024]{1,0:T(8,128)(2,1)S(1)} collective-permute-done((bf16[256,1024]{1,0:T(8,128)(2,1)S(1)}, bf16[256,1024]{1,0:T(8,128)(2,1)S(1)}, u32[]{:S(2)}, u32[]{:S(2)}) %collective-permute-start.17) | collective-permute-done | bytes 524320 | tf_op jit(solution)/shard_map/ppermute | solution.py:956
  68.3 1.0 collective-permute-start.18
  69.3 0.3 collective-permute-start.15
  69.6 3.1 %collective-permute-done.15.refs_9_.came = bf16[16,1024]{1,0:T(8,128)(2,1)S(1)} collective-permute-done((bf16[16,1024]{1,0:T(8,128)(2,1)S(1)}, bf16[16,1024]{1,0:T(8,128)(2,1)S(1)}, u32[]{:S(2)}, u32[]{:S(2)}) %collective-permute-start.15) | collective-permute-done | bytes 32800 | tf_op jit(solution)/shard_map/ppermute | solution.py:956
  72.7 1.4 collective-permute-start.19
  74.1 4.2 %collective-permute-start.16 = (bf16[16,1024]{1,0:T(8,128)(2,1)S(1)}, bf16[16,1024]{1,0:T(8,128)(2,1)S(1)}, u32[]{:S(2)}, u32[]{:S(2)}) collective-permute-start(bf16[16,1024]{1,0:T(8,128)(2,1)S(1)} %collective-permute-done.15.refs_9_.came), channel_id=1, source_target_pairs={{0,1},{1,0},{2,3},{3,2},{4,5},{5,4},{6,7},{7,6},{8,9},{9,8},{10,11... | collective-permute-start | bytes 98312 | tf_op jit(solution)/shard_map/ppermute | solution.py:956
  78.3 3.8 %collective-permute-start.20 = (bf16[16,1024]{1,0:T(8,128)(2,1)S(1)}, bf16[16,1024]{1,0:T(8,128)(2,1)S(1)}, u32[]{:S(2)}, u32[]{:S(2)}) collective-permute-start(bf16[16,1024]{1,0:T(8,128)(2,1)S(1)} %collective-permute-done.19.refs_8_), channel_id=1, source_target_pairs={{0,1},{1,0},{2,3},{3,2},{4,5},{5,4},{6,7},{7,6},{8,9},{9,8},{10,11... | collective-permute-start | bytes 98312 | tf_op jit(solution)/shard_map/ppermute | solution.py:956
  82.1 1.0 coarse_params.1
  83.1 5.9 %shard_map.231 = (f32[512,512]{1,0:T(8,128)S(1)}, f32[512,512]{1,0:T(8,128)S(1)}, bf16[512,256]{1,0:T(8,128)(2,1)S(1)}, bf16[512,256]{1,0:T(8,128)(2,1)S(1)}, f3...) custom-call(f32[1,1024]{1,0:T(1,128)S(1)} %get-tuple-element.97.refs_0_, bf16[1024,512]{1,0:T(8,128)(2,1)S(1)} %copy-done, ...), custom_call_target="tpu_custom_call" | custom-call | tf_op jit(solution)/shard_map/pallas_call | solution.py:755
  89.0 2.8 %shard_map.232 = (f32[256,512]{1,0:T(8,128)S(1)}, f32[256,512]{1,0:T(8,128)S(1)}, bf16[256,256]{1,0:T(8,128)(2,1)S(1)}, bf16[256,256]{1,0:T(8,128)(2,1)S(1)}, f3...) custom-call(f32[1,1024]{1,0:T(1,128)S(1)} %get-tuple-element.97.refs_0_, ...), custom_call_target="tpu_custom_call" | custom-call | tf_op jit(solution)/shard_map/pallas_call | solution.py:755
  91.8 2.9 %shard_map.233 = (f32[256,512]{1,0:T(8,128)S(1)}, f32[256,512]{1,0:T(8,128)S(1)}, bf16[256,256]{1,0:T(8,128)(2,1)S(1)}, bf16[256,256]{1,0:T(8,128)(2,1)S(1)}, f3...) custom-call(f32[1,1024]{1,0:T(1,128)S(1)} %get-tuple-element.97.refs, ...), custom_call_target="tpu_custom_call" | custom-call | tf_op jit(solution)/shard_map/pallas_call | solution.py:755
  94.7 0.0 copy-start.3
  94.7 13.9 %all_to_all.10.got = bf16[32,24,256]{2,1,0:T(8,128)(2,1)S(1)} all-to-all(bf16[32,24,256]{2,1,0:T(8,128)(2,1)S(1)} %get-tuple-element.161), channel_id=1, replica_groups=mesh['z'=4,'u'=2,'x'=4,'y'=2,'c'=2] {'z','u','x'}, dimensions={0} | all-to-all | bytes 786432 | tf_op jit(solution)/shard_map/all_to_all | solution.py:1022
  108.6 0.1 prefix.1
  108.7 13.9 %all_to_all.11.refs_3_.refs_6_ = bf16[32,16,256]{2,1,0:T(8,128)(2,1)S(1)} all-to-all(bf16[32,16,256]{2,1,0:T(8,128)(2,1)S(1)} %prefix.1), channel_id=1, replica_groups=mesh['z'=4,'u'=2,'x'=4,'y'=2,'c'=2] {'z','u','x'}, dimensions={0} | all-to-all | bytes 524288 | tf_op jit(solution)/shard_map/all_to_all | solution.py:1023
  122.6 1.2 coarse_close_near.1
  123.8 2.9 %collective-permute-start.22 = (bf16[528,256]{1,0:T(8,128)(2,1)S(1)}, bf16[528,256]{1,0:T(8,128)(2,1)S(1)}, u32[]{:S(2)}, u32[]{:S(2)}) collective-permute-start(bf16[528,256]{1,0:T(8,128)(2,1)S(1)} %get-tuple-element.179), channel_id=1, source_target_pairs={{0,1},{1,0},{2,3},{3,2},{4,5},{5,4},{6,7},{7,6},{8,9},{9,8},{10,11... | collective-permute-start | bytes 811016 | tf_op jit(solution)/shard_map/ppermute | solution.py:956
  126.7 1.3 coarse_close_far.1
  128.0 0.1 collective-permute-start.23
  128.1 0.7 close_rest.1
  128.8 0.6 collective-permute-start.21
  129.4 0.1 shard_map.234
  129.5 0.4 collective-permute-start.25
  129.9 0.1 shard_map.235
  130.0 1.2 collective-permute-start.24
  131.2 6.4 %collective-permute-done.25.refs_5_ = bf16[528,256]{1,0:T(8,128)(2,1)S(1)} collective-permute-done((bf16[528,256]{1,0:T(8,128)(2,1)S(1)}, bf16[528,256]{1,0:T(8,128)(2,1)S(1)}, u32[]{:S(2)}, u32[]{:S(2)}) %collective-permute-start.25) | collective-permute-done | bytes 270368 | tf_op jit(solution)/shard_map/ppermute | solution.py:956
  137.6 1.0 shard_map.236.refs_5_
  138.6 4.8 %collective-permute-done.24.refs_4_ = bf16[528,256]{1,0:T(8,128)(2,1)S(1)} collective-permute-done((bf16[528,256]{1,0:T(8,128)(2,1)S(1)}, bf16[528,256]{1,0:T(8,128)(2,1)S(1)}, u32[]{:S(2)}, u32[]{:S(2)}) %collective-permute-start.24) | collective-permute-done | bytes 270368 | tf_op jit(solution)/shard_map/ppermute | solution.py:956
  143.4 1.0 shard_map.237
  (23 shorter events, 0.1 us)
Async XLA Ops:
  1.4 10.5 %collective-permute-start.3 = (bf16[16,256]{1,0:T(8,128)(2,1)S(1)}, bf16[16,256]{1,0:T(8,128)(2,1)S(1)}, u32[]{:S(2)}, u32[]{:S(2)}) collective-permute-start(bf16[16,256]{1,0:T(8,128)(2,1)S(1)} %get-tuple-element.107), channel_id=1, source_target_pairs={{0,4},{4,8},{8,12},{12,16},{16,20},{20,24},{24,28},{28,32},{32,36}... | collective-permute-start | bytes 24584 | tf_op jit(solution)/shard_map/ppermute | solution.py:956
  14.0 4.7 %collective-permute-start.6 = (bf16[272,128]{1,0:T(8,128)(2,1)S(1)}, bf16[272,128]{1,0:T(8,128)(2,1)S(1)}, u32[]{:S(2)}, u32[]{:S(2)}) collective-permute-start(bf16[272,128]{1,0:T(8,128)(2,1)S(1)} %get-tuple-element.133), channel_id=1, source_target_pairs={{0,12},{4,0},{8,4},{12,8},{1,13},{5,1},{9,5},{13,9},{2,14},{6,2},{... | collective-permute-start | bytes 208904 | tf_op jit(solution)/shard_map/ppermute | solution.py:956
  16.2 4.8 %collective-permute-start.5 = (bf16[272,128]{1,0:T(8,128)(2,1)S(1)}, bf16[272,128]{1,0:T(8,128)(2,1)S(1)}, u32[]{:S(2)}, u32[]{:S(2)}) collective-permute-start(bf16[272,128]{1,0:T(8,128)(2,1)S(1)} %get-tuple-element.133), channel_id=1, source_target_pairs={{0,8},{4,12},{8,0},{12,4},{1,9},{5,13},{9,1},{13,5},{2,10},{6,14},... | collective-permute-start | bytes 208904 | tf_op jit(solution)/shard_map/ppermute | solution.py:956
  16.2 5.1 %collective-permute-start.4 = (bf16[272,128]{1,0:T(8,128)(2,1)S(1)}, bf16[272,128]{1,0:T(8,128)(2,1)S(1)}, u32[]{:S(2)}, u32[]{:S(2)}) collective-permute-start(bf16[272,128]{1,0:T(8,128)(2,1)S(1)} %get-tuple-element.133), channel_id=1, source_target_pairs={{0,4},{4,8},{8,12},{12,0},{1,5},{5,9},{9,13},{13,1},{2,6},{6,10},{... | collective-permute-start | bytes 208904 | tf_op jit(solution)/shard_map/ppermute | solution.py:956
  16.9 26.0 %collective-permute-start.2 = (bf16[416,256]{1,0:T(8,128)(2,1)S(1)}, bf16[416,256]{1,0:T(8,128)(2,1)S(1)}, u32[]{:S(2)}, u32[]{:S(2)}) collective-permute-start(bf16[416,256]{1,0:T(8,128)(2,1)S(1)} %get-tuple-element.103.pack.refs_4_.refs_14_), channel_id=1, source_target_pairs={{0,3},{1,2},{2,1},{3,0},{4,7},{5,6},{6,5},{7,4},{8,11},{9,10},{10,... | collective-permute-start | bytes 638984 | tf_op jit(solution)/shard_map/ppermute | solution.py:956
  21.5 5.7 %collective-permute-start.7 = (bf16[272,128]{1,0:T(8,128)(2,1)S(1)}, bf16[272,128]{1,0:T(8,128)(2,1)S(1)}, u32[]{:S(2)}, u32[]{:S(2)}) collective-permute-start(bf16[272,128]{1,0:T(8,128)(2,1)S(1)} %get-tuple-element.138), channel_id=1, source_target_pairs={{0,16},{16,0},{1,17},{17,1},{2,18},{18,2},{3,19},{19,3},{4,20},{20... | collective-permute-start | bytes 208904 | tf_op jit(solution)/shard_map/ppermute | solution.py:956
  23.3 21.0 %collective-permute-start.1 = (bf16[416,256]{1,0:T(8,128)(2,1)S(1)}, bf16[416,256]{1,0:T(8,128)(2,1)S(1)}, u32[]{:S(2)}, u32[]{:S(2)}) collective-permute-start(bf16[416,256]{1,0:T(8,128)(2,1)S(1)} %get-tuple-element.103.pack.refs_4_.refs_14_), channel_id=1, source_target_pairs={{0,2},{1,3},{2,0},{3,1},{4,6},{5,7},{6,4},{7,5},{8,10},{9,11},{10,... | collective-permute-start | bytes 638984 | tf_op jit(solution)/shard_map/ppermute | solution.py:956
  24.3 20.0 %collective-permute-start = (bf16[416,256]{1,0:T(8,128)(2,1)S(1)}, bf16[416,256]{1,0:T(8,128)(2,1)S(1)}, u32[]{:S(2)}, u32[]{:S(2)}) collective-permute-start(bf16[416,256]{1,0:T(8,128)(2,1)S(1)} %get-tuple-element.103.pack.refs_4_.refs_14_), channel_id=1, source_target_pairs={{0,1},{1,0},{2,3},{3,2},{4,5},{5,4},{6,7},{7,6},{8,9},{9,8},{10,11... | collective-permute-start | bytes 638984 | tf_op jit(solution)/shard_map/ppermute | solution.py:956
  27.3 4.6 %collective-permute-start.10 = (bf16[272,128]{1,0:T(8,128)(2,1)S(1)}, bf16[272,128]{1,0:T(8,128)(2,1)S(1)}, u32[]{:S(2)}, u32[]{:S(2)}) collective-permute-start(bf16[272,128]{1,0:T(8,128)(2,1)S(1)} %get-tuple-element.143), channel_id=1, source_target_pairs={{0,96},{32,0},{64,32},{96,64},{1,97},{33,1},{65,33},{97,65},{2,98}... | collective-permute-start | bytes 208904 | tf_op jit(solution)/shard_map/ppermute | solution.py:956
  30.5 4.7 %collective-permute-start.9 = (bf16[272,128]{1,0:T(8,128)(2,1)S(1)}, bf16[272,128]{1,0:T(8,128)(2,1)S(1)}, u32[]{:S(2)}, u32[]{:S(2)}) collective-permute-start(bf16[272,128]{1,0:T(8,128)(2,1)S(1)} %get-tuple-element.143), channel_id=1, source_target_pairs={{0,64},{32,96},{64,0},{96,32},{1,65},{33,97},{65,1},{97,33},{2,66}... | collective-permute-start | bytes 208904 | tf_op jit(solution)/shard_map/ppermute | solution.py:956
  31.8 4.7 %collective-permute-start.8 = (bf16[272,128]{1,0:T(8,128)(2,1)S(1)}, bf16[272,128]{1,0:T(8,128)(2,1)S(1)}, u32[]{:S(2)}, u32[]{:S(2)}) collective-permute-start(bf16[272,128]{1,0:T(8,128)(2,1)S(1)} %get-tuple-element.143), channel_id=1, source_target_pairs={{0,32},{32,64},{64,96},{96,0},{1,33},{33,65},{65,97},{97,1},{2,34}... | collective-permute-start | bytes 208904 | tf_op jit(solution)/shard_map/ppermute | solution.py:956
  36.7 15.8 %collective-permute-start.11 = (bf16[256,128]{1,0:T(8,128)(2,1)S(1)}, bf16[256,128]{1,0:T(8,128)(2,1)S(1)}, u32[]{:S(2)}, u32[]{:S(2)}) collective-permute-start(bf16[256,128]{1,0:T(8,128)(2,1)S(1)} %get-tuple-element.147), channel_id=1, source_target_pairs={{0,1},{1,0},{2,3},{3,2},{4,5},{5,4},{6,7},{7,6},{8,9},{9,8},{10,11... | collective-permute-start | bytes 196616 | tf_op jit(solution)/shard_map/ppermute | solution.py:956
  42.5 10.0 %collective-permute-start.12 = (bf16[256,128]{1,0:T(8,128)(2,1)S(1)}, bf16[256,128]{1,0:T(8,128)(2,1)S(1)}, u32[]{:S(2)}, u32[]{:S(2)}) collective-permute-start(bf16[256,128]{1,0:T(8,128)(2,1)S(1)} %get-tuple-element.148), channel_id=1, source_target_pairs={{0,2},{1,3},{2,0},{3,1},{4,6},{5,7},{6,4},{7,5},{8,10},{9,11},{10,... | collective-permute-start | bytes 196616 | tf_op jit(solution)/shard_map/ppermute | solution.py:956
  42.9 9.6 %collective-permute-start.13 = (bf16[256,128]{1,0:T(8,128)(2,1)S(1)}, bf16[256,128]{1,0:T(8,128)(2,1)S(1)}, u32[]{:S(2)}, u32[]{:S(2)}) collective-permute-start(bf16[256,128]{1,0:T(8,128)(2,1)S(1)} %get-tuple-element.149), channel_id=1, source_target_pairs={{0,3},{1,2},{2,1},{3,0},{4,7},{5,6},{6,5},{7,4},{8,11},{9,10},{10,... | collective-permute-start | bytes 196616 | tf_op jit(solution)/shard_map/ppermute | solution.py:956
  48.5 4.1 %copy-start.4 = (bf16[1024,1024]{1,0:T(8,128)(2,1)S(1)}, bf16[1024,1024]{1,0:T(8,128)(2,1)}, u32[]{:S(2)}) copy-start(bf16[1024,1024]{1,0:T(8,128)(2,1)} %refs_18_.1) | copy-start | bytes 6291460
  52.5 30.5 %copy-start = (bf16[1024,512]{1,0:T(8,128)(2,1)S(1)}, bf16[1024,512]{1,0:T(8,128)(2,1)}, u32[]{:S(2)}) copy-start(bf16[1024,512]{1,0:T(8,128)(2,1)} %refs_1_.5) | copy-start | bytes 3145732
  52.6 30.5 %copy-start.1 = (bf16[1024,512]{1,0:T(8,128)(2,1)S(1)}, bf16[1024,512]{1,0:T(8,128)(2,1)}, u32[]{:S(2)}) copy-start(bf16[1024,512]{1,0:T(8,128)(2,1)} %refs_2_.5) | copy-start | bytes 3145732
  52.6 30.5 %copy-start.2 = (bf16[1024,512]{1,0:T(8,128)(2,1)S(1)}, bf16[1024,512]{1,0:T(8,128)(2,1)}, u32[]{:S(2)}) copy-start(bf16[1024,512]{1,0:T(8,128)(2,1)} %refs_3_.5) | copy-start | bytes 3145732
  54.9 13.4 %collective-permute-start.17 = (bf16[256,1024]{1,0:T(8,128)(2,1)S(1)}, bf16[256,1024]{1,0:T(8,128)(2,1)S(1)}, u32[]{:S(2)}, u32[]{:S(2)}) collective-permute-start(bf16[256,1024]{1,0:T(8,128)(2,1)S(1)} %get-tuple-element.150.refs_7_), channel_id=1, source_target_pairs={{0,2},{1,3},{2,0},{3,1},{4,6},{5,7},{6,4},{7,5},{8,10},{9,11},{10,... | collective-permute-start | bytes 1572872 | tf_op jit(solution)/shard_map/ppermute | solution.py:956
  55.4 17.3 %collective-permute-start.14 = (bf16[256,1024]{1,0:T(8,128)(2,1)S(1)}, bf16[256,1024]{1,0:T(8,128)(2,1)S(1)}, u32[]{:S(2)}, u32[]{:S(2)}) collective-permute-start(bf16[256,1024]{1,0:T(8,128)(2,1)S(1)} %get-tuple-element.150.refs_7_), channel_id=1, source_target_pairs={{0,1},{1,0},{2,3},{3,2},{4,5},{5,4},{6,7},{7,6},{8,9},{9,8},{10,11... | collective-permute-start | bytes 1572872 | tf_op jit(solution)/shard_map/ppermute | solution.py:956
  68.3 23.5 %collective-permute-start.18 = (bf16[256,1024]{1,0:T(8,128)(2,1)S(1)}, bf16[256,1024]{1,0:T(8,128)(2,1)S(1)}, u32[]{:S(2)}, u32[]{:S(2)}) collective-permute-start(bf16[256,1024]{1,0:T(8,128)(2,1)S(1)} %collective-permute-done.17.refs_7_), channel_id=1, source_target_pairs={{0,1},{1,0},{2,3},{3,2},{4,5},{5,4},{6,7},{7,6},{8,9},{9,8},{10,11... | collective-permute-start | bytes 1572872 | tf_op jit(solution)/shard_map/ppermute | solution.py:956
  69.3 3.3 %collective-permute-start.15 = (bf16[16,1024]{1,0:T(8,128)(2,1)S(1)}, bf16[16,1024]{1,0:T(8,128)(2,1)S(1)}, u32[]{:S(2)}, u32[]{:S(2)}) collective-permute-start(bf16[16,1024]{1,0:T(8,128)(2,1)S(1)} %get-tuple-element.151), channel_id=1, source_target_pairs={{0,127},{1,2},{2,1},{3,4},{4,3},{5,6},{6,5},{7,8},{8,7},{9,10},{10... | collective-permute-start | bytes 98312 | tf_op jit(solution)/shard_map/ppermute | solution.py:956
  72.7 5.6 %collective-permute-start.19 = (bf16[16,1024]{1,0:T(8,128)(2,1)S(1)}, bf16[16,1024]{1,0:T(8,128)(2,1)S(1)}, u32[]{:S(2)}, u32[]{:S(2)}) collective-permute-start(bf16[16,1024]{1,0:T(8,128)(2,1)S(1)} %own_rim.1), channel_id=1, source_target_pairs={{0,2},{1,3},{2,0},{3,1},{4,6},{5,7},{6,4},{7,5},{8,10},{9,11},{10,... | collective-permute-start | bytes 98312 | tf_op jit(solution)/shard_map/ppermute | solution.py:956
  74.1 9.0 %collective-permute-start.16 = (bf16[16,1024]{1,0:T(8,128)(2,1)S(1)}, bf16[16,1024]{1,0:T(8,128)(2,1)S(1)}, u32[]{:S(2)}, u32[]{:S(2)}) collective-permute-start(bf16[16,1024]{1,0:T(8,128)(2,1)S(1)} %collective-permute-done.15.refs_9_.came), channel_id=1, source_target_pairs={{0,1},{1,0},{2,3},{3,2},{4,5},{5,4},{6,7},{7,6},{8,9},{9,8},{10,11... | collective-permute-start | bytes 98312 | tf_op jit(solution)/shard_map/ppermute | solution.py:956
  78.3 13.5 %collective-permute-start.20 = (bf16[16,1024]{1,0:T(8,128)(2,1)S(1)}, bf16[16,1024]{1,0:T(8,128)(2,1)S(1)}, u32[]{:S(2)}, u32[]{:S(2)}) collective-permute-start(bf16[16,1024]{1,0:T(8,128)(2,1)S(1)} %collective-permute-done.19.refs_8_), channel_id=1, source_target_pairs={{0,1},{1,0},{2,3},{3,2},{4,5},{5,4},{6,7},{7,6},{8,9},{9,8},{10,11... | collective-permute-start | bytes 98312 | tf_op jit(solution)/shard_map/ppermute | solution.py:956
  94.7 27.9 %copy-start.3 = (bf16[512,1024]{1,0:T(8,128)(2,1)S(1)}, bf16[512,1024]{1,0:T(8,128)(2,1)}, u32[]{:S(2)}) copy-start(bf16[512,1024]{1,0:T(8,128)(2,1)} %wo.1) | copy-start | bytes 3145732
  123.8 5.6 %collective-permute-start.22 = (bf16[528,256]{1,0:T(8,128)(2,1)S(1)}, bf16[528,256]{1,0:T(8,128)(2,1)S(1)}, u32[]{:S(2)}, u32[]{:S(2)}) collective-permute-start(bf16[528,256]{1,0:T(8,128)(2,1)S(1)} %get-tuple-element.179), channel_id=1, source_target_pairs={{0,1},{1,0},{2,3},{3,2},{4,5},{5,4},{6,7},{7,6},{8,9},{9,8},{10,11... | collective-permute-start | bytes 811016 | tf_op jit(solution)/shard_map/ppermute | solution.py:956
  128.0 1.9 %collective-permute-start.23 = (bf16[528,256]{1,0:T(8,128)(2,1)S(1)}, bf16[528,256]{1,0:T(8,128)(2,1)S(1)}, u32[]{:S(2)}, u32[]{:S(2)}) collective-permute-start(bf16[528,256]{1,0:T(8,128)(2,1)S(1)} %get-tuple-element.183), channel_id=1, source_target_pairs={{0,1},{1,0},{2,3},{3,2},{4,5},{5,4},{6,7},{7,6},{8,9},{9,8},{10,11... | collective-permute-start | bytes 811016 | tf_op jit(solution)/shard_map/ppermute | solution.py:956
  128.8 2.4 %collective-permute-start.21 = (bf16[1024,256]{1,0:T(8,128)(2,1)S(1)}, bf16[1024,256]{1,0:T(8,128)(2,1)S(1)}, u32[]{:S(2)}, u32[]{:S(2)}) collective-permute-start(bf16[1024,256]{1,0:T(8,128)(2,1)S(1)} %get-tuple-element.176), channel_id=1, source_target_pairs={{0,1},{1,0},{2,3},{3,2},{4,5},{5,4},{6,7},{7,6},{8,9},{9,8},{10,11... | collective-permute-start | bytes 1572872 | tf_op jit(solution)/shard_map/ppermute | solution.py:956
  129.5 8.1 %collective-permute-start.25 = (bf16[528,256]{1,0:T(8,128)(2,1)S(1)}, bf16[528,256]{1,0:T(8,128)(2,1)S(1)}, u32[]{:S(2)}, u32[]{:S(2)}) collective-permute-start(bf16[528,256]{1,0:T(8,128)(2,1)S(1)} %get-tuple-element.188), channel_id=1, source_target_pairs={{0,2},{1,3},{2,0},{3,1},{4,6},{5,7},{6,4},{7,5},{8,10},{9,11},{10,... | collective-permute-start | bytes 811016 | tf_op jit(solution)/shard_map/ppermute | solution.py:956
  130.0 13.3 %collective-permute-start.24 = (bf16[528,256]{1,0:T(8,128)(2,1)S(1)}, bf16[528,256]{1,0:T(8,128)(2,1)S(1)}, u32[]{:S(2)}, u32[]{:S(2)}) collective-permute-start(bf16[528,256]{1,0:T(8,128)(2,1)S(1)} %get-tuple-element.184), channel_id=1, source_target_pairs={{0,2},{1,3},{2,0},{3,1},{4,6},{5,7},{6,4},{7,5},{8,10},{9,11},{10,... | collective-permute-start | bytes 811016 | tf_op jit(solution)/shard_map/ppermute | solution.py:956
